TPU v7x, 256 devices: a whole 4x4x8 slice. The times are simulated.
256 devices in a mesh: row: 16 (over z_lo, y), col: 16 (over z_hi, x, core).
Axes of the slice: x: 4, y: 4, z: 8 (z_hi: 2, z_lo: 4; z = z_hi * 4 + z_lo), core: 2. Of those that a mesh axis runs over, the one named last changes fastest.
Arguments:
- object_field: float32 [2, 2048, 2048], P(None, 'row', 'col'), may hold values from -5 to 5
- probe: float32 [2, 2, 256, 256], replicated, may hold values from -5 to 5
- amplitudes: float32 [16, 16, 2, 256, 256], P('row', 'col'), may hold values from 0.2 to 2.5
- offsets: int32 [16, 16, 2, 2], P('row', 'col'), may hold values from -128 to 0
Outputs:
- object_out: float32 [2, 2048, 2048], P(None, 'row', 'col')
- probe_out: float32 [2, 2, 256, 256], replicated
Inputs may be any that keep to these rules, and one draw needn't show every extreme that they name: `offsets`: each scan's 256 x 256 window starts at this offset from its own tile's anchor, so it reaches at most 128 pixels into neighbouring tiles.
All inputs are finite; a program needn't handle non-finite values.
Results may differ from a plain program's by a relative error of at most 0.0003.
Values sent between devices are 32-bit elements; how exact they have to be, the bound alone decides.
No kernel may reach another device: no remote copies, remote signals or barrier semaphores. Data moves between devices by JAX's collectives and lax.ppermute only.
A program may use at most 128 MiB of HBM per device.

v0:
```python
import math

import jax
import jax.numpy as jnp
from jax import lax
from jax.sharding import PartitionSpec as P

ITERS = 2


FLOOR = 0.5
OBJECT_STEP = 0.5
OBJECT_REG = 0.5
PROBE_STEP = 1.0
PROBE_REG = 1.0
HIGHEST = lax.Precision.HIGHEST


def padded_2(cells, sides, width):
    for axis, dim in sides:
        count = lax.axis_size(axis)
        ends = count - 1
        head = lax.slice_in_dim(cells, 0, width, axis=dim)
        tail = lax.slice_in_dim(cells, cells.shape[dim] - width, cells.shape[dim], axis=dim)
        cells = jnp.concatenate(
            [
                lax.ppermute(tail, axis, [(i, (i + 1) % count) for i in range(ends)]),
                cells,
                lax.ppermute(head, axis, [((i + 1) % count, i) for i in range(ends)]),
            ],
            axis=dim,
        )
    return cells


def tables(side):
    indices = lax.iota(jnp.int32, side)
    phases = indices[:, None] * indices[None, :] % side
    angles = phases.astype(jnp.float32) * (2.0 * math.pi / side)
    scaling = 1.0 / math.sqrt(side)
    return (jnp.cos(angles) * scaling, jnp.sin(angles) * scaling)


def last_axis(real_part, imag_part, cos_table, sin_table):
    product_one = jnp.matmul(real_part, cos_table, precision=HIGHEST)
    product_two = jnp.matmul(imag_part, sin_table, precision=HIGHEST)
    product_three = jnp.matmul(real_part + imag_part, cos_table + sin_table, precision=HIGHEST)
    return (product_one - product_two, product_three - product_one - product_two)


def first_axis(real_part, imag_part, cos_table, sin_table):
    product_one = jnp.einsum("jk,bkl->bjl", cos_table, real_part, precision=HIGHEST)
    product_two = jnp.einsum("jk,bkl->bjl", sin_table, imag_part, precision=HIGHEST)
    product_three = jnp.einsum(
        "jk,bkl->bjl", cos_table + sin_table, real_part + imag_part, precision=HIGHEST
    )
    return (product_one - product_two, product_three - product_one - product_two)


def transform(real_part, imag_part, cos_table, sin_table):
    real_part, imag_part = last_axis(real_part, imag_part, cos_table, sin_table)
    return first_axis(real_part, imag_part, cos_table, sin_table)


def fold_axis(extended, axis_number, tile_side, half_width):
    own_part = lax.slice_in_dim(
        extended, 2 * half_width, 2 * half_width + tile_side, axis=axis_number
    )
    low_rim = lax.slice_in_dim(extended, 0, half_width, axis=axis_number)
    high_rim = lax.slice_in_dim(
        extended, tile_side + 3 * half_width, tile_side + 4 * half_width, axis=axis_number
    )
    low_widths = [(0, 0)] * extended.ndim
    high_widths = [(0, 0)] * extended.ndim
    low_widths[axis_number] = (0, tile_side - half_width)
    high_widths[axis_number] = (tile_side - half_width, 0)
    return own_part + low_rim + high_rim


def cut_windows(padded, starts, probe_side):
    zero_index = jnp.zeros((), jnp.int32)

    def cut_one(corner):
        return lax.dynamic_slice(
            padded, (zero_index, corner[0], corner[1]), (padded.shape[0], probe_side, probe_side)
        )

    return jax.vmap(cut_one)(starts)


def local(object_field, probe, amplitudes, offsets):
    tile_side = object_field.shape[1]
    mode_count = probe.shape[1]
    probe_side = probe.shape[2]
    half_width = probe_side // 2
    starts = offsets[0, 0] + half_width
    measured = amplitudes[0, 0]
    scan_count = starts.shape[0]
    zero_index = jnp.zeros((), jnp.int32)
    cos_table, sin_table = tables(probe_side)
    padded = padded_2(object_field, (("row", 1), ("col", 2)), half_width)
    for iteration in range(ITERS):
        windows = cut_windows(padded, starts, probe_side)
        win_real = windows[:, 0][:, None]
        win_imag = windows[:, 1][:, None]
        probe_real = probe[0][None]
        probe_imag = probe[1][None]
        exit_real = (probe_real * win_real - probe_imag * win_imag).reshape(
            -1, probe_side, probe_side
        )
        exit_imag = (probe_real * win_imag + probe_imag * win_real).reshape(
            -1, probe_side, probe_side
        )
        far_real, far_imag = transform(exit_real, exit_imag, cos_table, -sin_table)
        far_real = far_real.reshape(scan_count, mode_count, probe_side, probe_side)
        far_imag = far_imag.reshape(scan_count, mode_count, probe_side, probe_side)
        intensity = jnp.sum(far_real * far_real + far_imag * far_imag, axis=1)
        factor = (measured / jnp.maximum(jnp.sqrt(intensity), FLOOR) - 1.0)[:, None]
        back_real, back_imag = transform(
            (far_real * factor).reshape(-1, probe_side, probe_side),
            (far_imag * factor).reshape(-1, probe_side, probe_side),
            cos_table,
            sin_table,
        )
        back_real = back_real.reshape(scan_count, mode_count, probe_side, probe_side)
        back_imag = back_imag.reshape(scan_count, mode_count, probe_side, probe_side)
        obj_real = jnp.sum(probe_real * back_real + probe_imag * back_imag, axis=1)
        obj_imag = jnp.sum(probe_real * back_imag - probe_imag * back_real, axis=1)
        probe_power = jnp.sum(probe[0] * probe[0] + probe[1] * probe[1], axis=0)
        grad_probe = jnp.stack(
            [
                jnp.sum(win_real * back_real + win_imag * back_imag, axis=0),
                jnp.sum(win_real * back_imag - win_imag * back_real, axis=0),
            ]
        )
        probe_weight = jnp.sum(
            windows[:, 0] * windows[:, 0] + windows[:, 1] * windows[:, 1], axis=0
        )
        channels = 3
        gradient = jnp.zeros(
            (channels, tile_side + 2 * half_width, tile_side + 2 * half_width), jnp.float32
        )
        for scan_index in range(scan_count):
            contrib = jnp.stack([obj_real[scan_index], obj_imag[scan_index], probe_power])
            corner = (zero_index, starts[scan_index, 0], starts[scan_index, 1])
            gradient = lax.dynamic_update_slice(
                gradient, lax.dynamic_slice(gradient, corner, contrib.shape) + contrib, corner
            )
        extended = padded_2(gradient, (("row", 1), ("col", 2)), half_width)
        totals = fold_axis(fold_axis(extended, 1, tile_side, half_width), 2, tile_side, half_width)
        summed_grad, summed_weight = lax.psum((grad_probe, probe_weight), ("row", "col"))
        new_probe = probe + PROBE_STEP * summed_grad / (summed_weight + PROBE_REG)
        object_field = object_field + OBJECT_STEP * totals[0:2] / (totals[2:3] + OBJECT_REG)
        if iteration + 1 < ITERS:
            padded = padded_2(object_field, (("row", 1), ("col", 2)), half_width)
        probe = new_probe
    return (object_field, probe)


def solution(mesh):
    return jax.shard_map(
        local,
        mesh=mesh,
        in_specs=(
            P(None, "row", "col"),
            P(),
            P("row", "col", None, None, None),
            P("row", "col", None, None),
        ),
        out_specs=(P(None, "row", "col"), P()),
        check_vma=False,
    )
```

profile of v0, /device:TPU:39, one launch (start us, length us, event | category | flops | bytes accessed | tf_op | source)
XLA Modules:
  0.0 826.2 jit_solution(15070879831426267204)
XLA Ops:
  7.2 3.3 collective-permute-start
  10.6 4.2 collective-permute-start.1
  17.7 9.1 %collective-permute-start.2 = (f32[2,384,128]{2,1,0:T(8,128)S(1)}, f32[2,384,128]{2,1,0:T(8,128)}, u32[]{:S(2)}, u32[]{:S(2)}) collective-permute-start(f32[2,384,128]{2,1,0:T(8,128)S(1)} %constant_dynamic-update-slice_fusion), channel_id=1, source_target_pairs={{0,1},{1,2},{2,3},{3,4},{4,5},{5,6},{6,7},{7,8},{8,9},{9,10},{10,1... | collective-permute-start | bytes 1179656 | tf_op jit(solution)/shard_map/ppermute | solution.py:27
  40.2 6.1 collective-permute-done.3
  47.6 4.3 while.2
  60.8 3.9 fusion.53
  83.9 13.8 %fusion.10 = f32[4,256,256]{2,1,0:T(8,128)S(1)} fusion(f32[4,256,256]{2,1,0:T(8,128)S(1)} %fusion.43, f32[4,256,256]{2,1,0:T(8,128)S(1)} %fusion.62, f32[4,256,256]{1,2,0:T(8,128)S(1)} %get-tuple-element.94, f32[4,256,256]{1,2,0:T(8,128)S(1)} %get-tuple-element.95), kind=kOutput, calls=%fused_computation.34 | convolution fusion | flops 807206912 | bytes 5242880 | tf_op jit(solution)/shard_map/dot_general | solution.py:47
  103.1 4.6 add_reduce_fusion.3
  109.5 10.4 %dynamic_update_slice.12 = f32[3,384,384]{1,2,0:T(8,128)S(1)} dynamic-update-slice(f32[3,384,384]{1,2,0:T(8,128)S(1)} %broadcast.83.clone, f32[3,256,256]{1,2,0:T(8,128)} %pad_maximum_fusion.5, s32[]{:T(128)} %constant.12.clone.1, s32[]{:T(128)S(6)} %select_n.86, s32[]{:T(128)S(6)} %select_n.87) | dynamic-update-slice | bytes 1572868 | tf_op jit(solution)/shard_map/dynamic_update_slice | solution.py:146
  122.1 10.6 %dynamic_update_slice.13 = f32[3,384,384]{1,2,0:T(8,128)S(1)} dynamic-update-slice(f32[3,384,384]{1,2,0:T(8,128)S(1)} %dynamic_update_slice.12, f32[3,256,256]{1,2,0:T(8,128)} %fusion.21, s32[]{:T(128)} %constant.12.clone.1, s32[]{:T(128)S(6)} %select_n.88, s32[]{:T(128)S(6)} %select_n.89) | dynamic-update-slice | bytes 1572868 | tf_op jit(solution)/shard_map/dynamic_update_slice | solution.py:146
  135.9 4.6 collective-permute-start.5
  148.8 5.1 collective-permute-start.6
  159.8 257.3 %all-reduce.7.cloned.1.call-done = (f32[2,2,256,256]{2,3,1,0:T(8,128)}, f32[256,256]{1,0:T(8,128)}) async-done(((f32[2,2,256,256]{2,3,1,0:T(8,128)}, f32[256,256]{1,0:T(8,128)}), (f32[2,2,256,256]{2,3,1,0:T(8,128)}, f32[256,256]{1,0:T(8,128)})) %all-reduce.7.cloned.1.call-update) | async-done | bytes 1310736 | tf_op jit(solution)/shard_map/psum | solution.py:151
  422.5 5.5 collective-permute-start.9
  431.0 6.3 collective-permute-start.10
  440.4 5.8 collective-permute-done.10
  446.3 10.4 %collective-permute-done.11 = f32[2,384,128]{1,2,0:T(8,128)S(1)} collective-permute-done((f32[2,384,128]{1,2,0:T(8,128)S(1)}, f32[2,384,128]{1,2,0:T(8,128)S(1)}, u32[]{:S(2)}, u32[]{:S(2)}) %collective-permute-start.11) | collective-permute-done | bytes 393248 | tf_op jit(solution)/shard_map/ppermute | solution.py:29
  457.9 7.5 while.3
  471.6 3.9 fusion.50
  504.6 4.5 add_reduce_fusion.1
  510.9 10.4 %dynamic_update_slice.14 = f32[3,384,384]{1,2,0:T(8,128)S(1)} dynamic-update-slice(f32[3,384,384]{1,2,0:T(8,128)S(1)} %broadcast.83, f32[3,256,256]{1,2,0:T(8,128)} %pad_maximum_fusion.7, s32[]{:T(128)} %constant.12.clone.1, s32[]{:T(128)S(6)} %select_n.86, s32[]{:T(128)S(6)} %select_n.87) | dynamic-update-slice | bytes 1572868 | tf_op jit(solution)/shard_map/dynamic_update_slice | solution.py:146
  523.5 10.9 %dynamic_update_slice.15 = f32[3,384,384]{1,2,0:T(8,128)S(1)} dynamic-update-slice(f32[3,384,384]{1,2,0:T(8,128)S(1)} %dynamic_update_slice.14, f32[3,256,256]{1,2,0:T(8,128)} %fusion.20, s32[]{:T(128)} %constant.12.clone.1, s32[]{:T(128)S(6)} %select_n.88, s32[]{:T(128)S(6)} %select_n.89) | dynamic-update-slice | bytes 1572868 | tf_op jit(solution)/shard_map/dynamic_update_slice | solution.py:146
  537.5 5.5 collective-permute-start.13
  557.0 251.2 %all-reduce.5.cloned.1.call-done = (f32[2,2,256,256]{2,3,1,0:T(8,128)}, f32[256,256]{1,0:T(8,128)}) async-done(((f32[2,2,256,256]{2,3,1,0:T(8,128)}, f32[256,256]{1,0:T(8,128)}), (f32[2,2,256,256]{2,3,1,0:T(8,128)}, f32[256,256]{1,0:T(8,128)})) %all-reduce.5.cloned.1.call-update) | async-done | bytes 1310736 | tf_op jit(solution)/shard_map/psum | solution.py:151
  (198 shorter events, 155.4 us)
Async XLA Ops:
  7.2 9.6 %copy-start = (f32[2,2,256,256]{3,2,1,0:T(8,128)S(1)}, f32[2,2,256,256]{3,2,1,0:T(8,128)}, u32[]{:S(2)}) copy-start(f32[2,2,256,256]{3,2,1,0:T(8,128)} %param.5) | copy-start | bytes 3145732
  7.2 409.9 %all-reduce.7.cloned.1.call-start = ((), (), s32[]{:S(2)}) async-start(), calls=%async_computation.1 | async-start | bytes 2621440 | tf_op jit(solution)/shard_map/psum | solution.py:151
  7.2 9.6 %collective-permute-start = (f32[2,128,128]{2,1,0:T(8,128)}, f32[2,128,128]{2,1,0:T(8,128)S(1)}, u32[]{:S(2)}, u32[]{:S(2)}) collective-permute-start(f32[2,128,128]{2,1,0:T(8,128)} %param.4), channel_id=1, source_target_pairs={{0,16},{16,32},{32,48},{48,64},{64,80},{80,96},{96,112},{112,128},... | collective-permute-start | bytes 393224 | tf_op jit(solution)/shard_map/ppermute | solution.py:27
  10.6 7.1 collective-permute-start.1
  17.7 18.7 %copy-start.29 = (f32[1,1,2,256,256]{4,3,2,1,0:T(8,128)S(1)}, f32[1,1,2,256,256]{4,3,2,1,0:T(8,128)}, u32[]{:S(2)}) copy-start(f32[1,1,2,256,256]{4,3,2,1,0:T(8,128)} %param.6) | copy-start | bytes 1572868
  17.7 19.7 %copy-start.27 = (f32[2,384,128]{2,1,0:T(8,128)}, f32[2,384,128]{2,1,0:T(8,128)S(1)}, u32[]{:S(2)}) copy-start(f32[2,384,128]{2,1,0:T(8,128)S(1)} %constant_dynamic-update-slice_fusion) | copy-start | bytes 1179652
  17.7 22.5 %collective-permute-start.2 = (f32[2,384,128]{2,1,0:T(8,128)S(1)}, f32[2,384,128]{2,1,0:T(8,128)}, u32[]{:S(2)}, u32[]{:S(2)}) collective-permute-start(f32[2,384,128]{2,1,0:T(8,128)S(1)} %constant_dynamic-update-slice_fusion), channel_id=1, source_target_pairs={{0,1},{1,2},{2,3},{3,4},{4,5},{5,6},{6,7},{7,8},{8,9},{9,10},{10,1... | collective-permute-start | bytes 1179656 | tf_op jit(solution)/shard_map/ppermute | solution.py:27
  26.8 19.4 %collective-permute-start.3 = (f32[2,384,128]{2,1,0:T(8,128)S(1)}, f32[2,384,128]{2,1,0:T(8,128)}, u32[]{:S(2)}, u32[]{:S(2)}) collective-permute-start(f32[2,384,128]{2,1,0:T(8,128)S(1)} %constant_dynamic-update-slice_fusion), channel_id=1, source_target_pairs={{1,0},{2,1},{3,2},{4,3},{5,4},{6,5},{7,6},{8,7},{9,8},{10,9},{11,1... | collective-permute-start | bytes 1179656 | tf_op jit(solution)/shard_map/ppermute | solution.py:29
  132.8 13.0 %collective-permute-start.4 = (f32[3,128,384]{1,2,0:T(8,128)S(1)}, f32[3,128,384]{1,2,0:T(8,128)S(1)}, u32[]{:S(2)}, u32[]{:S(2)}) collective-permute-start(f32[3,128,384]{1,2,0:T(8,128)S(1)} %get-tuple-element.78), channel_id=1, source_target_pairs={{0,16},{16,32},{32,48},{48,64},{64,80},{80,96},{96,112},{112,128},... | collective-permute-start | bytes 1769480 | tf_op jit(solution)/shard_map/ppermute | solution.py:27
  135.9 11.4 %collective-permute-start.5 = (f32[3,128,384]{1,2,0:T(8,128)S(1)}, f32[3,128,384]{1,2,0:T(8,128)S(1)}, u32[]{:S(2)}, u32[]{:S(2)}) collective-permute-start(f32[3,128,384]{1,2,0:T(8,128)S(1)} %get-tuple-element.79), channel_id=1, source_target_pairs={{16,0},{32,16},{48,32},{64,48},{80,64},{96,80},{112,96},{128,112},... | collective-permute-start | bytes 1769480 | tf_op jit(solution)/shard_map/ppermute | solution.py:29
  148.8 270.1 %collective-permute-start.6 = (f32[3,640,128]{1,2,0:T(8,128)}, f32[3,640,128]{1,2,0:T(8,128)}, u32[]{:S(2)}, u32[]{:S(2)}) collective-permute-start(f32[3,640,128]{1,2,0:T(8,128)} %get-tuple-element.70), channel_id=1, source_target_pairs={{0,1},{1,2},{2,3},{3,4},{4,5},{5,6},{6,7},{7,8},{8,9},{9,10},{10,1... | collective-permute-start | bytes 2949128 | tf_op jit(solution)/shard_map/ppermute | solution.py:27
  153.9 265.0 %collective-permute-start.7 = (f32[3,640,128]{1,2,0:T(8,128)}, f32[3,640,128]{1,2,0:T(8,128)}, u32[]{:S(2)}, u32[]{:S(2)}) collective-permute-start(f32[3,640,128]{1,2,0:T(8,128)} %get-tuple-element.71), channel_id=1, source_target_pairs={{1,0},{2,1},{3,2},{4,3},{5,4},{6,5},{7,6},{8,7},{9,8},{10,9},{11,1... | collective-permute-start | bytes 2949128 | tf_op jit(solution)/shard_map/ppermute | solution.py:29
  156.8 651.4 %all-reduce.5.cloned.1.call-start = ((), (), s32[]{:S(2)}) async-start(), calls=%async_computation | async-start | bytes 2621440 | tf_op jit(solution)/shard_map/psum | solution.py:151
  159.8 259.1 %copy-start.24 = (f32[3,128,384]{1,2,0:T(8,128)S(1)}, f32[3,128,384]{1,2,0:T(8,128)}, u32[]{:S(2)}) copy-start(f32[3,128,384]{1,2,0:T(8,128)} %copy-done.23) | copy-start | bytes 1769476
  418.9 9.1 %copy-start.26 = (f32[256,256]{0,1:T(8,128)S(1)}, f32[256,256]{0,1:T(8,128)}, u32[]{:S(2)}) copy-start(f32[256,256]{0,1:T(8,128)} %copy.101) | copy-start | bytes 786436
  418.9 9.1 %copy-start.22 = (f32[2,2,256,256]{2,3,1,0:T(8,128)S(1)}, f32[2,2,256,256]{2,3,1,0:T(8,128)}, u32[]{:S(2)}) copy-start(f32[2,2,256,256]{2,3,1,0:T(8,128)} %copy.102) | copy-start | bytes 3145732
  420.6 9.4 %collective-permute-start.8 = (f32[2,128,128]{1,2,0:T(8,128)S(1)}, f32[2,128,128]{1,2,0:T(8,128)S(1)}, u32[]{:S(2)}, u32[]{:S(2)}) collective-permute-start(f32[2,128,128]{1,2,0:T(8,128)S(1)} %fusion.83), channel_id=1, source_target_pairs={{0,16},{16,32},{32,48},{48,64},{64,80},{80,96},{96,112},{112,128},... | collective-permute-start | bytes 393224 | tf_op jit(solution)/shard_map/ppermute | solution.py:27
  422.5 8.5 %collective-permute-start.9 = (f32[2,128,128]{1,2,0:T(8,128)S(1)}, f32[2,128,128]{1,2,0:T(8,128)S(1)}, u32[]{:S(2)}, u32[]{:S(2)}) collective-permute-start(f32[2,128,128]{1,2,0:T(8,128)S(1)} %fusion.83), channel_id=1, source_target_pairs={{16,0},{32,16},{48,32},{64,48},{80,64},{96,80},{112,96},{128,112},... | collective-permute-start | bytes 393224 | tf_op jit(solution)/shard_map/ppermute | solution.py:29
  431.0 15.2 %collective-permute-start.10 = (f32[2,384,128]{1,2,0:T(8,128)S(1)}, f32[2,384,128]{1,2,0:T(8,128)S(1)}, u32[]{:S(2)}, u32[]{:S(2)}) collective-permute-start(f32[2,384,128]{1,2,0:T(8,128)S(1)} %pad_maximum_fusion.14), channel_id=1, source_target_pairs={{0,1},{1,2},{2,3},{3,4},{4,5},{5,6},{6,7},{7,8},{8,9},{9,10},{10,1... | collective-permute-start | bytes 1179656 | tf_op jit(solution)/shard_map/ppermute | solution.py:27
  437.4 19.3 %collective-permute-start.11 = (f32[2,384,128]{1,2,0:T(8,128)S(1)}, f32[2,384,128]{1,2,0:T(8,128)S(1)}, u32[]{:S(2)}, u32[]{:S(2)}) collective-permute-start(f32[2,384,128]{1,2,0:T(8,128)S(1)} %pad_maximum_fusion.14), channel_id=1, source_target_pairs={{1,0},{2,1},{3,2},{4,3},{5,4},{6,5},{7,6},{8,7},{9,8},{10,9},{11,1... | collective-permute-start | bytes 1179656 | tf_op jit(solution)/shard_map/ppermute | solution.py:29
  535.6 12.9 %collective-permute-start.12 = (f32[3,128,384]{1,2,0:T(8,128)}, f32[3,128,384]{1,2,0:T(8,128)S(1)}, u32[]{:S(2)}, u32[]{:S(2)}) collective-permute-start(f32[3,128,384]{1,2,0:T(8,128)} %get-tuple-element.76), channel_id=1, source_target_pairs={{0,16},{16,32},{32,48},{48,64},{64,80},{80,96},{96,112},{112,128},... | collective-permute-start | bytes 1769480 | tf_op jit(solution)/shard_map/ppermute | solution.py:27
  537.5 12.6 %collective-permute-start.13 = (f32[3,128,384]{1,2,0:T(8,128)}, f32[3,128,384]{1,2,0:T(8,128)}, u32[]{:S(2)}, u32[]{:S(2)}) collective-permute-start(f32[3,128,384]{1,2,0:T(8,128)} %get-tuple-element.77), channel_id=1, source_target_pairs={{16,0},{32,16},{48,32},{64,48},{80,64},{96,80},{112,96},{128,112},... | collective-permute-start | bytes 1769480 | tf_op jit(solution)/shard_map/ppermute | solution.py:29
  552.6 264.0 %collective-permute-start.14 = (f32[3,640,128]{1,2,0:T(8,128)}, f32[3,640,128]{1,2,0:T(8,128)}, u32[]{:S(2)}, u32[]{:S(2)}) collective-permute-start(f32[3,640,128]{1,2,0:T(8,128)} %get-tuple-element.68), channel_id=1, source_target_pairs={{0,1},{1,2},{2,3},{3,4},{4,5},{5,6},{6,7},{7,8},{8,9},{9,10},{10,1... | collective-permute-start | bytes 2949128 | tf_op jit(solution)/shard_map/ppermute | solution.py:27
  555.0 261.6 %collective-permute-start.15 = (f32[3,640,128]{1,2,0:T(8,128)}, f32[3,640,128]{1,2,0:T(8,128)}, u32[]{:S(2)}, u32[]{:S(2)}) collective-permute-start(f32[3,640,128]{1,2,0:T(8,128)} %get-tuple-element.69), channel_id=1, source_target_pairs={{1,0},{2,1},{3,2},{4,3},{5,4},{6,5},{7,6},{8,7},{9,8},{10,9},{11,1... | collective-permute-start | bytes 2949128 | tf_op jit(solution)/shard_map/ppermute | solution.py:29
  (26 other events, 105.7 us)
Sparse Core Ops, SparseCore 0:
  157.0 260.0 all-reduce.6
  547.3 260.8 all-reduce.4
where the time goes:
time: 840 us; the launch traced here: 826 us
  waiting for transfers between devices  541 us (64%)
  local copies, waits for them, and re-layouts  84.9 us (10%)
  matrix products  82 us (10%)
  starting transfers between devices  60.7 us (7%)
  other arithmetic  34.4 us (4%)
  between operations  22.9 us (3%)
    psum x2, waiting for transfers between devices, local(): lax.psum((grad_probe, probe_weight), ('row', 'col'))  509 us
    dynamic_update_slice x4, local copies, waits for them, and re-layouts, local(): lax.dynamic_update_slice(gradient, lax.dynamic_slice(gradient, corner, co...  42.3 us
    ppermute x8, starting transfers between devices, padded_2(): lax.ppermute(tail, axis, [(i, (i + 1) % count) for i in range(ends)])  33.2 us
    ppermute x8, starting transfers between devices, padded_2(): lax.ppermute(head, axis, [((i + 1) % count, i) for i in range(ends)])  27.4 us
    dot_general x4, matrix products, last_axis(): jnp.matmul(real_part + imag_part, cos_table + sin_table, precision=HIGHEST)  21.1 us
    ppermute x8, waiting for transfers between devices, padded_2(): lax.ppermute(head, axis, [((i + 1) % count, i) for i in range(ends)])  20.5 us
  transfers between devices with their start and end apart: 18, of which 11 were waited for; matrix products, arithmetic and copies ran while one was open for 4% of the time, Pallas kernels for 0%

commit v1 on v0

v1 whole, which is shorter than its diff:
```python
import functools
import math

import jax
import jax.numpy as jnp
import ml_dtypes
import numpy as np
from jax import lax
from jax.experimental import pallas as pl
from jax.experimental.pallas import tpu as pltpu
from jax.sharding import PartitionSpec as P

ITERS = 2
FLOOR = 0.5
OBJECT_STEP = 0.5
OBJECT_REG = 0.5
PROBE_STEP = 1.0
PROBE_REG = 1.0
TILE = 128
SIDE = 256
HALF = SIDE // 2
WIDE = 3 * TILE
CHUNK = 64
F32 = jnp.float32
BF16 = jnp.bfloat16


def split_np(table):
    high = table.astype(np.float32).astype(ml_dtypes.bfloat16)
    low = (table - high.astype(np.float64)).astype(np.float32).astype(ml_dtypes.bfloat16)
    return np.stack([high, low])


def tables():
    out = []
    for parity in range(2):
        u = 2 * np.arange(HALF)[:, None] + parity
        angle = 2.0 * math.pi * ((u * np.arange(HALF)[None, :]) % SIDE) / SIDE
        cos, sin = np.cos(angle) / 16.0, np.sin(angle) / 16.0
        forward = np.block([[cos, sin], [-sin, cos]])
        out.append(np.stack([split_np(forward), split_np(forward.T)]))
    return np.stack(out)


def split(x):
    high = x.astype(BF16)
    return high, (x - high.astype(F32)).astype(BF16)


def split_whole(x):
    high = x.astype(BF16)
    rest = x - high.astype(F32)
    middle = rest.astype(BF16)
    return high, middle, (rest - middle.astype(F32)).astype(BF16)


def dot(a, b):
    return jnp.dot(a, b, preferred_element_type=F32)


def sort_kernel(measured_ref, out_ref):
    source = lax.broadcasted_iota(jnp.int32, (SIDE, SIDE), 0)
    place = lax.broadcasted_iota(jnp.int32, (SIDE, SIDE), 1)
    wanted = jnp.where(place < HALF, 2 * place, 2 * place - (SIDE - 1))
    select = jnp.where(source == wanted, 1.0, 0.0).astype(BF16)
    wanted = jnp.where(source < HALF, 2 * source, 2 * source - (SIDE - 1))
    select_rows = jnp.where(place == wanted, 1.0, 0.0).astype(BF16)
    for scan in range(2):
        high, middle, low = split_whole(measured_ref[scan])
        turned = (dot(low, select) + dot(middle, select)) + dot(high, select)
        high, middle, low = split_whole(turned)
        turned = (dot(select_rows, low) + dot(select_rows, middle)) + dot(select_rows, high)
        out_ref[scan, 0] = turned[:HALF]
        out_ref[scan, 1] = turned[HALF:]


def step_kernel(
    starts_ref,
    table_ref,
    probe_ref,
    measured_ref,
    left_ref,
    middle_ref,
    right_ref,
    probe_out,
    grad_left,
    grad_middle,
    grad_right,
    padded,
    windows,
    folded,
    stacked,
    far,
    back,
    contrib,
    total,
):
    lane = lax.broadcasted_iota(jnp.int32, (CHUNK // 8, 8, TILE), 2)
    sublane = lax.broadcasted_iota(jnp.int32, (CHUNK // 8, 8, TILE), 1)
    for channel in range(2):
        for block in range(3):
            rows = pl.ds(block * TILE, TILE)
            padded[channel, rows, 0:TILE] = left_ref[block, channel]
            padded[channel, rows, TILE : 2 * TILE] = middle_ref[block, channel]
            padded[channel, rows, 2 * TILE :] = right_ref[block, channel]
    for channel in range(3):
        total[channel] = jnp.zeros((WIDE + 8, WIDE), F32)

    def cut(scan, carry):
        row, column = starts_ref[scan, 0], starts_ref[scan, 1]
        inner = lax.rem(row, 8)
        base = pl.multiple_of(row - inner, 8)
        turn, keep = lax.rem(TILE - column, TILE), lane < TILE - column
        lift, stay = lax.rem(8 - inner, 8), sublane < 8 - inner
        for channel in range(2):
            for piece in range(SIDE // CHUNK):
                turned = []
                for b in range(3):
                    rows = padded[channel, pl.ds(base + piece * CHUNK, CHUNK + 8), pl.ds(b * TILE, TILE)]
                    rows = pltpu.roll(rows.reshape(CHUNK // 8 + 1, 8, TILE), lift, 1)
                    rows = jnp.where(stay, rows[:-1], rows[1:])
                    turned.append(pltpu.roll(rows, turn, 2))
                for b in range(2):
                    windows[scan, channel, pl.ds(piece * CHUNK, CHUNK), pl.ds(b * TILE, TILE)] = (
                        jnp.where(keep, turned[b], turned[b + 1]).reshape(CHUNK, TILE)
                    )
        return carry

    lax.fori_loop(0, 2, cut, 0)

    def forward(image, carry):
        scan, mode = image // 2, image % 2
        for piece in range(SIDE // CHUNK):
            rows = pl.ds(piece * CHUNK, CHUNK)
            p_re, p_im = probe_ref[0, mode, rows, :], probe_ref[1, mode, rows, :]
            w_re, w_im = windows[scan, 0, rows, :], windows[scan, 1, rows, :]
            e_re = p_re * w_re - p_im * w_im
            e_im = p_re * w_im + p_im * w_re
            for parity in range(2):
                sign = 1.0 if parity == 0 else -1.0
                for part, value in enumerate((e_re, e_im)):
                    half = value[:, :HALF] + sign * value[:, HALF:]
                    high, low = split(half)
                    folded[parity, 0, rows, part * HALF : (part + 1) * HALF] = high
                    folded[parity, 1, rows, part * HALF : (part + 1) * HALF] = low
        for parity in range(2):
            out = (
                dot(folded[parity, 1], table_ref[parity, 1, 0])
                + dot(folded[parity, 0], table_ref[parity, 1, 1])
                + dot(folded[parity, 0], table_ref[parity, 1, 0])
            )
            for other in range(2):
                sign = 1.0 if other == 0 else -1.0
                half = out[:HALF] + sign * out[HALF:]
                high, low = split(half)
                place = pl.ds(parity * HALF, HALF)
                stacked[other, 0, 0:HALF, place] = high[:, :HALF]
                stacked[other, 0, HALF:, place] = high[:, HALF:]
                stacked[other, 1, 0:HALF, place] = low[:, :HALF]
                stacked[other, 1, HALF:, place] = low[:, HALF:]
        for other in range(2):
            far[image, other] = (
                dot(table_ref[other, 0, 0], stacked[other, 1])
                + dot(table_ref[other, 0, 1], stacked[other, 0])
                + dot(table_ref[other, 0, 0], stacked[other, 0])
            )
        return carry

    lax.fori_loop(0, 4, forward, 0)

    def scale(index, carry):
        scan, other = index // 2, index % 2
        for piece in range(HALF // 32):
            upper, lower = pl.ds(piece * 32, 32), pl.ds(HALF + piece * 32, 32)
            parts = [
                far[2 * scan + mode, other, rows, :] for mode in range(2) for rows in (upper, lower)
            ]
            intensity = (parts[0] * parts[0] + parts[1] * parts[1]) + (
                parts[2] * parts[2] + parts[3] * parts[3]
            )
            measured = measured_ref[scan, other, upper, :]
            factor = measured / jnp.maximum(jnp.sqrt(intensity), FLOOR) - 1.0
            for mode in range(2):
                far[2 * scan + mode, other, upper, :] = parts[2 * mode] * factor
                far[2 * scan + mode, other, lower, :] = parts[2 * mode + 1] * factor
        return carry

    lax.fori_loop(0, 4, scale, 0)

    def backward(image, carry):
        scan, mode = image // 2, image % 2
        halves = []
        for other in range(2):
            high, low = split(far[image, other])
            halves.append(
                dot(table_ref[other, 1, 0], low)
                + dot(table_ref[other, 1, 1], high)
                + dot(table_ref[other, 1, 0], high)
            )
        for place, value in ((0, halves[0] + halves[1]), (HALF, halves[0] - halves[1])):
            high, low = split(value)
            for parity in range(2):
                columns = slice(parity * HALF, (parity + 1) * HALF)
                for part in range(2):
                    rows = slice(part * HALF, (part + 1) * HALF)
                    target = pl.ds(part * HALF, HALF)
                    folded[parity, 0, pl.ds(place, HALF), target] = high[rows, columns]
                    folded[parity, 1, pl.ds(place, HALF), target] = low[rows, columns]
        for parity in range(2):
            back[parity] = (
                dot(folded[parity, 1], table_ref[parity, 0, 0])
                + dot(folded[parity, 0], table_ref[parity, 0, 1])
                + dot(folded[parity, 0], table_ref[parity, 0, 0])
            )
        first_scan, first_mode = scan == 0, mode == 0
        for piece in range(SIDE // CHUNK):
            rows = pl.ds(piece * CHUNK, CHUNK)
            even, odd = back[0, rows, :], back[1, rows, :]
            for b in range(2):
                columns = pl.ds(b * HALF, HALF)
                sign = 1.0 if b == 0 else -1.0
                b_re = even[:, :HALF] + sign * odd[:, :HALF]
                b_im = even[:, HALF:] + sign * odd[:, HALF:]
                p_re, p_im = probe_ref[0, mode, rows, columns], probe_ref[1, mode, rows, columns]
                w_re, w_im = windows[scan, 0, rows, columns], windows[scan, 1, rows, columns]
                o_re = p_re * b_re + p_im * b_im
                o_im = p_re * b_im - p_im * b_re
                zero = jnp.zeros_like(o_re)
                contrib[0, rows, columns] = o_re + jnp.where(
                    first_mode, zero, contrib[0, rows, columns]
                )
                contrib[1, rows, columns] = o_im + jnp.where(
                    first_mode, zero, contrib[1, rows, columns]
                )
                g_re = w_re * b_re + w_im * b_im
                g_im = w_re * b_im - w_im * b_re
                for slot in range(CHUNK // 8):
                    group = piece * (CHUNK // 8) + slot
                    inner = slice(slot * 8, slot * 8 + 8)
                    for part, value in enumerate((g_re, g_im)):
                        place = 2 * part + mode
                        old = probe_out[group, place, :, columns]
                        probe_out[group, place, :, columns] = value[inner] + jnp.where(
                            first_scan, jnp.zeros_like(old), old
                        )

        @pl.when(mode == 1)
        def _():
            row, column = starts_ref[scan, 0], starts_ref[scan, 1]
            inner = lax.rem(row, 8)
            base = pl.multiple_of(row - inner, 8)
            turn, keep = lax.rem(column, TILE), lane >= column
            zero = jnp.zeros((CHUNK // 8, 8, TILE), F32)
            edge = jnp.zeros((1, 8, TILE), F32)
            stay = lax.broadcasted_iota(jnp.int32, (CHUNK // 8 + 1, 8, TILE), 1) >= inner
            for channel in range(3):
                for piece in range(SIDE // CHUNK):
                    halves = []
                    for b in range(2):
                        value = contrib[channel, pl.ds(piece * CHUNK, CHUNK), pl.ds(b * TILE, TILE)]
                        halves.append(pltpu.roll(value.reshape(CHUNK // 8, 8, TILE), turn, 2))
                    thirds = (
                        jnp.where(keep, halves[0], zero),
                        jnp.where(keep, halves[1], halves[0]),
                        jnp.where(keep, zero, halves[1]),
                    )
                    place = pl.ds(base + piece * CHUNK, CHUNK + 8)
                    for b in range(3):
                        value = pltpu.roll(thirds[b], inner, 1)
                        value = jnp.where(
                            stay,
                            jnp.concatenate([value, edge]),
                            jnp.concatenate([edge, value]),
                        )
                        total[channel, place, pl.ds(b * TILE, TILE)] += value.reshape(CHUNK + 8, TILE)

        return carry

    for piece in range(SIDE // CHUNK):
        rows = pl.ds(piece * CHUNK, CHUNK)
        power = None
        for mode in range(2):
            for part in range(2):
                value = probe_ref[part, mode, rows, :]
                power = value * value if power is None else power + value * value
        contrib[2, rows, :] = power
        weight = None
        for scan in range(2):
            for part in range(2):
                value = windows[scan, part, rows, :]
                weight = value * value if weight is None else weight + value * value
        for slot in range(CHUNK // 8):
            probe_out[piece * (CHUNK // 8) + slot, 4] = weight[slot * 8 : slot * 8 + 8]

    lax.fori_loop(0, 4, backward, 0)

    for channel in range(3):
        for block in range(3):
            rows = pl.ds(block * TILE, TILE)
            grad_left[block, channel] = total[channel, rows, 0:TILE]
            grad_middle[block, channel] = total[channel, rows, TILE : 2 * TILE]
            grad_right[block, channel] = total[channel, rows, 2 * TILE :]


VMEM_SPEC = pl.BlockSpec(memory_space=pltpu.VMEM)


def sort_measured(measured):
    return pl.pallas_call(
        sort_kernel,
        out_shape=jax.ShapeDtypeStruct((2, 2, HALF, SIDE), F32),
        in_specs=[VMEM_SPEC],
        out_specs=VMEM_SPEC,
        compiler_params=pltpu.CompilerParams(vmem_limit_bytes=40 * 2**20),
        name="sort_measured",
    )(measured)


def step(starts, table, probe, measured, left, middle, right):
    column = jax.ShapeDtypeStruct((3, 3, TILE, TILE), F32)
    return pl.pallas_call(
        step_kernel,
        out_shape=[jax.ShapeDtypeStruct((SIDE // 8, 5, 8, SIDE), F32), column, column, column],
        in_specs=[pl.BlockSpec(memory_space=pltpu.SMEM)] + [VMEM_SPEC] * 6,
        out_specs=[VMEM_SPEC] * 4,
        scratch_shapes=[
            pltpu.VMEM((2, WIDE + 8, WIDE), F32),
            pltpu.VMEM((2, 2, SIDE, SIDE), F32),
            pltpu.VMEM((2, 2, SIDE, SIDE), BF16),
            pltpu.VMEM((2, 2, SIDE, SIDE), BF16),
            pltpu.VMEM((4, 2, SIDE, SIDE), F32),
            pltpu.VMEM((2, SIDE, SIDE), F32),
            pltpu.VMEM((3, SIDE, SIDE), F32),
            pltpu.VMEM((3, WIDE + 8, WIDE), F32),
        ],
        compiler_params=pltpu.CompilerParams(vmem_limit_bytes=40 * 2**20),
        name="step",
    )(starts, table, probe, measured, left, middle, right)


def up(axis):
    return [(i, i + 1) for i in range(lax.axis_size(axis) - 1)]


def down(axis):
    return [(i + 1, i) for i in range(lax.axis_size(axis) - 1)]


def neighbourhood(tile):
    above = lax.ppermute(tile, "row", up("row"))
    below = lax.ppermute(tile, "row", down("row"))
    middle = jnp.stack([above, tile, below])
    left = lax.ppermute(middle, "col", up("col"))
    right = lax.ppermute(middle, "col", down("col"))
    return left, middle, right


def fold(left, middle, right):
    column = middle + lax.ppermute(left, "col", down("col")) + lax.ppermute(right, "col", up("col"))
    return (
        column[1]
        + lax.ppermute(column[0], "row", down("row"))
        + lax.ppermute(column[2], "row", up("row"))
    )


def scatter_sum(value, axis, count, groups=None):
    pieces = lax.all_to_all(value, axis, 0, 0, axis_index_groups=groups, tiled=True)
    return pieces.reshape((count, value.shape[0] // count) + value.shape[1:]).sum(0)


def gather(value, axis, count, groups=None):
    copies = jnp.broadcast_to(value[None], (count,) + value.shape)
    copies = copies.reshape((count * value.shape[0],) + value.shape[1:])
    return lax.all_to_all(copies, axis, 0, 0, axis_index_groups=groups, tiled=True)


def new_probe(sums, probe_rows):
    core = lax.axis_index("col") % 2
    swap = [(i, i ^ 1) for i in range(16)]
    groups = [[2 * i + c for i in range(8)] for c in range(2)]
    halves = sums.reshape((2, 16) + sums.shape[1:])
    mine = lax.dynamic_index_in_dim(halves, core, 0, False)
    other = lax.dynamic_index_in_dim(halves, 1 - core, 0, False)
    mine = mine + lax.ppermute(other, "col", swap)
    mine = scatter_sum(mine, "row", 16)
    mine = gather(mine, "col", 8, groups).sum(0, keepdims=True)
    place = core * 16 + lax.axis_index("row")
    old = lax.dynamic_slice_in_dim(probe_rows, place, 1, 0)
    mine = old + PROBE_STEP * mine[:, :4] / (mine[:, 4:] + PROBE_REG)
    mine = gather(mine, "row", 16)
    other = lax.ppermute(mine, "col", swap)
    return jnp.where(
        core == 0, jnp.concatenate([mine, other]), jnp.concatenate([other, mine])
    )


def local(object_field, probe, amplitudes, offsets):
    table = jnp.asarray(tables())
    starts = offsets[0, 0] + HALF
    measured = sort_measured(amplitudes[0, 0])
    for iteration in range(ITERS):
        left, middle, right = neighbourhood(object_field)
        sums, grad_left, grad_middle, grad_right = step(
            starts, table, probe, measured, left, middle, right
        )
        rows = probe.reshape(4, SIDE // 8, 8, SIDE).transpose(1, 0, 2, 3)
        rows = new_probe(sums, rows)
        totals = fold(grad_left, grad_middle, grad_right)
        object_field = object_field + OBJECT_STEP * totals[0:2] / (totals[2:3] + OBJECT_REG)
        probe = rows.transpose(1, 0, 2, 3).reshape(2, 2, SIDE, SIDE)
    return (object_field, probe)


def solution(mesh):
    return jax.shard_map(
        local,
        mesh=mesh,
        in_specs=(
            P(None, "row", "col"),
            P(),
            P("row", "col", None, None, None),
            P("row", "col", None, None),
        ),
        out_specs=(P(None, "row", "col"), P()),
        check_vma=False,
    )
```

time: 840 us -> 262 us (0.31); the launches traced: 826 us -> 258 us
  waiting for transfers between devices: 541 us -> 65.5 us
  matrix products: 82 us -> 0 us
  local copies, waits for them, and re-layouts: 84.9 us -> 13.7 us
  blocking collectives: 0 us -> 45.7 us
  starting transfers between devices: 60.7 us -> 100 us
  other arithmetic: 34.4 us -> 11.4 us
  between operations: 22.9 us -> 1.13 us
  Pallas kernels: 0 us -> 20.2 us
    psum x2 -> x0, waiting for transfers between devices: 509 us -> none  [local(): lax.psum((grad_probe, probe_weight), ('row', 'col'))]
    dot_general x24 -> x0, matrix products: 82 us -> none  [the longest x4 21.1 us: last_axis(): jnp.matmul(real_part + imag_part, cos_table + sin_table, precision=HIGHEST)]
    all_to_all x0 -> x2, blocking collectives: none -> 45.7 us  [scatter_sum(): lax.all_to_all(value, axis, 0, 0, axis_index_groups=groups, tiled=True)]
    dynamic_update_slice x4 -> x0, local copies, waits for them, and re-layouts: 42.3 us -> none  [local(): lax.dynamic_update_slice(gradient, lax.dynamic_slice(gradient, corner, co...]
    ppermute x16 -> x20, waiting for transfers between devices: 32.3 us -> 63.7 us  [the longest x2 32.3 us: fold(): lax.ppermute(left, 'col', down('col'))]
    all_to_all x0 -> x4, starting transfers between devices: none -> 28.6 us  [gather(): lax.all_to_all(copies, axis, 0, 0, axis_index_groups=groups, tiled=True)]
    pallas_call x0 -> x3, Pallas kernels: none -> 20.2 us  [the longest x2 19.3 us: step(): pl.pallas_call(step_kernel, out_shape=[jax.ShapeDtypeStruct((SIDE // 8, 5...]
    gather x16 -> x0, local copies, waits for them, and re-layouts: 11.2 us -> none
  transfers between devices with their start and end apart: 18 -> 24, of which waited for: 11 -> 18; matrix products, arithmetic and copies ran while one was open for 4% -> 4% of each run, Pallas kernels for 0% -> 0%
where the time goes in v1:
time: 262 us; the launch traced here: 258 us
  starting transfers between devices  100 us (38%)
  waiting for transfers between devices  65.5 us (25%)
  blocking collectives  45.7 us (17%)
  Pallas kernels  20.2 us (8%)
  local copies, waits for them, and re-layouts  13.7 us (5%)
  other arithmetic  11.4 us (4%)
    all_to_all x2, blocking collectives, scatter_sum(): lax.all_to_all(value, axis, 0, 0, axis_index_groups=groups, tiled=True)  45.7 us
    ppermute x2, waiting for transfers between devices, fold(): lax.ppermute(left, 'col', down('col'))  32.3 us
    all_to_all x4, starting transfers between devices, gather(): lax.all_to_all(copies, axis, 0, 0, axis_index_groups=groups, tiled=True)  28.6 us
    pallas_call x2, Pallas kernels, step(): pl.pallas_call(step_kernel, out_shape=[jax.ShapeDtypeStruct((SIDE // 8, 5...  19.3 us
    ppermute x2, starting transfers between devices, neighbourhood(): left = lax.ppermute(middle, 'col', up('col'))  17.8 us
    ppermute x2, starting transfers between devices, fold(): lax.ppermute(right, 'col', up('col'))  15.2 us
    unnamed x38, local copies, waits for them, and re-layouts  8.31 us
    ppermute x2, waiting for transfers between devices, fold(): lax.ppermute(column[2], 'row', up('row'))  8.07 us
  transfers between devices with their start and end apart: 24, of which 18 were waited for; matrix products, arithmetic and copies ran while one was open for 4% of the time, Pallas kernels for 0%

profile of v1, /device:TPU:39, one launch (start us, length us, event | category | flops | bytes accessed | tf_op | source)
XLA Modules:
  0.0 257.9 jit_solution(6972001405663626072)
XLA Ops:
  4.0 4.2 %collective-permute-start.1 = (f32[2,128,128]{2,1,0:T(8,128)}, f32[2,128,128]{2,1,0:T(8,128)S(1)}, u32[]{:S(2)}, u32[]{:S(2)}) collective-permute-start(f32[2,128,128]{2,1,0:T(8,128)} %param.5), channel_id=1, source_target_pairs={{16,0},{32,16},{48,32},{64,48},{80,64},{96,80},{112,96},{128,112},... | collective-permute-start | bytes 393224 | tf_op jit(solution)/shard_map/ppermute | solution.py:351
  11.4 3.7 %collective-permute-start.3 = (f32[3,2,128,128]{3,2,1,0:T(8,128)S(1)}, f32[3,2,128,128]{3,2,1,0:T(8,128)S(1)}, u32[]{:S(2)}, u32[]{:S(2)}) collective-permute-start(f32[3,2,128,128]{3,2,1,0:T(8,128)S(1)} %pad_maximum_fusion.middle_ref), channel_id=1, source_target_pairs={{1,0},{2,1},{3,2},{4,3},{5,4},{6,5},{7,6},{8,7},{9,8},{10,9},{11,1... | collective-permute-start | bytes 1179656 | tf_op jit(solution)/shard_map/ppermute | solution.py:354
  15.1 7.9 %collective-permute-start.2 = (f32[3,2,128,128]{3,2,1,0:T(8,128)S(1)}, f32[3,2,128,128]{3,2,1,0:T(8,128)S(1)}, u32[]{:S(2)}, u32[]{:S(2)}) collective-permute-start(f32[3,2,128,128]{3,2,1,0:T(8,128)S(1)} %pad_maximum_fusion.middle_ref), channel_id=1, source_target_pairs={{0,1},{1,2},{2,3},{3,4},{4,5},{5,6},{6,7},{7,8},{8,9},{9,10},{10,1... | collective-permute-start | bytes 1179656 | tf_op jit(solution)/shard_map/ppermute | solution.py:353
  25.6 5.1 %collective-permute-done.3.right_ref = f32[3,2,128,128]{3,2,1,0:T(8,128)S(1)} collective-permute-done((f32[3,2,128,128]{3,2,1,0:T(8,128)S(1)}, f32[3,2,128,128]{3,2,1,0:T(8,128)S(1)}, u32[]{:S(2)}, u32[]{:S(2)}) %collective-permute-start.3) | collective-permute-done | bytes 393248 | tf_op jit(solution)/shard_map/ppermute | solution.py:354
  35.8 9.7 %step.2 = (f32[32,5,8,256]{3,2,1,0:T(8,128)S(1)}, f32[3,3,128,128]{3,2,1,0:T(8,128)S(1)}, f32[3,3,128,128]{3,2,1,0:T(8,128)S(1)}, f32[3,3,128,128]{3,2,1,0:T(8,128)S(1)}) custom-call(s32[2,2]{1,0:T(2,128)S(1)} %add_bitcast_fusion.starts_ref, bf16[2,2,2,256,256]{4,3,2,1,0:T(8,128)(2,1)S(1)} %copy-done, f32[2,2,256,256]{3,2,1,0:T(8,128)S(1)} %copy-done.1, ...), custom_call_target="tpu_custom_call" | custom-call | tf_op jit(solution)/shard_map/step/pallas_call | solution.py:321
  52.6 25.0 %all_to_all.30 = f32[16,5,8,256]{3,2,1,0:T(8,128)} all-to-all(f32[16,5,8,256]{3,2,1,0:T(8,128)S(1)} %bitcast_add_fusion.1), channel_id=1, replica_groups=mesh['row'=16,'col'=16] {'row'}, dimensions={0} | all-to-all | bytes 1310720 | tf_op jit(solution)/shard_map/all_to_all | solution.py:368
  79.4 10.0 %all-to-all-start.1 = ((f32[8,5,8,256]{3,2,1,0:T(8,128)}), f32[8,5,8,256]{3,2,1,0:T(8,128)}, u32[]{:S(2)}, u32[]{:S(2)}) async-start(f32[8,5,8,256]{3,2,1,0:T(8,128)} %reshape.58), calls=%async_computation.1 | async-start | bytes 655360 | tf_op jit(solution)/shard_map/all_to_all | solution.py:375
  89.4 4.0 %collective-permute-start.4 = (f32[3,3,128,128]{3,2,1,0:T(8,128)S(1)}, f32[3,3,128,128]{3,2,1,0:T(8,128)}, u32[]{:S(2)}, u32[]{:S(2)}) collective-permute-start(f32[3,3,128,128]{3,2,1,0:T(8,128)S(1)} %copy-done.12), channel_id=1, source_target_pairs={{1,0},{2,1},{3,2},{4,3},{5,4},{6,5},{7,6},{8,7},{9,8},{10,9},{11,1... | collective-permute-start | bytes 1769480 | tf_op jit(solution)/shard_map/ppermute | solution.py:359
  93.4 7.6 %collective-permute-start.5 = (f32[3,3,128,128]{3,2,1,0:T(8,128)S(1)}, f32[3,3,128,128]{3,2,1,0:T(8,128)}, u32[]{:S(2)}, u32[]{:S(2)}) collective-permute-start(f32[3,3,128,128]{3,2,1,0:T(8,128)S(1)} %copy-done.10), channel_id=1, source_target_pairs={{0,1},{1,2},{2,3},{3,4},{4,5},{5,6},{6,7},{7,8},{8,9},{9,10},{10,1... | collective-permute-start | bytes 1769480 | tf_op jit(solution)/shard_map/ppermute | solution.py:359
  104.6 4.4 %all-to-all-start.2 = ((f32[16,4,8,256]{3,2,1,0:T(8,128)}), f32[16,4,8,256]{3,2,1,0:T(8,128)}, u32[]{:S(2)}, u32[]{:S(2)}) async-start(f32[16,4,8,256]{3,2,1,0:T(8,128)} %reshape.59), calls=%async_computation.2 | async-start | bytes 1048576 | tf_op jit(solution)/shard_map/all_to_all | solution.py:375
  109.0 15.7 %collective-permute-done.4 = f32[3,3,128,128]{3,2,1,0:T(8,128)} collective-permute-done((f32[3,3,128,128]{3,2,1,0:T(8,128)S(1)}, f32[3,3,128,128]{3,2,1,0:T(8,128)}, u32[]{:S(2)}, u32[]{:S(2)}) %collective-permute-start.4) | collective-permute-done | bytes 589856 | tf_op jit(solution)/shard_map/ppermute | solution.py:359
  128.1 3.4 %collective-permute-start.7 = (f32[3,128,128]{2,1,0:T(8,128)S(1)}, f32[3,128,128]{2,1,0:T(8,128)S(1)}, u32[]{:S(2)}, u32[]{:S(2)}) collective-permute-start(f32[3,128,128]{2,1,0:T(8,128)S(1)} %get-tuple-element.21), channel_id=1, source_target_pairs={{0,16},{16,32},{32,48},{48,64},{64,80},{80,96},{96,112},{112,128},... | collective-permute-start | bytes 589832 | tf_op jit(solution)/shard_map/ppermute | solution.py:363
  132.6 4.0 %collective-permute-done.7 = f32[3,128,128]{2,1,0:T(8,128)S(1)} collective-permute-done((f32[3,128,128]{2,1,0:T(8,128)S(1)}, f32[3,128,128]{2,1,0:T(8,128)S(1)}, u32[]{:S(2)}, u32[]{:S(2)}) %collective-permute-start.7) | collective-permute-done | bytes 196640 | tf_op jit(solution)/shard_map/ppermute | solution.py:363
  138.8 3.4 %collective-permute-start.10 = (f32[2,128,128]{2,1,0:T(8,128)S(1)}, f32[2,128,128]{2,1,0:T(8,128)S(1)}, u32[]{:S(2)}, u32[]{:S(2)}) collective-permute-start(f32[2,128,128]{2,1,0:T(8,128)S(1)} %fusion.8), channel_id=1, source_target_pairs={{0,16},{16,32},{32,48},{48,64},{64,80},{80,96},{96,112},{112,128},... | collective-permute-start | bytes 393224 | tf_op jit(solution)/shard_map/ppermute | solution.py:350
  143.3 4.0 %collective-permute-done.10 = f32[2,128,128]{2,1,0:T(8,128)S(1)} collective-permute-done((f32[2,128,128]{2,1,0:T(8,128)S(1)}, f32[2,128,128]{2,1,0:T(8,128)S(1)}, u32[]{:S(2)}, u32[]{:S(2)}) %collective-permute-start.10) | collective-permute-done | bytes 131104 | tf_op jit(solution)/shard_map/ppermute | solution.py:350
  150.6 10.0 %collective-permute-start.12 = (f32[3,2,128,128]{3,2,1,0:T(8,128)S(1)}, f32[3,2,128,128]{3,2,1,0:T(8,128)S(1)}, u32[]{:S(2)}, u32[]{:S(2)}) collective-permute-start(f32[3,2,128,128]{3,2,1,0:T(8,128)S(1)} %pad_maximum_fusion.1.middle_ref), channel_id=1, source_target_pairs={{0,1},{1,2},{2,3},{3,4},{4,5},{5,6},{6,7},{7,8},{8,9},{9,10},{10,1... | collective-permute-start | bytes 1179656 | tf_op jit(solution)/shard_map/ppermute | solution.py:353
  165.8 9.7 %step.3 = (f32[32,5,8,256]{3,2,1,0:T(8,128)S(1)}, f32[3,3,128,128]{3,2,1,0:T(8,128)S(1)}, f32[3,3,128,128]{3,2,1,0:T(8,128)S(1)}, f32[3,3,128,128]{3,2,1,0:T(8,128)S(1)}) custom-call(s32[2,2]{1,0:T(2,128)S(1)} %add_bitcast_fusion.starts_ref, bf16[2,2,2,256,256]{4,3,2,1,0:T(8,128)(2,1)S(1)} %copy-done, f32[2,2,256,256]{3,2,1,0:T(8,128)S(1)} %bitcast.63, ...), custom_call_target="tpu_custom_call" | custom-call | tf_op jit(solution)/shard_map/step/pallas_call | solution.py:321
  177.9 20.7 %all_to_all.31 = f32[16,5,8,256]{3,2,1,0:T(8,128)S(1)} all-to-all(f32[16,5,8,256]{3,2,1,0:T(8,128)S(1)} %bitcast_add_fusion), channel_id=1, replica_groups=mesh['row'=16,'col'=16] {'row'}, dimensions={0} | all-to-all | bytes 1310720 | tf_op jit(solution)/shard_map/all_to_all | solution.py:368
  199.3 9.8 %all-to-all-start.4 = ((f32[8,5,8,256]{3,2,1,0:T(8,128)}), f32[8,5,8,256]{3,2,1,0:T(8,128)S(1)}, u32[]{:S(2)}, u32[]{:S(2)}) async-start(f32[8,5,8,256]{3,2,1,0:T(8,128)} %reshape.62), calls=%async_computation.4 | async-start | bytes 655360 | tf_op jit(solution)/shard_map/all_to_all | solution.py:375
  209.2 4.0 %collective-permute-start.14 = (f32[3,3,128,128]{3,2,1,0:T(8,128)S(1)}, f32[3,3,128,128]{3,2,1,0:T(8,128)S(1)}, u32[]{:S(2)}, u32[]{:S(2)}) collective-permute-start(f32[3,3,128,128]{3,2,1,0:T(8,128)S(1)} %copy-done.16), channel_id=1, source_target_pairs={{1,0},{2,1},{3,2},{4,3},{5,4},{6,5},{7,6},{8,7},{9,8},{10,9},{11,1... | collective-permute-start | bytes 1769480 | tf_op jit(solution)/shard_map/ppermute | solution.py:359
  213.2 7.6 %collective-permute-start.15 = (f32[3,3,128,128]{3,2,1,0:T(8,128)S(1)}, f32[3,3,128,128]{3,2,1,0:T(8,128)}, u32[]{:S(2)}, u32[]{:S(2)}) collective-permute-start(f32[3,3,128,128]{3,2,1,0:T(8,128)S(1)} %copy-done.14), channel_id=1, source_target_pairs={{0,1},{1,2},{2,3},{3,4},{4,5},{5,6},{6,7},{7,8},{8,9},{9,10},{10,1... | collective-permute-start | bytes 1769480 | tf_op jit(solution)/shard_map/ppermute | solution.py:359
  223.3 4.4 %all-to-all-start.5 = ((f32[16,4,8,256]{3,2,1,0:T(8,128)}), f32[16,4,8,256]{3,2,1,0:T(8,128)S(1)}, u32[]{:S(2)}, u32[]{:S(2)}) async-start(f32[16,4,8,256]{3,2,1,0:T(8,128)} %reshape.63), calls=%async_computation.5 | async-start | bytes 1048576 | tf_op jit(solution)/shard_map/all_to_all | solution.py:375
  227.7 16.7 %collective-permute-done.14 = f32[3,3,128,128]{3,2,1,0:T(8,128)S(1)} collective-permute-done((f32[3,3,128,128]{3,2,1,0:T(8,128)S(1)}, f32[3,3,128,128]{3,2,1,0:T(8,128)S(1)}, u32[]{:S(2)}, u32[]{:S(2)}) %collective-permute-start.14) | collective-permute-done | bytes 589856 | tf_op jit(solution)/shard_map/ppermute | solution.py:359
  252.0 4.0 %collective-permute-done.17 = f32[3,128,128]{2,1,0:T(8,128)S(1)} collective-permute-done((f32[3,128,128]{2,1,0:T(8,128)S(1)}, f32[3,128,128]{2,1,0:T(8,128)S(1)}, u32[]{:S(2)}, u32[]{:S(2)}) %collective-permute-start.17) | collective-permute-done | bytes 196640 | tf_op jit(solution)/shard_map/ppermute | solution.py:363
  (100 shorter events, 58.0 us)
Async XLA Ops:
  0.6 8.7 %collective-permute-start = (f32[2,128,128]{2,1,0:T(8,128)}, f32[2,128,128]{2,1,0:T(8,128)S(1)}, u32[]{:S(2)}, u32[]{:S(2)}) collective-permute-start(f32[2,128,128]{2,1,0:T(8,128)} %param.5), channel_id=1, source_target_pairs={{0,16},{16,32},{32,48},{48,64},{64,80},{80,96},{96,112},{112,128},... | collective-permute-start | bytes 393224 | tf_op jit(solution)/shard_map/ppermute | solution.py:350
  4.0 6.4 %collective-permute-start.1 = (f32[2,128,128]{2,1,0:T(8,128)}, f32[2,128,128]{2,1,0:T(8,128)S(1)}, u32[]{:S(2)}, u32[]{:S(2)}) collective-permute-start(f32[2,128,128]{2,1,0:T(8,128)} %param.5), channel_id=1, source_target_pairs={{16,0},{32,16},{48,32},{64,48},{80,64},{96,80},{112,96},{128,112},... | collective-permute-start | bytes 393224 | tf_op jit(solution)/shard_map/ppermute | solution.py:351
  11.4 19.3 %collective-permute-start.3 = (f32[3,2,128,128]{3,2,1,0:T(8,128)S(1)}, f32[3,2,128,128]{3,2,1,0:T(8,128)S(1)}, u32[]{:S(2)}, u32[]{:S(2)}) collective-permute-start(f32[3,2,128,128]{3,2,1,0:T(8,128)S(1)} %pad_maximum_fusion.middle_ref), channel_id=1, source_target_pairs={{1,0},{2,1},{3,2},{4,3},{5,4},{6,5},{7,6},{8,7},{9,8},{10,9},{11,1... | collective-permute-start | bytes 1179656 | tf_op jit(solution)/shard_map/ppermute | solution.py:354
  15.1 16.8 %collective-permute-start.2 = (f32[3,2,128,128]{3,2,1,0:T(8,128)S(1)}, f32[3,2,128,128]{3,2,1,0:T(8,128)S(1)}, u32[]{:S(2)}, u32[]{:S(2)}) collective-permute-start(f32[3,2,128,128]{3,2,1,0:T(8,128)S(1)} %pad_maximum_fusion.middle_ref), channel_id=1, source_target_pairs={{0,1},{1,2},{2,3},{3,4},{4,5},{5,6},{6,7},{7,8},{8,9},{9,10},{10,1... | collective-permute-start | bytes 1179656 | tf_op jit(solution)/shard_map/ppermute | solution.py:353
  48.9 2.4 collective-permute-start.8
  79.4 22.5 %all-to-all-start.1 = ((f32[8,5,8,256]{3,2,1,0:T(8,128)}), f32[8,5,8,256]{3,2,1,0:T(8,128)}, u32[]{:S(2)}, u32[]{:S(2)}) async-start(f32[8,5,8,256]{3,2,1,0:T(8,128)} %reshape.58), calls=%async_computation.1 | async-start | bytes 655360 | tf_op jit(solution)/shard_map/all_to_all | solution.py:375
  89.4 35.2 %collective-permute-start.4 = (f32[3,3,128,128]{3,2,1,0:T(8,128)S(1)}, f32[3,3,128,128]{3,2,1,0:T(8,128)}, u32[]{:S(2)}, u32[]{:S(2)}) collective-permute-start(f32[3,3,128,128]{3,2,1,0:T(8,128)S(1)} %copy-done.12), channel_id=1, source_target_pairs={{1,0},{2,1},{3,2},{4,3},{5,4},{6,5},{7,6},{8,7},{9,8},{10,9},{11,1... | collective-permute-start | bytes 1769480 | tf_op jit(solution)/shard_map/ppermute | solution.py:359
  93.4 31.2 %collective-permute-start.5 = (f32[3,3,128,128]{3,2,1,0:T(8,128)S(1)}, f32[3,3,128,128]{3,2,1,0:T(8,128)}, u32[]{:S(2)}, u32[]{:S(2)}) collective-permute-start(f32[3,3,128,128]{3,2,1,0:T(8,128)S(1)} %copy-done.10), channel_id=1, source_target_pairs={{0,1},{1,2},{2,3},{3,4},{4,5},{5,6},{6,7},{7,8},{8,9},{9,10},{10,1... | collective-permute-start | bytes 1769480 | tf_op jit(solution)/shard_map/ppermute | solution.py:359
  104.6 32.1 %all-to-all-start.2 = ((f32[16,4,8,256]{3,2,1,0:T(8,128)}), f32[16,4,8,256]{3,2,1,0:T(8,128)}, u32[]{:S(2)}, u32[]{:S(2)}) async-start(f32[16,4,8,256]{3,2,1,0:T(8,128)} %reshape.59), calls=%async_computation.2 | async-start | bytes 1048576 | tf_op jit(solution)/shard_map/all_to_all | solution.py:375
  126.1 6.5 %collective-permute-start.6 = (f32[3,128,128]{2,1,0:T(8,128)S(1)}, f32[3,128,128]{2,1,0:T(8,128)S(1)}, u32[]{:S(2)}, u32[]{:S(2)}) collective-permute-start(f32[3,128,128]{2,1,0:T(8,128)S(1)} %get-tuple-element.20), channel_id=1, source_target_pairs={{16,0},{32,16},{48,32},{64,48},{80,64},{96,80},{112,96},{128,112},... | collective-permute-start | bytes 589832 | tf_op jit(solution)/shard_map/ppermute | solution.py:362
  128.1 8.5 %collective-permute-start.7 = (f32[3,128,128]{2,1,0:T(8,128)S(1)}, f32[3,128,128]{2,1,0:T(8,128)S(1)}, u32[]{:S(2)}, u32[]{:S(2)}) collective-permute-start(f32[3,128,128]{2,1,0:T(8,128)S(1)} %get-tuple-element.21), channel_id=1, source_target_pairs={{0,16},{16,32},{32,48},{48,64},{64,80},{80,96},{96,112},{112,128},... | collective-permute-start | bytes 589832 | tf_op jit(solution)/shard_map/ppermute | solution.py:363
  136.7 23.9 %collective-permute-start.9 = (f32[16,4,8,256]{3,2,1,0:T(8,128)}, f32[16,4,8,256]{3,2,1,0:T(8,128)S(1)}, u32[]{:S(2)}, u32[]{:S(2)}) collective-permute-start(f32[16,4,8,256]{3,2,1,0:T(8,128)} %all-to-all-done.2), channel_id=1, source_target_pairs={{0,1},{1,0},{2,3},{3,2},{4,5},{5,4},{6,7},{7,6},{8,9},{9,8},{10,11... | collective-permute-start | bytes 1572872 | tf_op jit(solution)/shard_map/ppermute | solution.py:392
  136.8 6.5 %collective-permute-start.11 = (f32[2,128,128]{2,1,0:T(8,128)S(1)}, f32[2,128,128]{2,1,0:T(8,128)S(1)}, u32[]{:S(2)}, u32[]{:S(2)}) collective-permute-start(f32[2,128,128]{2,1,0:T(8,128)S(1)} %fusion.8), channel_id=1, source_target_pairs={{16,0},{32,16},{48,32},{64,48},{80,64},{96,80},{112,96},{128,112},... | collective-permute-start | bytes 393224 | tf_op jit(solution)/shard_map/ppermute | solution.py:351
  138.8 8.6 %collective-permute-start.10 = (f32[2,128,128]{2,1,0:T(8,128)S(1)}, f32[2,128,128]{2,1,0:T(8,128)S(1)}, u32[]{:S(2)}, u32[]{:S(2)}) collective-permute-start(f32[2,128,128]{2,1,0:T(8,128)S(1)} %fusion.8), channel_id=1, source_target_pairs={{0,16},{16,32},{32,48},{48,64},{64,80},{80,96},{96,112},{112,128},... | collective-permute-start | bytes 393224 | tf_op jit(solution)/shard_map/ppermute | solution.py:350
  147.4 17.2 %collective-permute-start.13 = (f32[3,2,128,128]{3,2,1,0:T(8,128)S(1)}, f32[3,2,128,128]{3,2,1,0:T(8,128)S(1)}, u32[]{:S(2)}, u32[]{:S(2)}) collective-permute-start(f32[3,2,128,128]{3,2,1,0:T(8,128)S(1)} %pad_maximum_fusion.1.middle_ref), channel_id=1, source_target_pairs={{1,0},{2,1},{3,2},{4,3},{5,4},{6,5},{7,6},{8,7},{9,8},{10,9},{11,1... | collective-permute-start | bytes 1179656 | tf_op jit(solution)/shard_map/ppermute | solution.py:354
  150.6 15.2 %collective-permute-start.12 = (f32[3,2,128,128]{3,2,1,0:T(8,128)S(1)}, f32[3,2,128,128]{3,2,1,0:T(8,128)S(1)}, u32[]{:S(2)}, u32[]{:S(2)}) collective-permute-start(f32[3,2,128,128]{3,2,1,0:T(8,128)S(1)} %pad_maximum_fusion.1.middle_ref), channel_id=1, source_target_pairs={{0,1},{1,2},{2,3},{3,4},{4,5},{5,6},{6,7},{7,8},{8,9},{9,10},{10,1... | collective-permute-start | bytes 1179656 | tf_op jit(solution)/shard_map/ppermute | solution.py:353
  175.6 2.2 collective-permute-start.18
  199.3 22.3 %all-to-all-start.4 = ((f32[8,5,8,256]{3,2,1,0:T(8,128)}), f32[8,5,8,256]{3,2,1,0:T(8,128)S(1)}, u32[]{:S(2)}, u32[]{:S(2)}) async-start(f32[8,5,8,256]{3,2,1,0:T(8,128)} %reshape.62), calls=%async_computation.4 | async-start | bytes 655360 | tf_op jit(solution)/shard_map/all_to_all | solution.py:375
  209.2 35.1 %collective-permute-start.14 = (f32[3,3,128,128]{3,2,1,0:T(8,128)S(1)}, f32[3,3,128,128]{3,2,1,0:T(8,128)S(1)}, u32[]{:S(2)}, u32[]{:S(2)}) collective-permute-start(f32[3,3,128,128]{3,2,1,0:T(8,128)S(1)} %copy-done.16), channel_id=1, source_target_pairs={{1,0},{2,1},{3,2},{4,3},{5,4},{6,5},{7,6},{8,7},{9,8},{10,9},{11,1... | collective-permute-start | bytes 1769480 | tf_op jit(solution)/shard_map/ppermute | solution.py:359
  213.2 31.1 %collective-permute-start.15 = (f32[3,3,128,128]{3,2,1,0:T(8,128)S(1)}, f32[3,3,128,128]{3,2,1,0:T(8,128)}, u32[]{:S(2)}, u32[]{:S(2)}) collective-permute-start(f32[3,3,128,128]{3,2,1,0:T(8,128)S(1)} %copy-done.14), channel_id=1, source_target_pairs={{0,1},{1,2},{2,3},{3,4},{4,5},{5,6},{6,7},{7,8},{8,9},{9,10},{10,1... | collective-permute-start | bytes 1769480 | tf_op jit(solution)/shard_map/ppermute | solution.py:359
  223.3 27.6 %all-to-all-start.5 = ((f32[16,4,8,256]{3,2,1,0:T(8,128)}), f32[16,4,8,256]{3,2,1,0:T(8,128)S(1)}, u32[]{:S(2)}, u32[]{:S(2)}) async-start(f32[16,4,8,256]{3,2,1,0:T(8,128)} %reshape.63), calls=%async_computation.5 | async-start | bytes 1048576 | tf_op jit(solution)/shard_map/all_to_all | solution.py:375
  245.6 6.4 %collective-permute-start.16 = (f32[3,128,128]{2,1,0:T(8,128)S(1)}, f32[3,128,128]{2,1,0:T(8,128)S(1)}, u32[]{:S(2)}, u32[]{:S(2)}) collective-permute-start(f32[3,128,128]{2,1,0:T(8,128)S(1)} %get-tuple-element.18), channel_id=1, source_target_pairs={{16,0},{32,16},{48,32},{64,48},{80,64},{96,80},{112,96},{128,112},... | collective-permute-start | bytes 589832 | tf_op jit(solution)/shard_map/ppermute | solution.py:362
  247.5 8.5 %collective-permute-start.17 = (f32[3,128,128]{2,1,0:T(8,128)S(1)}, f32[3,128,128]{2,1,0:T(8,128)S(1)}, u32[]{:S(2)}, u32[]{:S(2)}) collective-permute-start(f32[3,128,128]{2,1,0:T(8,128)S(1)} %get-tuple-element.19), channel_id=1, source_target_pairs={{0,16},{16,32},{32,48},{48,64},{64,80},{80,96},{96,112},{112,128},... | collective-permute-start | bytes 589832 | tf_op jit(solution)/shard_map/ppermute | solution.py:363
  250.9 5.9 %collective-permute-start.19 = (f32[16,4,8,256]{3,2,1,0:T(8,128)S(1)}, f32[16,4,8,256]{3,2,1,0:T(8,128)S(1)}, u32[]{:S(2)}, u32[]{:S(2)}) collective-permute-start(f32[16,4,8,256]{3,2,1,0:T(8,128)S(1)} %all-to-all-done.5), channel_id=1, source_target_pairs={{0,1},{1,0},{2,3},{3,2},{4,5},{5,4},{6,7},{7,6},{8,9},{9,8},{10,11... | collective-permute-start | bytes 1572872 | tf_op jit(solution)/shard_map/ppermute | solution.py:392
  (19 other events, 217.5 us)

commit v2 on v1

--- a/solution.py
+++ b/solution.py
@@ -21,6 +21,8 @@
 HALF = SIDE // 2
 WIDE = 3 * TILE
 CHUNK = 64
+GROUPS = 16
+DEPTH = 8
 F32 = jnp.float32
 BF16 = jnp.bfloat16
 
@@ -74,40 +76,82 @@
         out_ref[scan, 1] = turned[HALF:]
 
 
-def step_kernel(
-    starts_ref,
-    table_ref,
-    probe_ref,
-    measured_ref,
-    left_ref,
-    middle_ref,
-    right_ref,
-    probe_out,
-    grad_left,
-    grad_middle,
-    grad_right,
-    padded,
-    windows,
-    folded,
-    stacked,
-    far,
-    back,
-    contrib,
-    total,
-):
+def lay_out_kernel(core_ref, mine_ref, other_ref, out_ref):
+    for half, ref in enumerate((mine_ref, other_ref)):
+        place = core_ref[0] if half == 0 else 1 - core_ref[0]
+        for part in range(4):
+            out_ref[part, pl.ds(place * GROUPS, GROUPS)] = ref[:, part]
+
+
+def step_kernel(halves, offsets_ref, core_ref, table_in, *refs):
+    probe_in, refs = refs[: 1 + halves], refs[1 + halves :]
+    (
+        measured_in,
+        left_in,
+        tile_in,
+        right_in,
+        above_in,
+        below_in,
+        mine_out,
+        other_out,
+        grad_above,
+        grad_middle,
+        grad_below,
+        table_ref,
+        probe,
+        measured_ref,
+        padded,
+        windows,
+        folded,
+        stacked,
+        far,
+        back,
+        contrib,
+        total,
+        sums,
+        semaphores,
+    ) = refs
+    core = core_ref[0]
+    copies = []
+
+    def start(source, target):
+        copy = pltpu.make_async_copy(source, target, semaphores.at[len(copies)])
+        copy.start()
+        copies.append(copy)
+
+    def third(block):
+        return pl.ds(block * TILE, TILE)
+
+    for block, piece in enumerate((left_in, tile_in, right_in)):
+        start(piece, padded.at[:, third(1), third(block)])
+        start(above_in.at[block], padded.at[:, third(0), third(block)])
+        start(below_in.at[block], padded.at[:, third(2), third(block)])
+    near = len(copies)
+    if halves:
+        for half, ref in enumerate(probe_in):
+            place = core if half == 0 else 1 - core
+            for part in range(4):
+                start(ref.at[:, part], probe.at[part, pl.ds(place * GROUPS, GROUPS)])
+    else:
+        start(probe_in[0], probe)
+    start(table_in, table_ref)
+    operands = len(copies)
+    start(measured_in, measured_ref)
+
+    def probe_rows(part, mode, piece, columns=slice(None)):
+        groups = pl.ds(piece * (CHUNK // 8), CHUNK // 8)
+        value = probe[2 * part + mode, groups, :, columns]
+        return value.reshape(CHUNK, value.shape[-1])
+
     lane = lax.broadcasted_iota(jnp.int32, (CHUNK // 8, 8, TILE), 2)
     sublane = lax.broadcasted_iota(jnp.int32, (CHUNK // 8, 8, TILE), 1)
-    for channel in range(2):
-        for block in range(3):
-            rows = pl.ds(block * TILE, TILE)
-            padded[channel, rows, 0:TILE] = left_ref[block, channel]
-            padded[channel, rows, TILE : 2 * TILE] = middle_ref[block, channel]
-            padded[channel, rows, 2 * TILE :] = right_ref[block, channel]
     for channel in range(3):
         total[channel] = jnp.zeros((WIDE + 8, WIDE), F32)
+    for copy in copies[:near]:
+        copy.wait()
 
     def cut(scan, carry):
-        row, column = starts_ref[scan, 0], starts_ref[scan, 1]
+        row, column = offsets_ref[0, 0, scan, 0] + HALF, offsets_ref[0, 0, scan, 1] + HALF
         inner = lax.rem(row, 8)
         base = pl.multiple_of(row - inner, 8)
         turn, keep = lax.rem(TILE - column, TILE), lane < TILE - column
@@ -127,12 +171,14 @@
         return carry
 
     lax.fori_loop(0, 2, cut, 0)
+    for copy in copies[near:operands]:
+        copy.wait()
 
     def forward(image, carry):
         scan, mode = image // 2, image % 2
         for piece in range(SIDE // CHUNK):
             rows = pl.ds(piece * CHUNK, CHUNK)
-            p_re, p_im = probe_ref[0, mode, rows, :], probe_ref[1, mode, rows, :]
+            p_re, p_im = probe_rows(0, mode, piece), probe_rows(1, mode, piece)
             w_re, w_im = windows[scan, 0, rows, :], windows[scan, 1, rows, :]
             e_re = p_re * w_re - p_im * w_im
             e_im = p_re * w_im + p_im * w_re
@@ -185,6 +231,7 @@
                 far[2 * scan + mode, other, lower, :] = parts[2 * mode + 1] * factor
         return carry
 
+    copies[operands].wait()
     lax.fori_loop(0, 4, scale, 0)
 
     def backward(image, carry):
@@ -221,7 +268,8 @@
                 sign = 1.0 if b == 0 else -1.0
                 b_re = even[:, :HALF] + sign * odd[:, :HALF]
                 b_im = even[:, HALF:] + sign * odd[:, HALF:]
-                p_re, p_im = probe_ref[0, mode, rows, columns], probe_ref[1, mode, rows, columns]
+                p_re = probe_rows(0, mode, piece, columns)
+                p_im = probe_rows(1, mode, piece, columns)
                 w_re, w_im = windows[scan, 0, rows, columns], windows[scan, 1, rows, columns]
                 o_re = p_re * b_re + p_im * b_im
                 o_im = p_re * b_im - p_im * b_re
@@ -239,14 +287,14 @@
                     inner = slice(slot * 8, slot * 8 + 8)
                     for part, value in enumerate((g_re, g_im)):
                         place = 2 * part + mode
-                        old = probe_out[group, place, :, columns]
-                        probe_out[group, place, :, columns] = value[inner] + jnp.where(
+                        old = sums[group, place, :, columns]
+                        sums[group, place, :, columns] = value[inner] + jnp.where(
                             first_scan, jnp.zeros_like(old), old
                         )
 
         @pl.when(mode == 1)
         def _():
-            row, column = starts_ref[scan, 0], starts_ref[scan, 1]
+            row, column = offsets_ref[0, 0, scan, 0] + HALF, offsets_ref[0, 0, scan, 1] + HALF
             inner = lax.rem(row, 8)
             base = pl.multiple_of(row - inner, 8)
             turn, keep = lax.rem(column, TILE), lane >= column
@@ -281,7 +329,7 @@
         power = None
         for mode in range(2):
             for part in range(2):
-                value = probe_ref[part, mode, rows, :]
+                value = probe_rows(part, mode, piece)
                 power = value * value if power is None else power + value * value
         contrib[2, rows, :] = power
         weight = None
@@ -290,19 +338,49 @@
                 value = windows[scan, part, rows, :]
                 weight = value * value if weight is None else weight + value * value
         for slot in range(CHUNK // 8):
-            probe_out[piece * (CHUNK // 8) + slot, 4] = weight[slot * 8 : slot * 8 + 8]
+            sums[piece * (CHUNK // 8) + slot, 4] = weight[slot * 8 : slot * 8 + 8]
 
     lax.fori_loop(0, 4, backward, 0)
 
-    for channel in range(3):
-        for block in range(3):
-            rows = pl.ds(block * TILE, TILE)
-            grad_left[block, channel] = total[channel, rows, 0:TILE]
-            grad_middle[block, channel] = total[channel, rows, TILE : 2 * TILE]
-            grad_right[block, channel] = total[channel, rows, 2 * TILE :]
+    done = len(copies)
+    for block, ref in enumerate((grad_above, grad_middle, grad_below)):
+        for column in range(3):
+            start(total.at[:, third(block), third(column)], ref.at[column])
+    start(sums.at[pl.ds(core * GROUPS, GROUPS)], mine_out)
+    start(sums.at[pl.ds((1 - core) * GROUPS, GROUPS)], other_out)
+    for copy in copies[done:]:
+        copy.wait()
+
+
+def spread_kernel(pieces_ref, out_ref):
+    total = pieces_ref[0]
+    for piece in range(1, GROUPS):
+        total = total + pieces_ref[piece]
+    for copy in range(DEPTH):
+        out_ref[copy] = total
+
+
+def update_kernel(pieces_ref, old_ref, out_ref, new_ref):
+    total = pieces_ref[0]
+    for piece in range(1, DEPTH):
+        total = total + pieces_ref[piece]
+    new = old_ref[...] + PROBE_STEP * total[:4] / (total[4:] + PROBE_REG)
+    new_ref[...] = new
+    for copy in range(GROUPS):
+        out_ref[copy] = new
 
 
 VMEM_SPEC = pl.BlockSpec(memory_space=pltpu.VMEM)
+SMEM_SPEC = pl.BlockSpec(memory_space=pltpu.SMEM)
+ANY_SPEC = pl.BlockSpec(memory_space=pl.ANY)
+
+
+def in_hbm(value):
+    return pltpu.with_memory_space_constraint(value, pltpu.HBM)
+
+
+def params(mebibytes):
+    return pltpu.CompilerParams(vmem_limit_bytes=mebibytes * 2**20)
 
 
 def sort_measured(measured):
@@ -311,19 +389,24 @@
         out_shape=jax.ShapeDtypeStruct((2, 2, HALF, SIDE), F32),
         in_specs=[VMEM_SPEC],
         out_specs=VMEM_SPEC,
-        compiler_params=pltpu.CompilerParams(vmem_limit_bytes=40 * 2**20),
+        compiler_params=params(8),
         name="sort_measured",
     )(measured)
 
 
-def step(starts, table, probe, measured, left, middle, right):
-    column = jax.ShapeDtypeStruct((3, 3, TILE, TILE), F32)
+def step(offsets, core, table, probe, measured, around):
+    halves = len(probe) - 1
+    band = jax.ShapeDtypeStruct((3, 3, TILE, TILE), F32)
+    half = jax.ShapeDtypeStruct((GROUPS, 5, 8, SIDE), F32)
     return pl.pallas_call(
-        step_kernel,
-        out_shape=[jax.ShapeDtypeStruct((SIDE // 8, 5, 8, SIDE), F32), column, column, column],
-        in_specs=[pl.BlockSpec(memory_space=pltpu.SMEM)] + [VMEM_SPEC] * 6,
-        out_specs=[VMEM_SPEC] * 4,
+        functools.partial(step_kernel, halves),
+        out_shape=[half, half, band, band, band],
+        in_specs=[SMEM_SPEC, SMEM_SPEC] + [ANY_SPEC] * (8 + halves),
+        out_specs=[ANY_SPEC] * 5,
         scratch_shapes=[
+            pltpu.VMEM(table.shape, BF16),
+            pltpu.VMEM((4, 2 * GROUPS, 8, SIDE), F32),
+            pltpu.VMEM(measured.shape, F32),
             pltpu.VMEM((2, WIDE + 8, WIDE), F32),
             pltpu.VMEM((2, 2, SIDE, SIDE), F32),
             pltpu.VMEM((2, 2, SIDE, SIDE), BF16),
@@ -332,10 +415,12 @@
             pltpu.VMEM((2, SIDE, SIDE), F32),
             pltpu.VMEM((3, SIDE, SIDE), F32),
             pltpu.VMEM((3, WIDE + 8, WIDE), F32),
+            pltpu.VMEM((2 * GROUPS, 5, 8, SIDE), F32),
+            pltpu.SemaphoreType.DMA((32,)),
         ],
-        compiler_params=pltpu.CompilerParams(vmem_limit_bytes=40 * 2**20),
+        compiler_params=params(20),
         name="step",
-    )(starts, table, probe, measured, left, middle, right)
+    )(offsets, core, table, *probe, measured, *around)
 
 
 def up(axis):
@@ -347,69 +432,96 @@
 
 
 def neighbourhood(tile):
-    above = lax.ppermute(tile, "row", up("row"))
-    below = lax.ppermute(tile, "row", down("row"))
-    middle = jnp.stack([above, tile, below])
-    left = lax.ppermute(middle, "col", up("col"))
-    right = lax.ppermute(middle, "col", down("col"))
-    return left, middle, right
-
-
-def fold(left, middle, right):
-    column = middle + lax.ppermute(left, "col", down("col")) + lax.ppermute(right, "col", up("col"))
-    return (
-        column[1]
-        + lax.ppermute(column[0], "row", down("row"))
-        + lax.ppermute(column[2], "row", up("row"))
-    )
-
-
-def scatter_sum(value, axis, count, groups=None):
-    pieces = lax.all_to_all(value, axis, 0, 0, axis_index_groups=groups, tiled=True)
-    return pieces.reshape((count, value.shape[0] // count) + value.shape[1:]).sum(0)
-
-
-def gather(value, axis, count, groups=None):
-    copies = jnp.broadcast_to(value[None], (count,) + value.shape)
-    copies = copies.reshape((count * value.shape[0],) + value.shape[1:])
-    return lax.all_to_all(copies, axis, 0, 0, axis_index_groups=groups, tiled=True)
-
-
-def new_probe(sums, probe_rows):
-    core = lax.axis_index("col") % 2
-    swap = [(i, i ^ 1) for i in range(16)]
-    groups = [[2 * i + c for i in range(8)] for c in range(2)]
-    halves = sums.reshape((2, 16) + sums.shape[1:])
-    mine = lax.dynamic_index_in_dim(halves, core, 0, False)
-    other = lax.dynamic_index_in_dim(halves, 1 - core, 0, False)
-    mine = mine + lax.ppermute(other, "col", swap)
-    mine = scatter_sum(mine, "row", 16)
-    mine = gather(mine, "col", 8, groups).sum(0, keepdims=True)
-    place = core * 16 + lax.axis_index("row")
-    old = lax.dynamic_slice_in_dim(probe_rows, place, 1, 0)
-    mine = old + PROBE_STEP * mine[:, :4] / (mine[:, 4:] + PROBE_REG)
-    mine = gather(mine, "row", 16)
-    other = lax.ppermute(mine, "col", swap)
-    return jnp.where(
-        core == 0, jnp.concatenate([mine, other]), jnp.concatenate([other, mine])
-    )
+    left = lax.ppermute(tile, "col", up("col"))
+    right = lax.ppermute(tile, "col", down("col"))
+    band = jnp.stack([left, tile, right])
+    above = lax.ppermute(band, "row", up("row"))
+    below = lax.ppermute(band, "row", down("row"))
+    return left, tile, right, above, below
+
+
+def fold(above, middle, below):
+    above = lax.ppermute(above, "row", down("row"))
+    below = lax.ppermute(below, "row", up("row"))
+    first, own, last = (middle[i] + above[i] + below[i] for i in range(3))
+    first = lax.ppermute(first, "col", down("col"))
+    last = lax.ppermute(last, "col", up("col"))
+    return own + first + last
+
+
+def places(device):
+    row, column = divmod(device, 16)
+    return (column // 8) * 4 + row // 4, row % 4, column // 2 % 4, column % 2
+
+
+def grouped(key):
+    groups = {}
+    for device in range(256):
+        groups.setdefault(key(*places(device)), []).append(device)
+    return list(groups.values())
+
+
+PLANES = grouped(lambda z, y, x, core: (z, core))
+LINES = grouped(lambda z, y, x, core: (y, x, core))
+BOTH = ("row", "col")
+SWAP = [(i, i ^ 1) for i in range(16)]
+
+
+def exchange(value, groups):
+    return lax.all_to_all(value, BOTH, 0, 0, axis_index_groups=groups, tiled=True)
+
+
+def new_probe(mine, other, old):
+    mine = mine + lax.ppermute(other, "col", SWAP)
+    pieces = exchange(mine, PLANES)
+    pieces = pl.pallas_call(
+        spread_kernel,
+        out_shape=jax.ShapeDtypeStruct((DEPTH, 5, 8, SIDE), F32),
+        compiler_params=params(8),
+        name="spread",
+    )(pieces)
+    pieces = exchange(pieces, LINES)
+    pieces, new = pl.pallas_call(
+        update_kernel,
+        out_shape=[
+            jax.ShapeDtypeStruct((GROUPS, 4, 8, SIDE), F32),
+            jax.ShapeDtypeStruct((4, 8, SIDE), F32),
+        ],
+        compiler_params=params(8),
+        name="update",
+    )(pieces, old)
+    mine = exchange(pieces, PLANES)
+    other = lax.ppermute(mine, "col", SWAP)
+    return mine, other, new
 
 
 def local(object_field, probe, amplitudes, offsets):
-    table = jnp.asarray(tables())
-    starts = offsets[0, 0] + HALF
+    table = in_hbm(jnp.asarray(tables()))
+    row, column = lax.axis_index("row"), lax.axis_index("col")
+    core = column & 1
+    group = core * GROUPS + (row & 3) * 4 + (lax.shift_right_logical(column, 1) & 3)
+    probe = probe.reshape(4, 2 * GROUPS, 8, SIDE)
+    old = lax.dynamic_index_in_dim(probe, group, 1, False)
+    core = core.reshape(1)
     measured = sort_measured(amplitudes[0, 0])
+    parts = (in_hbm(probe),)
     for iteration in range(ITERS):
-        left, middle, right = neighbourhood(object_field)
-        sums, grad_left, grad_middle, grad_right = step(
-            starts, table, probe, measured, left, middle, right
+        mine, other, above, middle, below = step(
+            offsets, core, table, parts, measured, neighbourhood(object_field)
         )
-        rows = probe.reshape(4, SIDE // 8, 8, SIDE).transpose(1, 0, 2, 3)
-        rows = new_probe(sums, rows)
-        totals = fold(grad_left, grad_middle, grad_right)
+        mine, other, old = new_probe(mine, other, old)
+        parts = (mine, other)
+        totals = fold(above, middle, below)
         object_field = object_field + OBJECT_STEP * totals[0:2] / (totals[2:3] + OBJECT_REG)
-        probe = rows.transpose(1, 0, 2, 3).reshape(2, 2, SIDE, SIDE)
-    return (object_field, probe)
+    probe = pl.pallas_call(
+        lay_out_kernel,
+        out_shape=jax.ShapeDtypeStruct((4, 2 * GROUPS, 8, SIDE), F32),
+        in_specs=[SMEM_SPEC, VMEM_SPEC, VMEM_SPEC],
+        out_specs=VMEM_SPEC,
+        compiler_params=params(8),
+        name="lay_out",
+    )(core, *parts)
+    return (object_field, probe.reshape(2, 2, SIDE, SIDE))
 
 
 def solution(mesh):

time: 262 us -> 221 us (0.84)
  blocking collectives: 45.7 us -> 15.9 us
  waiting for transfers between devices: 65.5 us -> 49.9 us
  starting transfers between devices: 100 us -> 113 us
  local copies, waits for them, and re-layouts: 13.7 us -> 2.28 us
  Pallas kernels: 20.2 us -> 27.7 us
  other arithmetic: 11.4 us -> 7.15 us
    all_to_all x2 -> x1, blocking collectives: 45.7 us -> 15.9 us  [exchange(): lax.all_to_all(value, BOTH, 0, 0, axis_index_groups=groups, tiled=True)]
    ppermute x20, waiting for transfers between devices: 63.7 us -> 38.7 us  [the longest x2 9.9 us: neighbourhood(): below = lax.ppermute(band, 'row', down('row'))]
    all_to_all x4 -> x5, waiting for transfers between devices: 1.74 us -> 11.2 us  [exchange(): lax.all_to_all(value, BOTH, 0, 0, axis_index_groups=groups, tiled=True)]
    all_to_all x4 -> x5, starting transfers between devices: 28.6 us -> 36.6 us  [exchange(): lax.all_to_all(value, BOTH, 0, 0, axis_index_groups=groups, tiled=True)]
    pallas_call x2 -> x7, Pallas kernels: 19.3 us -> 26.8 us  [the longest x2 22.5 us: step(): pl.pallas_call(functools.partial(step_kernel, halves), out_shape=[half, h...]
    unnamed x38 -> x10, local copies, waits for them, and re-layouts: 8.31 us -> 1.52 us
    ppermute x20, starting transfers between devices: 71.7 us -> 76.8 us  [the longest x2 22.9 us: fold(): last = lax.ppermute(last, 'col', up('col'))]
    reshape x4 -> x0, local copies, waits for them, and re-layouts: 3.2 us -> none  [gather(): copies = copies.reshape((count * value.shape[0],) + value.shape[1:])]
  transfers between devices with their start and end apart: 24 -> 25, of which waited for: 18 -> 17; matrix products, arithmetic and copies ran while one was open for 4% -> 3% of each run, Pallas kernels for 0% -> 1%
where the time goes in v2:
time: 221 us; the launch traced here: 217 us
  starting transfers between devices  113 us (51%)
  waiting for transfers between devices  49.9 us (23%)
  Pallas kernels  27.7 us (13%)
  blocking collectives  15.9 us (7%)
  other arithmetic  7.15 us (3%)
  local copies, waits for them, and re-layouts  2.28 us (1%)
    all_to_all x5, starting transfers between devices, exchange(): lax.all_to_all(value, BOTH, 0, 0, axis_index_groups=groups, tiled=True)  36.6 us
    ppermute x2, starting transfers between devices, fold(): last = lax.ppermute(last, 'col', up('col'))  22.9 us
    pallas_call x2, Pallas kernels, step(): pl.pallas_call(functools.partial(step_kernel, halves), out_shape=[half, h...  22.5 us
    ppermute x2, starting transfers between devices, neighbourhood(): left = lax.ppermute(tile, 'col', up('col'))  18.7 us
    all_to_all x1, blocking collectives, exchange(): lax.all_to_all(value, BOTH, 0, 0, axis_index_groups=groups, tiled=True)  15.9 us
    all_to_all x5, waiting for transfers between devices, exchange(): lax.all_to_all(value, BOTH, 0, 0, axis_index_groups=groups, tiled=True)  11.2 us
    ppermute x2, waiting for transfers between devices, neighbourhood(): below = lax.ppermute(band, 'row', down('row'))  9.9 us
    ppermute x2, waiting for transfers between devices, neighbourhood(): above = lax.ppermute(band, 'row', up('row'))  8.98 us
  transfers between devices with their start and end apart: 25, of which 17 were waited for; matrix products, arithmetic and copies ran while one was open for 3% of the time, Pallas kernels for 1%

profile of v2, /device:TPU:39, one launch (start us, length us, event | category | flops | bytes accessed | tf_op | source)
XLA Modules:
  0.0 217.3 jit_solution(5535527079811530497)
XLA Ops:
  3.4 9.0 %collective-permute-start = (f32[2,128,128]{2,1,0:T(8,128)}, f32[2,128,128]{2,1,0:T(8,128)S(1)}, u32[]{:S(2)}, u32[]{:S(2)}) collective-permute-start(f32[2,128,128]{2,1,0:T(8,128)} %refs_3_.1), channel_id=1, source_target_pairs={{0,1},{1,2},{2,3},{3,4},{4,5},{5,6},{6,7},{7,8},{8,9},{9,10},{10,1... | collective-permute-start | bytes 393224 | tf_op jit(solution)/shard_map/ppermute | solution.py:435
  15.5 4.2 %collective-permute-start.3 = (f32[3,2,128,128]{3,2,1,0:T(8,128)S(1)}, f32[3,2,128,128]{3,2,1,0:T(8,128)S(1)}, u32[]{:S(2)}, u32[]{:S(2)}) collective-permute-start(f32[3,2,128,128]{3,2,1,0:T(8,128)S(1)} %pad_maximum_fusion), channel_id=1, source_target_pairs={{16,0},{32,16},{48,32},{64,48},{80,64},{96,80},{112,96},{128,112},... | collective-permute-start | bytes 1179656 | tf_op jit(solution)/shard_map/ppermute | solution.py:439
  25.6 5.2 %collective-permute-done.2.refs_5_ = f32[3,2,128,128]{3,2,1,0:T(8,128)S(1)} collective-permute-done((f32[3,2,128,128]{3,2,1,0:T(8,128)S(1)}, f32[3,2,128,128]{3,2,1,0:T(8,128)S(1)}, u32[]{:S(2)}, u32[]{:S(2)}) %collective-permute-start.2) | collective-permute-done | bytes 393248 | tf_op jit(solution)/shard_map/ppermute | solution.py:438
  31.5 11.4 %step.2 = (f32[16,5,8,256]{3,2,1,0:T(8,128)S(1)}, f32[16,5,8,256]{3,2,1,0:T(8,128)S(1)}, f32[3,3,128,128]{3,2,1,0:T(8,128)S(1)}, f32[3,3,128,128]{3,2,1,0:T(8,128)S(1)}, f32[3,3,128,128]{3,2,1,0:T(8,128)S(1)}) custom-call(s32[1,1,2,2]{3,2,1,0:T(2,128)S(1)} %copy-done.2, s32[1]{0:T(128)} %bitcast.core_ref, ...), custom_call_target="tpu_custom_call" | custom-call | tf_op jit(solution)/shard_map/step/pallas_call | solution.py:401
  46.7 4.1 %all-to-all-start = ((f32[16,5,8,256]{3,2,1,0:T(8,128)}), f32[16,5,8,256]{3,2,1,0:T(8,128)S(1)}, u32[]{:S(2)}, u32[]{:S(2)}) async-start(f32[16,5,8,256]{3,2,1,0:T(8,128)} %add.113), calls=%async_computation | async-start | bytes 1310720 | tf_op jit(solution)/shard_map/all_to_all | solution.py:471
  50.8 3.6 %collective-permute-start.4 = (f32[3,3,128,128]{3,2,1,0:T(8,128)S(1)}, f32[3,3,128,128]{3,2,1,0:T(8,128)}, u32[]{:S(2)}, u32[]{:S(2)}) collective-permute-start(f32[3,3,128,128]{3,2,1,0:T(8,128)S(1)} %copy-done.4), channel_id=1, source_target_pairs={{16,0},{32,16},{48,32},{64,48},{80,64},{96,80},{112,96},{128,112},... | collective-permute-start | bytes 1769480 | tf_op jit(solution)/shard_map/ppermute | solution.py:444
  56.3 5.1 %all-to-all-done.pieces_ref = f32[16,5,8,256]{3,2,1,0:T(8,128)S(1)} async-done(((f32[16,5,8,256]{3,2,1,0:T(8,128)}), f32[16,5,8,256]{3,2,1,0:T(8,128)S(1)}, u32[]{:S(2)}, u32[]{:S(2)}) %all-to-all-start) | async-done | bytes 655392 | tf_op jit(solution)/shard_map/all_to_all | solution.py:471
  62.2 12.0 %all-to-all-start.1 = ((f32[8,5,8,256]{3,2,1,0:T(8,128)}), f32[8,5,8,256]{3,2,1,0:T(8,128)S(1)}, u32[]{:S(2)}, u32[]{:S(2)}) async-start(f32[8,5,8,256]{3,2,1,0:T(8,128)} %spread.2), calls=%async_computation.1 | async-start | bytes 655360 | tf_op jit(solution)/shard_map/all_to_all | solution.py:471
  75.5 4.3 %collective-permute-start.6 = (f32[3,128,128]{2,1,0:T(8,128)S(1)}, f32[3,128,128]{2,1,0:T(8,128)S(1)}, u32[]{:S(2)}, u32[]{:S(2)}) collective-permute-start(f32[3,128,128]{2,1,0:T(8,128)S(1)} %get-tuple-element.30), channel_id=1, source_target_pairs={{1,0},{2,1},{3,2},{4,3},{5,4},{6,5},{7,6},{8,7},{9,8},{10,9},{11,1... | collective-permute-start | bytes 589832 | tf_op jit(solution)/shard_map/ppermute | solution.py:447
  79.8 12.3 %collective-permute-start.7 = (f32[3,128,128]{2,1,0:T(8,128)S(1)}, f32[3,128,128]{2,1,0:T(8,128)S(1)}, u32[]{:S(2)}, u32[]{:S(2)}) collective-permute-start(f32[3,128,128]{2,1,0:T(8,128)S(1)} %get-tuple-element.31), channel_id=1, source_target_pairs={{0,1},{1,2},{2,3},{3,4},{4,5},{5,6},{6,7},{7,8},{8,9},{9,10},{10,1... | collective-permute-start | bytes 589832 | tf_op jit(solution)/shard_map/ppermute | solution.py:448
  96.7 5.5 %all-to-all-start.2 = ((f32[16,4,8,256]{3,2,1,0:T(8,128)}), f32[16,4,8,256]{3,2,1,0:T(8,128)S(1)}, u32[]{:S(2)}, u32[]{:S(2)}) async-start(f32[16,4,8,256]{3,2,1,0:T(8,128)} %get-tuple-element.20), calls=%async_computation.2 | async-start | bytes 1048576 | tf_op jit(solution)/shard_map/all_to_all | solution.py:471
  104.2 9.7 %collective-permute-start.10 = (f32[2,128,128]{2,1,0:T(8,128)S(1)}, f32[2,128,128]{2,1,0:T(8,128)S(1)}, u32[]{:S(2)}, u32[]{:S(2)}) collective-permute-start(f32[2,128,128]{2,1,0:T(8,128)S(1)} %fusion.13.refs_4_), channel_id=1, source_target_pairs={{0,1},{1,2},{2,3},{3,4},{4,5},{5,6},{6,7},{7,8},{8,9},{9,10},{10,1... | collective-permute-start | bytes 393224 | tf_op jit(solution)/shard_map/ppermute | solution.py:435
  117.8 3.4 %collective-permute-start.12 = (f32[3,2,128,128]{3,2,1,0:T(8,128)S(1)}, f32[3,2,128,128]{3,2,1,0:T(8,128)S(1)}, u32[]{:S(2)}, u32[]{:S(2)}) collective-permute-start(f32[3,2,128,128]{3,2,1,0:T(8,128)S(1)} %pad_maximum_fusion.1), channel_id=1, source_target_pairs={{0,16},{16,32},{32,48},{48,64},{64,80},{80,96},{96,112},{112,128},... | collective-permute-start | bytes 1179656 | tf_op jit(solution)/shard_map/ppermute | solution.py:438
  121.1 6.9 %collective-permute-done.13.refs_7_ = f32[3,2,128,128]{3,2,1,0:T(8,128)S(1)} collective-permute-done((f32[3,2,128,128]{3,2,1,0:T(8,128)S(1)}, f32[3,2,128,128]{3,2,1,0:T(8,128)S(1)}, u32[]{:S(2)}, u32[]{:S(2)}) %collective-permute-start.13) | collective-permute-done | bytes 393248 | tf_op jit(solution)/shard_map/ppermute | solution.py:439
  128.0 3.7 %collective-permute-done.12.refs_6_ = f32[3,2,128,128]{3,2,1,0:T(8,128)S(1)} collective-permute-done((f32[3,2,128,128]{3,2,1,0:T(8,128)S(1)}, f32[3,2,128,128]{3,2,1,0:T(8,128)S(1)}, u32[]{:S(2)}, u32[]{:S(2)}) %collective-permute-start.12) | collective-permute-done | bytes 393248 | tf_op jit(solution)/shard_map/ppermute | solution.py:438
  131.8 11.2 %step.3 = (f32[16,5,8,256]{3,2,1,0:T(8,128)S(1)}, f32[16,5,8,256]{3,2,1,0:T(8,128)S(1)}, f32[3,3,128,128]{3,2,1,0:T(8,128)S(1)}, f32[3,3,128,128]{3,2,1,0:T(8,128)S(1)}, f32[3,3,128,128]{3,2,1,0:T(8,128)S(1)}) custom-call(s32[1,1,2,2]{3,2,1,0:T(2,128)S(1)} %copy-done.2, s32[1]{0:T(128)} %bitcast.core_ref, ...), custom_call_target="tpu_custom_call" | custom-call | tf_op jit(solution)/shard_map/step/pallas_call | solution.py:401
  145.2 15.9 %all_to_all.30.pieces_ref = f32[16,5,8,256]{3,2,1,0:T(8,128)S(1)} all-to-all(f32[16,5,8,256]{3,2,1,0:T(8,128)S(1)} %add.130), channel_id=1, replica_groups={{0,2,4,6,16,18,20,22,32,34,36,38,48,50,52,54},{1,3,5,7,17,19,21,23,33,3..., dimensions={0} | all-to-all | bytes 1310720 | tf_op jit(solution)/shard_map/all_to_all | solution.py:471
  161.9 8.6 %all-to-all-start.4 = ((f32[8,5,8,256]{3,2,1,0:T(8,128)}), f32[8,5,8,256]{3,2,1,0:T(8,128)S(1)}, u32[]{:S(2)}, u32[]{:S(2)}) async-start(f32[8,5,8,256]{3,2,1,0:T(8,128)} %spread.3), calls=%async_computation.4 | async-start | bytes 655360 | tf_op jit(solution)/shard_map/all_to_all | solution.py:471
  175.8 6.1 %all-to-all-done.4.pieces_ref = f32[8,5,8,256]{3,2,1,0:T(8,128)S(1)} async-done(((f32[8,5,8,256]{3,2,1,0:T(8,128)}), f32[8,5,8,256]{3,2,1,0:T(8,128)S(1)}, u32[]{:S(2)}, u32[]{:S(2)}) %all-to-all-start.4) | async-done | bytes 327712 | tf_op jit(solution)/shard_map/all_to_all | solution.py:471
  182.8 6.4 %all-to-all-start.5 = ((f32[16,4,8,256]{3,2,1,0:T(8,128)}), f32[16,4,8,256]{3,2,1,0:T(8,128)S(1)}, u32[]{:S(2)}, u32[]{:S(2)}) async-start(f32[16,4,8,256]{3,2,1,0:T(8,128)} %get-tuple-element.27), calls=%async_computation.5 | async-start | bytes 1048576 | tf_op jit(solution)/shard_map/all_to_all | solution.py:471
  189.2 5.2 %collective-permute-done.14 = f32[3,3,128,128]{3,2,1,0:T(8,128)S(1)} collective-permute-done((f32[3,3,128,128]{3,2,1,0:T(8,128)S(1)}, f32[3,3,128,128]{3,2,1,0:T(8,128)S(1)}, u32[]{:S(2)}, u32[]{:S(2)}) %collective-permute-start.14) | collective-permute-done | bytes 589856 | tf_op jit(solution)/shard_map/ppermute | solution.py:444
  195.4 3.8 %collective-permute-start.16 = (f32[3,128,128]{2,1,0:T(8,128)S(1)}, f32[3,128,128]{2,1,0:T(8,128)S(1)}, u32[]{:S(2)}, u32[]{:S(2)}) collective-permute-start(f32[3,128,128]{2,1,0:T(8,128)S(1)} %get-tuple-element.28), channel_id=1, source_target_pairs={{1,0},{2,1},{3,2},{4,3},{5,4},{6,5},{7,6},{8,7},{9,8},{10,9},{11,1... | collective-permute-start | bytes 589832 | tf_op jit(solution)/shard_map/ppermute | solution.py:447
  199.3 10.6 %collective-permute-start.17 = (f32[3,128,128]{2,1,0:T(8,128)S(1)}, f32[3,128,128]{2,1,0:T(8,128)S(1)}, u32[]{:S(2)}, u32[]{:S(2)}) collective-permute-start(f32[3,128,128]{2,1,0:T(8,128)S(1)} %get-tuple-element.29), channel_id=1, source_target_pairs={{0,1},{1,2},{2,3},{3,4},{4,5},{5,6},{6,7},{7,8},{8,9},{9,10},{10,1... | collective-permute-start | bytes 589832 | tf_op jit(solution)/shard_map/ppermute | solution.py:448
  210.0 3.4 %collective-permute-done.16 = f32[3,128,128]{2,1,0:T(8,128)S(1)} collective-permute-done((f32[3,128,128]{2,1,0:T(8,128)S(1)}, f32[3,128,128]{2,1,0:T(8,128)S(1)}, u32[]{:S(2)}, u32[]{:S(2)}) %collective-permute-start.16) | collective-permute-done | bytes 196640 | tf_op jit(solution)/shard_map/ppermute | solution.py:447
  (58 shorter events, 44.9 us)
Async XLA Ops:
  0.6 12.6 %collective-permute-start.1 = (f32[2,128,128]{2,1,0:T(8,128)}, f32[2,128,128]{2,1,0:T(8,128)S(1)}, u32[]{:S(2)}, u32[]{:S(2)}) collective-permute-start(f32[2,128,128]{2,1,0:T(8,128)} %refs_3_.1), channel_id=1, source_target_pairs={{1,0},{2,1},{3,2},{4,3},{5,4},{6,5},{7,6},{8,7},{9,8},{10,9},{11,1... | collective-permute-start | bytes 393224 | tf_op jit(solution)/shard_map/ppermute | solution.py:436
  3.4 11.2 %collective-permute-start = (f32[2,128,128]{2,1,0:T(8,128)}, f32[2,128,128]{2,1,0:T(8,128)S(1)}, u32[]{:S(2)}, u32[]{:S(2)}) collective-permute-start(f32[2,128,128]{2,1,0:T(8,128)} %refs_3_.1), channel_id=1, source_target_pairs={{0,1},{1,2},{2,3},{3,4},{4,5},{5,6},{6,7},{7,8},{8,9},{9,10},{10,1... | collective-permute-start | bytes 393224 | tf_op jit(solution)/shard_map/ppermute | solution.py:435
  15.5 10.1 %collective-permute-start.3 = (f32[3,2,128,128]{3,2,1,0:T(8,128)S(1)}, f32[3,2,128,128]{3,2,1,0:T(8,128)S(1)}, u32[]{:S(2)}, u32[]{:S(2)}) collective-permute-start(f32[3,2,128,128]{3,2,1,0:T(8,128)S(1)} %pad_maximum_fusion), channel_id=1, source_target_pairs={{16,0},{32,16},{48,32},{64,48},{80,64},{96,80},{112,96},{128,112},... | collective-permute-start | bytes 1179656 | tf_op jit(solution)/shard_map/ppermute | solution.py:439
  19.7 11.1 %collective-permute-start.2 = (f32[3,2,128,128]{3,2,1,0:T(8,128)S(1)}, f32[3,2,128,128]{3,2,1,0:T(8,128)S(1)}, u32[]{:S(2)}, u32[]{:S(2)}) collective-permute-start(f32[3,2,128,128]{3,2,1,0:T(8,128)S(1)} %pad_maximum_fusion), channel_id=1, source_target_pairs={{0,16},{16,32},{32,48},{48,64},{64,80},{80,96},{96,112},{112,128},... | collective-permute-start | bytes 1179656 | tf_op jit(solution)/shard_map/ppermute | solution.py:438
  46.7 14.7 %all-to-all-start = ((f32[16,5,8,256]{3,2,1,0:T(8,128)}), f32[16,5,8,256]{3,2,1,0:T(8,128)S(1)}, u32[]{:S(2)}, u32[]{:S(2)}) async-start(f32[16,5,8,256]{3,2,1,0:T(8,128)} %add.113), calls=%async_computation | async-start | bytes 1310720 | tf_op jit(solution)/shard_map/all_to_all | solution.py:471
  50.8 23.4 %collective-permute-start.4 = (f32[3,3,128,128]{3,2,1,0:T(8,128)S(1)}, f32[3,3,128,128]{3,2,1,0:T(8,128)}, u32[]{:S(2)}, u32[]{:S(2)}) collective-permute-start(f32[3,3,128,128]{3,2,1,0:T(8,128)S(1)} %copy-done.4), channel_id=1, source_target_pairs={{16,0},{32,16},{48,32},{64,48},{80,64},{96,80},{112,96},{128,112},... | collective-permute-start | bytes 1769480 | tf_op jit(solution)/shard_map/ppermute | solution.py:444
  54.4 19.8 %collective-permute-start.5 = (f32[3,3,128,128]{3,2,1,0:T(8,128)S(1)}, f32[3,3,128,128]{3,2,1,0:T(8,128)}, u32[]{:S(2)}, u32[]{:S(2)}) collective-permute-start(f32[3,3,128,128]{3,2,1,0:T(8,128)S(1)} %get-tuple-element.17), channel_id=1, source_target_pairs={{0,16},{16,32},{32,48},{48,64},{64,80},{80,96},{96,112},{112,128},... | collective-permute-start | bytes 1769480 | tf_op jit(solution)/shard_map/ppermute | solution.py:445
  62.2 33.6 %all-to-all-start.1 = ((f32[8,5,8,256]{3,2,1,0:T(8,128)}), f32[8,5,8,256]{3,2,1,0:T(8,128)S(1)}, u32[]{:S(2)}, u32[]{:S(2)}) async-start(f32[8,5,8,256]{3,2,1,0:T(8,128)} %spread.2), calls=%async_computation.1 | async-start | bytes 655360 | tf_op jit(solution)/shard_map/all_to_all | solution.py:471
  75.5 18.0 %collective-permute-start.6 = (f32[3,128,128]{2,1,0:T(8,128)S(1)}, f32[3,128,128]{2,1,0:T(8,128)S(1)}, u32[]{:S(2)}, u32[]{:S(2)}) collective-permute-start(f32[3,128,128]{2,1,0:T(8,128)S(1)} %get-tuple-element.30), channel_id=1, source_target_pairs={{1,0},{2,1},{3,2},{4,3},{5,4},{6,5},{7,6},{8,7},{9,8},{10,9},{11,1... | collective-permute-start | bytes 589832 | tf_op jit(solution)/shard_map/ppermute | solution.py:447
  79.8 14.9 %collective-permute-start.7 = (f32[3,128,128]{2,1,0:T(8,128)S(1)}, f32[3,128,128]{2,1,0:T(8,128)S(1)}, u32[]{:S(2)}, u32[]{:S(2)}) collective-permute-start(f32[3,128,128]{2,1,0:T(8,128)S(1)} %get-tuple-element.31), channel_id=1, source_target_pairs={{0,1},{1,2},{2,3},{3,4},{4,5},{5,6},{6,7},{7,8},{8,9},{9,10},{10,1... | collective-permute-start | bytes 589832 | tf_op jit(solution)/shard_map/ppermute | solution.py:448
  96.7 17.2 %all-to-all-start.2 = ((f32[16,4,8,256]{3,2,1,0:T(8,128)}), f32[16,4,8,256]{3,2,1,0:T(8,128)S(1)}, u32[]{:S(2)}, u32[]{:S(2)}) async-start(f32[16,4,8,256]{3,2,1,0:T(8,128)} %get-tuple-element.20), calls=%async_computation.2 | async-start | bytes 1048576 | tf_op jit(solution)/shard_map/all_to_all | solution.py:471
  102.3 12.3 %collective-permute-start.11 = (f32[2,128,128]{2,1,0:T(8,128)S(1)}, f32[2,128,128]{2,1,0:T(8,128)S(1)}, u32[]{:S(2)}, u32[]{:S(2)}) collective-permute-start(f32[2,128,128]{2,1,0:T(8,128)S(1)} %fusion.13.refs_4_), channel_id=1, source_target_pairs={{1,0},{2,1},{3,2},{4,3},{5,4},{6,5},{7,6},{8,7},{9,8},{10,9},{11,1... | collective-permute-start | bytes 393224 | tf_op jit(solution)/shard_map/ppermute | solution.py:436
  104.2 11.6 %collective-permute-start.10 = (f32[2,128,128]{2,1,0:T(8,128)S(1)}, f32[2,128,128]{2,1,0:T(8,128)S(1)}, u32[]{:S(2)}, u32[]{:S(2)}) collective-permute-start(f32[2,128,128]{2,1,0:T(8,128)S(1)} %fusion.13.refs_4_), channel_id=1, source_target_pairs={{0,1},{1,2},{2,3},{3,4},{4,5},{5,6},{6,7},{7,8},{8,9},{9,10},{10,1... | collective-permute-start | bytes 393224 | tf_op jit(solution)/shard_map/ppermute | solution.py:435
  113.9 17.9 %collective-permute-start.9 = (f32[16,4,8,256]{3,2,1,0:T(8,128)S(1)}, f32[16,4,8,256]{3,2,1,0:T(8,128)S(1)}, u32[]{:S(2)}, u32[]{:S(2)}) collective-permute-start(f32[16,4,8,256]{3,2,1,0:T(8,128)S(1)} %all-to-all-done.2.refs_0_), channel_id=1, source_target_pairs={{0,1},{1,0},{2,3},{3,2},{4,5},{5,4},{6,7},{7,6},{8,9},{9,8},{10,11... | collective-permute-start | bytes 1572872 | tf_op jit(solution)/shard_map/ppermute | solution.py:494
  115.8 12.2 %collective-permute-start.13 = (f32[3,2,128,128]{3,2,1,0:T(8,128)S(1)}, f32[3,2,128,128]{3,2,1,0:T(8,128)S(1)}, u32[]{:S(2)}, u32[]{:S(2)}) collective-permute-start(f32[3,2,128,128]{3,2,1,0:T(8,128)S(1)} %pad_maximum_fusion.1), channel_id=1, source_target_pairs={{16,0},{32,16},{48,32},{64,48},{80,64},{96,80},{112,96},{128,112},... | collective-permute-start | bytes 1179656 | tf_op jit(solution)/shard_map/ppermute | solution.py:439
  117.8 14.0 %collective-permute-start.12 = (f32[3,2,128,128]{3,2,1,0:T(8,128)S(1)}, f32[3,2,128,128]{3,2,1,0:T(8,128)S(1)}, u32[]{:S(2)}, u32[]{:S(2)}) collective-permute-start(f32[3,2,128,128]{3,2,1,0:T(8,128)S(1)} %pad_maximum_fusion.1), channel_id=1, source_target_pairs={{0,16},{16,32},{32,48},{48,64},{64,80},{80,96},{96,112},{112,128},... | collective-permute-start | bytes 1179656 | tf_op jit(solution)/shard_map/ppermute | solution.py:438
  142.9 2.2 %collective-permute-start.18 = (f32[16,5,8,256]{3,2,1,0:T(8,128)S(1)}, f32[16,5,8,256]{3,2,1,0:T(8,128)S(1)}, u32[]{:S(2)}, u32[]{:S(2)}) collective-permute-start(f32[16,5,8,256]{3,2,1,0:T(8,128)S(1)} %get-tuple-element.25), channel_id=1, source_target_pairs={{0,1},{1,0},{2,3},{3,2},{4,5},{5,4},{6,7},{7,6},{8,9},{9,8},{10,11... | collective-permute-start | bytes 1966088 | tf_op jit(solution)/shard_map/ppermute | solution.py:475
  161.9 20.0 %all-to-all-start.4 = ((f32[8,5,8,256]{3,2,1,0:T(8,128)}), f32[8,5,8,256]{3,2,1,0:T(8,128)S(1)}, u32[]{:S(2)}, u32[]{:S(2)}) async-start(f32[8,5,8,256]{3,2,1,0:T(8,128)} %spread.3), calls=%async_computation.4 | async-start | bytes 655360 | tf_op jit(solution)/shard_map/all_to_all | solution.py:471
  170.5 23.8 %collective-permute-start.14 = (f32[3,3,128,128]{3,2,1,0:T(8,128)S(1)}, f32[3,3,128,128]{3,2,1,0:T(8,128)S(1)}, u32[]{:S(2)}, u32[]{:S(2)}) collective-permute-start(f32[3,3,128,128]{3,2,1,0:T(8,128)S(1)} %get-tuple-element.22), channel_id=1, source_target_pairs={{16,0},{32,16},{48,32},{64,48},{80,64},{96,80},{112,96},{128,112},... | collective-permute-start | bytes 1769480 | tf_op jit(solution)/shard_map/ppermute | solution.py:444
  173.0 21.3 %collective-permute-start.15 = (f32[3,3,128,128]{3,2,1,0:T(8,128)S(1)}, f32[3,3,128,128]{3,2,1,0:T(8,128)}, u32[]{:S(2)}, u32[]{:S(2)}) collective-permute-start(f32[3,3,128,128]{3,2,1,0:T(8,128)S(1)} %get-tuple-element.23), channel_id=1, source_target_pairs={{0,16},{16,32},{32,48},{48,64},{64,80},{80,96},{96,112},{112,128},... | collective-permute-start | bytes 1769480 | tf_op jit(solution)/shard_map/ppermute | solution.py:445
  182.8 27.1 %all-to-all-start.5 = ((f32[16,4,8,256]{3,2,1,0:T(8,128)}), f32[16,4,8,256]{3,2,1,0:T(8,128)S(1)}, u32[]{:S(2)}, u32[]{:S(2)}) async-start(f32[16,4,8,256]{3,2,1,0:T(8,128)} %get-tuple-element.27), calls=%async_computation.5 | async-start | bytes 1048576 | tf_op jit(solution)/shard_map/all_to_all | solution.py:471
  195.4 18.0 %collective-permute-start.16 = (f32[3,128,128]{2,1,0:T(8,128)S(1)}, f32[3,128,128]{2,1,0:T(8,128)S(1)}, u32[]{:S(2)}, u32[]{:S(2)}) collective-permute-start(f32[3,128,128]{2,1,0:T(8,128)S(1)} %get-tuple-element.28), channel_id=1, source_target_pairs={{1,0},{2,1},{3,2},{4,3},{5,4},{6,5},{7,6},{8,7},{9,8},{10,9},{11,1... | collective-permute-start | bytes 589832 | tf_op jit(solution)/shard_map/ppermute | solution.py:447
  199.3 15.3 %collective-permute-start.17 = (f32[3,128,128]{2,1,0:T(8,128)S(1)}, f32[3,128,128]{2,1,0:T(8,128)S(1)}, u32[]{:S(2)}, u32[]{:S(2)}) collective-permute-start(f32[3,128,128]{2,1,0:T(8,128)S(1)} %get-tuple-element.29), channel_id=1, source_target_pairs={{0,1},{1,2},{2,3},{3,4},{4,5},{5,6},{6,7},{7,8},{8,9},{9,10},{10,1... | collective-permute-start | bytes 589832 | tf_op jit(solution)/shard_map/ppermute | solution.py:448
  209.9 6.4 %collective-permute-start.19 = (f32[16,4,8,256]{3,2,1,0:T(8,128)S(1)}, f32[16,4,8,256]{3,2,1,0:T(8,128)S(1)}, u32[]{:S(2)}, u32[]{:S(2)}) collective-permute-start(f32[16,4,8,256]{3,2,1,0:T(8,128)S(1)} %all-to-all-done.5.mine_ref), channel_id=1, source_target_pairs={{0,1},{1,0},{2,3},{3,2},{4,5},{5,4},{6,7},{7,6},{8,9},{9,8},{10,11... | collective-permute-start | bytes 1572872 | tf_op jit(solution)/shard_map/ppermute | solution.py:494
  (6 other events, 37.9 us)

commit v3 on v2

--- a/solution.py
+++ b/solution.py
@@ -431,22 +431,18 @@
     return [(i + 1, i) for i in range(lax.axis_size(axis) - 1)]
 
 
-def neighbourhood(tile):
+def beside(tile):
     left = lax.ppermute(tile, "col", up("col"))
     right = lax.ppermute(tile, "col", down("col"))
-    band = jnp.stack([left, tile, right])
-    above = lax.ppermute(band, "row", up("row"))
-    below = lax.ppermute(band, "row", down("row"))
-    return left, tile, right, above, below
-
-
-def fold(above, middle, below):
-    above = lax.ppermute(above, "row", down("row"))
-    below = lax.ppermute(below, "row", up("row"))
-    first, own, last = (middle[i] + above[i] + below[i] for i in range(3))
-    first = lax.ppermute(first, "col", down("col"))
-    last = lax.ppermute(last, "col", up("col"))
-    return own + first + last
+    return left, right, jnp.stack([left, tile, right])
+
+
+def beyond(band):
+    return lax.ppermute(band, "row", up("row")), lax.ppermute(band, "row", down("row"))
+
+
+def after(value, *others):
+    return lax.optimization_barrier((value,) + others)[0]
 
 
 def places(device):
@@ -471,17 +467,17 @@
     return lax.all_to_all(value, BOTH, 0, 0, axis_index_groups=groups, tiled=True)
 
 
-def new_probe(mine, other, old):
-    mine = mine + lax.ppermute(other, "col", SWAP)
-    pieces = exchange(mine, PLANES)
-    pieces = pl.pallas_call(
+def spread(pieces):
+    return pl.pallas_call(
         spread_kernel,
         out_shape=jax.ShapeDtypeStruct((DEPTH, 5, 8, SIDE), F32),
         compiler_params=params(8),
         name="spread",
     )(pieces)
-    pieces = exchange(pieces, LINES)
-    pieces, new = pl.pallas_call(
+
+
+def update(pieces, old):
+    return pl.pallas_call(
         update_kernel,
         out_shape=[
             jax.ShapeDtypeStruct((GROUPS, 4, 8, SIDE), F32),
@@ -490,9 +486,6 @@
         compiler_params=params(8),
         name="update",
     )(pieces, old)
-    mine = exchange(pieces, PLANES)
-    other = lax.ppermute(mine, "col", SWAP)
-    return mine, other, new
 
 
 def local(object_field, probe, amplitudes, offsets):
@@ -505,14 +498,36 @@
     core = core.reshape(1)
     measured = sort_measured(amplitudes[0, 0])
     parts = (in_hbm(probe),)
+    tile = object_field
+    left, right, band = beside(tile)
+    above, below = beyond(band)
     for iteration in range(ITERS):
         mine, other, above, middle, below = step(
-            offsets, core, table, parts, measured, neighbourhood(object_field)
+            offsets, core, table, parts, measured, (left, tile, right, above, below)
         )
-        mine, other, old = new_probe(mine, other, old)
-        parts = (mine, other)
-        totals = fold(above, middle, below)
-        object_field = object_field + OBJECT_STEP * totals[0:2] / (totals[2:3] + OBJECT_REG)
+        above = lax.ppermute(above, "row", down("row"))
+        below = lax.ppermute(below, "row", up("row"))
+        mine = mine + lax.ppermute(other, "col", SWAP)
+        pieces = exchange(mine, PLANES)
+        first, own, last = (middle[i] + above[i] + below[i] for i in range(3))
+        pieces = spread(after(pieces, first, own, last))
+        first = lax.ppermute(first, "col", down("col"))
+        last = lax.ppermute(last, "col", up("col"))
+        pieces = exchange(pieces, LINES)
+        totals = own + first + last
+        tile = tile + OBJECT_STEP * totals[0:2] / (totals[2:3] + OBJECT_REG)
+        last_iteration = iteration + 1 == ITERS
+        if last_iteration:
+            pieces = after(pieces, tile)
+        else:
+            left, right, band = beside(tile)
+            pieces = after(pieces, band)
+        pieces, old = update(pieces, old)
+        mine = exchange(pieces, PLANES)
+        if not last_iteration:
+            above, below = beyond(band)
+            mine = after(mine, above, below)
+        parts = (mine, lax.ppermute(mine, "col", SWAP))
     probe = pl.pallas_call(
         lay_out_kernel,
         out_shape=jax.ShapeDtypeStruct((4, 2 * GROUPS, 8, SIDE), F32),
@@ -521,7 +536,7 @@
         compiler_params=params(8),
         name="lay_out",
     )(core, *parts)
-    return (object_field, probe.reshape(2, 2, SIDE, SIDE))
+    return (tile, probe.reshape(2, 2, SIDE, SIDE))
 
 
 def solution(mesh):

time: 221 us -> 233 us (1.054)
  waiting for transfers between devices: 49.9 us -> 65.2 us
  blocking collectives: 15.9 us -> 10.4 us
  starting transfers between devices: 113 us -> 116 us
    ppermute x20, waiting for transfers between devices: 38.7 us -> 54 us  [the longest x2 14 us: local(): below = lax.ppermute(below, 'row', up('row'))]
    all_to_all x1, blocking collectives: 15.9 us -> 10.4 us  [exchange(): lax.all_to_all(value, BOTH, 0, 0, axis_index_groups=groups, tiled=True)]
    ppermute x20, starting transfers between devices: 76.8 us -> 80.7 us  [the longest x2 21.4 us: beside(): left = lax.ppermute(tile, 'col', up('col'))]
  transfers between devices with their start and end apart: 25 -> 25, of which waited for: 17 -> 18; matrix products, arithmetic and copies ran while one was open for 3% -> 3% of each run, Pallas kernels for 1% -> 0%
where the time goes in v3:
time: 233 us; the launch traced here: 230 us
  starting transfers between devices  116 us (50%)
  waiting for transfers between devices  65.2 us (28%)
  Pallas kernels  28.1 us (12%)
  blocking collectives  10.4 us (4%)
  other arithmetic  7.69 us (3%)
    all_to_all x5, starting transfers between devices, exchange(): lax.all_to_all(value, BOTH, 0, 0, axis_index_groups=groups, tiled=True)  35.1 us
    pallas_call x2, Pallas kernels, step(): pl.pallas_call(functools.partial(step_kernel, halves), out_shape=[half, h...  23 us
    ppermute x2, starting transfers between devices, beside(): left = lax.ppermute(tile, 'col', up('col'))  21.4 us
    ppermute x2, starting transfers between devices, local(): last = lax.ppermute(last, 'col', up('col'))  18.3 us
    ppermute x2, waiting for transfers between devices, local(): below = lax.ppermute(below, 'row', up('row'))  14 us
    ppermute x2, waiting for transfers between devices, beyond(): lax.ppermute(band, 'row', down('row'))  11.8 us
    all_to_all x5, waiting for transfers between devices, exchange(): lax.all_to_all(value, BOTH, 0, 0, axis_index_groups=groups, tiled=True)  11.2 us
    all_to_all x1, blocking collectives, exchange(): lax.all_to_all(value, BOTH, 0, 0, axis_index_groups=groups, tiled=True)  10.4 us
  transfers between devices with their start and end apart: 25, of which 18 were waited for; matrix products, arithmetic and copies ran while one was open for 3% of the time, Pallas kernels for 0%

profile of v3, /device:TPU:39, one launch (start us, length us, event | category | flops | bytes accessed | tf_op | source)
XLA Modules:
  0.0 229.6 jit_solution(3659131703593875346)
XLA Ops:
  3.4 9.0 %collective-permute-start = (f32[2,128,128]{2,1,0:T(8,128)}, f32[2,128,128]{2,1,0:T(8,128)S(1)}, u32[]{:S(2)}, u32[]{:S(2)}) collective-permute-start(f32[2,128,128]{2,1,0:T(8,128)} %refs_3_.1), channel_id=1, source_target_pairs={{0,1},{1,2},{2,3},{3,4},{4,5},{5,6},{6,7},{7,8},{8,9},{9,10},{10,1... | collective-permute-start | bytes 393224 | tf_op jit(solution)/shard_map/ppermute | solution.py:435
  15.5 4.2 %collective-permute-start.3 = (f32[3,2,128,128]{3,2,1,0:T(8,128)S(1)}, f32[3,2,128,128]{3,2,1,0:T(8,128)S(1)}, u32[]{:S(2)}, u32[]{:S(2)}) collective-permute-start(f32[3,2,128,128]{3,2,1,0:T(8,128)S(1)} %pad_maximum_fusion), channel_id=1, source_target_pairs={{16,0},{32,16},{48,32},{64,48},{80,64},{96,80},{112,96},{128,112},... | collective-permute-start | bytes 1179656 | tf_op jit(solution)/shard_map/ppermute | solution.py:441
  25.6 5.2 %collective-permute-done.2.refs_5_ = f32[3,2,128,128]{3,2,1,0:T(8,128)S(1)} collective-permute-done((f32[3,2,128,128]{3,2,1,0:T(8,128)S(1)}, f32[3,2,128,128]{3,2,1,0:T(8,128)S(1)}, u32[]{:S(2)}, u32[]{:S(2)}) %collective-permute-start.2) | collective-permute-done | bytes 393248 | tf_op jit(solution)/shard_map/ppermute | solution.py:441
  31.5 11.6 %step.2 = (f32[16,5,8,256]{3,2,1,0:T(8,128)S(1)}, f32[16,5,8,256]{3,2,1,0:T(8,128)S(1)}, f32[3,3,128,128]{3,2,1,0:T(8,128)}, f32[3,3,128,128]{3,2,1,0:T(8,128)S(1)}, f32[3,3,128,128]{3,2,1,0:T(8,128)S(1)}) custom-call(s32[1,1,2,2]{3,2,1,0:T(2,128)S(1)} %copy-done.2, s32[1]{0:T(128)} %bitcast.core_ref, bf16[2,2,2,256,256]{4,3,2,1,0:T(8,128)(2,1)} %constant.26.clone.table_in, ...), custom_call_target="tpu_custom_call" | custom-call | tf_op jit(solution)/shard_map/step/pallas_call | solution.py:401
  45.2 3.4 %collective-permute-start.5 = (f32[3,3,128,128]{3,2,1,0:T(8,128)S(1)}, f32[3,3,128,128]{3,2,1,0:T(8,128)}, u32[]{:S(2)}, u32[]{:S(2)}) collective-permute-start(f32[3,3,128,128]{3,2,1,0:T(8,128)S(1)} %get-tuple-element.22), channel_id=1, source_target_pairs={{0,16},{16,32},{32,48},{48,64},{64,80},{80,96},{96,112},{112,128},... | collective-permute-start | bytes 1769480 | tf_op jit(solution)/shard_map/ppermute | solution.py:509
  49.5 6.2 %all-to-all-start = ((f32[16,5,8,256]{3,2,1,0:T(8,128)}), f32[16,5,8,256]{3,2,1,0:T(8,128)S(1)}, u32[]{:S(2)}, u32[]{:S(2)}) async-start(f32[16,5,8,256]{3,2,1,0:T(8,128)} %add.113), calls=%async_computation | async-start | bytes 1310720 | tf_op jit(solution)/shard_map/all_to_all | solution.py:467
  55.7 5.3 %collective-permute-done.4 = f32[3,3,128,128]{3,2,1,0:T(8,128)S(1)} collective-permute-done((f32[3,3,128,128]{3,2,1,0:T(8,128)}, f32[3,3,128,128]{3,2,1,0:T(8,128)S(1)}, u32[]{:S(2)}, u32[]{:S(2)}) %collective-permute-start.4) | collective-permute-done | bytes 589856 | tf_op jit(solution)/shard_map/ppermute | solution.py:508
  61.0 7.8 %collective-permute-done.5 = f32[3,3,128,128]{3,2,1,0:T(8,128)} collective-permute-done((f32[3,3,128,128]{3,2,1,0:T(8,128)S(1)}, f32[3,3,128,128]{3,2,1,0:T(8,128)}, u32[]{:S(2)}, u32[]{:S(2)}) %collective-permute-start.5) | collective-permute-done | bytes 589856 | tf_op jit(solution)/shard_map/ppermute | solution.py:509
  69.9 4.3 %collective-permute-start.6 = (f32[3,128,128]{2,1,0:T(8,128)S(1)}, f32[3,128,128]{2,1,0:T(8,128)S(1)}, u32[]{:S(2)}, u32[]{:S(2)}) collective-permute-start(f32[3,128,128]{2,1,0:T(8,128)S(1)} %get-tuple-element.44), channel_id=1, source_target_pairs={{1,0},{2,1},{3,2},{4,3},{5,4},{6,5},{7,6},{8,7},{9,8},{10,9},{11,1... | collective-permute-start | bytes 589832 | tf_op jit(solution)/shard_map/ppermute | solution.py:514
  74.2 11.3 %collective-permute-start.7 = (f32[3,128,128]{2,1,0:T(8,128)S(1)}, f32[3,128,128]{2,1,0:T(8,128)S(1)}, u32[]{:S(2)}, u32[]{:S(2)}) collective-permute-start(f32[3,128,128]{2,1,0:T(8,128)S(1)} %get-tuple-element.45), channel_id=1, source_target_pairs={{0,1},{1,2},{2,3},{3,4},{4,5},{5,6},{6,7},{7,8},{8,9},{9,10},{10,1... | collective-permute-start | bytes 589832 | tf_op jit(solution)/shard_map/ppermute | solution.py:515
  89.9 5.9 %all-to-all-start.1 = ((f32[8,5,8,256]{3,2,1,0:T(8,128)}), f32[8,5,8,256]{3,2,1,0:T(8,128)S(1)}, u32[]{:S(2)}, u32[]{:S(2)}) async-start(f32[8,5,8,256]{3,2,1,0:T(8,128)} %spread.2), calls=%async_computation.1 | async-start | bytes 655360 | tf_op jit(solution)/shard_map/all_to_all | solution.py:467
  97.8 12.4 %collective-permute-start.9 = (f32[2,128,128]{2,1,0:T(8,128)S(1)}, f32[2,128,128]{2,1,0:T(8,128)S(1)}, u32[]{:S(2)}, u32[]{:S(2)}) collective-permute-start(f32[2,128,128]{2,1,0:T(8,128)S(1)} %fusion.9.refs_4_), channel_id=1, source_target_pairs={{0,1},{1,2},{2,3},{3,4},{4,5},{5,6},{6,7},{7,8},{8,9},{9,10},{10,1... | collective-permute-start | bytes 393224 | tf_op jit(solution)/shard_map/ppermute | solution.py:435
  115.0 5.6 %all-to-all-start.2 = ((f32[16,4,8,256]{3,2,1,0:T(8,128)}), f32[16,4,8,256]{3,2,1,0:T(8,128)S(1)}, u32[]{:S(2)}, u32[]{:S(2)}) async-start(f32[16,4,8,256]{3,2,1,0:T(8,128)} %get-tuple-element.27), calls=%async_computation.2 | async-start | bytes 1048576 | tf_op jit(solution)/shard_map/all_to_all | solution.py:467
  120.6 3.8 %collective-permute-start.12 = (f32[3,2,128,128]{3,2,1,0:T(8,128)S(1)}, f32[3,2,128,128]{3,2,1,0:T(8,128)S(1)}, u32[]{:S(2)}, u32[]{:S(2)}) collective-permute-start(f32[3,2,128,128]{3,2,1,0:T(8,128)S(1)} %pad_maximum_fusion.1), channel_id=1, source_target_pairs={{16,0},{32,16},{48,32},{64,48},{80,64},{96,80},{112,96},{128,112},... | collective-permute-start | bytes 1179656 | tf_op jit(solution)/shard_map/ppermute | solution.py:441
  126.4 8.8 %collective-permute-done.12.refs_7_ = f32[3,2,128,128]{3,2,1,0:T(8,128)S(1)} collective-permute-done((f32[3,2,128,128]{3,2,1,0:T(8,128)S(1)}, f32[3,2,128,128]{3,2,1,0:T(8,128)S(1)}, u32[]{:S(2)}, u32[]{:S(2)}) %collective-permute-start.12) | collective-permute-done | bytes 393248 | tf_op jit(solution)/shard_map/ppermute | solution.py:441
  138.2 11.4 %step.3 = (f32[16,5,8,256]{3,2,1,0:T(8,128)S(1)}, f32[16,5,8,256]{3,2,1,0:T(8,128)S(1)}, f32[3,3,128,128]{3,2,1,0:T(8,128)}, f32[3,3,128,128]{3,2,1,0:T(8,128)S(1)}, f32[3,3,128,128]{3,2,1,0:T(8,128)S(1)}) custom-call(s32[1,1,2,2]{3,2,1,0:T(2,128)S(1)} %copy-done.2, s32[1]{0:T(128)} %bitcast.core_ref, bf16[2,2,2,256,256]{4,3,2,1,0:T(8,128)(2,1)} %constant.26.clone.table_in, ...), custom_call_target="tpu_custom_call" | custom-call | tf_op jit(solution)/shard_map/step/pallas_call | solution.py:401
  156.1 7.9 %all-to-all-start.3 = ((f32[16,5,8,256]{3,2,1,0:T(8,128)}), f32[16,5,8,256]{3,2,1,0:T(8,128)S(1)}, u32[]{:S(2)}, u32[]{:S(2)}) async-start(f32[16,5,8,256]{3,2,1,0:T(8,128)} %add.130), calls=%async_computation.3 | async-start | bytes 1310720 | tf_op jit(solution)/shard_map/all_to_all | solution.py:467
  166.6 6.2 %collective-permute-done.15 = f32[3,3,128,128]{3,2,1,0:T(8,128)} collective-permute-done((f32[3,3,128,128]{3,2,1,0:T(8,128)S(1)}, f32[3,3,128,128]{3,2,1,0:T(8,128)}, u32[]{:S(2)}, u32[]{:S(2)}) %collective-permute-start.15) | collective-permute-done | bytes 589856 | tf_op jit(solution)/shard_map/ppermute | solution.py:509
  173.9 5.1 %collective-permute-start.16 = (f32[3,128,128]{2,1,0:T(8,128)S(1)}, f32[3,128,128]{2,1,0:T(8,128)S(1)}, u32[]{:S(2)}, u32[]{:S(2)}) collective-permute-start(f32[3,128,128]{2,1,0:T(8,128)S(1)} %get-tuple-element.42), channel_id=1, source_target_pairs={{1,0},{2,1},{3,2},{4,3},{5,4},{6,5},{7,6},{8,7},{9,8},{10,9},{11,1... | collective-permute-start | bytes 589832 | tf_op jit(solution)/shard_map/ppermute | solution.py:514
  179.0 7.0 %collective-permute-start.17 = (f32[3,128,128]{2,1,0:T(8,128)S(1)}, f32[3,128,128]{2,1,0:T(8,128)S(1)}, u32[]{:S(2)}, u32[]{:S(2)}) collective-permute-start(f32[3,128,128]{2,1,0:T(8,128)S(1)} %get-tuple-element.43), channel_id=1, source_target_pairs={{0,1},{1,2},{2,3},{3,4},{4,5},{5,6},{6,7},{7,8},{8,9},{9,10},{10,1... | collective-permute-start | bytes 589832 | tf_op jit(solution)/shard_map/ppermute | solution.py:515
  190.4 9.4 %all-to-all-start.4 = ((f32[8,5,8,256]{3,2,1,0:T(8,128)}), f32[8,5,8,256]{3,2,1,0:T(8,128)S(1)}, u32[]{:S(2)}, u32[]{:S(2)}) async-start(f32[8,5,8,256]{3,2,1,0:T(8,128)} %spread.3), calls=%async_computation.4 | async-start | bytes 655360 | tf_op jit(solution)/shard_map/all_to_all | solution.py:467
  200.5 11.1 %all-to-all-done.4.pieces_ref = f32[8,5,8,256]{3,2,1,0:T(8,128)S(1)} async-done(((f32[8,5,8,256]{3,2,1,0:T(8,128)}), f32[8,5,8,256]{3,2,1,0:T(8,128)S(1)}, u32[]{:S(2)}, u32[]{:S(2)}) %all-to-all-start.4) | async-done | bytes 327712 | tf_op jit(solution)/shard_map/all_to_all | solution.py:467
  212.3 10.4 %all_to_all.30.mine_ref = f32[16,4,8,256]{3,2,1,0:T(8,128)S(1)} all-to-all(f32[16,4,8,256]{3,2,1,0:T(8,128)S(1)} %get-tuple-element.37), channel_id=1, replica_groups={{0,2,4,6,16,18,20,22,32,34,36,38,48,50,52,54},{1,3,5,7,17,19,21,23,33,3..., dimensions={0} | all-to-all | bytes 1048576 | tf_op jit(solution)/shard_map/all_to_all | solution.py:467
  222.7 4.3 %collective-permute-start.19 = (f32[16,4,8,256]{3,2,1,0:T(8,128)S(1)}, f32[16,4,8,256]{3,2,1,0:T(8,128)S(1)}, u32[]{:S(2)}, u32[]{:S(2)}) collective-permute-start(f32[16,4,8,256]{3,2,1,0:T(8,128)S(1)} %all_to_all.30.mine_ref), channel_id=1, source_target_pairs={{0,1},{1,0},{2,3},{3,2},{4,5},{5,4},{6,7},{7,6},{8,9},{9,8},{10,11... | collective-permute-start | bytes 1572872 | tf_op jit(solution)/shard_map/ppermute | solution.py:530
  (54 shorter events, 50.9 us)
Async XLA Ops:
  0.6 12.6 %collective-permute-start.1 = (f32[2,128,128]{2,1,0:T(8,128)}, f32[2,128,128]{2,1,0:T(8,128)S(1)}, u32[]{:S(2)}, u32[]{:S(2)}) collective-permute-start(f32[2,128,128]{2,1,0:T(8,128)} %refs_3_.1), channel_id=1, source_target_pairs={{1,0},{2,1},{3,2},{4,3},{5,4},{6,5},{7,6},{8,7},{9,8},{10,9},{11,1... | collective-permute-start | bytes 393224 | tf_op jit(solution)/shard_map/ppermute | solution.py:436
  3.4 11.2 %collective-permute-start = (f32[2,128,128]{2,1,0:T(8,128)}, f32[2,128,128]{2,1,0:T(8,128)S(1)}, u32[]{:S(2)}, u32[]{:S(2)}) collective-permute-start(f32[2,128,128]{2,1,0:T(8,128)} %refs_3_.1), channel_id=1, source_target_pairs={{0,1},{1,2},{2,3},{3,4},{4,5},{5,6},{6,7},{7,8},{8,9},{9,10},{10,1... | collective-permute-start | bytes 393224 | tf_op jit(solution)/shard_map/ppermute | solution.py:435
  15.5 10.1 %collective-permute-start.3 = (f32[3,2,128,128]{3,2,1,0:T(8,128)S(1)}, f32[3,2,128,128]{3,2,1,0:T(8,128)S(1)}, u32[]{:S(2)}, u32[]{:S(2)}) collective-permute-start(f32[3,2,128,128]{3,2,1,0:T(8,128)S(1)} %pad_maximum_fusion), channel_id=1, source_target_pairs={{16,0},{32,16},{48,32},{64,48},{80,64},{96,80},{112,96},{128,112},... | collective-permute-start | bytes 1179656 | tf_op jit(solution)/shard_map/ppermute | solution.py:441
  19.7 11.1 %collective-permute-start.2 = (f32[3,2,128,128]{3,2,1,0:T(8,128)S(1)}, f32[3,2,128,128]{3,2,1,0:T(8,128)S(1)}, u32[]{:S(2)}, u32[]{:S(2)}) collective-permute-start(f32[3,2,128,128]{3,2,1,0:T(8,128)S(1)} %pad_maximum_fusion), channel_id=1, source_target_pairs={{0,16},{16,32},{32,48},{48,64},{64,80},{80,96},{96,112},{112,128},... | collective-permute-start | bytes 1179656 | tf_op jit(solution)/shard_map/ppermute | solution.py:441
  43.2 5.4 %collective-permute-start.8 = (f32[16,5,8,256]{3,2,1,0:T(8,128)S(1)}, f32[16,5,8,256]{3,2,1,0:T(8,128)S(1)}, u32[]{:S(2)}, u32[]{:S(2)}) collective-permute-start(f32[16,5,8,256]{3,2,1,0:T(8,128)S(1)} %get-tuple-element.24), channel_id=1, source_target_pairs={{0,1},{1,0},{2,3},{3,2},{4,5},{5,4},{6,7},{7,6},{8,9},{9,8},{10,11... | collective-permute-start | bytes 1966088 | tf_op jit(solution)/shard_map/ppermute | solution.py:510
  43.3 17.7 %collective-permute-start.4 = (f32[3,3,128,128]{3,2,1,0:T(8,128)}, f32[3,3,128,128]{3,2,1,0:T(8,128)S(1)}, u32[]{:S(2)}, u32[]{:S(2)}) collective-permute-start(f32[3,3,128,128]{3,2,1,0:T(8,128)} %get-tuple-element.21), channel_id=1, source_target_pairs={{16,0},{32,16},{48,32},{64,48},{80,64},{96,80},{112,96},{128,112},... | collective-permute-start | bytes 1769480 | tf_op jit(solution)/shard_map/ppermute | solution.py:508
  45.2 23.6 %collective-permute-start.5 = (f32[3,3,128,128]{3,2,1,0:T(8,128)S(1)}, f32[3,3,128,128]{3,2,1,0:T(8,128)}, u32[]{:S(2)}, u32[]{:S(2)}) collective-permute-start(f32[3,3,128,128]{3,2,1,0:T(8,128)S(1)} %get-tuple-element.22), channel_id=1, source_target_pairs={{0,16},{16,32},{32,48},{48,64},{64,80},{80,96},{96,112},{112,128},... | collective-permute-start | bytes 1769480 | tf_op jit(solution)/shard_map/ppermute | solution.py:509
  49.5 39.6 %all-to-all-start = ((f32[16,5,8,256]{3,2,1,0:T(8,128)}), f32[16,5,8,256]{3,2,1,0:T(8,128)S(1)}, u32[]{:S(2)}, u32[]{:S(2)}) async-start(f32[16,5,8,256]{3,2,1,0:T(8,128)} %add.113), calls=%async_computation | async-start | bytes 1310720 | tf_op jit(solution)/shard_map/all_to_all | solution.py:467
  69.9 17.0 %collective-permute-start.6 = (f32[3,128,128]{2,1,0:T(8,128)S(1)}, f32[3,128,128]{2,1,0:T(8,128)S(1)}, u32[]{:S(2)}, u32[]{:S(2)}) collective-permute-start(f32[3,128,128]{2,1,0:T(8,128)S(1)} %get-tuple-element.44), channel_id=1, source_target_pairs={{1,0},{2,1},{3,2},{4,3},{5,4},{6,5},{7,6},{8,7},{9,8},{10,9},{11,1... | collective-permute-start | bytes 589832 | tf_op jit(solution)/shard_map/ppermute | solution.py:514
  74.2 13.9 %collective-permute-start.7 = (f32[3,128,128]{2,1,0:T(8,128)S(1)}, f32[3,128,128]{2,1,0:T(8,128)S(1)}, u32[]{:S(2)}, u32[]{:S(2)}) collective-permute-start(f32[3,128,128]{2,1,0:T(8,128)S(1)} %get-tuple-element.45), channel_id=1, source_target_pairs={{0,1},{1,2},{2,3},{3,4},{4,5},{5,6},{6,7},{7,8},{8,9},{9,10},{10,1... | collective-permute-start | bytes 589832 | tf_op jit(solution)/shard_map/ppermute | solution.py:515
  89.9 24.2 %all-to-all-start.1 = ((f32[8,5,8,256]{3,2,1,0:T(8,128)}), f32[8,5,8,256]{3,2,1,0:T(8,128)S(1)}, u32[]{:S(2)}, u32[]{:S(2)}) async-start(f32[8,5,8,256]{3,2,1,0:T(8,128)} %spread.2), calls=%async_computation.1 | async-start | bytes 655360 | tf_op jit(solution)/shard_map/all_to_all | solution.py:467
  95.8 18.2 %collective-permute-start.10 = (f32[2,128,128]{2,1,0:T(8,128)S(1)}, f32[2,128,128]{2,1,0:T(8,128)S(1)}, u32[]{:S(2)}, u32[]{:S(2)}) collective-permute-start(f32[2,128,128]{2,1,0:T(8,128)S(1)} %fusion.9.refs_4_), channel_id=1, source_target_pairs={{1,0},{2,1},{3,2},{4,3},{5,4},{6,5},{7,6},{8,7},{9,8},{10,9},{11,1... | collective-permute-start | bytes 393224 | tf_op jit(solution)/shard_map/ppermute | solution.py:436
  97.8 16.3 %collective-permute-start.9 = (f32[2,128,128]{2,1,0:T(8,128)S(1)}, f32[2,128,128]{2,1,0:T(8,128)S(1)}, u32[]{:S(2)}, u32[]{:S(2)}) collective-permute-start(f32[2,128,128]{2,1,0:T(8,128)S(1)} %fusion.9.refs_4_), channel_id=1, source_target_pairs={{0,1},{1,2},{2,3},{3,4},{4,5},{5,6},{6,7},{7,8},{8,9},{9,10},{10,1... | collective-permute-start | bytes 393224 | tf_op jit(solution)/shard_map/ppermute | solution.py:435
  115.0 21.3 %all-to-all-start.2 = ((f32[16,4,8,256]{3,2,1,0:T(8,128)}), f32[16,4,8,256]{3,2,1,0:T(8,128)S(1)}, u32[]{:S(2)}, u32[]{:S(2)}) async-start(f32[16,4,8,256]{3,2,1,0:T(8,128)} %get-tuple-element.27), calls=%async_computation.2 | async-start | bytes 1048576 | tf_op jit(solution)/shard_map/all_to_all | solution.py:467
  120.6 14.5 %collective-permute-start.12 = (f32[3,2,128,128]{3,2,1,0:T(8,128)S(1)}, f32[3,2,128,128]{3,2,1,0:T(8,128)S(1)}, u32[]{:S(2)}, u32[]{:S(2)}) collective-permute-start(f32[3,2,128,128]{3,2,1,0:T(8,128)S(1)} %pad_maximum_fusion.1), channel_id=1, source_target_pairs={{16,0},{32,16},{48,32},{64,48},{80,64},{96,80},{112,96},{128,112},... | collective-permute-start | bytes 1179656 | tf_op jit(solution)/shard_map/ppermute | solution.py:441
  124.4 11.8 %collective-permute-start.11 = (f32[3,2,128,128]{3,2,1,0:T(8,128)S(1)}, f32[3,2,128,128]{3,2,1,0:T(8,128)S(1)}, u32[]{:S(2)}, u32[]{:S(2)}) collective-permute-start(f32[3,2,128,128]{3,2,1,0:T(8,128)S(1)} %pad_maximum_fusion.1), channel_id=1, source_target_pairs={{0,16},{16,32},{32,48},{48,64},{64,80},{80,96},{96,112},{112,128},... | collective-permute-start | bytes 1179656 | tf_op jit(solution)/shard_map/ppermute | solution.py:441
  149.7 5.5 %collective-permute-start.18 = (f32[16,5,8,256]{3,2,1,0:T(8,128)S(1)}, f32[16,5,8,256]{3,2,1,0:T(8,128)S(1)}, u32[]{:S(2)}, u32[]{:S(2)}) collective-permute-start(f32[16,5,8,256]{3,2,1,0:T(8,128)S(1)} %get-tuple-element.33), channel_id=1, source_target_pairs={{0,1},{1,0},{2,3},{3,2},{4,5},{5,4},{6,7},{7,6},{8,9},{9,8},{10,11... | collective-permute-start | bytes 1966088 | tf_op jit(solution)/shard_map/ppermute | solution.py:510
  149.9 16.7 %collective-permute-start.14 = (f32[3,3,128,128]{3,2,1,0:T(8,128)}, f32[3,3,128,128]{3,2,1,0:T(8,128)S(1)}, u32[]{:S(2)}, u32[]{:S(2)}) collective-permute-start(f32[3,3,128,128]{3,2,1,0:T(8,128)} %get-tuple-element.30), channel_id=1, source_target_pairs={{16,0},{32,16},{48,32},{64,48},{80,64},{96,80},{112,96},{128,112},... | collective-permute-start | bytes 1769480 | tf_op jit(solution)/shard_map/ppermute | solution.py:508
  151.8 21.0 %collective-permute-start.15 = (f32[3,3,128,128]{3,2,1,0:T(8,128)S(1)}, f32[3,3,128,128]{3,2,1,0:T(8,128)}, u32[]{:S(2)}, u32[]{:S(2)}) collective-permute-start(f32[3,3,128,128]{3,2,1,0:T(8,128)S(1)} %get-tuple-element.31), channel_id=1, source_target_pairs={{0,16},{16,32},{32,48},{48,64},{64,80},{80,96},{96,112},{112,128},... | collective-permute-start | bytes 1769480 | tf_op jit(solution)/shard_map/ppermute | solution.py:509
  156.1 33.5 %all-to-all-start.3 = ((f32[16,5,8,256]{3,2,1,0:T(8,128)}), f32[16,5,8,256]{3,2,1,0:T(8,128)S(1)}, u32[]{:S(2)}, u32[]{:S(2)}) async-start(f32[16,5,8,256]{3,2,1,0:T(8,128)} %add.130), calls=%async_computation.3 | async-start | bytes 1310720 | tf_op jit(solution)/shard_map/all_to_all | solution.py:467
  173.9 13.6 %collective-permute-start.16 = (f32[3,128,128]{2,1,0:T(8,128)S(1)}, f32[3,128,128]{2,1,0:T(8,128)S(1)}, u32[]{:S(2)}, u32[]{:S(2)}) collective-permute-start(f32[3,128,128]{2,1,0:T(8,128)S(1)} %get-tuple-element.42), channel_id=1, source_target_pairs={{1,0},{2,1},{3,2},{4,3},{5,4},{6,5},{7,6},{8,7},{9,8},{10,9},{11,1... | collective-permute-start | bytes 589832 | tf_op jit(solution)/shard_map/ppermute | solution.py:514
  179.0 9.6 %collective-permute-start.17 = (f32[3,128,128]{2,1,0:T(8,128)S(1)}, f32[3,128,128]{2,1,0:T(8,128)S(1)}, u32[]{:S(2)}, u32[]{:S(2)}) collective-permute-start(f32[3,128,128]{2,1,0:T(8,128)S(1)} %get-tuple-element.43), channel_id=1, source_target_pairs={{0,1},{1,2},{2,3},{3,4},{4,5},{5,6},{6,7},{7,8},{8,9},{9,10},{10,1... | collective-permute-start | bytes 589832 | tf_op jit(solution)/shard_map/ppermute | solution.py:515
  190.4 21.2 %all-to-all-start.4 = ((f32[8,5,8,256]{3,2,1,0:T(8,128)}), f32[8,5,8,256]{3,2,1,0:T(8,128)S(1)}, u32[]{:S(2)}, u32[]{:S(2)}) async-start(f32[8,5,8,256]{3,2,1,0:T(8,128)} %spread.3), calls=%async_computation.4 | async-start | bytes 655360 | tf_op jit(solution)/shard_map/all_to_all | solution.py:467
  222.7 5.8 %collective-permute-start.19 = (f32[16,4,8,256]{3,2,1,0:T(8,128)S(1)}, f32[16,4,8,256]{3,2,1,0:T(8,128)S(1)}, u32[]{:S(2)}, u32[]{:S(2)}) collective-permute-start(f32[16,4,8,256]{3,2,1,0:T(8,128)S(1)} %all_to_all.30.mine_ref), channel_id=1, source_target_pairs={{0,1},{1,0},{2,3},{3,2},{4,5},{5,4},{6,7},{7,6},{8,9},{9,8},{10,11... | collective-permute-start | bytes 1572872 | tf_op jit(solution)/shard_map/ppermute | solution.py:530
  (4 other events, 32.8 us)

commit v4 on v2

--- a/solution.py
+++ b/solution.py
@@ -76,27 +76,27 @@
         out_ref[scan, 1] = turned[HALF:]
 
 
-def lay_out_kernel(core_ref, mine_ref, other_ref, out_ref):
+def lay_out_kernel(parity_ref, mine_ref, other_ref, out_ref):
     for half, ref in enumerate((mine_ref, other_ref)):
-        place = core_ref[0] if half == 0 else 1 - core_ref[0]
+        place = parity_ref[1] if half == 0 else 1 - parity_ref[1]
         for part in range(4):
             out_ref[part, pl.ds(place * GROUPS, GROUPS)] = ref[:, part]
 
 
-def step_kernel(halves, offsets_ref, core_ref, table_in, *refs):
+def step_kernel(halves, offsets_ref, parity_ref, table_in, *refs):
     probe_in, refs = refs[: 1 + halves], refs[1 + halves :]
     (
         measured_in,
-        left_in,
+        outer_in,
         tile_in,
-        right_in,
-        above_in,
-        below_in,
+        inner_in,
+        second_in,
+        first_in,
         mine_out,
         other_out,
-        grad_above,
+        grad_second,
         grad_middle,
-        grad_below,
+        grad_first,
         table_ref,
         probe,
         measured_ref,
@@ -107,11 +107,14 @@
         far,
         back,
         contrib,
+        power_ref,
         total,
         sums,
         semaphores,
     ) = refs
-    core = core_ref[0]
+    row_parity, core = parity_ref[0], parity_ref[1]
+    across = (row_parity * 2, 1, 2 - row_parity * 2)
+    along = (core * 2, 1, 2 - core * 2)
     copies = []
 
     def start(source, target):
@@ -120,12 +123,13 @@
         copies.append(copy)
 
     def third(block):
-        return pl.ds(block * TILE, TILE)
-
-    for block, piece in enumerate((left_in, tile_in, right_in)):
-        start(piece, padded.at[:, third(1), third(block)])
-        start(above_in.at[block], padded.at[:, third(0), third(block)])
-        start(below_in.at[block], padded.at[:, third(2), third(block)])
+        return pl.ds(pl.multiple_of(block * TILE, TILE), TILE)
+
+    for place, piece in enumerate((outer_in, tile_in, inner_in)):
+        columns = third(along[place])
+        start(piece, padded.at[:, third(1), columns])
+        start(second_in.at[place], padded.at[:, third(across[0]), columns])
+        start(first_in.at[place], padded.at[:, third(across[2]), columns])
     near = len(copies)
     if halves:
         for half, ref in enumerate(probe_in):
@@ -274,11 +278,11 @@
                 o_re = p_re * b_re + p_im * b_im
                 o_im = p_re * b_im - p_im * b_re
                 zero = jnp.zeros_like(o_re)
-                contrib[0, rows, columns] = o_re + jnp.where(
-                    first_mode, zero, contrib[0, rows, columns]
+                contrib[scan, 0, rows, columns] = o_re + jnp.where(
+                    first_mode, zero, contrib[scan, 0, rows, columns]
                 )
-                contrib[1, rows, columns] = o_im + jnp.where(
-                    first_mode, zero, contrib[1, rows, columns]
+                contrib[scan, 1, rows, columns] = o_im + jnp.where(
+                    first_mode, zero, contrib[scan, 1, rows, columns]
                 )
                 g_re = w_re * b_re + w_im * b_im
                 g_im = w_re * b_im - w_im * b_re
@@ -292,36 +296,6 @@
                             first_scan, jnp.zeros_like(old), old
                         )
 
-        @pl.when(mode == 1)
-        def _():
-            row, column = offsets_ref[0, 0, scan, 0] + HALF, offsets_ref[0, 0, scan, 1] + HALF
-            inner = lax.rem(row, 8)
-            base = pl.multiple_of(row - inner, 8)
-            turn, keep = lax.rem(column, TILE), lane >= column
-            zero = jnp.zeros((CHUNK // 8, 8, TILE), F32)
-            edge = jnp.zeros((1, 8, TILE), F32)
-            stay = lax.broadcasted_iota(jnp.int32, (CHUNK // 8 + 1, 8, TILE), 1) >= inner
-            for channel in range(3):
-                for piece in range(SIDE // CHUNK):
-                    halves = []
-                    for b in range(2):
-                        value = contrib[channel, pl.ds(piece * CHUNK, CHUNK), pl.ds(b * TILE, TILE)]
-                        halves.append(pltpu.roll(value.reshape(CHUNK // 8, 8, TILE), turn, 2))
-                    thirds = (
-                        jnp.where(keep, halves[0], zero),
-                        jnp.where(keep, halves[1], halves[0]),
-                        jnp.where(keep, zero, halves[1]),
-                    )
-                    place = pl.ds(base + piece * CHUNK, CHUNK + 8)
-                    for b in range(3):
-                        value = pltpu.roll(thirds[b], inner, 1)
-                        value = jnp.where(
-                            stay,
-                            jnp.concatenate([value, edge]),
-                            jnp.concatenate([edge, value]),
-                        )
-                        total[channel, place, pl.ds(b * TILE, TILE)] += value.reshape(CHUNK + 8, TILE)
-
         return carry
 
     for piece in range(SIDE // CHUNK):
@@ -331,7 +305,7 @@
             for part in range(2):
                 value = probe_rows(part, mode, piece)
                 power = value * value if power is None else power + value * value
-        contrib[2, rows, :] = power
+        power_ref[rows, :] = power
         weight = None
         for scan in range(2):
             for part in range(2):
@@ -342,12 +316,45 @@
 
     lax.fori_loop(0, 4, backward, 0)
 
+    def scatter(scan, carry):
+        row, column = offsets_ref[0, 0, scan, 0] + HALF, offsets_ref[0, 0, scan, 1] + HALF
+        inner = lax.rem(row, 8)
+        base = pl.multiple_of(row - inner, 8)
+        turn, keep = lax.rem(column, TILE), lane >= column
+        zero = jnp.zeros((CHUNK // 8, 8, TILE), F32)
+        edge = jnp.zeros((1, 8, TILE), F32)
+        stay = lax.broadcasted_iota(jnp.int32, (CHUNK // 8 + 1, 8, TILE), 1) >= inner
+        for channel in range(3):
+            for piece in range(SIDE // CHUNK):
+                halves = []
+                for b in range(2):
+                    value = (power_ref if channel == 2 else contrib.at[scan, channel])[
+                        pl.ds(piece * CHUNK, CHUNK), pl.ds(b * TILE, TILE)
+                    ]
+                    halves.append(pltpu.roll(value.reshape(CHUNK // 8, 8, TILE), turn, 2))
+                thirds = (
+                    jnp.where(keep, halves[0], zero),
+                    jnp.where(keep, halves[1], halves[0]),
+                    jnp.where(keep, zero, halves[1]),
+                )
+                place = pl.ds(base + piece * CHUNK, CHUNK + 8)
+                for b in range(3):
+                    value = pltpu.roll(thirds[b], inner, 1)
+                    value = jnp.where(
+                        stay,
+                        jnp.concatenate([value, edge]),
+                        jnp.concatenate([edge, value]),
+                    )
+                    total[channel, place, pl.ds(b * TILE, TILE)] += value.reshape(CHUNK + 8, TILE)
+        return carry
+
     done = len(copies)
-    for block, ref in enumerate((grad_above, grad_middle, grad_below)):
-        for column in range(3):
-            start(total.at[:, third(block), third(column)], ref.at[column])
     start(sums.at[pl.ds(core * GROUPS, GROUPS)], mine_out)
     start(sums.at[pl.ds((1 - core) * GROUPS, GROUPS)], other_out)
+    lax.fori_loop(0, 2, scatter, 0)
+    for block, ref in enumerate((grad_second, grad_middle, grad_first)):
+        for column in range(3):
+            start(total.at[:, third(across[block]), third(along[column])], ref.at[column])
     for copy in copies[done:]:
         copy.wait()
 
@@ -394,7 +401,7 @@
     )(measured)
 
 
-def step(offsets, core, table, probe, measured, around):
+def step(offsets, parity, table, probe, measured, around):
     halves = len(probe) - 1
     band = jax.ShapeDtypeStruct((3, 3, TILE, TILE), F32)
     half = jax.ShapeDtypeStruct((GROUPS, 5, 8, SIDE), F32)
@@ -413,40 +420,38 @@
             pltpu.VMEM((2, 2, SIDE, SIDE), BF16),
             pltpu.VMEM((4, 2, SIDE, SIDE), F32),
             pltpu.VMEM((2, SIDE, SIDE), F32),
-            pltpu.VMEM((3, SIDE, SIDE), F32),
+            pltpu.VMEM((2, 2, SIDE, SIDE), F32),
+            pltpu.VMEM((SIDE, SIDE), F32),
             pltpu.VMEM((3, WIDE + 8, WIDE), F32),
             pltpu.VMEM((2 * GROUPS, 5, 8, SIDE), F32),
             pltpu.SemaphoreType.DMA((32,)),
         ],
         compiler_params=params(20),
         name="step",
-    )(offsets, core, table, *probe, measured, *around)
-
-
-def up(axis):
-    return [(i, i + 1) for i in range(lax.axis_size(axis) - 1)]
-
-
-def down(axis):
-    return [(i + 1, i) for i in range(lax.axis_size(axis) - 1)]
+    )(offsets, parity, table, *probe, measured, *around)
+
+
+def pairs(first):
+    both = [(i, i + 1) for i in range(first, 15, 2)]
+    return both + [(j, i) for i, j in both]
 
 
 def neighbourhood(tile):
-    left = lax.ppermute(tile, "col", up("col"))
-    right = lax.ppermute(tile, "col", down("col"))
-    band = jnp.stack([left, tile, right])
-    above = lax.ppermute(band, "row", up("row"))
-    below = lax.ppermute(band, "row", down("row"))
-    return left, tile, right, above, below
-
-
-def fold(above, middle, below):
-    above = lax.ppermute(above, "row", down("row"))
-    below = lax.ppermute(below, "row", up("row"))
-    first, own, last = (middle[i] + above[i] + below[i] for i in range(3))
-    first = lax.ppermute(first, "col", down("col"))
-    last = lax.ppermute(last, "col", up("col"))
-    return own + first + last
+    inner = lax.ppermute(tile, "col", pairs(0))
+    outer = lax.ppermute(tile, "col", pairs(1))
+    band = jnp.stack([outer, tile, inner])
+    first = lax.ppermute(band, "row", pairs(0))
+    second = lax.ppermute(band, "row", pairs(1))
+    return outer, tile, inner, second, first
+
+
+def fold(second, middle, first):
+    first = lax.ppermute(first, "row", pairs(0))
+    second = lax.ppermute(second, "row", pairs(1))
+    outer, own, inner = (middle[i] + first[i] + second[i] for i in range(3))
+    inner = lax.ppermute(inner, "col", pairs(0))
+    outer = lax.ppermute(outer, "col", pairs(1))
+    return own + inner + outer
 
 
 def places(device):
@@ -502,16 +507,16 @@
     group = core * GROUPS + (row & 3) * 4 + (lax.shift_right_logical(column, 1) & 3)
     probe = probe.reshape(4, 2 * GROUPS, 8, SIDE)
     old = lax.dynamic_index_in_dim(probe, group, 1, False)
-    core = core.reshape(1)
+    parity = jnp.stack([row & 1, core])
     measured = sort_measured(amplitudes[0, 0])
     parts = (in_hbm(probe),)
     for iteration in range(ITERS):
-        mine, other, above, middle, below = step(
-            offsets, core, table, parts, measured, neighbourhood(object_field)
+        mine, other, second, middle, first = step(
+            offsets, parity, table, parts, measured, neighbourhood(object_field)
         )
         mine, other, old = new_probe(mine, other, old)
         parts = (mine, other)
-        totals = fold(above, middle, below)
+        totals = fold(second, middle, first)
         object_field = object_field + OBJECT_STEP * totals[0:2] / (totals[2:3] + OBJECT_REG)
     probe = pl.pallas_call(
         lay_out_kernel,
@@ -520,7 +525,7 @@
         out_specs=VMEM_SPEC,
         compiler_params=params(8),
         name="lay_out",
-    )(core, *parts)
+    )(parity, *parts)
     return (object_field, probe.reshape(2, 2, SIDE, SIDE))
 
 

time: 221 us -> 208 us (0.941)
  starting transfers between devices: 113 us -> 91.2 us
  waiting for transfers between devices: 49.9 us -> 60.4 us
    ppermute x16, starting transfers between devices: 76.5 us -> 60.8 us  [the longest x2 22.3 us: fold(): outer = lax.ppermute(outer, 'col', pairs(1))]
    all_to_all x5, starting transfers between devices: 36.6 us -> 30.1 us  [exchange(): lax.all_to_all(value, BOTH, 0, 0, axis_index_groups=groups, tiled=True)]
    ppermute x16, waiting for transfers between devices: 34.5 us -> 40.4 us  [the longest x2 10.4 us: neighbourhood(): second = lax.ppermute(band, 'row', pairs(1))]
    all_to_all x5, waiting for transfers between devices: 11.2 us -> 15.8 us  [exchange(): lax.all_to_all(value, BOTH, 0, 0, axis_index_groups=groups, tiled=True)]
  transfers between devices with their start and end apart: 25 -> 25, of which waited for: 17 -> 15; matrix products, arithmetic and copies ran while one was open for 3% -> 3% of each run, Pallas kernels for 1% -> 1%
where the time goes in v4:
time: 208 us; the launch traced here: 205 us
  starting transfers between devices  91.2 us (44%)
  waiting for transfers between devices  60.4 us (29%)
  Pallas kernels  28.3 us (14%)
  blocking collectives  15.5 us (7%)
  other arithmetic  7.28 us (4%)
    all_to_all x5, starting transfers between devices, exchange(): lax.all_to_all(value, BOTH, 0, 0, axis_index_groups=groups, tiled=True)  30.1 us
    pallas_call x2, Pallas kernels, step(): pl.pallas_call(functools.partial(step_kernel, halves), out_shape=[half, h...  22.6 us
    ppermute x2, starting transfers between devices, fold(): outer = lax.ppermute(outer, 'col', pairs(1))  22.3 us
    ppermute x2, starting transfers between devices, neighbourhood(): outer = lax.ppermute(tile, 'col', pairs(1))  16.2 us
    all_to_all x5, waiting for transfers between devices, exchange(): lax.all_to_all(value, BOTH, 0, 0, axis_index_groups=groups, tiled=True)  15.8 us
    all_to_all x1, blocking collectives, exchange(): lax.all_to_all(value, BOTH, 0, 0, axis_index_groups=groups, tiled=True)  15.5 us
    ppermute x2, waiting for transfers between devices, neighbourhood(): second = lax.ppermute(band, 'row', pairs(1))  10.4 us
    ppermute x2, waiting for transfers between devices, fold(): outer = lax.ppermute(outer, 'col', pairs(1))  8.79 us
  transfers between devices with their start and end apart: 25, of which 15 were waited for; matrix products, arithmetic and copies ran while one was open for 3% of the time, Pallas kernels for 1%

profile of v4, /device:TPU:39, one launch (start us, length us, event | category | flops | bytes accessed | tf_op | source)
XLA Modules:
  0.0 205.2 jit_solution(1979420457423412835)
XLA Ops:
  1.4 7.9 %collective-permute-start = (f32[2,128,128]{2,1,0:T(8,128)}, f32[2,128,128]{2,1,0:T(8,128)S(1)}, u32[]{:S(2)}, u32[]{:S(2)}) collective-permute-start(f32[2,128,128]{2,1,0:T(8,128)} %refs_3_.1), channel_id=1, source_target_pairs={{1,2},{3,4},{5,6},{7,8},{9,10},{11,12},{13,14},{2,1},{4,3},{6,5},{... | collective-permute-start | bytes 393224 | tf_op jit(solution)/shard_map/ppermute | solution.py:441
  9.3 4.7 %collective-permute-done.refs_2_ = f32[2,128,128]{2,1,0:T(8,128)S(1)} collective-permute-done((f32[2,128,128]{2,1,0:T(8,128)}, f32[2,128,128]{2,1,0:T(8,128)S(1)}, u32[]{:S(2)}, u32[]{:S(2)}) %collective-permute-start) | collective-permute-done | bytes 131104 | tf_op jit(solution)/shard_map/ppermute | solution.py:441
  16.2 3.4 %collective-permute-start.2 = (f32[3,2,128,128]{3,2,1,0:T(8,128)S(1)}, f32[3,2,128,128]{3,2,1,0:T(8,128)S(1)}, u32[]{:S(2)}, u32[]{:S(2)}) collective-permute-start(f32[3,2,128,128]{3,2,1,0:T(8,128)S(1)} %pad_maximum_fusion), channel_id=1, source_target_pairs={{16,32},{48,64},{80,96},{112,128},{144,160},{176,192},{208,224},{3... | collective-permute-start | bytes 1179656 | tf_op jit(solution)/shard_map/ppermute | solution.py:444
  22.0 4.9 %collective-permute-done.2.refs_5_ = f32[3,2,128,128]{3,2,1,0:T(8,128)S(1)} collective-permute-done((f32[3,2,128,128]{3,2,1,0:T(8,128)S(1)}, f32[3,2,128,128]{3,2,1,0:T(8,128)S(1)}, u32[]{:S(2)}, u32[]{:S(2)}) %collective-permute-start.2) | collective-permute-done | bytes 393248 | tf_op jit(solution)/shard_map/ppermute | solution.py:444
  26.8 11.4 %step.2 = (f32[16,5,8,256]{3,2,1,0:T(8,128)S(1)}, f32[16,5,8,256]{3,2,1,0:T(8,128)S(1)}, f32[3,3,128,128]{3,2,1,0:T(8,128)S(1)}, f32[3,3,128,128]{3,2,1,0:T(8,128)S(1)}, f32[3,3,128,128]{3,2,1,0:T(8,128)S(1)}) custom-call(s32[1,1,2,2]{3,2,1,0:T(2,128)S(1)} %copy-done.2, s32[2]{0:T(128)S(1)} %pad_add_fusion.parity_ref, ...), custom_call_target="tpu_custom_call" | custom-call | tf_op jit(solution)/shard_map/step/pallas_call | solution.py:408
  42.1 5.7 %all-to-all-start = ((f32[16,5,8,256]{3,2,1,0:T(8,128)}), f32[16,5,8,256]{3,2,1,0:T(8,128)S(1)}, u32[]{:S(2)}, u32[]{:S(2)}) async-start(f32[16,5,8,256]{3,2,1,0:T(8,128)} %add.113), calls=%async_computation | async-start | bytes 1310720 | tf_op jit(solution)/shard_map/all_to_all | solution.py:476
  52.4 7.8 %all-to-all-done.pieces_ref = f32[16,5,8,256]{3,2,1,0:T(8,128)S(1)} async-done(((f32[16,5,8,256]{3,2,1,0:T(8,128)}), f32[16,5,8,256]{3,2,1,0:T(8,128)S(1)}, u32[]{:S(2)}, u32[]{:S(2)}) %all-to-all-start) | async-done | bytes 655392 | tf_op jit(solution)/shard_map/all_to_all | solution.py:476
  60.9 8.3 %all-to-all-start.1 = ((f32[8,5,8,256]{3,2,1,0:T(8,128)}), f32[8,5,8,256]{3,2,1,0:T(8,128)S(1)}, u32[]{:S(2)}, u32[]{:S(2)}) async-start(f32[8,5,8,256]{3,2,1,0:T(8,128)} %spread.2), calls=%async_computation.1 | async-start | bytes 655360 | tf_op jit(solution)/shard_map/all_to_all | solution.py:476
  71.4 4.0 %collective-permute-start.6 = (f32[3,128,128]{2,1,0:T(8,128)S(1)}, f32[3,128,128]{2,1,0:T(8,128)S(1)}, u32[]{:S(2)}, u32[]{:S(2)}) collective-permute-start(f32[3,128,128]{2,1,0:T(8,128)S(1)} %get-tuple-element.30), channel_id=1, source_target_pairs={{0,1},{2,3},{4,5},{6,7},{8,9},{10,11},{12,13},{14,15},{1,0},{3,2},... | collective-permute-start | bytes 589832 | tf_op jit(solution)/shard_map/ppermute | solution.py:452
  75.4 12.0 %collective-permute-start.7 = (f32[3,128,128]{2,1,0:T(8,128)S(1)}, f32[3,128,128]{2,1,0:T(8,128)S(1)}, u32[]{:S(2)}, u32[]{:S(2)}) collective-permute-start(f32[3,128,128]{2,1,0:T(8,128)S(1)} %get-tuple-element.31), channel_id=1, source_target_pairs={{1,2},{3,4},{5,6},{7,8},{9,10},{11,12},{13,14},{2,1},{4,3},{6,5},{... | collective-permute-start | bytes 589832 | tf_op jit(solution)/shard_map/ppermute | solution.py:453
  88.2 3.5 %collective-permute-done.7 = f32[3,128,128]{2,1,0:T(8,128)S(1)} collective-permute-done((f32[3,128,128]{2,1,0:T(8,128)S(1)}, f32[3,128,128]{2,1,0:T(8,128)S(1)}, u32[]{:S(2)}, u32[]{:S(2)}) %collective-permute-start.7) | collective-permute-done | bytes 196640 | tf_op jit(solution)/shard_map/ppermute | solution.py:453
  93.6 4.0 %all-to-all-start.2 = ((f32[16,4,8,256]{3,2,1,0:T(8,128)}), f32[16,4,8,256]{3,2,1,0:T(8,128)S(1)}, u32[]{:S(2)}, u32[]{:S(2)}) async-start(f32[16,4,8,256]{3,2,1,0:T(8,128)} %get-tuple-element.20), calls=%async_computation.2 | async-start | bytes 1048576 | tf_op jit(solution)/shard_map/all_to_all | solution.py:476
  97.7 8.4 %collective-permute-start.10 = (f32[2,128,128]{2,1,0:T(8,128)S(1)}, f32[2,128,128]{2,1,0:T(8,128)S(1)}, u32[]{:S(2)}, u32[]{:S(2)}) collective-permute-start(f32[2,128,128]{2,1,0:T(8,128)S(1)} %fusion.13.refs_4_), channel_id=1, source_target_pairs={{1,2},{3,4},{5,6},{7,8},{9,10},{11,12},{13,14},{2,1},{4,3},{6,5},{... | collective-permute-start | bytes 393224 | tf_op jit(solution)/shard_map/ppermute | solution.py:441
  106.2 3.8 %collective-permute-done.10.refs_3_ = f32[2,128,128]{2,1,0:T(8,128)S(1)} collective-permute-done((f32[2,128,128]{2,1,0:T(8,128)S(1)}, f32[2,128,128]{2,1,0:T(8,128)S(1)}, u32[]{:S(2)}, u32[]{:S(2)}) %collective-permute-start.10) | collective-permute-done | bytes 131104 | tf_op jit(solution)/shard_map/ppermute | solution.py:441
  113.4 5.0 %collective-permute-done.13.refs_7_ = f32[3,2,128,128]{3,2,1,0:T(8,128)S(1)} collective-permute-done((f32[3,2,128,128]{3,2,1,0:T(8,128)S(1)}, f32[3,2,128,128]{3,2,1,0:T(8,128)S(1)}, u32[]{:S(2)}, u32[]{:S(2)}) %collective-permute-start.13) | collective-permute-done | bytes 393248 | tf_op jit(solution)/shard_map/ppermute | solution.py:443
  118.4 5.5 %collective-permute-done.12.refs_6_ = f32[3,2,128,128]{3,2,1,0:T(8,128)S(1)} collective-permute-done((f32[3,2,128,128]{3,2,1,0:T(8,128)S(1)}, f32[3,2,128,128]{3,2,1,0:T(8,128)S(1)}, u32[]{:S(2)}, u32[]{:S(2)}) %collective-permute-start.12) | collective-permute-done | bytes 393248 | tf_op jit(solution)/shard_map/ppermute | solution.py:444
  124.0 11.2 %step.3 = (f32[16,5,8,256]{3,2,1,0:T(8,128)S(1)}, f32[16,5,8,256]{3,2,1,0:T(8,128)S(1)}, f32[3,3,128,128]{3,2,1,0:T(8,128)S(1)}, f32[3,3,128,128]{3,2,1,0:T(8,128)S(1)}, f32[3,3,128,128]{3,2,1,0:T(8,128)S(1)}) custom-call(s32[1,1,2,2]{3,2,1,0:T(2,128)S(1)} %copy-done.2, s32[2]{0:T(128)S(1)} %pad_add_fusion.parity_ref, ...), custom_call_target="tpu_custom_call" | custom-call | tf_op jit(solution)/shard_map/step/pallas_call | solution.py:408
  137.5 15.5 %all_to_all.30.pieces_ref = f32[16,5,8,256]{3,2,1,0:T(8,128)S(1)} all-to-all(f32[16,5,8,256]{3,2,1,0:T(8,128)S(1)} %add.130), channel_id=1, replica_groups={{0,2,4,6,16,18,20,22,32,34,36,38,48,50,52,54},{1,3,5,7,17,19,21,23,33,3..., dimensions={0} | all-to-all | bytes 1310720 | tf_op jit(solution)/shard_map/all_to_all | solution.py:476
  153.7 5.6 %all-to-all-start.4 = ((f32[8,5,8,256]{3,2,1,0:T(8,128)}), f32[8,5,8,256]{3,2,1,0:T(8,128)S(1)}, u32[]{:S(2)}, u32[]{:S(2)}) async-start(f32[8,5,8,256]{3,2,1,0:T(8,128)} %spread.3), calls=%async_computation.4 | async-start | bytes 655360 | tf_op jit(solution)/shard_map/all_to_all | solution.py:476
  162.2 8.0 %all-to-all-done.4.pieces_ref = f32[8,5,8,256]{3,2,1,0:T(8,128)S(1)} async-done(((f32[8,5,8,256]{3,2,1,0:T(8,128)}), f32[8,5,8,256]{3,2,1,0:T(8,128)S(1)}, u32[]{:S(2)}, u32[]{:S(2)}) %all-to-all-start.4) | async-done | bytes 327712 | tf_op jit(solution)/shard_map/all_to_all | solution.py:476
  171.1 6.6 %all-to-all-start.5 = ((f32[16,4,8,256]{3,2,1,0:T(8,128)}), f32[16,4,8,256]{3,2,1,0:T(8,128)S(1)}, u32[]{:S(2)}, u32[]{:S(2)}) async-start(f32[16,4,8,256]{3,2,1,0:T(8,128)} %get-tuple-element.27), calls=%async_computation.5 | async-start | bytes 1048576 | tf_op jit(solution)/shard_map/all_to_all | solution.py:476
  177.7 5.5 %collective-permute-done.15 = f32[3,3,128,128]{3,2,1,0:T(8,128)} collective-permute-done((f32[3,3,128,128]{3,2,1,0:T(8,128)S(1)}, f32[3,3,128,128]{3,2,1,0:T(8,128)}, u32[]{:S(2)}, u32[]{:S(2)}) %collective-permute-start.15) | collective-permute-done | bytes 589856 | tf_op jit(solution)/shard_map/ppermute | solution.py:450
  186.2 10.3 %collective-permute-start.17 = (f32[3,128,128]{2,1,0:T(8,128)S(1)}, f32[3,128,128]{2,1,0:T(8,128)S(1)}, u32[]{:S(2)}, u32[]{:S(2)}) collective-permute-start(f32[3,128,128]{2,1,0:T(8,128)S(1)} %get-tuple-element.29), channel_id=1, source_target_pairs={{1,2},{3,4},{5,6},{7,8},{9,10},{11,12},{13,14},{2,1},{4,3},{6,5},{... | collective-permute-start | bytes 589832 | tf_op jit(solution)/shard_map/ppermute | solution.py:453
  196.6 5.3 %collective-permute-done.17 = f32[3,128,128]{2,1,0:T(8,128)S(1)} collective-permute-done((f32[3,128,128]{2,1,0:T(8,128)S(1)}, f32[3,128,128]{2,1,0:T(8,128)S(1)}, u32[]{:S(2)}, u32[]{:S(2)}) %collective-permute-start.17) | collective-permute-done | bytes 196640 | tf_op jit(solution)/shard_map/ppermute | solution.py:453
  (59 shorter events, 36.2 us)
Async XLA Ops:
  0.6 8.6 %collective-permute-start.1 = (f32[2,128,128]{2,1,0:T(8,128)}, f32[2,128,128]{2,1,0:T(8,128)S(1)}, u32[]{:S(2)}, u32[]{:S(2)}) collective-permute-start(f32[2,128,128]{2,1,0:T(8,128)} %refs_3_.1), channel_id=1, source_target_pairs={{0,1},{2,3},{4,5},{6,7},{8,9},{10,11},{12,13},{14,15},{1,0},{3,2},... | collective-permute-start | bytes 393224 | tf_op jit(solution)/shard_map/ppermute | solution.py:440
  1.4 12.6 %collective-permute-start = (f32[2,128,128]{2,1,0:T(8,128)}, f32[2,128,128]{2,1,0:T(8,128)S(1)}, u32[]{:S(2)}, u32[]{:S(2)}) collective-permute-start(f32[2,128,128]{2,1,0:T(8,128)} %refs_3_.1), channel_id=1, source_target_pairs={{1,2},{3,4},{5,6},{7,8},{9,10},{11,12},{13,14},{2,1},{4,3},{6,5},{... | collective-permute-start | bytes 393224 | tf_op jit(solution)/shard_map/ppermute | solution.py:441
  14.9 7.0 %collective-permute-start.3 = (f32[3,2,128,128]{3,2,1,0:T(8,128)S(1)}, f32[3,2,128,128]{3,2,1,0:T(8,128)S(1)}, u32[]{:S(2)}, u32[]{:S(2)}) collective-permute-start(f32[3,2,128,128]{3,2,1,0:T(8,128)S(1)} %pad_maximum_fusion), channel_id=1, source_target_pairs={{0,16},{32,48},{64,80},{96,112},{128,144},{160,176},{192,208},{224... | collective-permute-start | bytes 1179656 | tf_op jit(solution)/shard_map/ppermute | solution.py:443
  16.2 10.6 %collective-permute-start.2 = (f32[3,2,128,128]{3,2,1,0:T(8,128)S(1)}, f32[3,2,128,128]{3,2,1,0:T(8,128)S(1)}, u32[]{:S(2)}, u32[]{:S(2)}) collective-permute-start(f32[3,2,128,128]{3,2,1,0:T(8,128)S(1)} %pad_maximum_fusion), channel_id=1, source_target_pairs={{16,32},{48,64},{80,96},{112,128},{144,160},{176,192},{208,224},{3... | collective-permute-start | bytes 1179656 | tf_op jit(solution)/shard_map/ppermute | solution.py:444
  42.1 18.1 %all-to-all-start = ((f32[16,5,8,256]{3,2,1,0:T(8,128)}), f32[16,5,8,256]{3,2,1,0:T(8,128)S(1)}, u32[]{:S(2)}, u32[]{:S(2)}) async-start(f32[16,5,8,256]{3,2,1,0:T(8,128)} %add.113), calls=%async_computation | async-start | bytes 1310720 | tf_op jit(solution)/shard_map/all_to_all | solution.py:476
  47.8 21.5 %collective-permute-start.4 = (f32[3,3,128,128]{3,2,1,0:T(8,128)S(1)}, f32[3,3,128,128]{3,2,1,0:T(8,128)}, u32[]{:S(2)}, u32[]{:S(2)}) collective-permute-start(f32[3,3,128,128]{3,2,1,0:T(8,128)S(1)} %copy-done.4), channel_id=1, source_target_pairs={{0,16},{32,48},{64,80},{96,112},{128,144},{160,176},{192,208},{224... | collective-permute-start | bytes 1769480 | tf_op jit(solution)/shard_map/ppermute | solution.py:449
  49.1 21.0 %collective-permute-start.5 = (f32[3,3,128,128]{3,2,1,0:T(8,128)S(1)}, f32[3,3,128,128]{3,2,1,0:T(8,128)}, u32[]{:S(2)}, u32[]{:S(2)}) collective-permute-start(f32[3,3,128,128]{3,2,1,0:T(8,128)S(1)} %get-tuple-element.17), channel_id=1, source_target_pairs={{16,32},{48,64},{80,96},{112,128},{144,160},{176,192},{208,224},{3... | collective-permute-start | bytes 1769480 | tf_op jit(solution)/shard_map/ppermute | solution.py:450
  60.9 31.8 %all-to-all-start.1 = ((f32[8,5,8,256]{3,2,1,0:T(8,128)}), f32[8,5,8,256]{3,2,1,0:T(8,128)S(1)}, u32[]{:S(2)}, u32[]{:S(2)}) async-start(f32[8,5,8,256]{3,2,1,0:T(8,128)} %spread.2), calls=%async_computation.1 | async-start | bytes 655360 | tf_op jit(solution)/shard_map/all_to_all | solution.py:476
  71.4 16.8 %collective-permute-start.6 = (f32[3,128,128]{2,1,0:T(8,128)S(1)}, f32[3,128,128]{2,1,0:T(8,128)S(1)}, u32[]{:S(2)}, u32[]{:S(2)}) collective-permute-start(f32[3,128,128]{2,1,0:T(8,128)S(1)} %get-tuple-element.30), channel_id=1, source_target_pairs={{0,1},{2,3},{4,5},{6,7},{8,9},{10,11},{12,13},{14,15},{1,0},{3,2},... | collective-permute-start | bytes 589832 | tf_op jit(solution)/shard_map/ppermute | solution.py:452
  75.4 16.3 %collective-permute-start.7 = (f32[3,128,128]{2,1,0:T(8,128)S(1)}, f32[3,128,128]{2,1,0:T(8,128)S(1)}, u32[]{:S(2)}, u32[]{:S(2)}) collective-permute-start(f32[3,128,128]{2,1,0:T(8,128)S(1)} %get-tuple-element.31), channel_id=1, source_target_pairs={{1,2},{3,4},{5,6},{7,8},{9,10},{11,12},{13,14},{2,1},{4,3},{6,5},{... | collective-permute-start | bytes 589832 | tf_op jit(solution)/shard_map/ppermute | solution.py:453
  93.6 12.5 %all-to-all-start.2 = ((f32[16,4,8,256]{3,2,1,0:T(8,128)}), f32[16,4,8,256]{3,2,1,0:T(8,128)S(1)}, u32[]{:S(2)}, u32[]{:S(2)}) async-start(f32[16,4,8,256]{3,2,1,0:T(8,128)} %get-tuple-element.20), calls=%async_computation.2 | async-start | bytes 1048576 | tf_op jit(solution)/shard_map/all_to_all | solution.py:476
  97.6 8.6 %collective-permute-start.11 = (f32[2,128,128]{2,1,0:T(8,128)S(1)}, f32[2,128,128]{2,1,0:T(8,128)S(1)}, u32[]{:S(2)}, u32[]{:S(2)}) collective-permute-start(f32[2,128,128]{2,1,0:T(8,128)S(1)} %fusion.13.refs_4_), channel_id=1, source_target_pairs={{0,1},{2,3},{4,5},{6,7},{8,9},{10,11},{12,13},{14,15},{1,0},{3,2},... | collective-permute-start | bytes 393224 | tf_op jit(solution)/shard_map/ppermute | solution.py:440
  97.7 12.3 %collective-permute-start.10 = (f32[2,128,128]{2,1,0:T(8,128)S(1)}, f32[2,128,128]{2,1,0:T(8,128)S(1)}, u32[]{:S(2)}, u32[]{:S(2)}) collective-permute-start(f32[2,128,128]{2,1,0:T(8,128)S(1)} %fusion.13.refs_4_), channel_id=1, source_target_pairs={{1,2},{3,4},{5,6},{7,8},{9,10},{11,12},{13,14},{2,1},{4,3},{6,5},{... | collective-permute-start | bytes 393224 | tf_op jit(solution)/shard_map/ppermute | solution.py:441
  106.1 17.8 %collective-permute-start.9 = (f32[16,4,8,256]{3,2,1,0:T(8,128)S(1)}, f32[16,4,8,256]{3,2,1,0:T(8,128)S(1)}, u32[]{:S(2)}, u32[]{:S(2)}) collective-permute-start(f32[16,4,8,256]{3,2,1,0:T(8,128)S(1)} %all-to-all-done.2.refs_0_), channel_id=1, source_target_pairs={{0,1},{1,0},{2,3},{3,2},{4,5},{5,4},{6,7},{7,6},{8,9},{9,8},{10,11... | collective-permute-start | bytes 1572872 | tf_op jit(solution)/shard_map/ppermute | solution.py:499
  110.1 8.4 %collective-permute-start.13 = (f32[3,2,128,128]{3,2,1,0:T(8,128)S(1)}, f32[3,2,128,128]{3,2,1,0:T(8,128)S(1)}, u32[]{:S(2)}, u32[]{:S(2)}) collective-permute-start(f32[3,2,128,128]{3,2,1,0:T(8,128)S(1)} %pad_maximum_fusion.1), channel_id=1, source_target_pairs={{0,16},{32,48},{64,80},{96,112},{128,144},{160,176},{192,208},{224... | collective-permute-start | bytes 1179656 | tf_op jit(solution)/shard_map/ppermute | solution.py:443
  111.3 12.6 %collective-permute-start.12 = (f32[3,2,128,128]{3,2,1,0:T(8,128)S(1)}, f32[3,2,128,128]{3,2,1,0:T(8,128)S(1)}, u32[]{:S(2)}, u32[]{:S(2)}) collective-permute-start(f32[3,2,128,128]{3,2,1,0:T(8,128)S(1)} %pad_maximum_fusion.1), channel_id=1, source_target_pairs={{16,32},{48,64},{80,96},{112,128},{144,160},{176,192},{208,224},{3... | collective-permute-start | bytes 1179656 | tf_op jit(solution)/shard_map/ppermute | solution.py:444
  135.2 2.2 %collective-permute-start.18 = (f32[16,5,8,256]{3,2,1,0:T(8,128)S(1)}, f32[16,5,8,256]{3,2,1,0:T(8,128)S(1)}, u32[]{:S(2)}, u32[]{:S(2)}) collective-permute-start(f32[16,5,8,256]{3,2,1,0:T(8,128)S(1)} %get-tuple-element.25), channel_id=1, source_target_pairs={{0,1},{1,0},{2,3},{3,2},{4,5},{5,4},{6,7},{7,6},{8,9},{9,8},{10,11... | collective-permute-start | bytes 1966088 | tf_op jit(solution)/shard_map/ppermute | solution.py:480
  153.7 16.5 %all-to-all-start.4 = ((f32[8,5,8,256]{3,2,1,0:T(8,128)}), f32[8,5,8,256]{3,2,1,0:T(8,128)S(1)}, u32[]{:S(2)}, u32[]{:S(2)}) async-start(f32[8,5,8,256]{3,2,1,0:T(8,128)} %spread.3), calls=%async_computation.4 | async-start | bytes 655360 | tf_op jit(solution)/shard_map/all_to_all | solution.py:476
  159.3 18.4 %collective-permute-start.14 = (f32[3,3,128,128]{3,2,1,0:T(8,128)S(1)}, f32[3,3,128,128]{3,2,1,0:T(8,128)S(1)}, u32[]{:S(2)}, u32[]{:S(2)}) collective-permute-start(f32[3,3,128,128]{3,2,1,0:T(8,128)S(1)} %get-tuple-element.22), channel_id=1, source_target_pairs={{0,16},{32,48},{64,80},{96,112},{128,144},{160,176},{192,208},{224... | collective-permute-start | bytes 1769480 | tf_op jit(solution)/shard_map/ppermute | solution.py:449
  159.5 23.6 %collective-permute-start.15 = (f32[3,3,128,128]{3,2,1,0:T(8,128)S(1)}, f32[3,3,128,128]{3,2,1,0:T(8,128)}, u32[]{:S(2)}, u32[]{:S(2)}) collective-permute-start(f32[3,3,128,128]{3,2,1,0:T(8,128)S(1)} %get-tuple-element.23), channel_id=1, source_target_pairs={{16,32},{48,64},{80,96},{112,128},{144,160},{176,192},{208,224},{3... | collective-permute-start | bytes 1769480 | tf_op jit(solution)/shard_map/ppermute | solution.py:450
  171.1 25.4 %all-to-all-start.5 = ((f32[16,4,8,256]{3,2,1,0:T(8,128)}), f32[16,4,8,256]{3,2,1,0:T(8,128)S(1)}, u32[]{:S(2)}, u32[]{:S(2)}) async-start(f32[16,4,8,256]{3,2,1,0:T(8,128)} %get-tuple-element.27), calls=%async_computation.5 | async-start | bytes 1048576 | tf_op jit(solution)/shard_map/all_to_all | solution.py:476
  184.3 12.4 %collective-permute-start.16 = (f32[3,128,128]{2,1,0:T(8,128)S(1)}, f32[3,128,128]{2,1,0:T(8,128)S(1)}, u32[]{:S(2)}, u32[]{:S(2)}) collective-permute-start(f32[3,128,128]{2,1,0:T(8,128)S(1)} %get-tuple-element.28), channel_id=1, source_target_pairs={{0,1},{2,3},{4,5},{6,7},{8,9},{10,11},{12,13},{14,15},{1,0},{3,2},... | collective-permute-start | bytes 589832 | tf_op jit(solution)/shard_map/ppermute | solution.py:452
  186.2 15.7 %collective-permute-start.17 = (f32[3,128,128]{2,1,0:T(8,128)S(1)}, f32[3,128,128]{2,1,0:T(8,128)S(1)}, u32[]{:S(2)}, u32[]{:S(2)}) collective-permute-start(f32[3,128,128]{2,1,0:T(8,128)S(1)} %get-tuple-element.29), channel_id=1, source_target_pairs={{1,2},{3,4},{5,6},{7,8},{9,10},{11,12},{13,14},{2,1},{4,3},{6,5},{... | collective-permute-start | bytes 589832 | tf_op jit(solution)/shard_map/ppermute | solution.py:453
  196.5 7.1 %collective-permute-start.19 = (f32[16,4,8,256]{3,2,1,0:T(8,128)S(1)}, f32[16,4,8,256]{3,2,1,0:T(8,128)S(1)}, u32[]{:S(2)}, u32[]{:S(2)}) collective-permute-start(f32[16,4,8,256]{3,2,1,0:T(8,128)S(1)} %all-to-all-done.5.mine_ref), channel_id=1, source_target_pairs={{0,1},{1,0},{2,3},{3,2},{4,5},{5,4},{6,7},{7,6},{8,9},{9,8},{10,11... | collective-permute-start | bytes 1572872 | tf_op jit(solution)/shard_map/ppermute | solution.py:499
  (6 other events, 41.1 us)

commit v5 on v4

--- a/solution.py
+++ b/solution.py
@@ -445,13 +445,8 @@
     return outer, tile, inner, second, first
 
 
-def fold(second, middle, first):
-    first = lax.ppermute(first, "row", pairs(0))
-    second = lax.ppermute(second, "row", pairs(1))
-    outer, own, inner = (middle[i] + first[i] + second[i] for i in range(3))
-    inner = lax.ppermute(inner, "col", pairs(0))
-    outer = lax.ppermute(outer, "col", pairs(1))
-    return own + inner + outer
+def after(value, other):
+    return lax.optimization_barrier((value, other))[0]
 
 
 def places(device):
@@ -476,17 +471,17 @@
     return lax.all_to_all(value, BOTH, 0, 0, axis_index_groups=groups, tiled=True)
 
 
-def new_probe(mine, other, old):
-    mine = mine + lax.ppermute(other, "col", SWAP)
-    pieces = exchange(mine, PLANES)
-    pieces = pl.pallas_call(
+def spread(pieces):
+    return pl.pallas_call(
         spread_kernel,
         out_shape=jax.ShapeDtypeStruct((DEPTH, 5, 8, SIDE), F32),
         compiler_params=params(8),
         name="spread",
     )(pieces)
-    pieces = exchange(pieces, LINES)
-    pieces, new = pl.pallas_call(
+
+
+def update(pieces, old):
+    return pl.pallas_call(
         update_kernel,
         out_shape=[
             jax.ShapeDtypeStruct((GROUPS, 4, 8, SIDE), F32),
@@ -495,9 +490,6 @@
         compiler_params=params(8),
         name="update",
     )(pieces, old)
-    mine = exchange(pieces, PLANES)
-    other = lax.ppermute(mine, "col", SWAP)
-    return mine, other, new
 
 
 def local(object_field, probe, amplitudes, offsets):
@@ -510,14 +502,25 @@
     parity = jnp.stack([row & 1, core])
     measured = sort_measured(amplitudes[0, 0])
     parts = (in_hbm(probe),)
+    tile = object_field
     for iteration in range(ITERS):
         mine, other, second, middle, first = step(
-            offsets, parity, table, parts, measured, neighbourhood(object_field)
+            offsets, parity, table, parts, measured, neighbourhood(tile)
         )
-        mine, other, old = new_probe(mine, other, old)
-        parts = (mine, other)
-        totals = fold(second, middle, first)
-        object_field = object_field + OBJECT_STEP * totals[0:2] / (totals[2:3] + OBJECT_REG)
+        first = lax.ppermute(first, "row", pairs(0))
+        second = lax.ppermute(second, "row", pairs(1))
+        mine = mine + lax.ppermute(other, "col", SWAP)
+        pieces = exchange(mine, PLANES)
+        outer, own, inner = (middle[i] + first[i] + second[i] for i in range(3))
+        pieces = spread(after(pieces, (outer, own, inner)))
+        inner = lax.ppermute(after(inner, pieces), "col", pairs(0))
+        outer = lax.ppermute(after(outer, pieces), "col", pairs(1))
+        pieces = exchange(pieces, LINES)
+        pieces, old = update(pieces, old)
+        totals = after(own, old) + inner + outer
+        tile = tile + OBJECT_STEP * totals[0:2] / (totals[2:3] + OBJECT_REG)
+        mine = exchange(pieces, PLANES)
+        parts = (mine, lax.ppermute(mine, "col", SWAP))
     probe = pl.pallas_call(
         lay_out_kernel,
         out_shape=jax.ShapeDtypeStruct((4, 2 * GROUPS, 8, SIDE), F32),
@@ -526,7 +529,7 @@
         compiler_params=params(8),
         name="lay_out",
     )(parity, *parts)
-    return (object_field, probe.reshape(2, 2, SIDE, SIDE))
+    return (tile, probe.reshape(2, 2, SIDE, SIDE))
 
 
 def solution(mesh):

time: 208 us -> 200 us (0.962)
  starting transfers between devices: 91.2 us -> 86.1 us
  waiting for transfers between devices: 60.4 us -> 62.9 us
  blocking collectives: 15.5 us -> 13.4 us
    ppermute x12, waiting for transfers between devices: 19.3 us -> 34.4 us  [the longest x2 14.4 us: local(): second = lax.ppermute(second, 'row', pairs(1))]
    all_to_all x5, waiting for transfers between devices: 15.8 us -> 3.85 us  [exchange(): lax.all_to_all(value, BOTH, 0, 0, axis_index_groups=groups, tiled=True)]
    ppermute x2, starting transfers between devices: 16.2 us -> 10.4 us  [neighbourhood(): outer = lax.ppermute(tile, 'col', pairs(1))]
    ppermute x12, starting transfers between devices: 35.9 us -> 31.5 us  [the longest x2 13.6 us: local(): outer = lax.ppermute(after(outer, pieces), 'col', pairs(1))]
    ppermute x2, starting transfers between devices: 0.85 us -> 4.54 us  [neighbourhood(): inner = lax.ppermute(tile, 'col', pairs(0))]
  transfers between devices with their start and end apart: 25 -> 25, of which waited for: 15 -> 16; matrix products, arithmetic and copies ran while one was open for 3% -> 3% of each run, Pallas kernels for 1% -> 1%
where the time goes in v5:
time: 200 us; the launch traced here: 199 us
  starting transfers between devices  86.1 us (43%)
  waiting for transfers between devices  62.9 us (31%)
  Pallas kernels  28.4 us (14%)
  blocking collectives  13.4 us (7%)
  other arithmetic  6.62 us (3%)
    all_to_all x5, starting transfers between devices, exchange(): lax.all_to_all(value, BOTH, 0, 0, axis_index_groups=groups, tiled=True)  31.8 us
    pallas_call x2, Pallas kernels, step(): pl.pallas_call(functools.partial(step_kernel, halves), out_shape=[half, h...  23.4 us
    ppermute x2, waiting for transfers between devices, local(): second = lax.ppermute(second, 'row', pairs(1))  14.4 us
    ppermute x2, starting transfers between devices, local(): outer = lax.ppermute(after(outer, pieces), 'col', pairs(1))  13.6 us
    all_to_all x1, blocking collectives, exchange(): lax.all_to_all(value, BOTH, 0, 0, axis_index_groups=groups, tiled=True)  13.4 us
    ppermute x2, waiting for transfers between devices, local(): first = lax.ppermute(first, 'row', pairs(0))  12.6 us
    ppermute x2, starting transfers between devices, neighbourhood(): outer = lax.ppermute(tile, 'col', pairs(1))  10.4 us
    ppermute x2, waiting for transfers between devices, neighbourhood(): second = lax.ppermute(band, 'row', pairs(1))  9.77 us
  transfers between devices with their start and end apart: 25, of which 16 were waited for; matrix products, arithmetic and copies ran while one was open for 3% of the time, Pallas kernels for 1%

profile of v5, /device:TPU:39, one launch (start us, length us, event | category | flops | bytes accessed | tf_op | source)
XLA Modules:
  0.0 199.0 jit_solution(3551541327846974742)
XLA Ops:
  1.4 7.9 %collective-permute-start = (f32[2,128,128]{2,1,0:T(8,128)}, f32[2,128,128]{2,1,0:T(8,128)S(1)}, u32[]{:S(2)}, u32[]{:S(2)}) collective-permute-start(f32[2,128,128]{2,1,0:T(8,128)} %refs_3_.1), channel_id=1, source_target_pairs={{1,2},{3,4},{5,6},{7,8},{9,10},{11,12},{13,14},{2,1},{4,3},{6,5},{... | collective-permute-start | bytes 393224 | tf_op jit(solution)/shard_map/ppermute | solution.py:441
  9.3 4.7 %collective-permute-done.refs_2_ = f32[2,128,128]{2,1,0:T(8,128)S(1)} collective-permute-done((f32[2,128,128]{2,1,0:T(8,128)}, f32[2,128,128]{2,1,0:T(8,128)S(1)}, u32[]{:S(2)}, u32[]{:S(2)}) %collective-permute-start) | collective-permute-done | bytes 131104 | tf_op jit(solution)/shard_map/ppermute | solution.py:441
  16.2 3.4 %collective-permute-start.2 = (f32[3,2,128,128]{3,2,1,0:T(8,128)S(1)}, f32[3,2,128,128]{3,2,1,0:T(8,128)S(1)}, u32[]{:S(2)}, u32[]{:S(2)}) collective-permute-start(f32[3,2,128,128]{3,2,1,0:T(8,128)S(1)} %pad_maximum_fusion), channel_id=1, source_target_pairs={{16,32},{48,64},{80,96},{112,128},{144,160},{176,192},{208,224},{3... | collective-permute-start | bytes 1179656 | tf_op jit(solution)/shard_map/ppermute | solution.py:444
  22.0 4.9 %collective-permute-done.2.refs_5_ = f32[3,2,128,128]{3,2,1,0:T(8,128)S(1)} collective-permute-done((f32[3,2,128,128]{3,2,1,0:T(8,128)S(1)}, f32[3,2,128,128]{3,2,1,0:T(8,128)S(1)}, u32[]{:S(2)}, u32[]{:S(2)}) %collective-permute-start.2) | collective-permute-done | bytes 393248 | tf_op jit(solution)/shard_map/ppermute | solution.py:444
  26.8 12.1 %step.2 = (f32[16,5,8,256]{3,2,1,0:T(8,128)S(1)}, f32[16,5,8,256]{3,2,1,0:T(8,128)S(1)}, f32[3,3,128,128]{3,2,1,0:T(8,128)S(1)}, f32[3,3,128,128]{3,2,1,0:T(8,128)S(1)}, f32[3,3,128,128]{3,2,1,0:T(8,128)}) custom-call(s32[1,1,2,2]{3,2,1,0:T(2,128)S(1)} %copy-done.2, s32[2]{0:T(128)S(1)} %pad_add_fusion.parity_ref, ...), custom_call_target="tpu_custom_call" | custom-call | tf_op jit(solution)/shard_map/step/pallas_call | solution.py:408
  39.2 3.4 %collective-permute-start.5 = (f32[3,3,128,128]{3,2,1,0:T(8,128)S(1)}, f32[3,3,128,128]{3,2,1,0:T(8,128)}, u32[]{:S(2)}, u32[]{:S(2)}) collective-permute-start(f32[3,3,128,128]{3,2,1,0:T(8,128)S(1)} %get-tuple-element.24), channel_id=1, source_target_pairs={{16,32},{48,64},{80,96},{112,128},{144,160},{176,192},{208,224},{3... | collective-permute-start | bytes 1769480 | tf_op jit(solution)/shard_map/ppermute | solution.py:511
  43.5 6.7 %all-to-all-start = ((f32[16,5,8,256]{3,2,1,0:T(8,128)}), f32[16,5,8,256]{3,2,1,0:T(8,128)S(1)}, u32[]{:S(2)}, u32[]{:S(2)}) async-start(f32[16,5,8,256]{3,2,1,0:T(8,128)} %add.103), calls=%async_computation | async-start | bytes 1310720 | tf_op jit(solution)/shard_map/all_to_all | solution.py:471
  50.2 3.9 %collective-permute-done.4 = f32[3,3,128,128]{3,2,1,0:T(8,128)} collective-permute-done((f32[3,3,128,128]{3,2,1,0:T(8,128)}, f32[3,3,128,128]{3,2,1,0:T(8,128)}, u32[]{:S(2)}, u32[]{:S(2)}) %collective-permute-start.4) | collective-permute-done | bytes 589856 | tf_op jit(solution)/shard_map/ppermute | solution.py:510
  54.1 8.3 %collective-permute-done.5 = f32[3,3,128,128]{3,2,1,0:T(8,128)} collective-permute-done((f32[3,3,128,128]{3,2,1,0:T(8,128)S(1)}, f32[3,3,128,128]{3,2,1,0:T(8,128)}, u32[]{:S(2)}, u32[]{:S(2)}) %collective-permute-start.5) | collective-permute-done | bytes 589856 | tf_op jit(solution)/shard_map/ppermute | solution.py:511
  66.2 5.4 %all-to-all-start.1 = ((f32[8,5,8,256]{3,2,1,0:T(8,128)}), f32[8,5,8,256]{3,2,1,0:T(8,128)S(1)}, u32[]{:S(2)}, u32[]{:S(2)}) async-start(f32[8,5,8,256]{3,2,1,0:T(8,128)} %spread.2), calls=%async_computation.1 | async-start | bytes 655360 | tf_op jit(solution)/shard_map/all_to_all | solution.py:471
  73.5 10.9 %collective-permute-start.8 = (f32[3,128,128]{2,1,0:T(8,128)S(1)}, f32[3,128,128]{2,1,0:T(8,128)S(1)}, u32[]{:S(2)}, u32[]{:S(2)}) collective-permute-start(f32[3,128,128]{2,1,0:T(8,128)S(1)} %get-tuple-element.31), channel_id=1, source_target_pairs={{1,2},{3,4},{5,6},{7,8},{9,10},{11,12},{13,14},{2,1},{4,3},{6,5},{... | collective-permute-start | bytes 589832 | tf_op jit(solution)/shard_map/ppermute | solution.py:517
  86.1 7.2 %all-to-all-start.2 = ((f32[16,4,8,256]{3,2,1,0:T(8,128)}), f32[16,4,8,256]{3,2,1,0:T(8,128)S(1)}, u32[]{:S(2)}, u32[]{:S(2)}) async-start(f32[16,4,8,256]{3,2,1,0:T(8,128)} %get-tuple-element.32), calls=%async_computation.2 | async-start | bytes 1048576 | tf_op jit(solution)/shard_map/all_to_all | solution.py:471
  93.4 3.8 %collective-permute-start.11 = (f32[2,128,128]{2,1,0:T(8,128)S(1)}, f32[2,128,128]{2,1,0:T(8,128)S(1)}, u32[]{:S(2)}, u32[]{:S(2)}) collective-permute-start(f32[2,128,128]{2,1,0:T(8,128)S(1)} %fusion.9.refs_4_), channel_id=1, source_target_pairs={{0,1},{2,3},{4,5},{6,7},{8,9},{10,11},{12,13},{14,15},{1,0},{3,2},... | collective-permute-start | bytes 393224 | tf_op jit(solution)/shard_map/ppermute | solution.py:440
  99.9 4.6 %collective-permute-start.9 = (f32[16,4,8,256]{3,2,1,0:T(8,128)S(1)}, f32[16,4,8,256]{3,2,1,0:T(8,128)S(1)}, u32[]{:S(2)}, u32[]{:S(2)}) collective-permute-start(f32[16,4,8,256]{3,2,1,0:T(8,128)S(1)} %all-to-all-done.2.refs_0_), channel_id=1, source_target_pairs={{0,1},{1,0},{2,3},{3,2},{4,5},{5,4},{6,7},{7,6},{8,9},{9,8},{10,11... | collective-permute-start | bytes 1572872 | tf_op jit(solution)/shard_map/ppermute | solution.py:523
  104.5 5.0 %collective-permute-done.10.refs_3_ = f32[2,128,128]{2,1,0:T(8,128)S(1)} collective-permute-done((f32[2,128,128]{2,1,0:T(8,128)S(1)}, f32[2,128,128]{2,1,0:T(8,128)S(1)}, u32[]{:S(2)}, u32[]{:S(2)}) %collective-permute-start.10) | collective-permute-done | bytes 131104 | tf_op jit(solution)/shard_map/ppermute | solution.py:441
  112.7 3.8 %collective-permute-done.13.refs_7_ = f32[3,2,128,128]{3,2,1,0:T(8,128)S(1)} collective-permute-done((f32[3,2,128,128]{3,2,1,0:T(8,128)S(1)}, f32[3,2,128,128]{3,2,1,0:T(8,128)S(1)}, u32[]{:S(2)}, u32[]{:S(2)}) %collective-permute-start.13) | collective-permute-done | bytes 393248 | tf_op jit(solution)/shard_map/ppermute | solution.py:443
  116.5 4.9 %collective-permute-done.12.refs_6_ = f32[3,2,128,128]{3,2,1,0:T(8,128)S(1)} collective-permute-done((f32[3,2,128,128]{3,2,1,0:T(8,128)S(1)}, f32[3,2,128,128]{3,2,1,0:T(8,128)S(1)}, u32[]{:S(2)}, u32[]{:S(2)}) %collective-permute-start.12) | collective-permute-done | bytes 393248 | tf_op jit(solution)/shard_map/ppermute | solution.py:444
  121.4 11.2 %step.3 = (f32[16,5,8,256]{3,2,1,0:T(8,128)S(1)}, f32[16,5,8,256]{3,2,1,0:T(8,128)S(1)}, f32[3,3,128,128]{3,2,1,0:T(8,128)S(1)}, f32[3,3,128,128]{3,2,1,0:T(8,128)S(1)}, f32[3,3,128,128]{3,2,1,0:T(8,128)S(1)}) custom-call(s32[1,1,2,2]{3,2,1,0:T(2,128)S(1)} %copy-done.2, s32[2]{0:T(128)S(1)} %pad_add_fusion.parity_ref, ...), custom_call_target="tpu_custom_call" | custom-call | tf_op jit(solution)/shard_map/step/pallas_call | solution.py:408
  135.9 6.9 %all-to-all-start.3 = ((f32[16,5,8,256]{3,2,1,0:T(8,128)}), f32[16,5,8,256]{3,2,1,0:T(8,128)S(1)}, u32[]{:S(2)}, u32[]{:S(2)}) async-start(f32[16,5,8,256]{3,2,1,0:T(8,128)} %add.123), calls=%async_computation.3 | async-start | bytes 1310720 | tf_op jit(solution)/shard_map/all_to_all | solution.py:471
  142.7 8.7 %collective-permute-done.14 = f32[3,3,128,128]{3,2,1,0:T(8,128)} collective-permute-done((f32[3,3,128,128]{3,2,1,0:T(8,128)S(1)}, f32[3,3,128,128]{3,2,1,0:T(8,128)}, u32[]{:S(2)}, u32[]{:S(2)}) %collective-permute-start.14) | collective-permute-done | bytes 589856 | tf_op jit(solution)/shard_map/ppermute | solution.py:510
  151.4 6.1 %collective-permute-done.15 = f32[3,3,128,128]{3,2,1,0:T(8,128)} collective-permute-done((f32[3,3,128,128]{3,2,1,0:T(8,128)S(1)}, f32[3,3,128,128]{3,2,1,0:T(8,128)}, u32[]{:S(2)}, u32[]{:S(2)}) %collective-permute-start.15) | collective-permute-done | bytes 589856 | tf_op jit(solution)/shard_map/ppermute | solution.py:511
  159.3 13.4 %all_to_all.30.pieces_ref = f32[8,5,8,256]{3,2,1,0:T(8,128)S(1)} all-to-all(f32[8,5,8,256]{3,2,1,0:T(8,128)S(1)} %spread.3), channel_id=1, replica_groups={{0,8,64,72,128,136,192,200},{1,9,65,73,129,137,193,201},{2,10,66,74,130..., dimensions={0} | all-to-all | bytes 655360 | tf_op jit(solution)/shard_map/all_to_all | solution.py:471
  173.6 5.6 %all-to-all-start.5 = ((f32[16,4,8,256]{3,2,1,0:T(8,128)}), f32[16,4,8,256]{3,2,1,0:T(8,128)S(1)}, u32[]{:S(2)}, u32[]{:S(2)}) async-start(f32[16,4,8,256]{3,2,1,0:T(8,128)} %get-tuple-element.41), calls=%async_computation.5 | async-start | bytes 1048576 | tf_op jit(solution)/shard_map/all_to_all | solution.py:471
  189.4 7.3 %collective-permute-done.18 = f32[3,128,128]{2,1,0:T(8,128)S(1)} collective-permute-done((f32[3,128,128]{2,1,0:T(8,128)S(1)}, f32[3,128,128]{2,1,0:T(8,128)S(1)}, u32[]{:S(2)}, u32[]{:S(2)}) %collective-permute-start.18) | collective-permute-done | bytes 196640 | tf_op jit(solution)/shard_map/ppermute | solution.py:517
  (55 shorter events, 38.1 us)
Async XLA Ops:
  0.6 8.6 %collective-permute-start.1 = (f32[2,128,128]{2,1,0:T(8,128)}, f32[2,128,128]{2,1,0:T(8,128)S(1)}, u32[]{:S(2)}, u32[]{:S(2)}) collective-permute-start(f32[2,128,128]{2,1,0:T(8,128)} %refs_3_.1), channel_id=1, source_target_pairs={{0,1},{2,3},{4,5},{6,7},{8,9},{10,11},{12,13},{14,15},{1,0},{3,2},... | collective-permute-start | bytes 393224 | tf_op jit(solution)/shard_map/ppermute | solution.py:440
  1.4 12.6 %collective-permute-start = (f32[2,128,128]{2,1,0:T(8,128)}, f32[2,128,128]{2,1,0:T(8,128)S(1)}, u32[]{:S(2)}, u32[]{:S(2)}) collective-permute-start(f32[2,128,128]{2,1,0:T(8,128)} %refs_3_.1), channel_id=1, source_target_pairs={{1,2},{3,4},{5,6},{7,8},{9,10},{11,12},{13,14},{2,1},{4,3},{6,5},{... | collective-permute-start | bytes 393224 | tf_op jit(solution)/shard_map/ppermute | solution.py:441
  14.9 7.0 %collective-permute-start.3 = (f32[3,2,128,128]{3,2,1,0:T(8,128)S(1)}, f32[3,2,128,128]{3,2,1,0:T(8,128)S(1)}, u32[]{:S(2)}, u32[]{:S(2)}) collective-permute-start(f32[3,2,128,128]{3,2,1,0:T(8,128)S(1)} %pad_maximum_fusion), channel_id=1, source_target_pairs={{0,16},{32,48},{64,80},{96,112},{128,144},{160,176},{192,208},{224... | collective-permute-start | bytes 1179656 | tf_op jit(solution)/shard_map/ppermute | solution.py:443
  16.2 10.6 %collective-permute-start.2 = (f32[3,2,128,128]{3,2,1,0:T(8,128)S(1)}, f32[3,2,128,128]{3,2,1,0:T(8,128)S(1)}, u32[]{:S(2)}, u32[]{:S(2)}) collective-permute-start(f32[3,2,128,128]{3,2,1,0:T(8,128)S(1)} %pad_maximum_fusion), channel_id=1, source_target_pairs={{16,32},{48,64},{80,96},{112,128},{144,160},{176,192},{208,224},{3... | collective-permute-start | bytes 1179656 | tf_op jit(solution)/shard_map/ppermute | solution.py:444
  39.0 3.6 %collective-permute-start.6 = (f32[16,5,8,256]{3,2,1,0:T(8,128)S(1)}, f32[16,5,8,256]{3,2,1,0:T(8,128)S(1)}, u32[]{:S(2)}, u32[]{:S(2)}) collective-permute-start(f32[16,5,8,256]{3,2,1,0:T(8,128)S(1)} %get-tuple-element.26), channel_id=1, source_target_pairs={{0,1},{1,0},{2,3},{3,2},{4,5},{5,4},{6,7},{7,6},{8,9},{9,8},{10,11... | collective-permute-start | bytes 1966088 | tf_op jit(solution)/shard_map/ppermute | solution.py:512
  39.1 15.0 %collective-permute-start.4 = (f32[3,3,128,128]{3,2,1,0:T(8,128)}, f32[3,3,128,128]{3,2,1,0:T(8,128)}, u32[]{:S(2)}, u32[]{:S(2)}) collective-permute-start(f32[3,3,128,128]{3,2,1,0:T(8,128)} %get-tuple-element.23), channel_id=1, source_target_pairs={{0,16},{32,48},{64,80},{96,112},{128,144},{160,176},{192,208},{224... | collective-permute-start | bytes 1769480 | tf_op jit(solution)/shard_map/ppermute | solution.py:510
  39.2 23.3 %collective-permute-start.5 = (f32[3,3,128,128]{3,2,1,0:T(8,128)S(1)}, f32[3,3,128,128]{3,2,1,0:T(8,128)}, u32[]{:S(2)}, u32[]{:S(2)}) collective-permute-start(f32[3,3,128,128]{3,2,1,0:T(8,128)S(1)} %get-tuple-element.24), channel_id=1, source_target_pairs={{16,32},{48,64},{80,96},{112,128},{144,160},{176,192},{208,224},{3... | collective-permute-start | bytes 1769480 | tf_op jit(solution)/shard_map/ppermute | solution.py:511
  43.5 21.9 %all-to-all-start = ((f32[16,5,8,256]{3,2,1,0:T(8,128)}), f32[16,5,8,256]{3,2,1,0:T(8,128)S(1)}, u32[]{:S(2)}, u32[]{:S(2)}) async-start(f32[16,5,8,256]{3,2,1,0:T(8,128)} %add.103), calls=%async_computation | async-start | bytes 1310720 | tf_op jit(solution)/shard_map/all_to_all | solution.py:471
  66.2 19.0 %all-to-all-start.1 = ((f32[8,5,8,256]{3,2,1,0:T(8,128)}), f32[8,5,8,256]{3,2,1,0:T(8,128)S(1)}, u32[]{:S(2)}, u32[]{:S(2)}) async-start(f32[8,5,8,256]{3,2,1,0:T(8,128)} %spread.2), calls=%async_computation.1 | async-start | bytes 655360 | tf_op jit(solution)/shard_map/all_to_all | solution.py:471
  71.7 21.6 %collective-permute-start.7 = (f32[3,128,128]{2,1,0:T(8,128)S(1)}, f32[3,128,128]{2,1,0:T(8,128)S(1)}, u32[]{:S(2)}, u32[]{:S(2)}) collective-permute-start(f32[3,128,128]{2,1,0:T(8,128)S(1)} %get-tuple-element.30), channel_id=1, source_target_pairs={{0,1},{2,3},{4,5},{6,7},{8,9},{10,11},{12,13},{14,15},{1,0},{3,2},... | collective-permute-start | bytes 589832 | tf_op jit(solution)/shard_map/ppermute | solution.py:516
  73.5 19.7 %collective-permute-start.8 = (f32[3,128,128]{2,1,0:T(8,128)S(1)}, f32[3,128,128]{2,1,0:T(8,128)S(1)}, u32[]{:S(2)}, u32[]{:S(2)}) collective-permute-start(f32[3,128,128]{2,1,0:T(8,128)S(1)} %get-tuple-element.31), channel_id=1, source_target_pairs={{1,2},{3,4},{5,6},{7,8},{9,10},{11,12},{13,14},{2,1},{4,3},{6,5},{... | collective-permute-start | bytes 589832 | tf_op jit(solution)/shard_map/ppermute | solution.py:517
  86.1 13.9 %all-to-all-start.2 = ((f32[16,4,8,256]{3,2,1,0:T(8,128)}), f32[16,4,8,256]{3,2,1,0:T(8,128)S(1)}, u32[]{:S(2)}, u32[]{:S(2)}) async-start(f32[16,4,8,256]{3,2,1,0:T(8,128)} %get-tuple-element.32), calls=%async_computation.2 | async-start | bytes 1048576 | tf_op jit(solution)/shard_map/all_to_all | solution.py:471
  93.4 11.1 %collective-permute-start.11 = (f32[2,128,128]{2,1,0:T(8,128)S(1)}, f32[2,128,128]{2,1,0:T(8,128)S(1)}, u32[]{:S(2)}, u32[]{:S(2)}) collective-permute-start(f32[2,128,128]{2,1,0:T(8,128)S(1)} %fusion.9.refs_4_), channel_id=1, source_target_pairs={{0,1},{2,3},{4,5},{6,7},{8,9},{10,11},{12,13},{14,15},{1,0},{3,2},... | collective-permute-start | bytes 393224 | tf_op jit(solution)/shard_map/ppermute | solution.py:440
  97.1 12.3 %collective-permute-start.10 = (f32[2,128,128]{2,1,0:T(8,128)S(1)}, f32[2,128,128]{2,1,0:T(8,128)S(1)}, u32[]{:S(2)}, u32[]{:S(2)}) collective-permute-start(f32[2,128,128]{2,1,0:T(8,128)S(1)} %fusion.9.refs_4_), channel_id=1, source_target_pairs={{1,2},{3,4},{5,6},{7,8},{9,10},{11,12},{13,14},{2,1},{4,3},{6,5},{... | collective-permute-start | bytes 393224 | tf_op jit(solution)/shard_map/ppermute | solution.py:441
  99.9 21.4 %collective-permute-start.9 = (f32[16,4,8,256]{3,2,1,0:T(8,128)S(1)}, f32[16,4,8,256]{3,2,1,0:T(8,128)S(1)}, u32[]{:S(2)}, u32[]{:S(2)}) collective-permute-start(f32[16,4,8,256]{3,2,1,0:T(8,128)S(1)} %all-to-all-done.2.refs_0_), channel_id=1, source_target_pairs={{0,1},{1,0},{2,3},{3,2},{4,5},{5,4},{6,7},{7,6},{8,9},{9,8},{10,11... | collective-permute-start | bytes 1572872 | tf_op jit(solution)/shard_map/ppermute | solution.py:523
  109.5 7.0 %collective-permute-start.13 = (f32[3,2,128,128]{3,2,1,0:T(8,128)S(1)}, f32[3,2,128,128]{3,2,1,0:T(8,128)S(1)}, u32[]{:S(2)}, u32[]{:S(2)}) collective-permute-start(f32[3,2,128,128]{3,2,1,0:T(8,128)S(1)} %pad_maximum_fusion.1), channel_id=1, source_target_pairs={{0,16},{32,48},{64,80},{96,112},{128,144},{160,176},{192,208},{224... | collective-permute-start | bytes 1179656 | tf_op jit(solution)/shard_map/ppermute | solution.py:443
  110.7 10.6 %collective-permute-start.12 = (f32[3,2,128,128]{3,2,1,0:T(8,128)S(1)}, f32[3,2,128,128]{3,2,1,0:T(8,128)S(1)}, u32[]{:S(2)}, u32[]{:S(2)}) collective-permute-start(f32[3,2,128,128]{3,2,1,0:T(8,128)S(1)} %pad_maximum_fusion.1), channel_id=1, source_target_pairs={{16,32},{48,64},{80,96},{112,128},{144,160},{176,192},{208,224},{3... | collective-permute-start | bytes 1179656 | tf_op jit(solution)/shard_map/ppermute | solution.py:444
  132.9 18.6 %collective-permute-start.14 = (f32[3,3,128,128]{3,2,1,0:T(8,128)S(1)}, f32[3,3,128,128]{3,2,1,0:T(8,128)}, u32[]{:S(2)}, u32[]{:S(2)}) collective-permute-start(f32[3,3,128,128]{3,2,1,0:T(8,128)S(1)} %get-tuple-element.34), channel_id=1, source_target_pairs={{0,16},{32,48},{64,80},{96,112},{128,144},{160,176},{192,208},{224... | collective-permute-start | bytes 1769480 | tf_op jit(solution)/shard_map/ppermute | solution.py:510
  133.0 24.6 %collective-permute-start.15 = (f32[3,3,128,128]{3,2,1,0:T(8,128)S(1)}, f32[3,3,128,128]{3,2,1,0:T(8,128)}, u32[]{:S(2)}, u32[]{:S(2)}) collective-permute-start(f32[3,3,128,128]{3,2,1,0:T(8,128)S(1)} %get-tuple-element.35), channel_id=1, source_target_pairs={{16,32},{48,64},{80,96},{112,128},{144,160},{176,192},{208,224},{3... | collective-permute-start | bytes 1769480 | tf_op jit(solution)/shard_map/ppermute | solution.py:511
  135.9 23.4 %all-to-all-start.3 = ((f32[16,5,8,256]{3,2,1,0:T(8,128)}), f32[16,5,8,256]{3,2,1,0:T(8,128)S(1)}, u32[]{:S(2)}, u32[]{:S(2)}) async-start(f32[16,5,8,256]{3,2,1,0:T(8,128)} %add.123), calls=%async_computation.3 | async-start | bytes 1310720 | tf_op jit(solution)/shard_map/all_to_all | solution.py:471
  173.6 12.6 %all-to-all-start.5 = ((f32[16,4,8,256]{3,2,1,0:T(8,128)}), f32[16,4,8,256]{3,2,1,0:T(8,128)S(1)}, u32[]{:S(2)}, u32[]{:S(2)}) async-start(f32[16,4,8,256]{3,2,1,0:T(8,128)} %get-tuple-element.41), calls=%async_computation.5 | async-start | bytes 1048576 | tf_op jit(solution)/shard_map/all_to_all | solution.py:471
  179.2 10.2 %collective-permute-start.17 = (f32[3,128,128]{2,1,0:T(8,128)S(1)}, f32[3,128,128]{2,1,0:T(8,128)S(1)}, u32[]{:S(2)}, u32[]{:S(2)}) collective-permute-start(f32[3,128,128]{2,1,0:T(8,128)S(1)} %get-tuple-element.39), channel_id=1, source_target_pairs={{0,1},{2,3},{4,5},{6,7},{8,9},{10,11},{12,13},{14,15},{1,0},{3,2},... | collective-permute-start | bytes 589832 | tf_op jit(solution)/shard_map/ppermute | solution.py:516
  181.7 15.0 %collective-permute-start.18 = (f32[3,128,128]{2,1,0:T(8,128)S(1)}, f32[3,128,128]{2,1,0:T(8,128)S(1)}, u32[]{:S(2)}, u32[]{:S(2)}) collective-permute-start(f32[3,128,128]{2,1,0:T(8,128)S(1)} %get-tuple-element.40), channel_id=1, source_target_pairs={{1,2},{3,4},{5,6},{7,8},{9,10},{11,12},{13,14},{2,1},{4,3},{6,5},{... | collective-permute-start | bytes 589832 | tf_op jit(solution)/shard_map/ppermute | solution.py:517
  186.3 11.2 %collective-permute-start.19 = (f32[16,4,8,256]{3,2,1,0:T(8,128)S(1)}, f32[16,4,8,256]{3,2,1,0:T(8,128)S(1)}, u32[]{:S(2)}, u32[]{:S(2)}) collective-permute-start(f32[16,4,8,256]{3,2,1,0:T(8,128)S(1)} %all-to-all-done.5.mine_ref), channel_id=1, source_target_pairs={{0,1},{1,0},{2,3},{3,2},{4,5},{5,4},{6,7},{7,6},{8,9},{9,8},{10,11... | collective-permute-start | bytes 1572872 | tf_op jit(solution)/shard_map/ppermute | solution.py:523
  (4 other events, 34.8 us)

commit v6 on v5

--- a/solution.py
+++ b/solution.py
@@ -87,11 +87,11 @@
     probe_in, refs = refs[: 1 + halves], refs[1 + halves :]
     (
         measured_in,
+        second_in,
+        tile_in,
+        first_in,
         outer_in,
-        tile_in,
         inner_in,
-        second_in,
-        first_in,
         mine_out,
         other_out,
         grad_second,
@@ -125,11 +125,11 @@
     def third(block):
         return pl.ds(pl.multiple_of(block * TILE, TILE), TILE)
 
-    for place, piece in enumerate((outer_in, tile_in, inner_in)):
-        columns = third(along[place])
-        start(piece, padded.at[:, third(1), columns])
-        start(second_in.at[place], padded.at[:, third(across[0]), columns])
-        start(first_in.at[place], padded.at[:, third(across[2]), columns])
+    for place, piece in enumerate((second_in, tile_in, first_in)):
+        rows = third(across[place])
+        start(piece, padded.at[:, rows, third(1)])
+        start(outer_in.at[place], padded.at[:, rows, third(along[0])])
+        start(inner_in.at[place], padded.at[:, rows, third(along[2])])
     near = len(copies)
     if halves:
         for half, ref in enumerate(probe_in):
@@ -437,12 +437,12 @@
 
 
 def neighbourhood(tile):
-    inner = lax.ppermute(tile, "col", pairs(0))
-    outer = lax.ppermute(tile, "col", pairs(1))
-    band = jnp.stack([outer, tile, inner])
-    first = lax.ppermute(band, "row", pairs(0))
-    second = lax.ppermute(band, "row", pairs(1))
-    return outer, tile, inner, second, first
+    first = lax.ppermute(tile, "row", pairs(0))
+    second = lax.ppermute(tile, "row", pairs(1))
+    band = jnp.stack([second, tile, first])
+    inner = lax.ppermute(band, "col", pairs(0))
+    outer = lax.ppermute(band, "col", pairs(1))
+    return second, tile, first, outer, inner
 
 
 def after(value, other):

time: 200 us -> 207 us (1.035)
  waiting for transfers between devices: 62.9 us -> 72.8 us
  starting transfers between devices: 86.1 us -> 82.9 us
    ppermute x2, waiting for transfers between devices: 12.6 us -> 18.4 us  [local(): first = lax.ppermute(first, 'row', pairs(0))]
    ppermute x8, waiting for transfers between devices: 24.6 us -> 30.3 us  [the longest x2 25.6 us: neighbourhood(): outer = lax.ppermute(band, 'col', pairs(1))]
    ppermute x2, waiting for transfers between devices: 14.4 us -> 11.2 us  [local(): second = lax.ppermute(second, 'row', pairs(1))]
  transfers between devices with their start and end apart: 25 -> 25, of which waited for: 16 -> 13; matrix products, arithmetic and copies ran while one was open for 3% -> 3% of each run, Pallas kernels for 1% -> 1%
where the time goes in v6:
time: 207 us; the launch traced here: 206 us
  starting transfers between devices  82.9 us (40%)
  waiting for transfers between devices  72.8 us (35%)
  Pallas kernels  28.3 us (14%)
  blocking collectives  13.7 us (7%)
  other arithmetic  6.62 us (3%)
    all_to_all x5, starting transfers between devices, exchange(): lax.all_to_all(value, BOTH, 0, 0, axis_index_groups=groups, tiled=True)  30.2 us
    ppermute x2, waiting for transfers between devices, neighbourhood(): outer = lax.ppermute(band, 'col', pairs(1))  25.6 us
    pallas_call x2, Pallas kernels, step(): pl.pallas_call(functools.partial(step_kernel, halves), out_shape=[half, h...  23.3 us
    ppermute x2, waiting for transfers between devices, local(): first = lax.ppermute(first, 'row', pairs(0))  18.4 us
    all_to_all x1, blocking collectives, exchange(): lax.all_to_all(value, BOTH, 0, 0, axis_index_groups=groups, tiled=True)  13.7 us
    ppermute x2, starting transfers between devices, local(): outer = lax.ppermute(after(outer, pieces), 'col', pairs(1))  13.1 us
    ppermute x2, waiting for transfers between devices, local(): second = lax.ppermute(second, 'row', pairs(1))  11.2 us
    ppermute x2, starting transfers between devices, neighbourhood(): outer = lax.ppermute(band, 'col', pairs(1))  9.72 us
  transfers between devices with their start and end apart: 25, of which 13 were waited for; matrix products, arithmetic and copies ran while one was open for 3% of the time, Pallas kernels for 1%

profile of v6, /device:TPU:39, one launch (start us, length us, event | category | flops | bytes accessed | tf_op | source)
XLA Modules:
  0.0 206.1 jit_solution(4717365030200901140)
XLA Ops:
  2.0 3.3 %collective-permute-start = (f32[2,128,128]{2,1,0:T(8,128)}, f32[2,128,128]{2,1,0:T(8,128)S(1)}, u32[]{:S(2)}, u32[]{:S(2)}) collective-permute-start(f32[2,128,128]{2,1,0:T(8,128)} %refs_3_.1), channel_id=1, source_target_pairs={{16,32},{48,64},{80,96},{112,128},{144,160},{176,192},{208,224},{3... | collective-permute-start | bytes 393224 | tf_op jit(solution)/shard_map/ppermute | solution.py:441
  5.4 4.7 %collective-permute-done.refs_2_ = f32[2,128,128]{2,1,0:T(8,128)S(1)} collective-permute-done((f32[2,128,128]{2,1,0:T(8,128)}, f32[2,128,128]{2,1,0:T(8,128)S(1)}, u32[]{:S(2)}, u32[]{:S(2)}) %collective-permute-start) | collective-permute-done | bytes 131104 | tf_op jit(solution)/shard_map/ppermute | solution.py:441
  13.2 7.7 %collective-permute-start.2 = (f32[3,2,128,128]{3,2,1,0:T(8,128)S(1)}, f32[3,2,128,128]{3,2,1,0:T(8,128)S(1)}, u32[]{:S(2)}, u32[]{:S(2)}) collective-permute-start(f32[3,2,128,128]{3,2,1,0:T(8,128)S(1)} %pad_maximum_fusion), channel_id=1, source_target_pairs={{1,2},{3,4},{5,6},{7,8},{9,10},{11,12},{13,14},{2,1},{4,3},{6,5},{... | collective-permute-start | bytes 1179656 | tf_op jit(solution)/shard_map/ppermute | solution.py:444
  21.9 10.6 %collective-permute-done.2.refs_5_ = f32[3,2,128,128]{3,2,1,0:T(8,128)S(1)} collective-permute-done((f32[3,2,128,128]{3,2,1,0:T(8,128)S(1)}, f32[3,2,128,128]{3,2,1,0:T(8,128)S(1)}, u32[]{:S(2)}, u32[]{:S(2)}) %collective-permute-start.2) | collective-permute-done | bytes 393248 | tf_op jit(solution)/shard_map/ppermute | solution.py:444
  32.5 12.1 %step.2 = (f32[16,5,8,256]{3,2,1,0:T(8,128)S(1)}, f32[16,5,8,256]{3,2,1,0:T(8,128)S(1)}, f32[3,3,128,128]{3,2,1,0:T(8,128)S(1)}, f32[3,3,128,128]{3,2,1,0:T(8,128)S(1)}, f32[3,3,128,128]{3,2,1,0:T(8,128)}) custom-call(s32[1,1,2,2]{3,2,1,0:T(2,128)S(1)} %copy-done.2, s32[2]{0:T(128)S(1)} %pad_add_fusion.parity_ref, ...), custom_call_target="tpu_custom_call" | custom-call | tf_op jit(solution)/shard_map/step/pallas_call | solution.py:408
  47.7 6.9 %all-to-all-start = ((f32[16,5,8,256]{3,2,1,0:T(8,128)}), f32[16,5,8,256]{3,2,1,0:T(8,128)S(1)}, u32[]{:S(2)}, u32[]{:S(2)}) async-start(f32[16,5,8,256]{3,2,1,0:T(8,128)} %add.103), calls=%async_computation | async-start | bytes 1310720 | tf_op jit(solution)/shard_map/all_to_all | solution.py:471
  54.6 9.7 %collective-permute-done.4 = f32[3,3,128,128]{3,2,1,0:T(8,128)} collective-permute-done((f32[3,3,128,128]{3,2,1,0:T(8,128)}, f32[3,3,128,128]{3,2,1,0:T(8,128)}, u32[]{:S(2)}, u32[]{:S(2)}) %collective-permute-start.4) | collective-permute-done | bytes 589856 | tf_op jit(solution)/shard_map/ppermute | solution.py:510
  64.3 5.1 %collective-permute-done.5 = f32[3,3,128,128]{3,2,1,0:T(8,128)} collective-permute-done((f32[3,3,128,128]{3,2,1,0:T(8,128)S(1)}, f32[3,3,128,128]{3,2,1,0:T(8,128)}, u32[]{:S(2)}, u32[]{:S(2)}) %collective-permute-start.5) | collective-permute-done | bytes 589856 | tf_op jit(solution)/shard_map/ppermute | solution.py:511
  71.9 3.4 %all-to-all-start.1 = ((f32[8,5,8,256]{3,2,1,0:T(8,128)}), f32[8,5,8,256]{3,2,1,0:T(8,128)S(1)}, u32[]{:S(2)}, u32[]{:S(2)}) async-start(f32[8,5,8,256]{3,2,1,0:T(8,128)} %spread.2), calls=%async_computation.1 | async-start | bytes 655360 | tf_op jit(solution)/shard_map/all_to_all | solution.py:471
  76.6 10.4 %collective-permute-start.8 = (f32[3,128,128]{2,1,0:T(8,128)S(1)}, f32[3,128,128]{2,1,0:T(8,128)S(1)}, u32[]{:S(2)}, u32[]{:S(2)}) collective-permute-start(f32[3,128,128]{2,1,0:T(8,128)S(1)} %get-tuple-element.31), channel_id=1, source_target_pairs={{1,2},{3,4},{5,6},{7,8},{9,10},{11,12},{13,14},{2,1},{4,3},{6,5},{... | collective-permute-start | bytes 589832 | tf_op jit(solution)/shard_map/ppermute | solution.py:517
  88.7 7.4 %all-to-all-start.2 = ((f32[16,4,8,256]{3,2,1,0:T(8,128)}), f32[16,4,8,256]{3,2,1,0:T(8,128)S(1)}, u32[]{:S(2)}, u32[]{:S(2)}) async-start(f32[16,4,8,256]{3,2,1,0:T(8,128)} %get-tuple-element.32), calls=%async_computation.2 | async-start | bytes 1048576 | tf_op jit(solution)/shard_map/all_to_all | solution.py:471
  99.9 3.0 %all-to-all-done.2.refs_0_ = f32[16,4,8,256]{3,2,1,0:T(8,128)S(1)} async-done(((f32[16,4,8,256]{3,2,1,0:T(8,128)}), f32[16,4,8,256]{3,2,1,0:T(8,128)S(1)}, u32[]{:S(2)}, u32[]{:S(2)}) %all-to-all-start.2) | async-done | bytes 524320 | tf_op jit(solution)/shard_map/all_to_all | solution.py:471
  102.8 5.6 %collective-permute-start.9 = (f32[16,4,8,256]{3,2,1,0:T(8,128)S(1)}, f32[16,4,8,256]{3,2,1,0:T(8,128)S(1)}, u32[]{:S(2)}, u32[]{:S(2)}) collective-permute-start(f32[16,4,8,256]{3,2,1,0:T(8,128)S(1)} %all-to-all-done.2.refs_0_), channel_id=1, source_target_pairs={{0,1},{1,0},{2,3},{3,2},{4,5},{5,4},{6,7},{7,6},{8,9},{9,8},{10,11... | collective-permute-start | bytes 1572872 | tf_op jit(solution)/shard_map/ppermute | solution.py:523
  112.3 15.1 %collective-permute-done.12.refs_6_ = f32[3,2,128,128]{3,2,1,0:T(8,128)S(1)} collective-permute-done((f32[3,2,128,128]{3,2,1,0:T(8,128)S(1)}, f32[3,2,128,128]{3,2,1,0:T(8,128)S(1)}, u32[]{:S(2)}, u32[]{:S(2)}) %collective-permute-start.12) | collective-permute-done | bytes 393248 | tf_op jit(solution)/shard_map/ppermute | solution.py:444
  127.3 11.2 %step.3 = (f32[16,5,8,256]{3,2,1,0:T(8,128)S(1)}, f32[16,5,8,256]{3,2,1,0:T(8,128)S(1)}, f32[3,3,128,128]{3,2,1,0:T(8,128)S(1)}, f32[3,3,128,128]{3,2,1,0:T(8,128)S(1)}, f32[3,3,128,128]{3,2,1,0:T(8,128)S(1)}) custom-call(s32[1,1,2,2]{3,2,1,0:T(2,128)S(1)} %copy-done.2, s32[2]{0:T(128)S(1)} %pad_add_fusion.parity_ref, ...), custom_call_target="tpu_custom_call" | custom-call | tf_op jit(solution)/shard_map/step/pallas_call | solution.py:408
  142.2 6.6 %all-to-all-start.3 = ((f32[16,5,8,256]{3,2,1,0:T(8,128)}), f32[16,5,8,256]{3,2,1,0:T(8,128)S(1)}, u32[]{:S(2)}, u32[]{:S(2)}) async-start(f32[16,5,8,256]{3,2,1,0:T(8,128)} %add.123), calls=%async_computation.3 | async-start | bytes 1310720 | tf_op jit(solution)/shard_map/all_to_all | solution.py:471
  148.7 8.7 %collective-permute-done.14 = f32[3,3,128,128]{3,2,1,0:T(8,128)} collective-permute-done((f32[3,3,128,128]{3,2,1,0:T(8,128)S(1)}, f32[3,3,128,128]{3,2,1,0:T(8,128)}, u32[]{:S(2)}, u32[]{:S(2)}) %collective-permute-start.14) | collective-permute-done | bytes 589856 | tf_op jit(solution)/shard_map/ppermute | solution.py:510
  157.4 6.1 %collective-permute-done.15 = f32[3,3,128,128]{3,2,1,0:T(8,128)} collective-permute-done((f32[3,3,128,128]{3,2,1,0:T(8,128)S(1)}, f32[3,3,128,128]{3,2,1,0:T(8,128)}, u32[]{:S(2)}, u32[]{:S(2)}) %collective-permute-start.15) | collective-permute-done | bytes 589856 | tf_op jit(solution)/shard_map/ppermute | solution.py:511
  165.6 13.7 %all_to_all.30.pieces_ref = f32[8,5,8,256]{3,2,1,0:T(8,128)S(1)} all-to-all(f32[8,5,8,256]{3,2,1,0:T(8,128)S(1)} %spread.3), channel_id=1, replica_groups={{0,8,64,72,128,136,192,200},{1,9,65,73,129,137,193,201},{2,10,66,74,130..., dimensions={0} | all-to-all | bytes 655360 | tf_op jit(solution)/shard_map/all_to_all | solution.py:471
  180.2 6.0 %all-to-all-start.5 = ((f32[16,4,8,256]{3,2,1,0:T(8,128)}), f32[16,4,8,256]{3,2,1,0:T(8,128)S(1)}, u32[]{:S(2)}, u32[]{:S(2)}) async-start(f32[16,4,8,256]{3,2,1,0:T(8,128)} %get-tuple-element.41), calls=%async_computation.5 | async-start | bytes 1048576 | tf_op jit(solution)/shard_map/all_to_all | solution.py:471
  186.1 2.6 %collective-permute-start.17 = (f32[3,128,128]{2,1,0:T(8,128)S(1)}, f32[3,128,128]{2,1,0:T(8,128)S(1)}, u32[]{:S(2)}, u32[]{:S(2)}) collective-permute-start(f32[3,128,128]{2,1,0:T(8,128)S(1)} %get-tuple-element.39), channel_id=1, source_target_pairs={{0,1},{2,3},{4,5},{6,7},{8,9},{10,11},{12,13},{14,15},{1,0},{3,2},... | collective-permute-start | bytes 589832 | tf_op jit(solution)/shard_map/ppermute | solution.py:516
  188.7 2.7 %collective-permute-start.18 = (f32[3,128,128]{2,1,0:T(8,128)S(1)}, f32[3,128,128]{2,1,0:T(8,128)S(1)}, u32[]{:S(2)}, u32[]{:S(2)}) collective-permute-start(f32[3,128,128]{2,1,0:T(8,128)S(1)} %get-tuple-element.40), channel_id=1, source_target_pairs={{1,2},{3,4},{5,6},{7,8},{9,10},{11,12},{13,14},{2,1},{4,3},{6,5},{... | collective-permute-start | bytes 589832 | tf_op jit(solution)/shard_map/ppermute | solution.py:517
  193.1 3.2 %collective-permute-start.19 = (f32[16,4,8,256]{3,2,1,0:T(8,128)S(1)}, f32[16,4,8,256]{3,2,1,0:T(8,128)S(1)}, u32[]{:S(2)}, u32[]{:S(2)}) collective-permute-start(f32[16,4,8,256]{3,2,1,0:T(8,128)S(1)} %all-to-all-done.5.mine_ref), channel_id=1, source_target_pairs={{0,1},{1,0},{2,3},{3,2},{4,5},{5,4},{6,7},{7,6},{8,9},{9,8},{10,11... | collective-permute-start | bytes 1572872 | tf_op jit(solution)/shard_map/ppermute | solution.py:523
  196.3 7.5 %collective-permute-done.18 = f32[3,128,128]{2,1,0:T(8,128)S(1)} collective-permute-done((f32[3,128,128]{2,1,0:T(8,128)S(1)}, f32[3,128,128]{2,1,0:T(8,128)S(1)}, u32[]{:S(2)}, u32[]{:S(2)}) %collective-permute-start.18) | collective-permute-done | bytes 196640 | tf_op jit(solution)/shard_map/ppermute | solution.py:517
  (55 shorter events, 32.1 us)
Async XLA Ops:
  0.6 4.7 %collective-permute-start.1 = (f32[2,128,128]{2,1,0:T(8,128)}, f32[2,128,128]{2,1,0:T(8,128)S(1)}, u32[]{:S(2)}, u32[]{:S(2)}) collective-permute-start(f32[2,128,128]{2,1,0:T(8,128)} %refs_3_.1), channel_id=1, source_target_pairs={{0,16},{32,48},{64,80},{96,112},{128,144},{160,176},{192,208},{224... | collective-permute-start | bytes 393224 | tf_op jit(solution)/shard_map/ppermute | solution.py:440
  2.0 8.0 %collective-permute-start = (f32[2,128,128]{2,1,0:T(8,128)}, f32[2,128,128]{2,1,0:T(8,128)S(1)}, u32[]{:S(2)}, u32[]{:S(2)}) collective-permute-start(f32[2,128,128]{2,1,0:T(8,128)} %refs_3_.1), channel_id=1, source_target_pairs={{16,32},{48,64},{80,96},{112,128},{144,160},{176,192},{208,224},{3... | collective-permute-start | bytes 393224 | tf_op jit(solution)/shard_map/ppermute | solution.py:441
  11.0 10.9 %collective-permute-start.3 = (f32[3,2,128,128]{3,2,1,0:T(8,128)S(1)}, f32[3,2,128,128]{3,2,1,0:T(8,128)S(1)}, u32[]{:S(2)}, u32[]{:S(2)}) collective-permute-start(f32[3,2,128,128]{3,2,1,0:T(8,128)S(1)} %pad_maximum_fusion), channel_id=1, source_target_pairs={{0,1},{2,3},{4,5},{6,7},{8,9},{10,11},{12,13},{14,15},{1,0},{3,2},... | collective-permute-start | bytes 1179656 | tf_op jit(solution)/shard_map/ppermute | solution.py:443
  13.2 19.3 %collective-permute-start.2 = (f32[3,2,128,128]{3,2,1,0:T(8,128)S(1)}, f32[3,2,128,128]{3,2,1,0:T(8,128)S(1)}, u32[]{:S(2)}, u32[]{:S(2)}) collective-permute-start(f32[3,2,128,128]{3,2,1,0:T(8,128)S(1)} %pad_maximum_fusion), channel_id=1, source_target_pairs={{1,2},{3,4},{5,6},{7,8},{9,10},{11,12},{13,14},{2,1},{4,3},{6,5},{... | collective-permute-start | bytes 1179656 | tf_op jit(solution)/shard_map/ppermute | solution.py:444
  44.7 19.6 %collective-permute-start.4 = (f32[3,3,128,128]{3,2,1,0:T(8,128)}, f32[3,3,128,128]{3,2,1,0:T(8,128)}, u32[]{:S(2)}, u32[]{:S(2)}) collective-permute-start(f32[3,3,128,128]{3,2,1,0:T(8,128)} %get-tuple-element.23), channel_id=1, source_target_pairs={{0,16},{32,48},{64,80},{96,112},{128,144},{160,176},{192,208},{224... | collective-permute-start | bytes 1769480 | tf_op jit(solution)/shard_map/ppermute | solution.py:510
  44.8 24.6 %collective-permute-start.5 = (f32[3,3,128,128]{3,2,1,0:T(8,128)S(1)}, f32[3,3,128,128]{3,2,1,0:T(8,128)}, u32[]{:S(2)}, u32[]{:S(2)}) collective-permute-start(f32[3,3,128,128]{3,2,1,0:T(8,128)S(1)} %get-tuple-element.24), channel_id=1, source_target_pairs={{16,32},{48,64},{80,96},{112,128},{144,160},{176,192},{208,224},{3... | collective-permute-start | bytes 1769480 | tf_op jit(solution)/shard_map/ppermute | solution.py:511
  47.7 23.4 %all-to-all-start = ((f32[16,5,8,256]{3,2,1,0:T(8,128)}), f32[16,5,8,256]{3,2,1,0:T(8,128)S(1)}, u32[]{:S(2)}, u32[]{:S(2)}) async-start(f32[16,5,8,256]{3,2,1,0:T(8,128)} %add.103), calls=%async_computation | async-start | bytes 1310720 | tf_op jit(solution)/shard_map/all_to_all | solution.py:471
  71.9 16.0 %all-to-all-start.1 = ((f32[8,5,8,256]{3,2,1,0:T(8,128)}), f32[8,5,8,256]{3,2,1,0:T(8,128)S(1)}, u32[]{:S(2)}, u32[]{:S(2)}) async-start(f32[8,5,8,256]{3,2,1,0:T(8,128)} %spread.2), calls=%async_computation.1 | async-start | bytes 655360 | tf_op jit(solution)/shard_map/all_to_all | solution.py:471
  75.3 20.9 %collective-permute-start.7 = (f32[3,128,128]{2,1,0:T(8,128)S(1)}, f32[3,128,128]{2,1,0:T(8,128)S(1)}, u32[]{:S(2)}, u32[]{:S(2)}) collective-permute-start(f32[3,128,128]{2,1,0:T(8,128)S(1)} %get-tuple-element.30), channel_id=1, source_target_pairs={{0,1},{2,3},{4,5},{6,7},{8,9},{10,11},{12,13},{14,15},{1,0},{3,2},... | collective-permute-start | bytes 589832 | tf_op jit(solution)/shard_map/ppermute | solution.py:516
  76.6 19.5 %collective-permute-start.8 = (f32[3,128,128]{2,1,0:T(8,128)S(1)}, f32[3,128,128]{2,1,0:T(8,128)S(1)}, u32[]{:S(2)}, u32[]{:S(2)}) collective-permute-start(f32[3,128,128]{2,1,0:T(8,128)S(1)} %get-tuple-element.31), channel_id=1, source_target_pairs={{1,2},{3,4},{5,6},{7,8},{9,10},{11,12},{13,14},{2,1},{4,3},{6,5},{... | collective-permute-start | bytes 589832 | tf_op jit(solution)/shard_map/ppermute | solution.py:517
  88.7 14.1 %all-to-all-start.2 = ((f32[16,4,8,256]{3,2,1,0:T(8,128)}), f32[16,4,8,256]{3,2,1,0:T(8,128)S(1)}, u32[]{:S(2)}, u32[]{:S(2)}) async-start(f32[16,4,8,256]{3,2,1,0:T(8,128)} %get-tuple-element.32), calls=%async_computation.2 | async-start | bytes 1048576 | tf_op jit(solution)/shard_map/all_to_all | solution.py:471
  96.2 12.2 %collective-permute-start.11 = (f32[2,128,128]{2,1,0:T(8,128)S(1)}, f32[2,128,128]{2,1,0:T(8,128)S(1)}, u32[]{:S(2)}, u32[]{:S(2)}) collective-permute-start(f32[2,128,128]{2,1,0:T(8,128)S(1)} %fusion.9.refs_4_), channel_id=1, source_target_pairs={{0,16},{32,48},{64,80},{96,112},{128,144},{160,176},{192,208},{224... | collective-permute-start | bytes 393224 | tf_op jit(solution)/shard_map/ppermute | solution.py:440
  97.5 10.9 %collective-permute-start.10 = (f32[2,128,128]{2,1,0:T(8,128)S(1)}, f32[2,128,128]{2,1,0:T(8,128)S(1)}, u32[]{:S(2)}, u32[]{:S(2)}) collective-permute-start(f32[2,128,128]{2,1,0:T(8,128)S(1)} %fusion.9.refs_4_), channel_id=1, source_target_pairs={{16,32},{48,64},{80,96},{112,128},{144,160},{176,192},{208,224},{3... | collective-permute-start | bytes 393224 | tf_op jit(solution)/shard_map/ppermute | solution.py:441
  102.8 24.5 %collective-permute-start.9 = (f32[16,4,8,256]{3,2,1,0:T(8,128)S(1)}, f32[16,4,8,256]{3,2,1,0:T(8,128)S(1)}, u32[]{:S(2)}, u32[]{:S(2)}) collective-permute-start(f32[16,4,8,256]{3,2,1,0:T(8,128)S(1)} %all-to-all-done.2.refs_0_), channel_id=1, source_target_pairs={{0,1},{1,0},{2,3},{3,2},{4,5},{5,4},{6,7},{7,6},{8,9},{9,8},{10,11... | collective-permute-start | bytes 1572872 | tf_op jit(solution)/shard_map/ppermute | solution.py:523
  108.4 3.9 %collective-permute-start.13 = (f32[3,2,128,128]{3,2,1,0:T(8,128)S(1)}, f32[3,2,128,128]{3,2,1,0:T(8,128)S(1)}, u32[]{:S(2)}, u32[]{:S(2)}) collective-permute-start(f32[3,2,128,128]{3,2,1,0:T(8,128)S(1)} %pad_maximum_fusion.1), channel_id=1, source_target_pairs={{0,1},{2,3},{4,5},{6,7},{8,9},{10,11},{12,13},{14,15},{1,0},{3,2},... | collective-permute-start | bytes 1179656 | tf_op jit(solution)/shard_map/ppermute | solution.py:443
  110.3 17.1 %collective-permute-start.12 = (f32[3,2,128,128]{3,2,1,0:T(8,128)S(1)}, f32[3,2,128,128]{3,2,1,0:T(8,128)S(1)}, u32[]{:S(2)}, u32[]{:S(2)}) collective-permute-start(f32[3,2,128,128]{3,2,1,0:T(8,128)S(1)} %pad_maximum_fusion.1), channel_id=1, source_target_pairs={{1,2},{3,4},{5,6},{7,8},{9,10},{11,12},{13,14},{2,1},{4,3},{6,5},{... | collective-permute-start | bytes 1179656 | tf_op jit(solution)/shard_map/ppermute | solution.py:444
  138.6 2.7 %collective-permute-start.16 = (f32[16,5,8,256]{3,2,1,0:T(8,128)S(1)}, f32[16,5,8,256]{3,2,1,0:T(8,128)S(1)}, u32[]{:S(2)}, u32[]{:S(2)}) collective-permute-start(f32[16,5,8,256]{3,2,1,0:T(8,128)S(1)} %get-tuple-element.37), channel_id=1, source_target_pairs={{0,1},{1,0},{2,3},{3,2},{4,5},{5,4},{6,7},{7,6},{8,9},{9,8},{10,11... | collective-permute-start | bytes 1966088 | tf_op jit(solution)/shard_map/ppermute | solution.py:512
  138.9 18.6 %collective-permute-start.14 = (f32[3,3,128,128]{3,2,1,0:T(8,128)S(1)}, f32[3,3,128,128]{3,2,1,0:T(8,128)}, u32[]{:S(2)}, u32[]{:S(2)}) collective-permute-start(f32[3,3,128,128]{3,2,1,0:T(8,128)S(1)} %get-tuple-element.34), channel_id=1, source_target_pairs={{0,16},{32,48},{64,80},{96,112},{128,144},{160,176},{192,208},{224... | collective-permute-start | bytes 1769480 | tf_op jit(solution)/shard_map/ppermute | solution.py:510
  139.3 24.2 %collective-permute-start.15 = (f32[3,3,128,128]{3,2,1,0:T(8,128)S(1)}, f32[3,3,128,128]{3,2,1,0:T(8,128)}, u32[]{:S(2)}, u32[]{:S(2)}) collective-permute-start(f32[3,3,128,128]{3,2,1,0:T(8,128)S(1)} %get-tuple-element.35), channel_id=1, source_target_pairs={{16,32},{48,64},{80,96},{112,128},{144,160},{176,192},{208,224},{3... | collective-permute-start | bytes 1769480 | tf_op jit(solution)/shard_map/ppermute | solution.py:511
  142.2 23.4 %all-to-all-start.3 = ((f32[16,5,8,256]{3,2,1,0:T(8,128)}), f32[16,5,8,256]{3,2,1,0:T(8,128)S(1)}, u32[]{:S(2)}, u32[]{:S(2)}) async-start(f32[16,5,8,256]{3,2,1,0:T(8,128)} %add.123), calls=%async_computation.3 | async-start | bytes 1310720 | tf_op jit(solution)/shard_map/all_to_all | solution.py:471
  180.2 12.9 %all-to-all-start.5 = ((f32[16,4,8,256]{3,2,1,0:T(8,128)}), f32[16,4,8,256]{3,2,1,0:T(8,128)S(1)}, u32[]{:S(2)}, u32[]{:S(2)}) async-start(f32[16,4,8,256]{3,2,1,0:T(8,128)} %get-tuple-element.41), calls=%async_computation.5 | async-start | bytes 1048576 | tf_op jit(solution)/shard_map/all_to_all | solution.py:471
  186.1 10.2 %collective-permute-start.17 = (f32[3,128,128]{2,1,0:T(8,128)S(1)}, f32[3,128,128]{2,1,0:T(8,128)S(1)}, u32[]{:S(2)}, u32[]{:S(2)}) collective-permute-start(f32[3,128,128]{2,1,0:T(8,128)S(1)} %get-tuple-element.39), channel_id=1, source_target_pairs={{0,1},{2,3},{4,5},{6,7},{8,9},{10,11},{12,13},{14,15},{1,0},{3,2},... | collective-permute-start | bytes 589832 | tf_op jit(solution)/shard_map/ppermute | solution.py:516
  188.7 15.0 %collective-permute-start.18 = (f32[3,128,128]{2,1,0:T(8,128)S(1)}, f32[3,128,128]{2,1,0:T(8,128)S(1)}, u32[]{:S(2)}, u32[]{:S(2)}) collective-permute-start(f32[3,128,128]{2,1,0:T(8,128)S(1)} %get-tuple-element.40), channel_id=1, source_target_pairs={{1,2},{3,4},{5,6},{7,8},{9,10},{11,12},{13,14},{2,1},{4,3},{6,5},{... | collective-permute-start | bytes 589832 | tf_op jit(solution)/shard_map/ppermute | solution.py:517
  193.1 11.4 %collective-permute-start.19 = (f32[16,4,8,256]{3,2,1,0:T(8,128)S(1)}, f32[16,4,8,256]{3,2,1,0:T(8,128)S(1)}, u32[]{:S(2)}, u32[]{:S(2)}) collective-permute-start(f32[16,4,8,256]{3,2,1,0:T(8,128)S(1)} %all-to-all-done.5.mine_ref), channel_id=1, source_target_pairs={{0,1},{1,0},{2,3},{3,2},{4,5},{5,4},{6,7},{7,6},{8,9},{9,8},{10,11... | collective-permute-start | bytes 1572872 | tf_op jit(solution)/shard_map/ppermute | solution.py:523
  (4 other events, 44.6 us)

commit v7 on v5

--- a/solution.py
+++ b/solution.py
@@ -23,6 +23,7 @@
 CHUNK = 64
 GROUPS = 16
 DEPTH = 8
+SHIFT = TILE + 1
 F32 = jnp.float32
 BF16 = jnp.bfloat16
 
@@ -97,6 +98,7 @@
         grad_second,
         grad_middle,
         grad_first,
+        power_out,
         table_ref,
         probe,
         measured_ref,
@@ -107,7 +109,6 @@
         far,
         back,
         contrib,
-        power_ref,
         total,
         sums,
         semaphores,
@@ -123,13 +124,13 @@
         copies.append(copy)
 
     def third(block):
-        return pl.ds(pl.multiple_of(block * TILE, TILE), TILE)
+        return pl.ds(block * TILE if isinstance(block, int) else pl.multiple_of(block * TILE, TILE), TILE)
 
     for place, piece in enumerate((outer_in, tile_in, inner_in)):
         columns = third(along[place])
-        start(piece, padded.at[:, third(1), columns])
-        start(second_in.at[place], padded.at[:, third(across[0]), columns])
-        start(first_in.at[place], padded.at[:, third(across[2]), columns])
+        start(piece.at[:, third(0)], padded.at[:, third(1), columns])
+        start(second_in.at[place, :, third(0)], padded.at[:, third(across[0]), columns])
+        start(first_in.at[place, :, third(0)], padded.at[:, third(across[2]), columns])
     near = len(copies)
     if halves:
         for half, ref in enumerate(probe_in):
@@ -149,7 +150,7 @@
 
     lane = lax.broadcasted_iota(jnp.int32, (CHUNK // 8, 8, TILE), 2)
     sublane = lax.broadcasted_iota(jnp.int32, (CHUNK // 8, 8, TILE), 1)
-    for channel in range(3):
+    for channel in range(2):
         total[channel] = jnp.zeros((WIDE + 8, WIDE), F32)
     for copy in copies[:near]:
         copy.wait()
@@ -305,7 +306,7 @@
             for part in range(2):
                 value = probe_rows(part, mode, piece)
                 power = value * value if power is None else power + value * value
-        power_ref[rows, :] = power
+        power_out[rows, :] = power
         weight = None
         for scan in range(2):
             for part in range(2):
@@ -324,13 +325,11 @@
         zero = jnp.zeros((CHUNK // 8, 8, TILE), F32)
         edge = jnp.zeros((1, 8, TILE), F32)
         stay = lax.broadcasted_iota(jnp.int32, (CHUNK // 8 + 1, 8, TILE), 1) >= inner
-        for channel in range(3):
+        for channel in range(2):
             for piece in range(SIDE // CHUNK):
                 halves = []
                 for b in range(2):
-                    value = (power_ref if channel == 2 else contrib.at[scan, channel])[
-                        pl.ds(piece * CHUNK, CHUNK), pl.ds(b * TILE, TILE)
-                    ]
+                    value = contrib[scan, channel, pl.ds(piece * CHUNK, CHUNK), pl.ds(b * TILE, TILE)]
                     halves.append(pltpu.roll(value.reshape(CHUNK // 8, 8, TILE), turn, 2))
                 thirds = (
                     jnp.where(keep, halves[0], zero),
@@ -359,6 +358,36 @@
         copy.wait()
 
 
+def weigh_kernel(parity_ref, near_ref, power_ref, out_ref, padded):
+    padded[...] = jnp.zeros_like(padded)
+    padded[pl.ds(TILE, SIDE), pl.ds(TILE, SIDE)] = power_ref[...]
+    lane = lax.broadcasted_iota(jnp.int32, (TILE // 8, 8, TILE), 2)
+    sublane = lax.broadcasted_iota(jnp.int32, (TILE // 8, 8, TILE), 1)
+
+    def add(index, total):
+        place, scan = index // 2, index % 2
+        across, along = place // 3, place % 3
+        across = 1 + (across - 1) * (1 - 2 * parity_ref[0])
+        along = 1 + (along - 1) * (1 - 2 * parity_ref[1])
+        row, column = near_ref[place, 2 * scan], near_ref[place, 2 * scan + 1]
+        column = jnp.where(row == 0, 0, 2 * TILE - along * TILE - (column - SHIFT))
+        row = jnp.where(row == 0, WIDE, 2 * TILE - across * TILE - (row - SHIFT))
+        inner = lax.rem(row, 8)
+        base = pl.multiple_of(row - inner, 8)
+        offset = lax.rem(column, TILE)
+        block = pl.multiple_of(column - offset, TILE)
+        turned = []
+        for b in range(2):
+            rows = padded[pl.ds(base, TILE + 8), pl.ds(block + b * TILE, TILE)]
+            rows = pltpu.roll(rows.reshape(TILE // 8 + 1, 8, TILE), lax.rem(8 - inner, 8), 1)
+            rows = jnp.where(sublane < 8 - inner, rows[:-1], rows[1:])
+            turned.append(pltpu.roll(rows, lax.rem(TILE - offset, TILE), 2))
+        return total + jnp.where(lane < TILE - offset, turned[0], turned[1])
+
+    total = lax.fori_loop(0, 18, add, jnp.zeros((TILE // 8, 8, TILE), F32))
+    out_ref[...] = total.reshape(TILE, TILE)
+
+
 def spread_kernel(pieces_ref, out_ref):
     total = pieces_ref[0]
     for piece in range(1, GROUPS):
@@ -403,13 +432,13 @@
 
 def step(offsets, parity, table, probe, measured, around):
     halves = len(probe) - 1
-    band = jax.ShapeDtypeStruct((3, 3, TILE, TILE), F32)
+    band = jax.ShapeDtypeStruct((3, 2, TILE, TILE), F32)
     half = jax.ShapeDtypeStruct((GROUPS, 5, 8, SIDE), F32)
     return pl.pallas_call(
         functools.partial(step_kernel, halves),
-        out_shape=[half, half, band, band, band],
+        out_shape=[half, half, band, band, band, jax.ShapeDtypeStruct((SIDE, SIDE), F32)],
         in_specs=[SMEM_SPEC, SMEM_SPEC] + [ANY_SPEC] * (8 + halves),
-        out_specs=[ANY_SPEC] * 5,
+        out_specs=[ANY_SPEC] * 5 + [VMEM_SPEC],
         scratch_shapes=[
             pltpu.VMEM(table.shape, BF16),
             pltpu.VMEM((4, 2 * GROUPS, 8, SIDE), F32),
@@ -421,8 +450,7 @@
             pltpu.VMEM((4, 2, SIDE, SIDE), F32),
             pltpu.VMEM((2, SIDE, SIDE), F32),
             pltpu.VMEM((2, 2, SIDE, SIDE), F32),
-            pltpu.VMEM((SIDE, SIDE), F32),
-            pltpu.VMEM((3, WIDE + 8, WIDE), F32),
+            pltpu.VMEM((2, WIDE + 8, WIDE), F32),
             pltpu.VMEM((2 * GROUPS, 5, 8, SIDE), F32),
             pltpu.SemaphoreType.DMA((32,)),
         ],
@@ -469,6 +497,24 @@
 
 def exchange(value, groups):
     return lax.all_to_all(value, BOTH, 0, 0, axis_index_groups=groups, tiled=True)
+
+
+def weigh(parity, near, power):
+    return pl.pallas_call(
+        weigh_kernel,
+        out_shape=jax.ShapeDtypeStruct((TILE, TILE), F32),
+        in_specs=[SMEM_SPEC, SMEM_SPEC, VMEM_SPEC],
+        out_specs=VMEM_SPEC,
+        scratch_shapes=[pltpu.VMEM((4 * TILE + 8, 5 * TILE), F32)],
+        compiler_params=params(8),
+        name="weigh",
+    )(parity, near, power)
+
+
+def offsets_near(outer, tile, inner, second, first):
+    rows = [[band[i, 0, TILE, :4] for i in range(3)] for band in (second, first)]
+    rows.insert(1, [piece[0, TILE, :4] for piece in (outer, tile, inner)])
+    return jnp.stack([value for row in rows for value in row]).astype(jnp.int32)
 
 
 def spread(pieces):
@@ -503,9 +549,12 @@
     measured = sort_measured(amplitudes[0, 0])
     parts = (in_hbm(probe),)
     tile = object_field
+    marks = jnp.pad((offsets + SHIFT).astype(F32).reshape(1, 1, 4), ((0, 1), (0, 7), (0, TILE - 4)))
+    around = neighbourhood(jnp.concatenate([tile, marks], axis=1))
+    near = offsets_near(*around)
     for iteration in range(ITERS):
-        mine, other, second, middle, first = step(
-            offsets, parity, table, parts, measured, neighbourhood(tile)
+        mine, other, second, middle, first, power = step(
+            offsets, parity, table, parts, measured, around
         )
         first = lax.ppermute(first, "row", pairs(0))
         second = lax.ppermute(second, "row", pairs(1))
@@ -515,11 +564,16 @@
         pieces = spread(after(pieces, (outer, own, inner)))
         inner = lax.ppermute(after(inner, pieces), "col", pairs(0))
         outer = lax.ppermute(after(outer, pieces), "col", pairs(1))
-        pieces = exchange(pieces, LINES)
+        weight = weigh(parity, near, after(power, pieces))
+        pieces = after(exchange(pieces, LINES), weight)
         pieces, old = update(pieces, old)
         totals = after(own, old) + inner + outer
-        tile = tile + OBJECT_STEP * totals[0:2] / (totals[2:3] + OBJECT_REG)
+        tile = tile + OBJECT_STEP * totals / (weight + OBJECT_REG)
+        if iteration + 1 < ITERS:
+            around = neighbourhood(tile)
         mine = exchange(pieces, PLANES)
+        if iteration + 1 == ITERS:
+            mine = after(mine, (inner, outer))
         parts = (mine, lax.ppermute(mine, "col", SWAP))
     probe = pl.pallas_call(
         lay_out_kernel,

time: 200 us -> 193 us (0.965)
  blocking collectives: 13.4 us -> 0 us
  Pallas kernels: 28.4 us -> 34.6 us
  starting transfers between devices: 86.1 us -> 82.4 us
  waiting for transfers between devices: 62.9 us -> 66.4 us
    all_to_all x5 -> x6, waiting for transfers between devices: 3.85 us -> 26 us  [exchange(): lax.all_to_all(value, BOTH, 0, 0, axis_index_groups=groups, tiled=True)]
    all_to_all x1 -> x0, blocking collectives: 13.4 us -> none  [exchange(): lax.all_to_all(value, BOTH, 0, 0, axis_index_groups=groups, tiled=True)]
    ppermute x2, waiting for transfers between devices: 12.6 us -> 0.01 us  [local(): first = lax.ppermute(first, 'row', pairs(0))]
    ppermute x2, waiting for transfers between devices: 14.4 us -> 5.97 us  [local(): second = lax.ppermute(second, 'row', pairs(1))]
    all_to_all x5 -> x6, starting transfers between devices: 31.8 us -> 38.3 us  [exchange(): lax.all_to_all(value, BOTH, 0, 0, axis_index_groups=groups, tiled=True)]
    ppermute x2, starting transfers between devices: 7.67 us -> 1.5 us  [local(): parts = (mine, lax.ppermute(mine, 'col', SWAP))]
    pallas_call x0 -> x2, Pallas kernels: none -> 5.98 us  [weigh(): pl.pallas_call(weigh_kernel, out_shape=jax.ShapeDtypeStruct((TILE, TILE),...]
    ppermute x2, starting transfers between devices: 4.54 us -> 1.1 us  [neighbourhood(): inner = lax.ppermute(tile, 'col', pairs(0))]
  transfers between devices with their start and end apart: 25 -> 26, of which waited for: 16 -> 14; matrix products, arithmetic and copies ran while one was open for 3% -> 3% of each run, Pallas kernels for 1% -> 4%
where the time goes in v7:
time: 193 us; the launch traced here: 192 us
  starting transfers between devices  82.4 us (43%)
  waiting for transfers between devices  66.4 us (34%)
  Pallas kernels  34.6 us (18%)
  other arithmetic  5.69 us (3%)
    all_to_all x6, starting transfers between devices, exchange(): lax.all_to_all(value, BOTH, 0, 0, axis_index_groups=groups, tiled=True)  38.3 us
    all_to_all x6, waiting for transfers between devices, exchange(): lax.all_to_all(value, BOTH, 0, 0, axis_index_groups=groups, tiled=True)  26 us
    pallas_call x2, Pallas kernels, step(): pl.pallas_call(functools.partial(step_kernel, halves), out_shape=[half, h...  22.9 us
    ppermute x2, starting transfers between devices, local(): outer = lax.ppermute(after(outer, pieces), 'col', pairs(1))  11.6 us
    ppermute x2, starting transfers between devices, neighbourhood(): outer = lax.ppermute(tile, 'col', pairs(1))  10.9 us
    ppermute x2, waiting for transfers between devices, local(): outer = lax.ppermute(after(outer, pieces), 'col', pairs(1))  10.2 us
    ppermute x2, waiting for transfers between devices, neighbourhood(): second = lax.ppermute(band, 'row', pairs(1))  9.69 us
    ppermute x2, waiting for transfers between devices, neighbourhood(): outer = lax.ppermute(tile, 'col', pairs(1))  9.21 us
  transfers between devices with their start and end apart: 26, of which 14 were waited for; matrix products, arithmetic and copies ran while one was open for 3% of the time, Pallas kernels for 4%

profile of v7, /device:TPU:39, one launch (start us, length us, event | category | flops | bytes accessed | tf_op | source)
XLA Modules:
  0.0 191.9 jit_solution(16998194484654658061)
XLA Ops:
  3.1 7.9 %collective-permute-start = (f32[2,136,128]{2,1,0:T(8,128)S(1)}, f32[2,136,128]{2,1,0:T(8,128)S(1)}, u32[]{:S(2)}, u32[]{:S(2)}) collective-permute-start(f32[2,136,128]{2,1,0:T(8,128)S(1)} %get-tuple-element.69.refs_3_), channel_id=1, source_target_pairs={{1,2},{3,4},{5,6},{7,8},{9,10},{11,12},{13,14},{2,1},{4,3},{6,5},{... | collective-permute-start | bytes 417800 | tf_op jit(solution)/shard_map/ppermute | solution.py:469
  11.0 4.6 %collective-permute-done.refs_2_ = f32[2,136,128]{2,1,0:T(8,128)S(1)} collective-permute-done((f32[2,136,128]{2,1,0:T(8,128)S(1)}, f32[2,136,128]{2,1,0:T(8,128)S(1)}, u32[]{:S(2)}, u32[]{:S(2)}) %collective-permute-start) | collective-permute-done | bytes 139296 | tf_op jit(solution)/shard_map/ppermute | solution.py:469
  16.9 3.4 %collective-permute-start.2 = (f32[3,2,136,128]{3,2,1,0:T(8,128)S(1)}, f32[3,2,136,128]{3,2,1,0:T(8,128)S(1)}, u32[]{:S(2)}, u32[]{:S(2)}) collective-permute-start(f32[3,2,136,128]{3,2,1,0:T(8,128)S(1)} %pad_maximum_fusion), channel_id=1, source_target_pairs={{16,32},{48,64},{80,96},{112,128},{144,160},{176,192},{208,224},{3... | collective-permute-start | bytes 1253384 | tf_op jit(solution)/shard_map/ppermute | solution.py:472
  22.9 4.9 %collective-permute-done.2.refs_5_ = f32[3,2,136,128]{3,2,1,0:T(8,128)S(1)} collective-permute-done((f32[3,2,136,128]{3,2,1,0:T(8,128)S(1)}, f32[3,2,136,128]{3,2,1,0:T(8,128)S(1)}, u32[]{:S(2)}, u32[]{:S(2)}) %collective-permute-start.2) | collective-permute-done | bytes 417824 | tf_op jit(solution)/shard_map/ppermute | solution.py:472
  27.8 11.9 %step.2 = (f32[16,5,8,256]{3,2,1,0:T(8,128)S(1)}, f32[16,5,8,256]{3,2,1,0:T(8,128)S(1)}, f32[3,2,128,128]{3,2,1,0:T(8,128)S(1)}, f32[3,2,128,128]{3,2,1,0:T(8,12...) custom-call(s32[1,1,2,2]{3,2,1,0:T(2,128)S(1)} %copy-done.1, s32[2]{0:T(128)S(1)} %pad_add_fusion.parity_ref, ...), custom_call_target="tpu_custom_call" | custom-call | tf_op jit(solution)/shard_map/step/pallas_call | solution.py:437
  39.8 3.4 %collective-permute-start.5 = (f32[3,2,128,128]{3,2,1,0:T(8,128)S(1)}, f32[3,2,128,128]{3,2,1,0:T(8,128)}, u32[]{:S(2)}, u32[]{:S(2)}) collective-permute-start(f32[3,2,128,128]{3,2,1,0:T(8,128)S(1)} %get-tuple-element.31), channel_id=1, source_target_pairs={{16,32},{48,64},{80,96},{112,128},{144,160},{176,192},{208,224},{3... | collective-permute-start | bytes 1179656 | tf_op jit(solution)/shard_map/ppermute | solution.py:560
  44.2 6.8 %all-to-all-start = ((f32[16,5,8,256]{3,2,1,0:T(8,128)}), f32[16,5,8,256]{3,2,1,0:T(8,128)S(1)}, u32[]{:S(2)}, u32[]{:S(2)}) async-start(f32[16,5,8,256]{3,2,1,0:T(8,128)} %add.109), calls=%async_computation | async-start | bytes 1310720 | tf_op jit(solution)/shard_map/all_to_all | solution.py:499
  55.5 4.8 %all-to-all-done.pieces_ref = f32[16,5,8,256]{3,2,1,0:T(8,128)S(1)} async-done(((f32[16,5,8,256]{3,2,1,0:T(8,128)}), f32[16,5,8,256]{3,2,1,0:T(8,128)S(1)}, u32[]{:S(2)}, u32[]{:S(2)}) %all-to-all-start) | async-done | bytes 655392 | tf_op jit(solution)/shard_map/all_to_all | solution.py:499
  61.1 9.0 %all-to-all-start.1 = ((f32[8,5,8,256]{3,2,1,0:T(8,128)}), f32[8,5,8,256]{3,2,1,0:T(8,128)S(1)}, u32[]{:S(2)}, u32[]{:S(2)}) async-start(f32[8,5,8,256]{3,2,1,0:T(8,128)} %spread.2), calls=%async_computation.1 | async-start | bytes 655360 | tf_op jit(solution)/shard_map/all_to_all | solution.py:499
  71.8 8.5 %collective-permute-start.8 = (f32[2,128,128]{2,1,0:T(8,128)S(1)}, f32[2,128,128]{2,1,0:T(8,128)S(1)}, u32[]{:S(2)}, u32[]{:S(2)}) collective-permute-start(f32[2,128,128]{2,1,0:T(8,128)S(1)} %get-tuple-element.41), channel_id=1, source_target_pairs={{1,2},{3,4},{5,6},{7,8},{9,10},{11,12},{13,14},{2,1},{4,3},{6,5},{... | collective-permute-start | bytes 393224 | tf_op jit(solution)/shard_map/ppermute | solution.py:566
  84.2 6.2 %all-to-all-start.2 = ((f32[16,4,8,256]{3,2,1,0:T(8,128)}), f32[16,4,8,256]{3,2,1,0:T(8,128)S(1)}, u32[]{:S(2)}, u32[]{:S(2)}) async-start(f32[16,4,8,256]{3,2,1,0:T(8,128)} %get-tuple-element.42), calls=%async_computation.2 | async-start | bytes 1048576 | tf_op jit(solution)/shard_map/all_to_all | solution.py:499
  94.7 4.4 %all-to-all-done.2.refs_0_ = f32[16,4,8,256]{3,2,1,0:T(8,128)S(1)} async-done(((f32[16,4,8,256]{3,2,1,0:T(8,128)}), f32[16,4,8,256]{3,2,1,0:T(8,128)S(1)}, u32[]{:S(2)}, u32[]{:S(2)}) %all-to-all-start.2) | async-done | bytes 524320 | tf_op jit(solution)/shard_map/all_to_all | solution.py:499
  100.5 4.6 %collective-permute-done.10.refs_3_ = f32[2,128,128]{2,1,0:T(8,128)S(1)} collective-permute-done((f32[2,128,128]{2,1,0:T(8,128)S(1)}, f32[2,128,128]{2,1,0:T(8,128)S(1)}, u32[]{:S(2)}, u32[]{:S(2)}) %collective-permute-start.10) | collective-permute-done | bytes 131104 | tf_op jit(solution)/shard_map/ppermute | solution.py:469
  106.4 3.3 %collective-permute-start.12 = (f32[3,2,128,128]{3,2,1,0:T(8,128)S(1)}, f32[3,2,128,128]{3,2,1,0:T(8,128)S(1)}, u32[]{:S(2)}, u32[]{:S(2)}) collective-permute-start(f32[3,2,128,128]{3,2,1,0:T(8,128)S(1)} %pad_maximum_fusion.1), channel_id=1, source_target_pairs={{16,32},{48,64},{80,96},{112,128},{144,160},{176,192},{208,224},{3... | collective-permute-start | bytes 1179656 | tf_op jit(solution)/shard_map/ppermute | solution.py:472
  112.3 4.8 %collective-permute-done.12.refs_6_ = f32[3,2,128,128]{3,2,1,0:T(8,128)S(1)} collective-permute-done((f32[3,2,128,128]{3,2,1,0:T(8,128)S(1)}, f32[3,2,128,128]{3,2,1,0:T(8,128)S(1)}, u32[]{:S(2)}, u32[]{:S(2)}) %collective-permute-start.12) | collective-permute-done | bytes 393248 | tf_op jit(solution)/shard_map/ppermute | solution.py:472
  117.1 11.0 %step.3 = (f32[16,5,8,256]{3,2,1,0:T(8,128)S(1)}, f32[16,5,8,256]{3,2,1,0:T(8,128)S(1)}, f32[3,2,128,128]{3,2,1,0:T(8,128)S(1)}, f32[3,2,128,128]{3,2,1,0:T(8,12...) custom-call(s32[1,1,2,2]{3,2,1,0:T(2,128)S(1)} %copy-done.1, s32[2]{0:T(128)S(1)} %pad_add_fusion.parity_ref, ...), custom_call_target="tpu_custom_call" | custom-call | tf_op jit(solution)/shard_map/step/pallas_call | solution.py:437
  128.5 3.3 %collective-permute-start.15 = (f32[3,2,128,128]{3,2,1,0:T(8,128)S(1)}, f32[3,2,128,128]{3,2,1,0:T(8,128)S(1)}, u32[]{:S(2)}, u32[]{:S(2)}) collective-permute-start(f32[3,2,128,128]{3,2,1,0:T(8,128)S(1)} %get-tuple-element.45), channel_id=1, source_target_pairs={{16,32},{48,64},{80,96},{112,128},{144,160},{176,192},{208,224},{3... | collective-permute-start | bytes 1179656 | tf_op jit(solution)/shard_map/ppermute | solution.py:560
  132.7 6.5 %all-to-all-start.3 = ((f32[16,5,8,256]{3,2,1,0:T(8,128)}), f32[16,5,8,256]{3,2,1,0:T(8,128)S(1)}, u32[]{:S(2)}, u32[]{:S(2)}) async-start(f32[16,5,8,256]{3,2,1,0:T(8,128)} %add.129), calls=%async_computation.3 | async-start | bytes 1310720 | tf_op jit(solution)/shard_map/all_to_all | solution.py:499
  139.2 3.5 %collective-permute-done.15 = f32[3,2,128,128]{3,2,1,0:T(8,128)S(1)} collective-permute-done((f32[3,2,128,128]{3,2,1,0:T(8,128)S(1)}, f32[3,2,128,128]{3,2,1,0:T(8,128)S(1)}, u32[]{:S(2)}, u32[]{:S(2)}) %collective-permute-start.15) | collective-permute-done | bytes 393248 | tf_op jit(solution)/shard_map/ppermute | solution.py:560
  142.9 7.7 %all-to-all-done.3.pieces_ref = f32[16,5,8,256]{3,2,1,0:T(8,128)S(1)} async-done(((f32[16,5,8,256]{3,2,1,0:T(8,128)}), f32[16,5,8,256]{3,2,1,0:T(8,128)S(1)}, u32[]{:S(2)}, u32[]{:S(2)}) %all-to-all-start.3) | async-done | bytes 655392 | tf_op jit(solution)/shard_map/all_to_all | solution.py:499
  151.3 4.3 %all-to-all-start.4 = ((f32[8,5,8,256]{3,2,1,0:T(8,128)}), f32[8,5,8,256]{3,2,1,0:T(8,128)S(1)}, u32[]{:S(2)}, u32[]{:S(2)}) async-start(f32[8,5,8,256]{3,2,1,0:T(8,128)} %spread.3), calls=%async_computation.4 | async-start | bytes 655360 | tf_op jit(solution)/shard_map/all_to_all | solution.py:499
  158.6 9.1 %all-to-all-done.4.pieces_ref = f32[8,5,8,256]{3,2,1,0:T(8,128)S(1)} async-done(((f32[8,5,8,256]{3,2,1,0:T(8,128)}), f32[8,5,8,256]{3,2,1,0:T(8,128)S(1)}, u32[]{:S(2)}, u32[]{:S(2)}) %all-to-all-start.4) | async-done | bytes 327712 | tf_op jit(solution)/shard_map/all_to_all | solution.py:499
  168.6 5.5 %all-to-all-start.5 = ((f32[16,4,8,256]{3,2,1,0:T(8,128)}), f32[16,4,8,256]{3,2,1,0:T(8,128)S(1)}, u32[]{:S(2)}, u32[]{:S(2)}) async-start(f32[16,4,8,256]{3,2,1,0:T(8,128)} %get-tuple-element.54), calls=%async_computation.5 | async-start | bytes 1048576 | tf_op jit(solution)/shard_map/all_to_all | solution.py:499
  178.2 10.2 %collective-permute-done.18 = f32[2,128,128]{2,1,0:T(8,128)S(1)} collective-permute-done((f32[2,128,128]{2,1,0:T(8,128)S(1)}, f32[2,128,128]{2,1,0:T(8,128)S(1)}, u32[]{:S(2)}, u32[]{:S(2)}) %collective-permute-start.18) | collective-permute-done | bytes 131104 | tf_op jit(solution)/shard_map/ppermute | solution.py:566
  (66 shorter events, 41.4 us)
Async XLA Ops:
  2.3 8.6 %collective-permute-start.1 = (f32[2,136,128]{2,1,0:T(8,128)S(1)}, f32[2,136,128]{2,1,0:T(8,128)S(1)}, u32[]{:S(2)}, u32[]{:S(2)}) collective-permute-start(f32[2,136,128]{2,1,0:T(8,128)S(1)} %get-tuple-element.69.refs_3_), channel_id=1, source_target_pairs={{0,1},{2,3},{4,5},{6,7},{8,9},{10,11},{12,13},{14,15},{1,0},{3,2},... | collective-permute-start | bytes 417800 | tf_op jit(solution)/shard_map/ppermute | solution.py:468
  3.1 12.5 %collective-permute-start = (f32[2,136,128]{2,1,0:T(8,128)S(1)}, f32[2,136,128]{2,1,0:T(8,128)S(1)}, u32[]{:S(2)}, u32[]{:S(2)}) collective-permute-start(f32[2,136,128]{2,1,0:T(8,128)S(1)} %get-tuple-element.69.refs_3_), channel_id=1, source_target_pairs={{1,2},{3,4},{5,6},{7,8},{9,10},{11,12},{13,14},{2,1},{4,3},{6,5},{... | collective-permute-start | bytes 417800 | tf_op jit(solution)/shard_map/ppermute | solution.py:469
  15.6 7.3 %collective-permute-start.3 = (f32[3,2,136,128]{3,2,1,0:T(8,128)S(1)}, f32[3,2,136,128]{3,2,1,0:T(8,128)S(1)}, u32[]{:S(2)}, u32[]{:S(2)}) collective-permute-start(f32[3,2,136,128]{3,2,1,0:T(8,128)S(1)} %pad_maximum_fusion), channel_id=1, source_target_pairs={{0,16},{32,48},{64,80},{96,112},{128,144},{160,176},{192,208},{224... | collective-permute-start | bytes 1253384 | tf_op jit(solution)/shard_map/ppermute | solution.py:471
  16.9 10.9 %collective-permute-start.2 = (f32[3,2,136,128]{3,2,1,0:T(8,128)S(1)}, f32[3,2,136,128]{3,2,1,0:T(8,128)S(1)}, u32[]{:S(2)}, u32[]{:S(2)}) collective-permute-start(f32[3,2,136,128]{3,2,1,0:T(8,128)S(1)} %pad_maximum_fusion), channel_id=1, source_target_pairs={{16,32},{48,64},{80,96},{112,128},{144,160},{176,192},{208,224},{3... | collective-permute-start | bytes 1253384 | tf_op jit(solution)/shard_map/ppermute | solution.py:472
  39.7 12.1 %collective-permute-start.4 = (f32[3,2,128,128]{3,2,1,0:T(8,128)}, f32[3,2,128,128]{3,2,1,0:T(8,128)}, u32[]{:S(2)}, u32[]{:S(2)}) collective-permute-start(f32[3,2,128,128]{3,2,1,0:T(8,128)} %get-tuple-element.30), channel_id=1, source_target_pairs={{0,16},{32,48},{64,80},{96,112},{128,144},{160,176},{192,208},{224... | collective-permute-start | bytes 1179656 | tf_op jit(solution)/shard_map/ppermute | solution.py:559
  39.8 14.4 %collective-permute-start.5 = (f32[3,2,128,128]{3,2,1,0:T(8,128)S(1)}, f32[3,2,128,128]{3,2,1,0:T(8,128)}, u32[]{:S(2)}, u32[]{:S(2)}) collective-permute-start(f32[3,2,128,128]{3,2,1,0:T(8,128)S(1)} %get-tuple-element.31), channel_id=1, source_target_pairs={{16,32},{48,64},{80,96},{112,128},{144,160},{176,192},{208,224},{3... | collective-permute-start | bytes 1179656 | tf_op jit(solution)/shard_map/ppermute | solution.py:560
  44.2 16.2 %all-to-all-start = ((f32[16,5,8,256]{3,2,1,0:T(8,128)}), f32[16,5,8,256]{3,2,1,0:T(8,128)S(1)}, u32[]{:S(2)}, u32[]{:S(2)}) async-start(f32[16,5,8,256]{3,2,1,0:T(8,128)} %add.109), calls=%async_computation | async-start | bytes 1310720 | tf_op jit(solution)/shard_map/all_to_all | solution.py:499
  61.1 22.2 %all-to-all-start.1 = ((f32[8,5,8,256]{3,2,1,0:T(8,128)}), f32[8,5,8,256]{3,2,1,0:T(8,128)S(1)}, u32[]{:S(2)}, u32[]{:S(2)}) async-start(f32[8,5,8,256]{3,2,1,0:T(8,128)} %spread.2), calls=%async_computation.1 | async-start | bytes 655360 | tf_op jit(solution)/shard_map/all_to_all | solution.py:499
  70.2 20.2 %collective-permute-start.7 = (f32[2,128,128]{2,1,0:T(8,128)S(1)}, f32[2,128,128]{2,1,0:T(8,128)S(1)}, u32[]{:S(2)}, u32[]{:S(2)}) collective-permute-start(f32[2,128,128]{2,1,0:T(8,128)S(1)} %get-tuple-element.40), channel_id=1, source_target_pairs={{0,1},{2,3},{4,5},{6,7},{8,9},{10,11},{12,13},{14,15},{1,0},{3,2},... | collective-permute-start | bytes 393224 | tf_op jit(solution)/shard_map/ppermute | solution.py:565
  71.8 18.6 %collective-permute-start.8 = (f32[2,128,128]{2,1,0:T(8,128)S(1)}, f32[2,128,128]{2,1,0:T(8,128)S(1)}, u32[]{:S(2)}, u32[]{:S(2)}) collective-permute-start(f32[2,128,128]{2,1,0:T(8,128)S(1)} %get-tuple-element.41), channel_id=1, source_target_pairs={{1,2},{3,4},{5,6},{7,8},{9,10},{11,12},{13,14},{2,1},{4,3},{6,5},{... | collective-permute-start | bytes 393224 | tf_op jit(solution)/shard_map/ppermute | solution.py:566
  84.2 14.8 %all-to-all-start.2 = ((f32[16,4,8,256]{3,2,1,0:T(8,128)}), f32[16,4,8,256]{3,2,1,0:T(8,128)S(1)}, u32[]{:S(2)}, u32[]{:S(2)}) async-start(f32[16,4,8,256]{3,2,1,0:T(8,128)} %get-tuple-element.42), calls=%async_computation.2 | async-start | bytes 1048576 | tf_op jit(solution)/shard_map/all_to_all | solution.py:499
  91.3 9.2 %collective-permute-start.11 = (f32[2,128,128]{2,1,0:T(8,128)S(1)}, f32[2,128,128]{2,1,0:T(8,128)S(1)}, u32[]{:S(2)}, u32[]{:S(2)}) collective-permute-start(f32[2,128,128]{2,1,0:T(8,128)S(1)} %divide_add_fusion.1.refs_4_), channel_id=1, source_target_pairs={{0,1},{2,3},{4,5},{6,7},{8,9},{10,11},{12,13},{14,15},{1,0},{3,2},... | collective-permute-start | bytes 393224 | tf_op jit(solution)/shard_map/ppermute | solution.py:468
  91.7 13.5 %collective-permute-start.10 = (f32[2,128,128]{2,1,0:T(8,128)S(1)}, f32[2,128,128]{2,1,0:T(8,128)S(1)}, u32[]{:S(2)}, u32[]{:S(2)}) collective-permute-start(f32[2,128,128]{2,1,0:T(8,128)S(1)} %divide_add_fusion.1.refs_4_), channel_id=1, source_target_pairs={{1,2},{3,4},{5,6},{7,8},{9,10},{11,12},{13,14},{2,1},{4,3},{6,5},{... | collective-permute-start | bytes 393224 | tf_op jit(solution)/shard_map/ppermute | solution.py:469
  99.0 18.0 %collective-permute-start.9 = (f32[16,4,8,256]{3,2,1,0:T(8,128)S(1)}, f32[16,4,8,256]{3,2,1,0:T(8,128)S(1)}, u32[]{:S(2)}, u32[]{:S(2)}) collective-permute-start(f32[16,4,8,256]{3,2,1,0:T(8,128)S(1)} %all-to-all-done.2.refs_0_), channel_id=1, source_target_pairs={{0,1},{1,0},{2,3},{3,2},{4,5},{5,4},{6,7},{7,6},{8,9},{9,8},{10,11... | collective-permute-start | bytes 1572872 | tf_op jit(solution)/shard_map/ppermute | solution.py:577
  105.2 7.1 %collective-permute-start.13 = (f32[3,2,128,128]{3,2,1,0:T(8,128)S(1)}, f32[3,2,128,128]{3,2,1,0:T(8,128)S(1)}, u32[]{:S(2)}, u32[]{:S(2)}) collective-permute-start(f32[3,2,128,128]{3,2,1,0:T(8,128)S(1)} %pad_maximum_fusion.1), channel_id=1, source_target_pairs={{0,16},{32,48},{64,80},{96,112},{128,144},{160,176},{192,208},{224... | collective-permute-start | bytes 1179656 | tf_op jit(solution)/shard_map/ppermute | solution.py:471
  106.4 10.6 %collective-permute-start.12 = (f32[3,2,128,128]{3,2,1,0:T(8,128)S(1)}, f32[3,2,128,128]{3,2,1,0:T(8,128)S(1)}, u32[]{:S(2)}, u32[]{:S(2)}) collective-permute-start(f32[3,2,128,128]{3,2,1,0:T(8,128)S(1)} %pad_maximum_fusion.1), channel_id=1, source_target_pairs={{16,32},{48,64},{80,96},{112,128},{144,160},{176,192},{208,224},{3... | collective-permute-start | bytes 1179656 | tf_op jit(solution)/shard_map/ppermute | solution.py:472
  128.1 3.7 %collective-permute-start.16 = (f32[16,5,8,256]{3,2,1,0:T(8,128)S(1)}, f32[16,5,8,256]{3,2,1,0:T(8,128)S(1)}, u32[]{:S(2)}, u32[]{:S(2)}) collective-permute-start(f32[16,5,8,256]{3,2,1,0:T(8,128)S(1)} %get-tuple-element.47), channel_id=1, source_target_pairs={{0,1},{1,0},{2,3},{3,2},{4,5},{5,4},{6,7},{7,6},{8,9},{9,8},{10,11... | collective-permute-start | bytes 1966088 | tf_op jit(solution)/shard_map/ppermute | solution.py:561
  128.4 10.9 %collective-permute-start.14 = (f32[3,2,128,128]{3,2,1,0:T(8,128)S(1)}, f32[3,2,128,128]{3,2,1,0:T(8,128)S(1)}, u32[]{:S(2)}, u32[]{:S(2)}) collective-permute-start(f32[3,2,128,128]{3,2,1,0:T(8,128)S(1)} %get-tuple-element.44), channel_id=1, source_target_pairs={{0,16},{32,48},{64,80},{96,112},{128,144},{160,176},{192,208},{224... | collective-permute-start | bytes 1179656 | tf_op jit(solution)/shard_map/ppermute | solution.py:559
  128.5 14.3 %collective-permute-start.15 = (f32[3,2,128,128]{3,2,1,0:T(8,128)S(1)}, f32[3,2,128,128]{3,2,1,0:T(8,128)S(1)}, u32[]{:S(2)}, u32[]{:S(2)}) collective-permute-start(f32[3,2,128,128]{3,2,1,0:T(8,128)S(1)} %get-tuple-element.45), channel_id=1, source_target_pairs={{16,32},{48,64},{80,96},{112,128},{144,160},{176,192},{208,224},{3... | collective-permute-start | bytes 1179656 | tf_op jit(solution)/shard_map/ppermute | solution.py:560
  132.7 17.8 %all-to-all-start.3 = ((f32[16,5,8,256]{3,2,1,0:T(8,128)}), f32[16,5,8,256]{3,2,1,0:T(8,128)S(1)}, u32[]{:S(2)}, u32[]{:S(2)}) async-start(f32[16,5,8,256]{3,2,1,0:T(8,128)} %add.129), calls=%async_computation.3 | async-start | bytes 1310720 | tf_op jit(solution)/shard_map/all_to_all | solution.py:499
  151.3 16.4 %all-to-all-start.4 = ((f32[8,5,8,256]{3,2,1,0:T(8,128)}), f32[8,5,8,256]{3,2,1,0:T(8,128)S(1)}, u32[]{:S(2)}, u32[]{:S(2)}) async-start(f32[8,5,8,256]{3,2,1,0:T(8,128)} %spread.3), calls=%async_computation.4 | async-start | bytes 655360 | tf_op jit(solution)/shard_map/all_to_all | solution.py:499
  168.6 19.8 %all-to-all-start.5 = ((f32[16,4,8,256]{3,2,1,0:T(8,128)}), f32[16,4,8,256]{3,2,1,0:T(8,128)S(1)}, u32[]{:S(2)}, u32[]{:S(2)}) async-start(f32[16,4,8,256]{3,2,1,0:T(8,128)} %get-tuple-element.54), calls=%async_computation.5 | async-start | bytes 1048576 | tf_op jit(solution)/shard_map/all_to_all | solution.py:499
  174.1 4.1 %collective-permute-start.17 = (f32[2,128,128]{2,1,0:T(8,128)S(1)}, f32[2,128,128]{2,1,0:T(8,128)S(1)}, u32[]{:S(2)}, u32[]{:S(2)}) collective-permute-start(f32[2,128,128]{2,1,0:T(8,128)S(1)} %get-tuple-element.49), channel_id=1, source_target_pairs={{0,1},{2,3},{4,5},{6,7},{8,9},{10,11},{12,13},{14,15},{1,0},{3,2},... | collective-permute-start | bytes 393224 | tf_op jit(solution)/shard_map/ppermute | solution.py:565
  175.1 13.3 %collective-permute-start.18 = (f32[2,128,128]{2,1,0:T(8,128)S(1)}, f32[2,128,128]{2,1,0:T(8,128)S(1)}, u32[]{:S(2)}, u32[]{:S(2)}) collective-permute-start(f32[2,128,128]{2,1,0:T(8,128)S(1)} %get-tuple-element.50), channel_id=1, source_target_pairs={{1,2},{3,4},{5,6},{7,8},{9,10},{11,12},{13,14},{2,1},{4,3},{6,5},{... | collective-permute-start | bytes 393224 | tf_op jit(solution)/shard_map/ppermute | solution.py:566
  (5 other events, 30.9 us)

commit v8 on v7

--- a/solution.py
+++ b/solution.py
@@ -217,7 +217,7 @@
             )
         return carry
 
-    lax.fori_loop(0, 4, forward, 0)
+    lax.fori_loop(0, 4, forward, 0, unroll=4)
 
     def scale(index, carry):
         scan, other = index // 2, index % 2
@@ -315,7 +315,7 @@
         for slot in range(CHUNK // 8):
             sums[piece * (CHUNK // 8) + slot, 4] = weight[slot * 8 : slot * 8 + 8]
 
-    lax.fori_loop(0, 4, backward, 0)
+    lax.fori_loop(0, 4, backward, 0, unroll=4)
 
     def scatter(scan, carry):
         row, column = offsets_ref[0, 0, scan, 0] + HALF, offsets_ref[0, 0, scan, 1] + HALF
@@ -556,16 +556,17 @@
         mine, other, second, middle, first, power = step(
             offsets, parity, table, parts, measured, around
         )
-        first = lax.ppermute(first, "row", pairs(0))
-        second = lax.ppermute(second, "row", pairs(1))
         mine = mine + lax.ppermute(other, "col", SWAP)
-        pieces = exchange(mine, PLANES)
+        first = lax.ppermute(after(first, mine), "row", pairs(0))
+        second = lax.ppermute(after(second, mine), "row", pairs(1))
+        pieces = spread(exchange(mine, PLANES))
+        middle = after(middle, pieces)
         outer, own, inner = (middle[i] + first[i] + second[i] for i in range(3))
-        pieces = spread(after(pieces, (outer, own, inner)))
-        inner = lax.ppermute(after(inner, pieces), "col", pairs(0))
-        outer = lax.ppermute(after(outer, pieces), "col", pairs(1))
+        folds = (outer, own, inner)
+        inner = lax.ppermute(inner, "col", pairs(0))
+        outer = lax.ppermute(outer, "col", pairs(1))
         weight = weigh(parity, near, after(power, pieces))
-        pieces = after(exchange(pieces, LINES), weight)
+        pieces = after(exchange(pieces, LINES), (weight, folds))
         pieces, old = update(pieces, old)
         totals = after(own, old) + inner + outer
         tile = tile + OBJECT_STEP * totals / (weight + OBJECT_REG)

time: 193 us -> 185 us (0.959)
  Pallas kernels: 34.6 us -> 31.1 us
  waiting for transfers between devices: 66.4 us -> 63 us
  starting transfers between devices: 82.4 us -> 79.5 us
    all_to_all x6, starting transfers between devices: 38.3 us -> 32 us  [exchange(): lax.all_to_all(value, BOTH, 0, 0, axis_index_groups=groups, tiled=True)]
    ppermute x8, waiting for transfers between devices: 16.2 us -> 10.2 us  [the longest x2 10.2 us: local(): outer = lax.ppermute(outer, 'col', pairs(1))]
    ppermute x2, waiting for transfers between devices: 0.01 us -> 4.18 us  [local(): mine = mine + lax.ppermute(other, 'col', SWAP)]
    pallas_call x2, Pallas kernels: 22.9 us -> 19.4 us  [step(): pl.pallas_call(functools.partial(step_kernel, halves), out_shape=[half, h...]
  transfers between devices with their start and end apart: 26 -> 26, of which waited for: 14 -> 14; matrix products, arithmetic and copies ran while one was open for 3% -> 2% of each run, Pallas kernels for 4% -> 5%
where the time goes in v8:
time: 185 us; the launch traced here: 184 us
  starting transfers between devices  79.5 us (43%)
  waiting for transfers between devices  63 us (34%)
  Pallas kernels  31.1 us (17%)
  other arithmetic  6.71 us (4%)
  local copies, waits for them, and re-layouts  2.61 us (1%)
    all_to_all x6, starting transfers between devices, exchange(): lax.all_to_all(value, BOTH, 0, 0, axis_index_groups=groups, tiled=True)  32 us
    all_to_all x6, waiting for transfers between devices, exchange(): lax.all_to_all(value, BOTH, 0, 0, axis_index_groups=groups, tiled=True)  24.4 us
    pallas_call x2, Pallas kernels, step(): pl.pallas_call(functools.partial(step_kernel, halves), out_shape=[half, h...  19.4 us
    ppermute x2, starting transfers between devices, neighbourhood(): outer = lax.ppermute(tile, 'col', pairs(1))  12.5 us
    ppermute x2, starting transfers between devices, local(): outer = lax.ppermute(outer, 'col', pairs(1))  10.2 us
    ppermute x2, waiting for transfers between devices, local(): outer = lax.ppermute(outer, 'col', pairs(1))  10.2 us
    ppermute x2, waiting for transfers between devices, neighbourhood(): second = lax.ppermute(band, 'row', pairs(1))  9.68 us
    ppermute x2, waiting for transfers between devices, neighbourhood(): outer = lax.ppermute(tile, 'col', pairs(1))  9.2 us
  transfers between devices with their start and end apart: 26, of which 14 were waited for; matrix products, arithmetic and copies ran while one was open for 2% of the time, Pallas kernels for 5%

profile of v8, /device:TPU:39, one launch (start us, length us, event | category | flops | bytes accessed | tf_op | source)
XLA Modules:
  0.0 183.9 jit_solution(256762929583437331)
XLA Ops:
  3.1 7.9 %collective-permute-start = (f32[2,136,128]{2,1,0:T(8,128)S(1)}, f32[2,136,128]{2,1,0:T(8,128)S(1)}, u32[]{:S(2)}, u32[]{:S(2)}) collective-permute-start(f32[2,136,128]{2,1,0:T(8,128)S(1)} %get-tuple-element.69.refs_3_), channel_id=1, source_target_pairs={{1,2},{3,4},{5,6},{7,8},{9,10},{11,12},{13,14},{2,1},{4,3},{6,5},{... | collective-permute-start | bytes 417800 | tf_op jit(solution)/shard_map/ppermute | solution.py:469
  11.0 4.6 %collective-permute-done.refs_2_ = f32[2,136,128]{2,1,0:T(8,128)S(1)} collective-permute-done((f32[2,136,128]{2,1,0:T(8,128)S(1)}, f32[2,136,128]{2,1,0:T(8,128)S(1)}, u32[]{:S(2)}, u32[]{:S(2)}) %collective-permute-start) | collective-permute-done | bytes 139296 | tf_op jit(solution)/shard_map/ppermute | solution.py:469
  16.9 3.4 %collective-permute-start.2 = (f32[3,2,136,128]{3,2,1,0:T(8,128)S(1)}, f32[3,2,136,128]{3,2,1,0:T(8,128)S(1)}, u32[]{:S(2)}, u32[]{:S(2)}) collective-permute-start(f32[3,2,136,128]{3,2,1,0:T(8,128)S(1)} %pad_maximum_fusion), channel_id=1, source_target_pairs={{16,32},{48,64},{80,96},{112,128},{144,160},{176,192},{208,224},{3... | collective-permute-start | bytes 1253384 | tf_op jit(solution)/shard_map/ppermute | solution.py:472
  22.9 4.9 %collective-permute-done.2.refs_5_ = f32[3,2,136,128]{3,2,1,0:T(8,128)S(1)} collective-permute-done((f32[3,2,136,128]{3,2,1,0:T(8,128)S(1)}, f32[3,2,136,128]{3,2,1,0:T(8,128)S(1)}, u32[]{:S(2)}, u32[]{:S(2)}) %collective-permute-start.2) | collective-permute-done | bytes 417824 | tf_op jit(solution)/shard_map/ppermute | solution.py:472
  27.8 9.8 %step.2 = (f32[16,5,8,256]{3,2,1,0:T(8,128)S(1)}, f32[16,5,8,256]{3,2,1,0:T(8,128)S(1)}, f32[3,2,128,128]{3,2,1,0:T(8,128)S(1)}, f32[3,2,128,128]{3,2,1,0:T(8,12...) custom-call(s32[1,1,2,2]{3,2,1,0:T(2,128)S(1)} %copy-done.1, s32[2]{0:T(128)S(1)} %pad_add_fusion.parity_ref, ...), custom_call_target="tpu_custom_call" | custom-call | tf_op jit(solution)/shard_map/step/pallas_call | solution.py:437
  41.4 5.6 %all-to-all-start = ((f32[16,5,8,256]{3,2,1,0:T(8,128)}), f32[16,5,8,256]{3,2,1,0:T(8,128)S(1)}, u32[]{:S(2)}, u32[]{:S(2)}) async-start(f32[16,5,8,256]{3,2,1,0:T(8,128)} %add.106), calls=%async_computation | async-start | bytes 1310720 | tf_op jit(solution)/shard_map/all_to_all | solution.py:499
  49.0 3.3 %collective-permute-start.6 = (f32[3,2,128,128]{3,2,1,0:T(8,128)S(1)}, f32[3,2,128,128]{3,2,1,0:T(8,128)}, u32[]{:S(2)}, u32[]{:S(2)}) collective-permute-start(f32[3,2,128,128]{3,2,1,0:T(8,128)S(1)} %get-tuple-element.36), channel_id=1, source_target_pairs={{16,32},{48,64},{80,96},{112,128},{144,160},{176,192},{208,224},{3... | collective-permute-start | bytes 1179656 | tf_op jit(solution)/shard_map/ppermute | solution.py:561
  52.3 6.5 %all-to-all-done.pieces_ref = f32[16,5,8,256]{3,2,1,0:T(8,128)S(1)} async-done(((f32[16,5,8,256]{3,2,1,0:T(8,128)}), f32[16,5,8,256]{3,2,1,0:T(8,128)S(1)}, u32[]{:S(2)}, u32[]{:S(2)}) %all-to-all-start) | async-done | bytes 655392 | tf_op jit(solution)/shard_map/all_to_all | solution.py:499
  59.6 8.4 %all-to-all-start.1 = ((f32[8,5,8,256]{3,2,1,0:T(8,128)}), f32[8,5,8,256]{3,2,1,0:T(8,128)S(1)}, u32[]{:S(2)}, u32[]{:S(2)}) async-start(f32[8,5,8,256]{3,2,1,0:T(8,128)} %spread.2), calls=%async_computation.1 | async-start | bytes 655360 | tf_op jit(solution)/shard_map/all_to_all | solution.py:499
  71.4 7.3 %collective-permute-start.8 = (f32[2,128,128]{2,1,0:T(8,128)S(1)}, f32[2,128,128]{2,1,0:T(8,128)S(1)}, u32[]{:S(2)}, u32[]{:S(2)}) collective-permute-start(f32[2,128,128]{2,1,0:T(8,128)S(1)} %get-tuple-element.60), channel_id=1, source_target_pairs={{1,2},{3,4},{5,6},{7,8},{9,10},{11,12},{13,14},{2,1},{4,3},{6,5},{... | collective-permute-start | bytes 393224 | tf_op jit(solution)/shard_map/ppermute | solution.py:567
  78.8 3.0 %weigh.2 = f32[128,128]{1,0:T(8,128)S(1)} custom-call(s32[2]{0:T(128)S(1)} %pad_add_fusion.parity_ref, s32[9,4]{1,0:T(8,128)S(1)} %convert_element_type.9.near_ref, f32[256,256]{1,0:T(8,128)S(1)} %get-tuple-element.38.power_ref), custom_call_target="tpu_custom_call" | custom-call | tf_op jit(solution)/shard_map/weigh/pallas_call | solution.py:503
  82.7 4.0 %all-to-all-start.2 = ((f32[16,4,8,256]{3,2,1,0:T(8,128)}), f32[16,4,8,256]{3,2,1,0:T(8,128)S(1)}, u32[]{:S(2)}, u32[]{:S(2)}) async-start(f32[16,4,8,256]{3,2,1,0:T(8,128)} %get-tuple-element.42), calls=%async_computation.2 | async-start | bytes 1048576 | tf_op jit(solution)/shard_map/all_to_all | solution.py:499
  88.0 4.7 %collective-permute-start.10 = (f32[2,128,128]{2,1,0:T(8,128)S(1)}, f32[2,128,128]{2,1,0:T(8,128)S(1)}, u32[]{:S(2)}, u32[]{:S(2)}) collective-permute-start(f32[2,128,128]{2,1,0:T(8,128)S(1)} %divide_add_fusion.1.refs_4_), channel_id=1, source_target_pairs={{1,2},{3,4},{5,6},{7,8},{9,10},{11,12},{13,14},{2,1},{4,3},{6,5},{... | collective-permute-start | bytes 393224 | tf_op jit(solution)/shard_map/ppermute | solution.py:469
  96.8 4.6 %collective-permute-done.10.refs_3_ = f32[2,128,128]{2,1,0:T(8,128)S(1)} collective-permute-done((f32[2,128,128]{2,1,0:T(8,128)S(1)}, f32[2,128,128]{2,1,0:T(8,128)S(1)}, u32[]{:S(2)}, u32[]{:S(2)}) %collective-permute-start.10) | collective-permute-done | bytes 131104 | tf_op jit(solution)/shard_map/ppermute | solution.py:469
  102.9 3.3 %collective-permute-start.12 = (f32[3,2,128,128]{3,2,1,0:T(8,128)S(1)}, f32[3,2,128,128]{3,2,1,0:T(8,128)S(1)}, u32[]{:S(2)}, u32[]{:S(2)}) collective-permute-start(f32[3,2,128,128]{3,2,1,0:T(8,128)S(1)} %pad_maximum_fusion.1), channel_id=1, source_target_pairs={{16,32},{48,64},{80,96},{112,128},{144,160},{176,192},{208,224},{3... | collective-permute-start | bytes 1179656 | tf_op jit(solution)/shard_map/ppermute | solution.py:472
  108.7 4.8 %collective-permute-done.12.refs_6_ = f32[3,2,128,128]{3,2,1,0:T(8,128)S(1)} collective-permute-done((f32[3,2,128,128]{3,2,1,0:T(8,128)S(1)}, f32[3,2,128,128]{3,2,1,0:T(8,128)S(1)}, u32[]{:S(2)}, u32[]{:S(2)}) %collective-permute-start.12) | collective-permute-done | bytes 393248 | tf_op jit(solution)/shard_map/ppermute | solution.py:472
  113.5 9.6 %step.3 = (f32[16,5,8,256]{3,2,1,0:T(8,128)S(1)}, f32[16,5,8,256]{3,2,1,0:T(8,128)S(1)}, f32[3,2,128,128]{3,2,1,0:T(8,128)S(1)}, f32[3,2,128,128]{3,2,1,0:T(8,12...) custom-call(s32[1,1,2,2]{3,2,1,0:T(2,128)S(1)} %copy-done.1, s32[2]{0:T(128)S(1)} %pad_add_fusion.parity_ref, ...), custom_call_target="tpu_custom_call" | custom-call | tf_op jit(solution)/shard_map/step/pallas_call | solution.py:437
  126.2 5.5 %all-to-all-start.3 = ((f32[16,5,8,256]{3,2,1,0:T(8,128)}), f32[16,5,8,256]{3,2,1,0:T(8,128)S(1)}, u32[]{:S(2)}, u32[]{:S(2)}) async-start(f32[16,5,8,256]{3,2,1,0:T(8,128)} %add.123), calls=%async_computation.3 | async-start | bytes 1310720 | tf_op jit(solution)/shard_map/all_to_all | solution.py:499
  132.9 3.3 %collective-permute-start.16 = (f32[3,2,128,128]{3,2,1,0:T(8,128)S(1)}, f32[3,2,128,128]{3,2,1,0:T(8,128)}, u32[]{:S(2)}, u32[]{:S(2)}) collective-permute-start(f32[3,2,128,128]{3,2,1,0:T(8,128)S(1)} %get-tuple-element.50), channel_id=1, source_target_pairs={{16,32},{48,64},{80,96},{112,128},{144,160},{176,192},{208,224},{3... | collective-permute-start | bytes 1179656 | tf_op jit(solution)/shard_map/ppermute | solution.py:561
  136.2 7.9 %all-to-all-done.3.pieces_ref = f32[16,5,8,256]{3,2,1,0:T(8,128)S(1)} async-done(((f32[16,5,8,256]{3,2,1,0:T(8,128)}), f32[16,5,8,256]{3,2,1,0:T(8,128)S(1)}, u32[]{:S(2)}, u32[]{:S(2)}) %all-to-all-start.3) | async-done | bytes 655392 | tf_op jit(solution)/shard_map/all_to_all | solution.py:499
  144.9 3.5 %all-to-all-start.4 = ((f32[8,5,8,256]{3,2,1,0:T(8,128)}), f32[8,5,8,256]{3,2,1,0:T(8,128)S(1)}, u32[]{:S(2)}, u32[]{:S(2)}) async-start(f32[8,5,8,256]{3,2,1,0:T(8,128)} %spread.3), calls=%async_computation.4 | async-start | bytes 655360 | tf_op jit(solution)/shard_map/all_to_all | solution.py:499
  152.5 7.5 %all-to-all-done.4.pieces_ref = f32[8,5,8,256]{3,2,1,0:T(8,128)S(1)} async-done(((f32[8,5,8,256]{3,2,1,0:T(8,128)}), f32[8,5,8,256]{3,2,1,0:T(8,128)S(1)}, u32[]{:S(2)}, u32[]{:S(2)}) %all-to-all-start.4) | async-done | bytes 327712 | tf_op jit(solution)/shard_map/all_to_all | solution.py:499
  160.9 5.2 %all-to-all-start.5 = ((f32[16,4,8,256]{3,2,1,0:T(8,128)}), f32[16,4,8,256]{3,2,1,0:T(8,128)S(1)}, u32[]{:S(2)}, u32[]{:S(2)}) async-start(f32[16,4,8,256]{3,2,1,0:T(8,128)} %get-tuple-element.54), calls=%async_computation.5 | async-start | bytes 1048576 | tf_op jit(solution)/shard_map/all_to_all | solution.py:499
  170.2 10.2 %collective-permute-done.18 = f32[2,128,128]{2,1,0:T(8,128)S(1)} collective-permute-done((f32[2,128,128]{2,1,0:T(8,128)S(1)}, f32[2,128,128]{2,1,0:T(8,128)S(1)}, u32[]{:S(2)}, u32[]{:S(2)}) %collective-permute-start.18) | collective-permute-done | bytes 131104 | tf_op jit(solution)/shard_map/ppermute | solution.py:567
  (68 shorter events, 44.4 us)
Async XLA Ops:
  2.3 8.6 %collective-permute-start.1 = (f32[2,136,128]{2,1,0:T(8,128)S(1)}, f32[2,136,128]{2,1,0:T(8,128)S(1)}, u32[]{:S(2)}, u32[]{:S(2)}) collective-permute-start(f32[2,136,128]{2,1,0:T(8,128)S(1)} %get-tuple-element.69.refs_3_), channel_id=1, source_target_pairs={{0,1},{2,3},{4,5},{6,7},{8,9},{10,11},{12,13},{14,15},{1,0},{3,2},... | collective-permute-start | bytes 417800 | tf_op jit(solution)/shard_map/ppermute | solution.py:468
  3.1 12.5 %collective-permute-start = (f32[2,136,128]{2,1,0:T(8,128)S(1)}, f32[2,136,128]{2,1,0:T(8,128)S(1)}, u32[]{:S(2)}, u32[]{:S(2)}) collective-permute-start(f32[2,136,128]{2,1,0:T(8,128)S(1)} %get-tuple-element.69.refs_3_), channel_id=1, source_target_pairs={{1,2},{3,4},{5,6},{7,8},{9,10},{11,12},{13,14},{2,1},{4,3},{6,5},{... | collective-permute-start | bytes 417800 | tf_op jit(solution)/shard_map/ppermute | solution.py:469
  15.6 7.3 %collective-permute-start.3 = (f32[3,2,136,128]{3,2,1,0:T(8,128)S(1)}, f32[3,2,136,128]{3,2,1,0:T(8,128)S(1)}, u32[]{:S(2)}, u32[]{:S(2)}) collective-permute-start(f32[3,2,136,128]{3,2,1,0:T(8,128)S(1)} %pad_maximum_fusion), channel_id=1, source_target_pairs={{0,16},{32,48},{64,80},{96,112},{128,144},{160,176},{192,208},{224... | collective-permute-start | bytes 1253384 | tf_op jit(solution)/shard_map/ppermute | solution.py:471
  16.9 10.9 %collective-permute-start.2 = (f32[3,2,136,128]{3,2,1,0:T(8,128)S(1)}, f32[3,2,136,128]{3,2,1,0:T(8,128)S(1)}, u32[]{:S(2)}, u32[]{:S(2)}) collective-permute-start(f32[3,2,136,128]{3,2,1,0:T(8,128)S(1)} %pad_maximum_fusion), channel_id=1, source_target_pairs={{16,32},{48,64},{80,96},{112,128},{144,160},{176,192},{208,224},{3... | collective-permute-start | bytes 1253384 | tf_op jit(solution)/shard_map/ppermute | solution.py:472
  41.4 17.4 %all-to-all-start = ((f32[16,5,8,256]{3,2,1,0:T(8,128)}), f32[16,5,8,256]{3,2,1,0:T(8,128)S(1)}, u32[]{:S(2)}, u32[]{:S(2)}) async-start(f32[16,5,8,256]{3,2,1,0:T(8,128)} %add.106), calls=%async_computation | async-start | bytes 1310720 | tf_op jit(solution)/shard_map/all_to_all | solution.py:499
  47.8 20.2 %collective-permute-start.5 = (f32[3,2,128,128]{3,2,1,0:T(8,128)}, f32[3,2,128,128]{3,2,1,0:T(8,128)}, u32[]{:S(2)}, u32[]{:S(2)}) collective-permute-start(f32[3,2,128,128]{3,2,1,0:T(8,128)} %copy-done.2), channel_id=1, source_target_pairs={{0,16},{32,48},{64,80},{96,112},{128,144},{160,176},{192,208},{224... | collective-permute-start | bytes 1179656 | tf_op jit(solution)/shard_map/ppermute | solution.py:560
  49.0 19.0 %collective-permute-start.6 = (f32[3,2,128,128]{3,2,1,0:T(8,128)S(1)}, f32[3,2,128,128]{3,2,1,0:T(8,128)}, u32[]{:S(2)}, u32[]{:S(2)}) collective-permute-start(f32[3,2,128,128]{3,2,1,0:T(8,128)S(1)} %get-tuple-element.36), channel_id=1, source_target_pairs={{16,32},{48,64},{80,96},{112,128},{144,160},{176,192},{208,224},{3... | collective-permute-start | bytes 1179656 | tf_op jit(solution)/shard_map/ppermute | solution.py:561
  59.6 22.2 %all-to-all-start.1 = ((f32[8,5,8,256]{3,2,1,0:T(8,128)}), f32[8,5,8,256]{3,2,1,0:T(8,128)S(1)}, u32[]{:S(2)}, u32[]{:S(2)}) async-start(f32[8,5,8,256]{3,2,1,0:T(8,128)} %spread.2), calls=%async_computation.1 | async-start | bytes 655360 | tf_op jit(solution)/shard_map/all_to_all | solution.py:499
  69.3 17.3 %collective-permute-start.7 = (f32[2,128,128]{2,1,0:T(8,128)S(1)}, f32[2,128,128]{2,1,0:T(8,128)S(1)}, u32[]{:S(2)}, u32[]{:S(2)}) collective-permute-start(f32[2,128,128]{2,1,0:T(8,128)S(1)} %get-tuple-element.59), channel_id=1, source_target_pairs={{0,1},{2,3},{4,5},{6,7},{8,9},{10,11},{12,13},{14,15},{1,0},{3,2},... | collective-permute-start | bytes 393224 | tf_op jit(solution)/shard_map/ppermute | solution.py:566
  71.4 15.2 %collective-permute-start.8 = (f32[2,128,128]{2,1,0:T(8,128)S(1)}, f32[2,128,128]{2,1,0:T(8,128)S(1)}, u32[]{:S(2)}, u32[]{:S(2)}) collective-permute-start(f32[2,128,128]{2,1,0:T(8,128)S(1)} %get-tuple-element.60), channel_id=1, source_target_pairs={{1,2},{3,4},{5,6},{7,8},{9,10},{11,12},{13,14},{2,1},{4,3},{6,5},{... | collective-permute-start | bytes 393224 | tf_op jit(solution)/shard_map/ppermute | solution.py:567
  82.7 12.4 %all-to-all-start.2 = ((f32[16,4,8,256]{3,2,1,0:T(8,128)}), f32[16,4,8,256]{3,2,1,0:T(8,128)S(1)}, u32[]{:S(2)}, u32[]{:S(2)}) async-start(f32[16,4,8,256]{3,2,1,0:T(8,128)} %get-tuple-element.42), calls=%async_computation.2 | async-start | bytes 1048576 | tf_op jit(solution)/shard_map/all_to_all | solution.py:499
  87.6 9.2 %collective-permute-start.11 = (f32[2,128,128]{2,1,0:T(8,128)S(1)}, f32[2,128,128]{2,1,0:T(8,128)S(1)}, u32[]{:S(2)}, u32[]{:S(2)}) collective-permute-start(f32[2,128,128]{2,1,0:T(8,128)S(1)} %divide_add_fusion.1.refs_4_), channel_id=1, source_target_pairs={{0,1},{2,3},{4,5},{6,7},{8,9},{10,11},{12,13},{14,15},{1,0},{3,2},... | collective-permute-start | bytes 393224 | tf_op jit(solution)/shard_map/ppermute | solution.py:468
  88.0 13.4 %collective-permute-start.10 = (f32[2,128,128]{2,1,0:T(8,128)S(1)}, f32[2,128,128]{2,1,0:T(8,128)S(1)}, u32[]{:S(2)}, u32[]{:S(2)}) collective-permute-start(f32[2,128,128]{2,1,0:T(8,128)S(1)} %divide_add_fusion.1.refs_4_), channel_id=1, source_target_pairs={{1,2},{3,4},{5,6},{7,8},{9,10},{11,12},{13,14},{2,1},{4,3},{6,5},{... | collective-permute-start | bytes 393224 | tf_op jit(solution)/shard_map/ppermute | solution.py:469
  95.0 18.4 %collective-permute-start.9 = (f32[16,4,8,256]{3,2,1,0:T(8,128)S(1)}, f32[16,4,8,256]{3,2,1,0:T(8,128)S(1)}, u32[]{:S(2)}, u32[]{:S(2)}) collective-permute-start(f32[16,4,8,256]{3,2,1,0:T(8,128)S(1)} %all-to-all-done.2.refs_0_), channel_id=1, source_target_pairs={{0,1},{1,0},{2,3},{3,2},{4,5},{5,4},{6,7},{7,6},{8,9},{9,8},{10,11... | collective-permute-start | bytes 1572872 | tf_op jit(solution)/shard_map/ppermute | solution.py:578
  101.4 7.3 %collective-permute-start.13 = (f32[3,2,128,128]{3,2,1,0:T(8,128)S(1)}, f32[3,2,128,128]{3,2,1,0:T(8,128)S(1)}, u32[]{:S(2)}, u32[]{:S(2)}) collective-permute-start(f32[3,2,128,128]{3,2,1,0:T(8,128)S(1)} %pad_maximum_fusion.1), channel_id=1, source_target_pairs={{0,16},{32,48},{64,80},{96,112},{128,144},{160,176},{192,208},{224... | collective-permute-start | bytes 1179656 | tf_op jit(solution)/shard_map/ppermute | solution.py:471
  102.9 10.6 %collective-permute-start.12 = (f32[3,2,128,128]{3,2,1,0:T(8,128)S(1)}, f32[3,2,128,128]{3,2,1,0:T(8,128)S(1)}, u32[]{:S(2)}, u32[]{:S(2)}) collective-permute-start(f32[3,2,128,128]{3,2,1,0:T(8,128)S(1)} %pad_maximum_fusion.1), channel_id=1, source_target_pairs={{16,32},{48,64},{80,96},{112,128},{144,160},{176,192},{208,224},{3... | collective-permute-start | bytes 1179656 | tf_op jit(solution)/shard_map/ppermute | solution.py:472
  123.1 2.2 %collective-permute-start.14 = (f32[16,5,8,256]{3,2,1,0:T(8,128)S(1)}, f32[16,5,8,256]{3,2,1,0:T(8,128)S(1)}, u32[]{:S(2)}, u32[]{:S(2)}) collective-permute-start(f32[16,5,8,256]{3,2,1,0:T(8,128)S(1)} %get-tuple-element.45), channel_id=1, source_target_pairs={{0,1},{1,0},{2,3},{3,2},{4,5},{5,4},{6,7},{7,6},{8,9},{9,8},{10,11... | collective-permute-start | bytes 1966088 | tf_op jit(solution)/shard_map/ppermute | solution.py:559
  126.2 17.9 %all-to-all-start.3 = ((f32[16,5,8,256]{3,2,1,0:T(8,128)}), f32[16,5,8,256]{3,2,1,0:T(8,128)S(1)}, u32[]{:S(2)}, u32[]{:S(2)}) async-start(f32[16,5,8,256]{3,2,1,0:T(8,128)} %add.123), calls=%async_computation.3 | async-start | bytes 1310720 | tf_op jit(solution)/shard_map/all_to_all | solution.py:499
  131.7 19.6 %collective-permute-start.15 = (f32[3,2,128,128]{3,2,1,0:T(8,128)S(1)}, f32[3,2,128,128]{3,2,1,0:T(8,128)S(1)}, u32[]{:S(2)}, u32[]{:S(2)}) collective-permute-start(f32[3,2,128,128]{3,2,1,0:T(8,128)S(1)} %get-tuple-element.48), channel_id=1, source_target_pairs={{0,16},{32,48},{64,80},{96,112},{128,144},{160,176},{192,208},{224... | collective-permute-start | bytes 1179656 | tf_op jit(solution)/shard_map/ppermute | solution.py:560
  132.9 18.5 %collective-permute-start.16 = (f32[3,2,128,128]{3,2,1,0:T(8,128)S(1)}, f32[3,2,128,128]{3,2,1,0:T(8,128)}, u32[]{:S(2)}, u32[]{:S(2)}) collective-permute-start(f32[3,2,128,128]{3,2,1,0:T(8,128)S(1)} %get-tuple-element.50), channel_id=1, source_target_pairs={{16,32},{48,64},{80,96},{112,128},{144,160},{176,192},{208,224},{3... | collective-permute-start | bytes 1179656 | tf_op jit(solution)/shard_map/ppermute | solution.py:561
  144.9 15.1 %all-to-all-start.4 = ((f32[8,5,8,256]{3,2,1,0:T(8,128)}), f32[8,5,8,256]{3,2,1,0:T(8,128)S(1)}, u32[]{:S(2)}, u32[]{:S(2)}) async-start(f32[8,5,8,256]{3,2,1,0:T(8,128)} %spread.3), calls=%async_computation.4 | async-start | bytes 655360 | tf_op jit(solution)/shard_map/all_to_all | solution.py:499
  160.9 19.5 %all-to-all-start.5 = ((f32[16,4,8,256]{3,2,1,0:T(8,128)}), f32[16,4,8,256]{3,2,1,0:T(8,128)S(1)}, u32[]{:S(2)}, u32[]{:S(2)}) async-start(f32[16,4,8,256]{3,2,1,0:T(8,128)} %get-tuple-element.54), calls=%async_computation.5 | async-start | bytes 1048576 | tf_op jit(solution)/shard_map/all_to_all | solution.py:499
  166.1 4.1 %collective-permute-start.17 = (f32[2,128,128]{2,1,0:T(8,128)S(1)}, f32[2,128,128]{2,1,0:T(8,128)S(1)}, u32[]{:S(2)}, u32[]{:S(2)}) collective-permute-start(f32[2,128,128]{2,1,0:T(8,128)S(1)} %get-tuple-element.56), channel_id=1, source_target_pairs={{0,1},{2,3},{4,5},{6,7},{8,9},{10,11},{12,13},{14,15},{1,0},{3,2},... | collective-permute-start | bytes 393224 | tf_op jit(solution)/shard_map/ppermute | solution.py:566
  167.2 13.1 %collective-permute-start.18 = (f32[2,128,128]{2,1,0:T(8,128)S(1)}, f32[2,128,128]{2,1,0:T(8,128)S(1)}, u32[]{:S(2)}, u32[]{:S(2)}) collective-permute-start(f32[2,128,128]{2,1,0:T(8,128)S(1)} %get-tuple-element.57), channel_id=1, source_target_pairs={{1,2},{3,4},{5,6},{7,8},{9,10},{11,12},{13,14},{2,1},{4,3},{6,5},{... | collective-permute-start | bytes 393224 | tf_op jit(solution)/shard_map/ppermute | solution.py:567
  (6 other events, 30.2 us)

commit v9 on v8

--- a/solution.py
+++ b/solution.py
@@ -77,11 +77,28 @@
         out_ref[scan, 1] = turned[HALF:]
 
 
-def lay_out_kernel(parity_ref, mine_ref, other_ref, out_ref):
-    for half, ref in enumerate((mine_ref, other_ref)):
-        place = parity_ref[1] if half == 0 else 1 - parity_ref[1]
-        for part in range(4):
-            out_ref[part, pl.ds(place * GROUPS, GROUPS)] = ref[:, part]
+def lay_out_kernel(whose, parity_ref, half_ref, *refs):
+    out_ref, semaphores = refs[-2:]
+    place = parity_ref[1] if whose == 0 else 1 - parity_ref[1]
+    copies = []
+    for part in range(4):
+        target = out_ref.at[part, pl.ds(place * GROUPS, GROUPS)]
+        copies.append(pltpu.make_async_copy(half_ref.at[:, part], target, semaphores.at[part]))
+        copies[-1].start()
+    for copy in copies:
+        copy.wait()
+
+
+def mark_kernel(offsets_ref, tile_ref, out_ref):
+    out_ref[:, :TILE, :] = tile_ref[...]
+    lane = lax.broadcasted_iota(jnp.int32, (8, TILE), 1)
+    values = jnp.zeros((8, TILE), jnp.int32)
+    for scan in range(2):
+        for axis in range(2):
+            value = offsets_ref[0, 0, scan, axis] + SHIFT
+            values = jnp.where(lane == 2 * scan + axis, value, values)
+    out_ref[0, TILE:, :] = values.astype(F32)
+    out_ref[1, TILE:, :] = jnp.zeros((8, TILE), F32)
 
 
 def step_kernel(halves, offsets_ref, parity_ref, table_in, *refs):
@@ -517,6 +534,29 @@
     return jnp.stack([value for row in rows for value in row]).astype(jnp.int32)
 
 
+def mark(offsets, tile):
+    return pl.pallas_call(
+        mark_kernel,
+        out_shape=jax.ShapeDtypeStruct((2, TILE + 8, TILE), F32),
+        in_specs=[SMEM_SPEC, pl.BlockSpec()],
+        compiler_params=params(4),
+        name="mark",
+    )(offsets, tile)
+
+
+def lay_out(whose, parity, half, into=None):
+    return pl.pallas_call(
+        functools.partial(lay_out_kernel, whose),
+        out_shape=jax.ShapeDtypeStruct((4, 2 * GROUPS, 8, SIDE), F32),
+        in_specs=[SMEM_SPEC] + [ANY_SPEC] * (1 + whose),
+        out_specs=ANY_SPEC,
+        scratch_shapes=[pltpu.SemaphoreType.DMA((4,))],
+        input_output_aliases={2: 0} if whose else {},
+        compiler_params=params(4),
+        name="lay_out",
+    )(parity, half, *([into] if whose else []))
+
+
 def spread(pieces):
     return pl.pallas_call(
         spread_kernel,
@@ -549,8 +589,7 @@
     measured = sort_measured(amplitudes[0, 0])
     parts = (in_hbm(probe),)
     tile = object_field
-    marks = jnp.pad((offsets + SHIFT).astype(F32).reshape(1, 1, 4), ((0, 1), (0, 7), (0, TILE - 4)))
-    around = neighbourhood(jnp.concatenate([tile, marks], axis=1))
+    around = neighbourhood(mark(offsets, tile))
     near = offsets_near(*around)
     for iteration in range(ITERS):
         mine, other, second, middle, first, power = step(
@@ -559,14 +598,14 @@
         mine = mine + lax.ppermute(other, "col", SWAP)
         first = lax.ppermute(after(first, mine), "row", pairs(0))
         second = lax.ppermute(after(second, mine), "row", pairs(1))
-        pieces = spread(exchange(mine, PLANES))
+        weight = weigh(parity, near, after(power, mine))
+        pieces = spread(after(exchange(mine, PLANES), weight))
         middle = after(middle, pieces)
         outer, own, inner = (middle[i] + first[i] + second[i] for i in range(3))
         folds = (outer, own, inner)
         inner = lax.ppermute(inner, "col", pairs(0))
         outer = lax.ppermute(outer, "col", pairs(1))
-        weight = weigh(parity, near, after(power, pieces))
-        pieces = after(exchange(pieces, LINES), (weight, folds))
+        pieces = after(exchange(pieces, LINES), folds)
         pieces, old = update(pieces, old)
         totals = after(own, old) + inner + outer
         tile = tile + OBJECT_STEP * totals / (weight + OBJECT_REG)
@@ -576,14 +615,8 @@
         if iteration + 1 == ITERS:
             mine = after(mine, (inner, outer))
         parts = (mine, lax.ppermute(mine, "col", SWAP))
-    probe = pl.pallas_call(
-        lay_out_kernel,
-        out_shape=jax.ShapeDtypeStruct((4, 2 * GROUPS, 8, SIDE), F32),
-        in_specs=[SMEM_SPEC, VMEM_SPEC, VMEM_SPEC],
-        out_specs=VMEM_SPEC,
-        compiler_params=params(8),
-        name="lay_out",
-    )(parity, *parts)
+    mine, other = parts
+    probe = lay_out(1, parity, other, lay_out(0, parity, mine))
     return (tile, probe.reshape(2, 2, SIDE, SIDE))
 
 

time: 185 us -> 185 us (level)
  waiting for transfers between devices: 63 us -> 60.9 us
    all_to_all x6, waiting for transfers between devices: 24.4 us -> 20.3 us  [exchange(): lax.all_to_all(value, BOTH, 0, 0, axis_index_groups=groups, tiled=True)]
  transfers between devices with their start and end apart: 26 -> 26, of which waited for: 14 -> 16; matrix products, arithmetic and copies ran while one was open for 2% -> 2% of each run, Pallas kernels for 5% -> 6%
where the time goes in v9:
time: 185 us; the launch traced here: 184 us
  starting transfers between devices  80.1 us (43%)
  waiting for transfers between devices  60.9 us (33%)
  Pallas kernels  32.8 us (18%)
  other arithmetic  4.91 us (3%)
  local copies, waits for them, and re-layouts  4.08 us (2%)
    all_to_all x6, starting transfers between devices, exchange(): lax.all_to_all(value, BOTH, 0, 0, axis_index_groups=groups, tiled=True)  32.9 us
    all_to_all x6, waiting for transfers between devices, exchange(): lax.all_to_all(value, BOTH, 0, 0, axis_index_groups=groups, tiled=True)  20.3 us
    pallas_call x2, Pallas kernels, step(): pl.pallas_call(functools.partial(step_kernel, halves), out_shape=[half, h...  19.4 us
    ppermute x2, starting transfers between devices, neighbourhood(): outer = lax.ppermute(tile, 'col', pairs(1))  13.6 us
    ppermute x2, starting transfers between devices, local(): outer = lax.ppermute(outer, 'col', pairs(1))  10.6 us
    ppermute x2, waiting for transfers between devices, neighbourhood(): outer = lax.ppermute(tile, 'col', pairs(1))  9.91 us
    ppermute x2, waiting for transfers between devices, neighbourhood(): second = lax.ppermute(band, 'row', pairs(1))  9.84 us
    ppermute x2, waiting for transfers between devices, local(): outer = lax.ppermute(outer, 'col', pairs(1))  9.78 us
  transfers between devices with their start and end apart: 26, of which 16 were waited for; matrix products, arithmetic and copies ran while one was open for 2% of the time, Pallas kernels for 6%

profile of v9, /device:TPU:39, one launch (start us, length us, event | category | flops | bytes accessed | tf_op | source)
XLA Modules:
  0.0 183.9 jit_solution(14104145938136007841)
XLA Ops:
  3.6 7.7 %collective-permute-start = (f32[2,136,128]{2,1,0:T(8,128)S(1)}, f32[2,136,128]{2,1,0:T(8,128)S(1)}, u32[]{:S(2)}, u32[]{:S(2)}) collective-permute-start(f32[2,136,128]{2,1,0:T(8,128)S(1)} %mark.1.refs_3_), channel_id=1, source_target_pairs={{1,2},{3,4},{5,6},{7,8},{9,10},{11,12},{13,14},{2,1},{4,3},{6,5},{... | collective-permute-start | bytes 417800 | tf_op jit(solution)/shard_map/ppermute | solution.py:486
  11.4 4.7 %collective-permute-done.refs_2_ = f32[2,136,128]{2,1,0:T(8,128)S(1)} collective-permute-done((f32[2,136,128]{2,1,0:T(8,128)S(1)}, f32[2,136,128]{2,1,0:T(8,128)S(1)}, u32[]{:S(2)}, u32[]{:S(2)}) %collective-permute-start) | collective-permute-done | bytes 139296 | tf_op jit(solution)/shard_map/ppermute | solution.py:486
  17.4 3.4 %collective-permute-start.2 = (f32[3,2,136,128]{3,2,1,0:T(8,128)S(1)}, f32[3,2,136,128]{3,2,1,0:T(8,128)S(1)}, u32[]{:S(2)}, u32[]{:S(2)}) collective-permute-start(f32[3,2,136,128]{3,2,1,0:T(8,128)S(1)} %pad_maximum_fusion), channel_id=1, source_target_pairs={{16,32},{48,64},{80,96},{112,128},{144,160},{176,192},{208,224},{3... | collective-permute-start | bytes 1253384 | tf_op jit(solution)/shard_map/ppermute | solution.py:489
  23.3 5.0 %collective-permute-done.2.refs_5_ = f32[3,2,136,128]{3,2,1,0:T(8,128)S(1)} collective-permute-done((f32[3,2,136,128]{3,2,1,0:T(8,128)S(1)}, f32[3,2,136,128]{3,2,1,0:T(8,128)S(1)}, u32[]{:S(2)}, u32[]{:S(2)}) %collective-permute-start.2) | collective-permute-done | bytes 417824 | tf_op jit(solution)/shard_map/ppermute | solution.py:489
  28.3 9.8 %step.2 = (f32[16,5,8,256]{3,2,1,0:T(8,128)S(1)}, f32[16,5,8,256]{3,2,1,0:T(8,128)S(1)}, f32[3,2,128,128]{3,2,1,0:T(8,128)S(1)}, f32[3,2,128,128]{3,2,1,0:T(8,12...) custom-call(s32[1,1,2,2]{3,2,1,0:T(2,128)S(1)} %copy-done.4, s32[2]{0:T(128)S(1)} %pad_add_fusion.parity_ref, ...), custom_call_target="tpu_custom_call" | custom-call | tf_op jit(solution)/shard_map/step/pallas_call | solution.py:454
  41.9 5.6 %all-to-all-start = ((f32[16,5,8,256]{3,2,1,0:T(8,128)}), f32[16,5,8,256]{3,2,1,0:T(8,128)S(1)}, u32[]{:S(2)}, u32[]{:S(2)}) async-start(f32[16,5,8,256]{3,2,1,0:T(8,128)} %add.100), calls=%async_computation | async-start | bytes 1310720 | tf_op jit(solution)/shard_map/all_to_all | solution.py:516
  48.7 3.3 %collective-permute-start.6 = (f32[3,2,128,128]{3,2,1,0:T(8,128)S(1)}, f32[3,2,128,128]{3,2,1,0:T(8,128)}, u32[]{:S(2)}, u32[]{:S(2)}) collective-permute-start(f32[3,2,128,128]{3,2,1,0:T(8,128)S(1)} %get-tuple-element.41), channel_id=1, source_target_pairs={{16,32},{48,64},{80,96},{112,128},{144,160},{176,192},{208,224},{3... | collective-permute-start | bytes 1179656 | tf_op jit(solution)/shard_map/ppermute | solution.py:600
  55.1 4.7 %all-to-all-done.pieces_ref = f32[16,5,8,256]{3,2,1,0:T(8,128)S(1)} async-done(((f32[16,5,8,256]{3,2,1,0:T(8,128)}), f32[16,5,8,256]{3,2,1,0:T(8,128)S(1)}, u32[]{:S(2)}, u32[]{:S(2)}) %all-to-all-start) | async-done | bytes 655392 | tf_op jit(solution)/shard_map/all_to_all | solution.py:516
  60.6 8.2 %all-to-all-start.1 = ((f32[8,5,8,256]{3,2,1,0:T(8,128)}), f32[8,5,8,256]{3,2,1,0:T(8,128)S(1)}, u32[]{:S(2)}, u32[]{:S(2)}) async-start(f32[8,5,8,256]{3,2,1,0:T(8,128)} %spread.2), calls=%async_computation.1 | async-start | bytes 655360 | tf_op jit(solution)/shard_map/all_to_all | solution.py:516
  72.8 7.2 %collective-permute-start.8 = (f32[2,128,128]{2,1,0:T(8,128)S(1)}, f32[2,128,128]{2,1,0:T(8,128)S(1)}, u32[]{:S(2)}, u32[]{:S(2)}) collective-permute-start(f32[2,128,128]{2,1,0:T(8,128)S(1)} %get-tuple-element.64), channel_id=1, source_target_pairs={{1,2},{3,4},{5,6},{7,8},{9,10},{11,12},{13,14},{2,1},{4,3},{6,5},{... | collective-permute-start | bytes 393224 | tf_op jit(solution)/shard_map/ppermute | solution.py:607
  81.4 5.1 %all-to-all-start.2 = ((f32[16,4,8,256]{3,2,1,0:T(8,128)}), f32[16,4,8,256]{3,2,1,0:T(8,128)S(1)}, u32[]{:S(2)}, u32[]{:S(2)}) async-start(f32[16,4,8,256]{3,2,1,0:T(8,128)} %get-tuple-element.45), calls=%async_computation.2 | async-start | bytes 1048576 | tf_op jit(solution)/shard_map/all_to_all | solution.py:516
  88.7 5.9 %collective-permute-start.10 = (f32[2,128,128]{2,1,0:T(8,128)S(1)}, f32[2,128,128]{2,1,0:T(8,128)S(1)}, u32[]{:S(2)}, u32[]{:S(2)}) collective-permute-start(f32[2,128,128]{2,1,0:T(8,128)S(1)} %divide_add_fusion.1.refs_4_), channel_id=1, source_target_pairs={{1,2},{3,4},{5,6},{7,8},{9,10},{11,12},{13,14},{2,1},{4,3},{6,5},{... | collective-permute-start | bytes 393224 | tf_op jit(solution)/shard_map/ppermute | solution.py:486
  96.6 5.2 %collective-permute-done.10.refs_3_ = f32[2,128,128]{2,1,0:T(8,128)S(1)} collective-permute-done((f32[2,128,128]{2,1,0:T(8,128)S(1)}, f32[2,128,128]{2,1,0:T(8,128)S(1)}, u32[]{:S(2)}, u32[]{:S(2)}) %collective-permute-start.10) | collective-permute-done | bytes 131104 | tf_op jit(solution)/shard_map/ppermute | solution.py:486
  105.2 3.8 %collective-permute-done.13.refs_7_ = f32[3,2,128,128]{3,2,1,0:T(8,128)S(1)} collective-permute-done((f32[3,2,128,128]{3,2,1,0:T(8,128)S(1)}, f32[3,2,128,128]{3,2,1,0:T(8,128)S(1)}, u32[]{:S(2)}, u32[]{:S(2)}) %collective-permute-start.13) | collective-permute-done | bytes 393248 | tf_op jit(solution)/shard_map/ppermute | solution.py:488
  109.0 4.9 %collective-permute-done.12.refs_6_ = f32[3,2,128,128]{3,2,1,0:T(8,128)S(1)} collective-permute-done((f32[3,2,128,128]{3,2,1,0:T(8,128)S(1)}, f32[3,2,128,128]{3,2,1,0:T(8,128)S(1)}, u32[]{:S(2)}, u32[]{:S(2)}) %collective-permute-start.12) | collective-permute-done | bytes 393248 | tf_op jit(solution)/shard_map/ppermute | solution.py:489
  113.9 9.6 %step.3 = (f32[16,5,8,256]{3,2,1,0:T(8,128)S(1)}, f32[16,5,8,256]{3,2,1,0:T(8,128)S(1)}, f32[3,2,128,128]{3,2,1,0:T(8,128)S(1)}, f32[3,2,128,128]{3,2,1,0:T(8,12...) custom-call(s32[1,1,2,2]{3,2,1,0:T(2,128)S(1)} %copy-done.4, s32[2]{0:T(128)S(1)} %pad_add_fusion.parity_ref, ...), custom_call_target="tpu_custom_call" | custom-call | tf_op jit(solution)/shard_map/step/pallas_call | solution.py:454
  126.6 5.5 %all-to-all-start.3 = ((f32[16,5,8,256]{3,2,1,0:T(8,128)}), f32[16,5,8,256]{3,2,1,0:T(8,128)S(1)}, u32[]{:S(2)}, u32[]{:S(2)}) async-start(f32[16,5,8,256]{3,2,1,0:T(8,128)} %add.117), calls=%async_computation.3 | async-start | bytes 1310720 | tf_op jit(solution)/shard_map/all_to_all | solution.py:516
  135.3 3.0 %weigh.3 = f32[128,128]{1,0:T(8,128)S(1)} custom-call(s32[2]{0:T(128)S(1)} %pad_add_fusion.parity_ref, s32[9,4]{1,0:T(8,128)S(1)} %convert_element_type.3.near_ref, f32[256,256]{1,0:T(8,128)S(1)} %get-tuple-element.50.power_ref), custom_call_target="tpu_custom_call" | custom-call | tf_op jit(solution)/shard_map/weigh/pallas_call | solution.py:520
  138.3 6.2 %all-to-all-done.3.pieces_ref = f32[16,5,8,256]{3,2,1,0:T(8,128)S(1)} async-done(((f32[16,5,8,256]{3,2,1,0:T(8,128)}), f32[16,5,8,256]{3,2,1,0:T(8,128)S(1)}, u32[]{:S(2)}, u32[]{:S(2)}) %all-to-all-start.3) | async-done | bytes 655392 | tf_op jit(solution)/shard_map/all_to_all | solution.py:516
  145.3 3.4 %all-to-all-start.4 = ((f32[8,5,8,256]{3,2,1,0:T(8,128)}), f32[8,5,8,256]{3,2,1,0:T(8,128)S(1)}, u32[]{:S(2)}, u32[]{:S(2)}) async-start(f32[8,5,8,256]{3,2,1,0:T(8,128)} %spread.3), calls=%async_computation.4 | async-start | bytes 655360 | tf_op jit(solution)/shard_map/all_to_all | solution.py:516
  151.3 8.7 %all-to-all-done.4.pieces_ref = f32[8,5,8,256]{3,2,1,0:T(8,128)S(1)} async-done(((f32[8,5,8,256]{3,2,1,0:T(8,128)}), f32[8,5,8,256]{3,2,1,0:T(8,128)S(1)}, u32[]{:S(2)}, u32[]{:S(2)}) %all-to-all-start.4) | async-done | bytes 327712 | tf_op jit(solution)/shard_map/all_to_all | solution.py:516
  160.9 5.1 %all-to-all-start.5 = ((f32[16,4,8,256]{3,2,1,0:T(8,128)}), f32[16,4,8,256]{3,2,1,0:T(8,128)S(1)}, u32[]{:S(2)}, u32[]{:S(2)}) async-start(f32[16,4,8,256]{3,2,1,0:T(8,128)} %get-tuple-element.58), calls=%async_computation.5 | async-start | bytes 1048576 | tf_op jit(solution)/shard_map/all_to_all | solution.py:516
  167.0 3.5 %collective-permute-start.18 = (f32[2,128,128]{2,1,0:T(8,128)S(1)}, f32[2,128,128]{2,1,0:T(8,128)S(1)}, u32[]{:S(2)}, u32[]{:S(2)}) collective-permute-start(f32[2,128,128]{2,1,0:T(8,128)S(1)} %get-tuple-element.61), channel_id=1, source_target_pairs={{1,2},{3,4},{5,6},{7,8},{9,10},{11,12},{13,14},{2,1},{4,3},{6,5},{... | collective-permute-start | bytes 393224 | tf_op jit(solution)/shard_map/ppermute | solution.py:607
  170.5 9.8 %collective-permute-done.18 = f32[2,128,128]{2,1,0:T(8,128)S(1)} collective-permute-done((f32[2,128,128]{2,1,0:T(8,128)S(1)}, f32[2,128,128]{2,1,0:T(8,128)S(1)}, u32[]{:S(2)}, u32[]{:S(2)}) %collective-permute-start.18) | collective-permute-done | bytes 131104 | tf_op jit(solution)/shard_map/ppermute | solution.py:607
  (71 shorter events, 43.6 us)
Async XLA Ops:
  2.8 8.5 %collective-permute-start.1 = (f32[2,136,128]{2,1,0:T(8,128)S(1)}, f32[2,136,128]{2,1,0:T(8,128)S(1)}, u32[]{:S(2)}, u32[]{:S(2)}) collective-permute-start(f32[2,136,128]{2,1,0:T(8,128)S(1)} %mark.1.refs_3_), channel_id=1, source_target_pairs={{0,1},{2,3},{4,5},{6,7},{8,9},{10,11},{12,13},{14,15},{1,0},{3,2},... | collective-permute-start | bytes 417800 | tf_op jit(solution)/shard_map/ppermute | solution.py:485
  3.6 12.5 %collective-permute-start = (f32[2,136,128]{2,1,0:T(8,128)S(1)}, f32[2,136,128]{2,1,0:T(8,128)S(1)}, u32[]{:S(2)}, u32[]{:S(2)}) collective-permute-start(f32[2,136,128]{2,1,0:T(8,128)S(1)} %mark.1.refs_3_), channel_id=1, source_target_pairs={{1,2},{3,4},{5,6},{7,8},{9,10},{11,12},{13,14},{2,1},{4,3},{6,5},{... | collective-permute-start | bytes 417800 | tf_op jit(solution)/shard_map/ppermute | solution.py:486
  16.1 7.2 %collective-permute-start.3 = (f32[3,2,136,128]{3,2,1,0:T(8,128)S(1)}, f32[3,2,136,128]{3,2,1,0:T(8,128)S(1)}, u32[]{:S(2)}, u32[]{:S(2)}) collective-permute-start(f32[3,2,136,128]{3,2,1,0:T(8,128)S(1)} %pad_maximum_fusion), channel_id=1, source_target_pairs={{0,16},{32,48},{64,80},{96,112},{128,144},{160,176},{192,208},{224... | collective-permute-start | bytes 1253384 | tf_op jit(solution)/shard_map/ppermute | solution.py:488
  17.4 10.9 %collective-permute-start.2 = (f32[3,2,136,128]{3,2,1,0:T(8,128)S(1)}, f32[3,2,136,128]{3,2,1,0:T(8,128)S(1)}, u32[]{:S(2)}, u32[]{:S(2)}) collective-permute-start(f32[3,2,136,128]{3,2,1,0:T(8,128)S(1)} %pad_maximum_fusion), channel_id=1, source_target_pairs={{16,32},{48,64},{80,96},{112,128},{144,160},{176,192},{208,224},{3... | collective-permute-start | bytes 1253384 | tf_op jit(solution)/shard_map/ppermute | solution.py:489
  41.9 17.9 %all-to-all-start = ((f32[16,5,8,256]{3,2,1,0:T(8,128)}), f32[16,5,8,256]{3,2,1,0:T(8,128)S(1)}, u32[]{:S(2)}, u32[]{:S(2)}) async-start(f32[16,5,8,256]{3,2,1,0:T(8,128)} %add.100), calls=%async_computation | async-start | bytes 1310720 | tf_op jit(solution)/shard_map/all_to_all | solution.py:516
  47.5 22.1 %collective-permute-start.5 = (f32[3,2,128,128]{3,2,1,0:T(8,128)}, f32[3,2,128,128]{3,2,1,0:T(8,128)S(1)}, u32[]{:S(2)}, u32[]{:S(2)}) collective-permute-start(f32[3,2,128,128]{3,2,1,0:T(8,128)} %copy-done.5), channel_id=1, source_target_pairs={{0,16},{32,48},{64,80},{96,112},{128,144},{160,176},{192,208},{224... | collective-permute-start | bytes 1179656 | tf_op jit(solution)/shard_map/ppermute | solution.py:599
  48.7 20.8 %collective-permute-start.6 = (f32[3,2,128,128]{3,2,1,0:T(8,128)S(1)}, f32[3,2,128,128]{3,2,1,0:T(8,128)}, u32[]{:S(2)}, u32[]{:S(2)}) collective-permute-start(f32[3,2,128,128]{3,2,1,0:T(8,128)S(1)} %get-tuple-element.41), channel_id=1, source_target_pairs={{16,32},{48,64},{80,96},{112,128},{144,160},{176,192},{208,224},{3... | collective-permute-start | bytes 1179656 | tf_op jit(solution)/shard_map/ppermute | solution.py:600
  60.6 19.9 %all-to-all-start.1 = ((f32[8,5,8,256]{3,2,1,0:T(8,128)}), f32[8,5,8,256]{3,2,1,0:T(8,128)S(1)}, u32[]{:S(2)}, u32[]{:S(2)}) async-start(f32[8,5,8,256]{3,2,1,0:T(8,128)} %spread.2), calls=%async_computation.1 | async-start | bytes 655360 | tf_op jit(solution)/shard_map/all_to_all | solution.py:516
  70.7 15.8 %collective-permute-start.7 = (f32[2,128,128]{2,1,0:T(8,128)S(1)}, f32[2,128,128]{2,1,0:T(8,128)S(1)}, u32[]{:S(2)}, u32[]{:S(2)}) collective-permute-start(f32[2,128,128]{2,1,0:T(8,128)S(1)} %get-tuple-element.63), channel_id=1, source_target_pairs={{0,1},{2,3},{4,5},{6,7},{8,9},{10,11},{12,13},{14,15},{1,0},{3,2},... | collective-permute-start | bytes 393224 | tf_op jit(solution)/shard_map/ppermute | solution.py:606
  72.8 13.7 %collective-permute-start.8 = (f32[2,128,128]{2,1,0:T(8,128)S(1)}, f32[2,128,128]{2,1,0:T(8,128)S(1)}, u32[]{:S(2)}, u32[]{:S(2)}) collective-permute-start(f32[2,128,128]{2,1,0:T(8,128)S(1)} %get-tuple-element.64), channel_id=1, source_target_pairs={{1,2},{3,4},{5,6},{7,8},{9,10},{11,12},{13,14},{2,1},{4,3},{6,5},{... | collective-permute-start | bytes 393224 | tf_op jit(solution)/shard_map/ppermute | solution.py:607
  81.4 13.3 %all-to-all-start.2 = ((f32[16,4,8,256]{3,2,1,0:T(8,128)}), f32[16,4,8,256]{3,2,1,0:T(8,128)S(1)}, u32[]{:S(2)}, u32[]{:S(2)}) async-start(f32[16,4,8,256]{3,2,1,0:T(8,128)} %get-tuple-element.45), calls=%async_computation.2 | async-start | bytes 1048576 | tf_op jit(solution)/shard_map/all_to_all | solution.py:516
  87.4 9.2 %collective-permute-start.11 = (f32[2,128,128]{2,1,0:T(8,128)S(1)}, f32[2,128,128]{2,1,0:T(8,128)S(1)}, u32[]{:S(2)}, u32[]{:S(2)}) collective-permute-start(f32[2,128,128]{2,1,0:T(8,128)S(1)} %divide_add_fusion.1.refs_4_), channel_id=1, source_target_pairs={{0,1},{2,3},{4,5},{6,7},{8,9},{10,11},{12,13},{14,15},{1,0},{3,2},... | collective-permute-start | bytes 393224 | tf_op jit(solution)/shard_map/ppermute | solution.py:485
  88.7 13.1 %collective-permute-start.10 = (f32[2,128,128]{2,1,0:T(8,128)S(1)}, f32[2,128,128]{2,1,0:T(8,128)S(1)}, u32[]{:S(2)}, u32[]{:S(2)}) collective-permute-start(f32[2,128,128]{2,1,0:T(8,128)S(1)} %divide_add_fusion.1.refs_4_), channel_id=1, source_target_pairs={{1,2},{3,4},{5,6},{7,8},{9,10},{11,12},{13,14},{2,1},{4,3},{6,5},{... | collective-permute-start | bytes 393224 | tf_op jit(solution)/shard_map/ppermute | solution.py:486
  94.7 19.2 %collective-permute-start.9 = (f32[16,4,8,256]{3,2,1,0:T(8,128)S(1)}, f32[16,4,8,256]{3,2,1,0:T(8,128)S(1)}, u32[]{:S(2)}, u32[]{:S(2)}) collective-permute-start(f32[16,4,8,256]{3,2,1,0:T(8,128)S(1)} %all-to-all-done.2.refs_0_), channel_id=1, source_target_pairs={{0,1},{1,0},{2,3},{3,2},{4,5},{5,4},{6,7},{7,6},{8,9},{9,8},{10,11... | collective-permute-start | bytes 1572872 | tf_op jit(solution)/shard_map/ppermute | solution.py:617
  101.8 7.2 %collective-permute-start.13 = (f32[3,2,128,128]{3,2,1,0:T(8,128)S(1)}, f32[3,2,128,128]{3,2,1,0:T(8,128)S(1)}, u32[]{:S(2)}, u32[]{:S(2)}) collective-permute-start(f32[3,2,128,128]{3,2,1,0:T(8,128)S(1)} %pad_maximum_fusion.1), channel_id=1, source_target_pairs={{0,16},{32,48},{64,80},{96,112},{128,144},{160,176},{192,208},{224... | collective-permute-start | bytes 1179656 | tf_op jit(solution)/shard_map/ppermute | solution.py:488
  103.3 10.6 %collective-permute-start.12 = (f32[3,2,128,128]{3,2,1,0:T(8,128)S(1)}, f32[3,2,128,128]{3,2,1,0:T(8,128)S(1)}, u32[]{:S(2)}, u32[]{:S(2)}) collective-permute-start(f32[3,2,128,128]{3,2,1,0:T(8,128)S(1)} %pad_maximum_fusion.1), channel_id=1, source_target_pairs={{16,32},{48,64},{80,96},{112,128},{144,160},{176,192},{208,224},{3... | collective-permute-start | bytes 1179656 | tf_op jit(solution)/shard_map/ppermute | solution.py:489
  123.5 2.2 %collective-permute-start.14 = (f32[16,5,8,256]{3,2,1,0:T(8,128)S(1)}, f32[16,5,8,256]{3,2,1,0:T(8,128)S(1)}, u32[]{:S(2)}, u32[]{:S(2)}) collective-permute-start(f32[16,5,8,256]{3,2,1,0:T(8,128)S(1)} %get-tuple-element.48), channel_id=1, source_target_pairs={{0,1},{1,0},{2,3},{3,2},{4,5},{5,4},{6,7},{7,6},{8,9},{9,8},{10,11... | collective-permute-start | bytes 1966088 | tf_op jit(solution)/shard_map/ppermute | solution.py:598
  126.6 17.9 %all-to-all-start.3 = ((f32[16,5,8,256]{3,2,1,0:T(8,128)}), f32[16,5,8,256]{3,2,1,0:T(8,128)S(1)}, u32[]{:S(2)}, u32[]{:S(2)}) async-start(f32[16,5,8,256]{3,2,1,0:T(8,128)} %add.117), calls=%async_computation.3 | async-start | bytes 1310720 | tf_op jit(solution)/shard_map/all_to_all | solution.py:516
  132.1 17.3 %collective-permute-start.15 = (f32[3,2,128,128]{3,2,1,0:T(8,128)S(1)}, f32[3,2,128,128]{3,2,1,0:T(8,128)S(1)}, u32[]{:S(2)}, u32[]{:S(2)}) collective-permute-start(f32[3,2,128,128]{3,2,1,0:T(8,128)S(1)} %get-tuple-element.54), channel_id=1, source_target_pairs={{0,16},{32,48},{64,80},{96,112},{128,144},{160,176},{192,208},{224... | collective-permute-start | bytes 1179656 | tf_op jit(solution)/shard_map/ppermute | solution.py:599
  133.3 16.9 %collective-permute-start.16 = (f32[3,2,128,128]{3,2,1,0:T(8,128)S(1)}, f32[3,2,128,128]{3,2,1,0:T(8,128)}, u32[]{:S(2)}, u32[]{:S(2)}) collective-permute-start(f32[3,2,128,128]{3,2,1,0:T(8,128)S(1)} %get-tuple-element.56), channel_id=1, source_target_pairs={{16,32},{48,64},{80,96},{112,128},{144,160},{176,192},{208,224},{3... | collective-permute-start | bytes 1179656 | tf_op jit(solution)/shard_map/ppermute | solution.py:600
  145.3 14.7 %all-to-all-start.4 = ((f32[8,5,8,256]{3,2,1,0:T(8,128)}), f32[8,5,8,256]{3,2,1,0:T(8,128)S(1)}, u32[]{:S(2)}, u32[]{:S(2)}) async-start(f32[8,5,8,256]{3,2,1,0:T(8,128)} %spread.3), calls=%async_computation.4 | async-start | bytes 655360 | tf_op jit(solution)/shard_map/all_to_all | solution.py:516
  160.9 19.4 %all-to-all-start.5 = ((f32[16,4,8,256]{3,2,1,0:T(8,128)}), f32[16,4,8,256]{3,2,1,0:T(8,128)S(1)}, u32[]{:S(2)}, u32[]{:S(2)}) async-start(f32[16,4,8,256]{3,2,1,0:T(8,128)} %get-tuple-element.58), calls=%async_computation.5 | async-start | bytes 1048576 | tf_op jit(solution)/shard_map/all_to_all | solution.py:516
  166.0 4.5 %collective-permute-start.17 = (f32[2,128,128]{2,1,0:T(8,128)S(1)}, f32[2,128,128]{2,1,0:T(8,128)S(1)}, u32[]{:S(2)}, u32[]{:S(2)}) collective-permute-start(f32[2,128,128]{2,1,0:T(8,128)S(1)} %get-tuple-element.60), channel_id=1, source_target_pairs={{0,1},{2,3},{4,5},{6,7},{8,9},{10,11},{12,13},{14,15},{1,0},{3,2},... | collective-permute-start | bytes 393224 | tf_op jit(solution)/shard_map/ppermute | solution.py:606
  167.0 13.3 %collective-permute-start.18 = (f32[2,128,128]{2,1,0:T(8,128)S(1)}, f32[2,128,128]{2,1,0:T(8,128)S(1)}, u32[]{:S(2)}, u32[]{:S(2)}) collective-permute-start(f32[2,128,128]{2,1,0:T(8,128)S(1)} %get-tuple-element.61), channel_id=1, source_target_pairs={{1,2},{3,4},{5,6},{7,8},{9,10},{11,12},{13,14},{2,1},{4,3},{6,5},{... | collective-permute-start | bytes 393224 | tf_op jit(solution)/shard_map/ppermute | solution.py:607
  (8 other events, 34.2 us)

commit v10 on v8

--- a/solution.py
+++ b/solution.py
@@ -88,11 +88,7 @@
     probe_in, refs = refs[: 1 + halves], refs[1 + halves :]
     (
         measured_in,
-        outer_in,
-        tile_in,
-        inner_in,
-        second_in,
-        first_in,
+        *around_in,
         mine_out,
         other_out,
         grad_second,
@@ -126,11 +122,9 @@
     def third(block):
         return pl.ds(block * TILE if isinstance(block, int) else pl.multiple_of(block * TILE, TILE), TILE)
 
-    for place, piece in enumerate((outer_in, tile_in, inner_in)):
-        columns = third(along[place])
-        start(piece.at[:, third(0)], padded.at[:, third(1), columns])
-        start(second_in.at[place, :, third(0)], padded.at[:, third(across[0]), columns])
-        start(first_in.at[place, :, third(0)], padded.at[:, third(across[2]), columns])
+    for place, piece in enumerate(around_in):
+        rows, columns = third(across[place // 3]), third(along[place % 3])
+        start(piece.at[:, third(0)], padded.at[:, rows, columns])
     near = len(copies)
     if halves:
         for half, ref in enumerate(probe_in):
@@ -437,7 +431,7 @@
     return pl.pallas_call(
         functools.partial(step_kernel, halves),
         out_shape=[half, half, band, band, band, jax.ShapeDtypeStruct((SIDE, SIDE), F32)],
-        in_specs=[SMEM_SPEC, SMEM_SPEC] + [ANY_SPEC] * (8 + halves),
+        in_specs=[SMEM_SPEC, SMEM_SPEC] + [ANY_SPEC] * (12 + halves),
         out_specs=[ANY_SPEC] * 5 + [VMEM_SPEC],
         scratch_shapes=[
             pltpu.VMEM(table.shape, BF16),
@@ -465,12 +459,19 @@
 
 
 def neighbourhood(tile):
-    inner = lax.ppermute(tile, "col", pairs(0))
-    outer = lax.ppermute(tile, "col", pairs(1))
-    band = jnp.stack([outer, tile, inner])
-    first = lax.ppermute(band, "row", pairs(0))
-    second = lax.ppermute(band, "row", pairs(1))
-    return outer, tile, inner, second, first
+    outer, inner = lax.ppermute(tile, "col", pairs(1)), lax.ppermute(tile, "col", pairs(0))
+    second, first = lax.ppermute(tile, "row", pairs(1)), lax.ppermute(tile, "row", pairs(0))
+    return (
+        lax.ppermute(outer, "row", pairs(1)),
+        second,
+        lax.ppermute(second, "col", pairs(0)),
+        outer,
+        tile,
+        inner,
+        lax.ppermute(outer, "row", pairs(0)),
+        first,
+        lax.ppermute(first, "col", pairs(0)),
+    )
 
 
 def after(value, other):
@@ -511,10 +512,8 @@
     )(parity, near, power)
 
 
-def offsets_near(outer, tile, inner, second, first):
-    rows = [[band[i, 0, TILE, :4] for i in range(3)] for band in (second, first)]
-    rows.insert(1, [piece[0, TILE, :4] for piece in (outer, tile, inner)])
-    return jnp.stack([value for row in rows for value in row]).astype(jnp.int32)
+def offsets_near(around):
+    return jnp.stack([piece[0, TILE, :4] for piece in around]).astype(jnp.int32)
 
 
 def spread(pieces):
@@ -551,7 +550,7 @@
     tile = object_field
     marks = jnp.pad((offsets + SHIFT).astype(F32).reshape(1, 1, 4), ((0, 1), (0, 7), (0, TILE - 4)))
     around = neighbourhood(jnp.concatenate([tile, marks], axis=1))
-    near = offsets_near(*around)
+    near = offsets_near(around)
     for iteration in range(ITERS):
         mine, other, second, middle, first, power = step(
             offsets, parity, table, parts, measured, around
@@ -559,22 +558,21 @@
         mine = mine + lax.ppermute(other, "col", SWAP)
         first = lax.ppermute(after(first, mine), "row", pairs(0))
         second = lax.ppermute(after(second, mine), "row", pairs(1))
-        pieces = spread(exchange(mine, PLANES))
+        weight = weigh(parity, near, after(power, mine))
+        pieces = spread(after(exchange(mine, PLANES), weight))
         middle = after(middle, pieces)
         outer, own, inner = (middle[i] + first[i] + second[i] for i in range(3))
         folds = (outer, own, inner)
         inner = lax.ppermute(inner, "col", pairs(0))
         outer = lax.ppermute(outer, "col", pairs(1))
-        weight = weigh(parity, near, after(power, pieces))
-        pieces = after(exchange(pieces, LINES), (weight, folds))
+        pieces = after(exchange(pieces, LINES), folds)
         pieces, old = update(pieces, old)
         totals = after(own, old) + inner + outer
         tile = tile + OBJECT_STEP * totals / (weight + OBJECT_REG)
         if iteration + 1 < ITERS:
             around = neighbourhood(tile)
         mine = exchange(pieces, PLANES)
-        if iteration + 1 == ITERS:
-            mine = after(mine, (inner, outer))
+        mine = after(mine, around[1::2] if iteration + 1 < ITERS else (inner, outer))
         parts = (mine, lax.ppermute(mine, "col", SWAP))
     probe = pl.pallas_call(
         lay_out_kernel,

time: 185 us -> 187 us (1.011)
  starting transfers between devices: 79.5 us -> 96.2 us
  waiting for transfers between devices: 63 us -> 50 us
    all_to_all x6, waiting for transfers between devices: 24.4 us -> 12.8 us  [exchange(): lax.all_to_all(value, BOTH, 0, 0, axis_index_groups=groups, tiled=True)]
    ppermute x8 -> x16, starting transfers between devices: 23.1 us -> 31 us  [the longest x2 12.4 us: neighbourhood(): lax.ppermute(tile, 'col', pairs(1))]
    ppermute x2, starting transfers between devices: 3.34 us -> 10.4 us  [local(): inner = lax.ppermute(inner, 'col', pairs(0))]
    ppermute x8 -> x16, waiting for transfers between devices: 23 us -> 16.8 us  [the longest x2 7.05 us: neighbourhood(): lax.ppermute(outer, 'row', pairs(1))]
    all_to_all x6, starting transfers between devices: 32 us -> 38.1 us  [exchange(): lax.all_to_all(value, BOTH, 0, 0, axis_index_groups=groups, tiled=True)]
    ppermute x2, starting transfers between devices: 10.2 us -> 5.14 us  [local(): outer = lax.ppermute(outer, 'col', pairs(1))]
    ppermute x2, waiting for transfers between devices: 10.2 us -> 15 us  [local(): outer = lax.ppermute(outer, 'col', pairs(1))]
    ppermute x2, starting transfers between devices: 0.1 us -> 2.95 us  [local(): mine = mine + lax.ppermute(other, 'col', SWAP)]
  transfers between devices with their start and end apart: 26 -> 34, of which waited for: 14 -> 15; matrix products, arithmetic and copies ran while one was open for 2% -> 2% of each run, Pallas kernels for 5% -> 5%
where the time goes in v10:
time: 187 us; the launch traced here: 186 us
  starting transfers between devices  96.2 us (51%)
  waiting for transfers between devices  50 us (27%)
  Pallas kernels  31.1 us (17%)
  other arithmetic  5.59 us (3%)
  local copies, waits for them, and re-layouts  2.03 us (1%)
    all_to_all x6, starting transfers between devices, exchange(): lax.all_to_all(value, BOTH, 0, 0, axis_index_groups=groups, tiled=True)  38.1 us
    pallas_call x2, Pallas kernels, step(): pl.pallas_call(functools.partial(step_kernel, halves), out_shape=[half, h...  19.4 us
    ppermute x2, waiting for transfers between devices, local(): outer = lax.ppermute(outer, 'col', pairs(1))  15 us
    all_to_all x6, waiting for transfers between devices, exchange(): lax.all_to_all(value, BOTH, 0, 0, axis_index_groups=groups, tiled=True)  12.8 us
    ppermute x2, starting transfers between devices, neighbourhood(): lax.ppermute(tile, 'col', pairs(1))  12.4 us
    ppermute x2, starting transfers between devices, local(): inner = lax.ppermute(inner, 'col', pairs(0))  10.4 us
    ppermute x2, starting transfers between devices, neighbourhood(): lax.ppermute(tile, 'row', pairs(1))  7.41 us
    ppermute x2, waiting for transfers between devices, neighbourhood(): lax.ppermute(outer, 'row', pairs(1))  7.05 us
  transfers between devices with their start and end apart: 34, of which 15 were waited for; matrix products, arithmetic and copies ran while one was open for 2% of the time, Pallas kernels for 5%

profile of v10, /device:TPU:39, one launch (start us, length us, event | category | flops | bytes accessed | tf_op | source)
XLA Modules:
  0.0 185.9 jit_solution(5537567565138650151)
XLA Ops:
  2.3 8.4 %collective-permute-start = (f32[2,136,128]{2,1,0:T(8,128)S(1)}, f32[2,136,128]{2,1,0:T(8,128)S(1)}, u32[]{:S(2)}, u32[]{:S(2)}) collective-permute-start(f32[2,136,128]{2,1,0:T(8,128)S(1)} %select_maximum_fusion.refs_6_), channel_id=1, source_target_pairs={{1,2},{3,4},{5,6},{7,8},{9,10},{11,12},{13,14},{2,1},{4,3},{6,5},{... | collective-permute-start | bytes 417800 | tf_op jit(solution)/shard_map/ppermute | solution.py:462
  12.1 4.2 %collective-permute-start.2 = (f32[2,136,128]{2,1,0:T(8,128)S(1)}, f32[2,136,128]{2,1,0:T(8,128)S(1)}, u32[]{:S(2)}, u32[]{:S(2)}) collective-permute-start(f32[2,136,128]{2,1,0:T(8,128)S(1)} %select_maximum_fusion.refs_6_), channel_id=1, source_target_pairs={{16,32},{48,64},{80,96},{112,128},{144,160},{176,192},{208,224},{3... | collective-permute-start | bytes 417800 | tf_op jit(solution)/shard_map/ppermute | solution.py:463
  18.6 3.1 %collective-permute-start.1 = (f32[2,136,128]{2,1,0:T(8,128)S(1)}, f32[2,136,128]{2,1,0:T(8,128)S(1)}, u32[]{:S(2)}, u32[]{:S(2)}) collective-permute-start(f32[2,136,128]{2,1,0:T(8,128)S(1)} %collective-permute-done.refs_5_), channel_id=1, source_target_pairs={{16,32},{48,64},{80,96},{112,128},{144,160},{176,192},{208,224},{3... | collective-permute-start | bytes 417800 | tf_op jit(solution)/shard_map/ppermute | solution.py:465
  24.0 3.1 %collective-permute-done.1.refs_2_ = f32[2,136,128]{2,1,0:T(8,128)S(1)} collective-permute-done((f32[2,136,128]{2,1,0:T(8,128)S(1)}, f32[2,136,128]{2,1,0:T(8,128)S(1)}, u32[]{:S(2)}, u32[]{:S(2)}) %collective-permute-start.1) | collective-permute-done | bytes 139296 | tf_op jit(solution)/shard_map/ppermute | solution.py:465
  27.1 9.8 %step.2 = (f32[16,5,8,256]{3,2,1,0:T(8,128)S(1)}, f32[16,5,8,256]{3,2,1,0:T(8,128)S(1)}, f32[3,2,128,128]{3,2,1,0:T(8,128)S(1)}, f32[3,2,128,128]{3,2,1,0:T(8,12...) custom-call(s32[1,1,2,2]{3,2,1,0:T(2,128)S(1)} %copy-done.1, s32[2]{0:T(128)S(1)} %pad_add_fusion.parity_ref, ...), custom_call_target="tpu_custom_call" | custom-call | tf_op jit(solution)/shard_map/step/pallas_call | solution.py:431
  41.2 4.5 %all-to-all-start = ((f32[16,5,8,256]{3,2,1,0:T(8,128)}), f32[16,5,8,256]{3,2,1,0:T(8,128)S(1)}, u32[]{:S(2)}, u32[]{:S(2)}) async-start(f32[16,5,8,256]{3,2,1,0:T(8,128)} %add.106), calls=%async_computation | async-start | bytes 1310720 | tf_op jit(solution)/shard_map/all_to_all | solution.py:500
  47.0 4.1 %collective-permute-start.10 = (f32[3,2,128,128]{3,2,1,0:T(8,128)S(1)}, f32[3,2,128,128]{3,2,1,0:T(8,128)}, u32[]{:S(2)}, u32[]{:S(2)}) collective-permute-start(f32[3,2,128,128]{3,2,1,0:T(8,128)S(1)} %get-tuple-element.42), channel_id=1, source_target_pairs={{16,32},{48,64},{80,96},{112,128},{144,160},{176,192},{208,224},{3... | collective-permute-start | bytes 1179656 | tf_op jit(solution)/shard_map/ppermute | solution.py:560
  56.3 8.1 %all-to-all-start.1 = ((f32[8,5,8,256]{3,2,1,0:T(8,128)}), f32[8,5,8,256]{3,2,1,0:T(8,128)S(1)}, u32[]{:S(2)}, u32[]{:S(2)}) async-start(f32[8,5,8,256]{3,2,1,0:T(8,128)} %spread.2), calls=%async_computation.1 | async-start | bytes 655360 | tf_op jit(solution)/shard_map/all_to_all | solution.py:500
  66.4 7.5 %collective-permute-start.11 = (f32[2,128,128]{2,1,0:T(8,128)S(1)}, f32[2,128,128]{2,1,0:T(8,128)S(1)}, u32[]{:S(2)}, u32[]{:S(2)}) collective-permute-start(f32[2,128,128]{2,1,0:T(8,128)S(1)} %get-tuple-element.65), channel_id=1, source_target_pairs={{0,1},{2,3},{4,5},{6,7},{8,9},{10,11},{12,13},{14,15},{1,0},{3,2},... | collective-permute-start | bytes 393224 | tf_op jit(solution)/shard_map/ppermute | solution.py:566
  76.9 5.1 %all-to-all-start.2 = ((f32[16,4,8,256]{3,2,1,0:T(8,128)}), f32[16,4,8,256]{3,2,1,0:T(8,128)S(1)}, u32[]{:S(2)}, u32[]{:S(2)}) async-start(f32[16,4,8,256]{3,2,1,0:T(8,128)} %get-tuple-element.46), calls=%async_computation.2 | async-start | bytes 1048576 | tf_op jit(solution)/shard_map/all_to_all | solution.py:500
  82.1 4.9 %collective-permute-done.12 = f32[2,128,128]{2,1,0:T(8,128)S(1)} collective-permute-done((f32[2,128,128]{2,1,0:T(8,128)S(1)}, f32[2,128,128]{2,1,0:T(8,128)S(1)}, u32[]{:S(2)}, u32[]{:S(2)}) %collective-permute-start.12) | collective-permute-done | bytes 131104 | tf_op jit(solution)/shard_map/ppermute | solution.py:567
  89.0 4.0 %collective-permute-start.14 = (f32[2,128,128]{2,1,0:T(8,128)S(1)}, f32[2,128,128]{2,1,0:T(8,128)S(1)}, u32[]{:S(2)}, u32[]{:S(2)}) collective-permute-start(f32[2,128,128]{2,1,0:T(8,128)S(1)} %divide_add_fusion.1.refs_7_), channel_id=1, source_target_pairs={{1,2},{3,4},{5,6},{7,8},{9,10},{11,12},{13,14},{2,1},{4,3},{6,5},{... | collective-permute-start | bytes 393224 | tf_op jit(solution)/shard_map/ppermute | solution.py:462
  93.0 3.2 %collective-permute-start.13 = (f32[2,128,128]{2,1,0:T(8,128)S(1)}, f32[2,128,128]{2,1,0:T(8,128)S(1)}, u32[]{:S(2)}, u32[]{:S(2)}) collective-permute-start(f32[2,128,128]{2,1,0:T(8,128)S(1)} %divide_add_fusion.1.refs_7_), channel_id=1, source_target_pairs={{16,32},{48,64},{80,96},{112,128},{144,160},{176,192},{208,224},{3... | collective-permute-start | bytes 393224 | tf_op jit(solution)/shard_map/ppermute | solution.py:463
  96.2 6.5 %collective-permute-done.14.refs_6_ = f32[2,128,128]{2,1,0:T(8,128)S(1)} collective-permute-done((f32[2,128,128]{2,1,0:T(8,128)S(1)}, f32[2,128,128]{2,1,0:T(8,128)S(1)}, u32[]{:S(2)}, u32[]{:S(2)}) %collective-permute-start.14) | collective-permute-done | bytes 131104 | tf_op jit(solution)/shard_map/ppermute | solution.py:462
  108.3 4.0 %collective-permute-done.18.refs_3_ = f32[2,128,128]{2,1,0:T(8,128)S(1)} collective-permute-done((f32[2,128,128]{2,1,0:T(8,128)S(1)}, f32[2,128,128]{2,1,0:T(8,128)S(1)}, u32[]{:S(2)}, u32[]{:S(2)}) %collective-permute-start.18) | collective-permute-done | bytes 131104 | tf_op jit(solution)/shard_map/ppermute | solution.py:465
  112.2 9.6 %step.3 = (f32[16,5,8,256]{3,2,1,0:T(8,128)S(1)}, f32[16,5,8,256]{3,2,1,0:T(8,128)S(1)}, f32[3,2,128,128]{3,2,1,0:T(8,128)S(1)}, f32[3,2,128,128]{3,2,1,0:T(8,12...) custom-call(s32[1,1,2,2]{3,2,1,0:T(2,128)S(1)} %copy-done.1, s32[2]{0:T(128)S(1)} %pad_add_fusion.parity_ref, ...), custom_call_target="tpu_custom_call" | custom-call | tf_op jit(solution)/shard_map/step/pallas_call | solution.py:431
  125.8 5.6 %all-to-all-start.3 = ((f32[16,5,8,256]{3,2,1,0:T(8,128)}), f32[16,5,8,256]{3,2,1,0:T(8,128)S(1)}, u32[]{:S(2)}, u32[]{:S(2)}) async-start(f32[16,5,8,256]{3,2,1,0:T(8,128)} %add.123), calls=%async_computation.3 | async-start | bytes 1310720 | tf_op jit(solution)/shard_map/all_to_all | solution.py:500
  134.6 3.0 %weigh.3 = f32[128,128]{1,0:T(8,128)S(1)} custom-call(s32[2]{0:T(128)S(1)} %pad_add_fusion.parity_ref, s32[9,4]{1,0:T(8,128)S(1)} %convert_element_type.9.near_ref, f32[256,256]{1,0:T(8,128)S(1)} %get-tuple-element.52.power_ref), custom_call_target="tpu_custom_call" | custom-call | tf_op jit(solution)/shard_map/weigh/pallas_call | solution.py:504
  137.6 3.7 %all-to-all-done.3.pieces_ref = f32[16,5,8,256]{3,2,1,0:T(8,128)S(1)} async-done(((f32[16,5,8,256]{3,2,1,0:T(8,128)}), f32[16,5,8,256]{3,2,1,0:T(8,128)S(1)}, u32[]{:S(2)}, u32[]{:S(2)}) %all-to-all-start.3) | async-done | bytes 655392 | tf_op jit(solution)/shard_map/all_to_all | solution.py:500
  142.1 6.5 %all-to-all-start.4 = ((f32[8,5,8,256]{3,2,1,0:T(8,128)}), f32[8,5,8,256]{3,2,1,0:T(8,128)S(1)}, u32[]{:S(2)}, u32[]{:S(2)}) async-start(f32[8,5,8,256]{3,2,1,0:T(8,128)} %spread.3), calls=%async_computation.4 | async-start | bytes 655360 | tf_op jit(solution)/shard_map/all_to_all | solution.py:500
  149.4 7.6 %all-to-all-done.4.pieces_ref = f32[8,5,8,256]{3,2,1,0:T(8,128)S(1)} async-done(((f32[8,5,8,256]{3,2,1,0:T(8,128)}), f32[8,5,8,256]{3,2,1,0:T(8,128)S(1)}, u32[]{:S(2)}, u32[]{:S(2)}) %all-to-all-start.4) | async-done | bytes 327712 | tf_op jit(solution)/shard_map/all_to_all | solution.py:500
  157.9 8.3 %all-to-all-start.5 = ((f32[16,4,8,256]{3,2,1,0:T(8,128)}), f32[16,4,8,256]{3,2,1,0:T(8,128)S(1)}, u32[]{:S(2)}, u32[]{:S(2)}) async-start(f32[16,4,8,256]{3,2,1,0:T(8,128)} %get-tuple-element.60), calls=%async_computation.5 | async-start | bytes 1048576 | tf_op jit(solution)/shard_map/all_to_all | solution.py:500
  169.1 3.1 %collective-permute-start.26 = (f32[2,128,128]{2,1,0:T(8,128)S(1)}, f32[2,128,128]{2,1,0:T(8,128)S(1)}, u32[]{:S(2)}, u32[]{:S(2)}) collective-permute-start(f32[2,128,128]{2,1,0:T(8,128)S(1)} %get-tuple-element.63), channel_id=1, source_target_pairs={{1,2},{3,4},{5,6},{7,8},{9,10},{11,12},{13,14},{2,1},{4,3},{6,5},{... | collective-permute-start | bytes 393224 | tf_op jit(solution)/shard_map/ppermute | solution.py:567
  172.2 10.2 %collective-permute-done.26 = f32[2,128,128]{2,1,0:T(8,128)S(1)} collective-permute-done((f32[2,128,128]{2,1,0:T(8,128)S(1)}, f32[2,128,128]{2,1,0:T(8,128)S(1)}, u32[]{:S(2)}, u32[]{:S(2)}) %collective-permute-start.26) | collective-permute-done | bytes 131104 | tf_op jit(solution)/shard_map/ppermute | solution.py:567
  (84 shorter events, 46.8 us)
Async XLA Ops:
  2.3 16.2 %collective-permute-start = (f32[2,136,128]{2,1,0:T(8,128)S(1)}, f32[2,136,128]{2,1,0:T(8,128)S(1)}, u32[]{:S(2)}, u32[]{:S(2)}) collective-permute-start(f32[2,136,128]{2,1,0:T(8,128)S(1)} %select_maximum_fusion.refs_6_), channel_id=1, source_target_pairs={{1,2},{3,4},{5,6},{7,8},{9,10},{11,12},{13,14},{2,1},{4,3},{6,5},{... | collective-permute-start | bytes 417800 | tf_op jit(solution)/shard_map/ppermute | solution.py:462
  10.7 11.0 %collective-permute-start.6 = (f32[2,136,128]{2,1,0:T(8,128)S(1)}, f32[2,136,128]{2,1,0:T(8,128)S(1)}, u32[]{:S(2)}, u32[]{:S(2)}) collective-permute-start(f32[2,136,128]{2,1,0:T(8,128)S(1)} %select_maximum_fusion.refs_6_), channel_id=1, source_target_pairs={{0,16},{32,48},{64,80},{96,112},{128,144},{160,176},{192,208},{224... | collective-permute-start | bytes 417800 | tf_op jit(solution)/shard_map/ppermute | solution.py:463
  12.1 10.6 %collective-permute-start.2 = (f32[2,136,128]{2,1,0:T(8,128)S(1)}, f32[2,136,128]{2,1,0:T(8,128)S(1)}, u32[]{:S(2)}, u32[]{:S(2)}) collective-permute-start(f32[2,136,128]{2,1,0:T(8,128)S(1)} %select_maximum_fusion.refs_6_), channel_id=1, source_target_pairs={{16,32},{48,64},{80,96},{112,128},{144,160},{176,192},{208,224},{3... | collective-permute-start | bytes 417800 | tf_op jit(solution)/shard_map/ppermute | solution.py:463
  18.6 8.5 %collective-permute-start.1 = (f32[2,136,128]{2,1,0:T(8,128)S(1)}, f32[2,136,128]{2,1,0:T(8,128)S(1)}, u32[]{:S(2)}, u32[]{:S(2)}) collective-permute-start(f32[2,136,128]{2,1,0:T(8,128)S(1)} %collective-permute-done.refs_5_), channel_id=1, source_target_pairs={{16,32},{48,64},{80,96},{112,128},{144,160},{176,192},{208,224},{3... | collective-permute-start | bytes 417800 | tf_op jit(solution)/shard_map/ppermute | solution.py:465
  41.2 14.3 %all-to-all-start = ((f32[16,5,8,256]{3,2,1,0:T(8,128)}), f32[16,5,8,256]{3,2,1,0:T(8,128)S(1)}, u32[]{:S(2)}, u32[]{:S(2)}) async-start(f32[16,5,8,256]{3,2,1,0:T(8,128)} %add.106), calls=%async_computation | async-start | bytes 1310720 | tf_op jit(solution)/shard_map/all_to_all | solution.py:500
  45.7 19.5 %collective-permute-start.9 = (f32[3,2,128,128]{3,2,1,0:T(8,128)S(1)}, f32[3,2,128,128]{3,2,1,0:T(8,128)}, u32[]{:S(2)}, u32[]{:S(2)}) collective-permute-start(f32[3,2,128,128]{3,2,1,0:T(8,128)S(1)} %get-tuple-element.40), channel_id=1, source_target_pairs={{0,16},{32,48},{64,80},{96,112},{128,144},{160,176},{192,208},{224... | collective-permute-start | bytes 1179656 | tf_op jit(solution)/shard_map/ppermute | solution.py:559
  47.0 18.2 %collective-permute-start.10 = (f32[3,2,128,128]{3,2,1,0:T(8,128)S(1)}, f32[3,2,128,128]{3,2,1,0:T(8,128)}, u32[]{:S(2)}, u32[]{:S(2)}) collective-permute-start(f32[3,2,128,128]{3,2,1,0:T(8,128)S(1)} %get-tuple-element.42), channel_id=1, source_target_pairs={{16,32},{48,64},{80,96},{112,128},{144,160},{176,192},{208,224},{3... | collective-permute-start | bytes 1179656 | tf_op jit(solution)/shard_map/ppermute | solution.py:560
  56.3 19.7 %all-to-all-start.1 = ((f32[8,5,8,256]{3,2,1,0:T(8,128)}), f32[8,5,8,256]{3,2,1,0:T(8,128)S(1)}, u32[]{:S(2)}, u32[]{:S(2)}) async-start(f32[8,5,8,256]{3,2,1,0:T(8,128)} %spread.2), calls=%async_computation.1 | async-start | bytes 655360 | tf_op jit(solution)/shard_map/all_to_all | solution.py:500
  66.4 15.6 %collective-permute-start.11 = (f32[2,128,128]{2,1,0:T(8,128)S(1)}, f32[2,128,128]{2,1,0:T(8,128)S(1)}, u32[]{:S(2)}, u32[]{:S(2)}) collective-permute-start(f32[2,128,128]{2,1,0:T(8,128)S(1)} %get-tuple-element.65), channel_id=1, source_target_pairs={{0,1},{2,3},{4,5},{6,7},{8,9},{10,11},{12,13},{14,15},{1,0},{3,2},... | collective-permute-start | bytes 393224 | tf_op jit(solution)/shard_map/ppermute | solution.py:566
  74.0 13.0 %collective-permute-start.12 = (f32[2,128,128]{2,1,0:T(8,128)S(1)}, f32[2,128,128]{2,1,0:T(8,128)S(1)}, u32[]{:S(2)}, u32[]{:S(2)}) collective-permute-start(f32[2,128,128]{2,1,0:T(8,128)S(1)} %get-tuple-element.66), channel_id=1, source_target_pairs={{1,2},{3,4},{5,6},{7,8},{9,10},{11,12},{13,14},{2,1},{4,3},{6,5},{... | collective-permute-start | bytes 393224 | tf_op jit(solution)/shard_map/ppermute | solution.py:567
  76.9 25.8 %all-to-all-start.2 = ((f32[16,4,8,256]{3,2,1,0:T(8,128)}), f32[16,4,8,256]{3,2,1,0:T(8,128)S(1)}, u32[]{:S(2)}, u32[]{:S(2)}) async-start(f32[16,4,8,256]{3,2,1,0:T(8,128)} %get-tuple-element.46), calls=%async_computation.2 | async-start | bytes 1048576 | tf_op jit(solution)/shard_map/all_to_all | solution.py:500
  87.0 9.2 %collective-permute-start.16 = (f32[2,128,128]{2,1,0:T(8,128)S(1)}, f32[2,128,128]{2,1,0:T(8,128)S(1)}, u32[]{:S(2)}, u32[]{:S(2)}) collective-permute-start(f32[2,128,128]{2,1,0:T(8,128)S(1)} %divide_add_fusion.1.refs_7_), channel_id=1, source_target_pairs={{0,16},{32,48},{64,80},{96,112},{128,144},{160,176},{192,208},{224... | collective-permute-start | bytes 393224 | tf_op jit(solution)/shard_map/ppermute | solution.py:463
  87.1 9.1 %collective-permute-start.15 = (f32[2,128,128]{2,1,0:T(8,128)S(1)}, f32[2,128,128]{2,1,0:T(8,128)S(1)}, u32[]{:S(2)}, u32[]{:S(2)}) collective-permute-start(f32[2,128,128]{2,1,0:T(8,128)S(1)} %divide_add_fusion.1.refs_7_), channel_id=1, source_target_pairs={{0,1},{2,3},{4,5},{6,7},{8,9},{10,11},{12,13},{14,15},{1,0},{3,2},... | collective-permute-start | bytes 393224 | tf_op jit(solution)/shard_map/ppermute | solution.py:462
  89.0 13.7 %collective-permute-start.14 = (f32[2,128,128]{2,1,0:T(8,128)S(1)}, f32[2,128,128]{2,1,0:T(8,128)S(1)}, u32[]{:S(2)}, u32[]{:S(2)}) collective-permute-start(f32[2,128,128]{2,1,0:T(8,128)S(1)} %divide_add_fusion.1.refs_7_), channel_id=1, source_target_pairs={{1,2},{3,4},{5,6},{7,8},{9,10},{11,12},{13,14},{2,1},{4,3},{6,5},{... | collective-permute-start | bytes 393224 | tf_op jit(solution)/shard_map/ppermute | solution.py:462
  93.0 9.7 %collective-permute-start.13 = (f32[2,128,128]{2,1,0:T(8,128)S(1)}, f32[2,128,128]{2,1,0:T(8,128)S(1)}, u32[]{:S(2)}, u32[]{:S(2)}) collective-permute-start(f32[2,128,128]{2,1,0:T(8,128)S(1)} %divide_add_fusion.1.refs_7_), channel_id=1, source_target_pairs={{16,32},{48,64},{80,96},{112,128},{144,160},{176,192},{208,224},{3... | collective-permute-start | bytes 393224 | tf_op jit(solution)/shard_map/ppermute | solution.py:463
  102.7 9.5 %collective-permute-start.17 = (f32[16,4,8,256]{3,2,1,0:T(8,128)S(1)}, f32[16,4,8,256]{3,2,1,0:T(8,128)S(1)}, u32[]{:S(2)}, u32[]{:S(2)}) collective-permute-start(f32[16,4,8,256]{3,2,1,0:T(8,128)S(1)} %all-to-all-done.2.refs_0_), channel_id=1, source_target_pairs={{0,1},{1,0},{2,3},{3,2},{4,5},{5,4},{6,7},{7,6},{8,9},{9,8},{10,11... | collective-permute-start | bytes 1572872 | tf_op jit(solution)/shard_map/ppermute | solution.py:576
  103.5 8.7 %collective-permute-start.18 = (f32[2,128,128]{2,1,0:T(8,128)S(1)}, f32[2,128,128]{2,1,0:T(8,128)S(1)}, u32[]{:S(2)}, u32[]{:S(2)}) collective-permute-start(f32[2,128,128]{2,1,0:T(8,128)S(1)} %collective-permute-done.14.refs_6_), channel_id=1, source_target_pairs={{16,32},{48,64},{80,96},{112,128},{144,160},{176,192},{208,224},{3... | collective-permute-start | bytes 393224 | tf_op jit(solution)/shard_map/ppermute | solution.py:465
  105.7 6.6 %collective-permute-start.19 = (f32[2,128,128]{2,1,0:T(8,128)S(1)}, f32[2,128,128]{2,1,0:T(8,128)S(1)}, u32[]{:S(2)}, u32[]{:S(2)}) collective-permute-start(f32[2,128,128]{2,1,0:T(8,128)S(1)} %collective-permute-done.13.refs_4_), channel_id=1, source_target_pairs={{0,1},{2,3},{4,5},{6,7},{8,9},{10,11},{12,13},{14,15},{1,0},{3,2},... | collective-permute-start | bytes 393224 | tf_op jit(solution)/shard_map/ppermute | solution.py:467
  125.8 15.5 %all-to-all-start.3 = ((f32[16,5,8,256]{3,2,1,0:T(8,128)}), f32[16,5,8,256]{3,2,1,0:T(8,128)S(1)}, u32[]{:S(2)}, u32[]{:S(2)}) async-start(f32[16,5,8,256]{3,2,1,0:T(8,128)} %add.123), calls=%async_computation.3 | async-start | bytes 1310720 | tf_op jit(solution)/shard_map/all_to_all | solution.py:500
  131.5 17.1 %collective-permute-start.23 = (f32[3,2,128,128]{3,2,1,0:T(8,128)S(1)}, f32[3,2,128,128]{3,2,1,0:T(8,128)S(1)}, u32[]{:S(2)}, u32[]{:S(2)}) collective-permute-start(f32[3,2,128,128]{3,2,1,0:T(8,128)S(1)} %get-tuple-element.56), channel_id=1, source_target_pairs={{0,16},{32,48},{64,80},{96,112},{128,144},{160,176},{192,208},{224... | collective-permute-start | bytes 1179656 | tf_op jit(solution)/shard_map/ppermute | solution.py:559
  132.6 16.7 %collective-permute-start.24 = (f32[3,2,128,128]{3,2,1,0:T(8,128)S(1)}, f32[3,2,128,128]{3,2,1,0:T(8,128)S(1)}, u32[]{:S(2)}, u32[]{:S(2)}) collective-permute-start(f32[3,2,128,128]{3,2,1,0:T(8,128)S(1)} %get-tuple-element.58), channel_id=1, source_target_pairs={{16,32},{48,64},{80,96},{112,128},{144,160},{176,192},{208,224},{3... | collective-permute-start | bytes 1179656 | tf_op jit(solution)/shard_map/ppermute | solution.py:560
  142.1 14.9 %all-to-all-start.4 = ((f32[8,5,8,256]{3,2,1,0:T(8,128)}), f32[8,5,8,256]{3,2,1,0:T(8,128)S(1)}, u32[]{:S(2)}, u32[]{:S(2)}) async-start(f32[8,5,8,256]{3,2,1,0:T(8,128)} %spread.3), calls=%async_computation.4 | async-start | bytes 655360 | tf_op jit(solution)/shard_map/all_to_all | solution.py:500
  157.9 24.5 %all-to-all-start.5 = ((f32[16,4,8,256]{3,2,1,0:T(8,128)}), f32[16,4,8,256]{3,2,1,0:T(8,128)S(1)}, u32[]{:S(2)}, u32[]{:S(2)}) async-start(f32[16,4,8,256]{3,2,1,0:T(8,128)} %get-tuple-element.60), calls=%async_computation.5 | async-start | bytes 1048576 | tf_op jit(solution)/shard_map/all_to_all | solution.py:500
  169.1 13.3 %collective-permute-start.26 = (f32[2,128,128]{2,1,0:T(8,128)S(1)}, f32[2,128,128]{2,1,0:T(8,128)S(1)}, u32[]{:S(2)}, u32[]{:S(2)}) collective-permute-start(f32[2,128,128]{2,1,0:T(8,128)S(1)} %get-tuple-element.63), channel_id=1, source_target_pairs={{1,2},{3,4},{5,6},{7,8},{9,10},{11,12},{13,14},{2,1},{4,3},{6,5},{... | collective-permute-start | bytes 393224 | tf_op jit(solution)/shard_map/ppermute | solution.py:567
  (13 other events, 48.3 us)

commit v11 on v10

--- a/solution.py
+++ b/solution.py
@@ -122,9 +122,15 @@
     def third(block):
         return pl.ds(block * TILE if isinstance(block, int) else pl.multiple_of(block * TILE, TILE), TILE)
 
-    for place, piece in enumerate(around_in):
-        rows, columns = third(across[place // 3]), third(along[place % 3])
-        start(piece.at[:, third(0)], padded.at[:, rows, columns])
+    if len(around_in) == 5:
+        bands = around_in[3:4], around_in[:3], around_in[4:]
+    else:
+        bands = around_in[:3], around_in[3:6], around_in[6:]
+    for row, band in enumerate(bands):
+        for column in range(3):
+            piece = band[0].at[column] if len(band) == 1 else band[column]
+            place = padded.at[:, third(across[row]), third(along[column])]
+            start(piece.at[:, third(0)], place)
     near = len(copies)
     if halves:
         for half, ref in enumerate(probe_in):
@@ -431,7 +437,7 @@
     return pl.pallas_call(
         functools.partial(step_kernel, halves),
         out_shape=[half, half, band, band, band, jax.ShapeDtypeStruct((SIDE, SIDE), F32)],
-        in_specs=[SMEM_SPEC, SMEM_SPEC] + [ANY_SPEC] * (12 + halves),
+        in_specs=[SMEM_SPEC, SMEM_SPEC] + [ANY_SPEC] * (3 + halves + len(around)),
         out_specs=[ANY_SPEC] * 5 + [VMEM_SPEC],
         scratch_shapes=[
             pltpu.VMEM(table.shape, BF16),
@@ -472,6 +478,13 @@
         first,
         lax.ppermute(first, "col", pairs(0)),
     )
+
+
+def band_neighbourhood(tile):
+    outer, inner = lax.ppermute(tile, "col", pairs(1)), lax.ppermute(tile, "col", pairs(0))
+    band = jnp.stack([outer, tile, inner])
+    second, first = lax.ppermute(band, "row", pairs(1)), lax.ppermute(band, "row", pairs(0))
+    return outer, tile, inner, second, first
 
 
 def after(value, other):
@@ -570,9 +583,10 @@
         totals = after(own, old) + inner + outer
         tile = tile + OBJECT_STEP * totals / (weight + OBJECT_REG)
         if iteration + 1 < ITERS:
-            around = neighbourhood(tile)
+            around = band_neighbourhood(tile)
         mine = exchange(pieces, PLANES)
-        mine = after(mine, around[1::2] if iteration + 1 < ITERS else (inner, outer))
+        if iteration + 1 == ITERS:
+            mine = after(mine, (inner, outer))
         parts = (mine, lax.ppermute(mine, "col", SWAP))
     probe = pl.pallas_call(
         lay_out_kernel,

time: 187 us -> 184 us (0.984)
  starting transfers between devices: 96.2 us -> 83.9 us
  waiting for transfers between devices: 50 us -> 58 us
    ppermute x0 -> x4, waiting for transfers between devices: none -> 16 us  [the longest x1 7.32 us: band_neighbourhood(): lax.ppermute(tile, 'col', pairs(1))]
    ppermute x0 -> x4, starting transfers between devices: none -> 6.88 us  [the longest x1 3.68 us: band_neighbourhood(): lax.ppermute(tile, 'col', pairs(1))]
    all_to_all x6, starting transfers between devices: 38.1 us -> 31.6 us  [exchange(): lax.all_to_all(value, BOTH, 0, 0, axis_index_groups=groups, tiled=True)]
    ppermute x2 -> x1, waiting for transfers between devices: 6.47 us -> 0.01 us  [neighbourhood(): lax.ppermute(tile, 'col', pairs(1))]
    ppermute x2 -> x1, starting transfers between devices: 12.4 us -> 8.39 us  [neighbourhood(): lax.ppermute(tile, 'col', pairs(1))]
    ppermute x2 -> x1, waiting for transfers between devices: 7.05 us -> 3.09 us  [neighbourhood(): lax.ppermute(outer, 'row', pairs(1))]
    all_to_all x6, waiting for transfers between devices: 12.8 us -> 16.4 us  [exchange(): lax.all_to_all(value, BOTH, 0, 0, axis_index_groups=groups, tiled=True)]
    ppermute x2 -> x1, starting transfers between devices: 7.41 us -> 4.24 us  [neighbourhood(): lax.ppermute(tile, 'row', pairs(1))]
  transfers between devices with their start and end apart: 34 -> 30, of which waited for: 15 -> 16; matrix products, arithmetic and copies ran while one was open for 2% -> 2% of each run, Pallas kernels for 5% -> 5%
where the time goes in v11:
time: 184 us; the launch traced here: 183 us
  starting transfers between devices  83.9 us (46%)
  waiting for transfers between devices  58 us (32%)
  Pallas kernels  31.1 us (17%)
  other arithmetic  6.66 us (4%)
  local copies, waits for them, and re-layouts  2.03 us (1%)
    all_to_all x6, starting transfers between devices, exchange(): lax.all_to_all(value, BOTH, 0, 0, axis_index_groups=groups, tiled=True)  31.6 us
    pallas_call x2, Pallas kernels, step(): pl.pallas_call(functools.partial(step_kernel, halves), out_shape=[half, h...  19.4 us
    all_to_all x6, waiting for transfers between devices, exchange(): lax.all_to_all(value, BOTH, 0, 0, axis_index_groups=groups, tiled=True)  16.4 us
    ppermute x2, waiting for transfers between devices, local(): outer = lax.ppermute(outer, 'col', pairs(1))  14.7 us
    ppermute x2, starting transfers between devices, local(): inner = lax.ppermute(inner, 'col', pairs(0))  8.58 us
    ppermute x1, starting transfers between devices, neighbourhood(): lax.ppermute(tile, 'col', pairs(1))  8.39 us
    ppermute x1, waiting for transfers between devices, band_neighbourhood(): lax.ppermute(tile, 'col', pairs(1))  7.32 us
    ppermute x2, starting transfers between devices, local(): second = lax.ppermute(after(second, mine), 'row', pairs(1))  6.04 us
  transfers between devices with their start and end apart: 30, of which 16 were waited for; matrix products, arithmetic and copies ran while one was open for 2% of the time, Pallas kernels for 5%

profile of v11, /device:TPU:39, one launch (start us, length us, event | category | flops | bytes accessed | tf_op | source)
XLA Modules:
  0.0 182.6 jit_solution(6099679778801227335)
XLA Ops:
  2.3 8.4 %collective-permute-start = (f32[2,136,128]{2,1,0:T(8,128)S(1)}, f32[2,136,128]{2,1,0:T(8,128)S(1)}, u32[]{:S(2)}, u32[]{:S(2)}) collective-permute-start(f32[2,136,128]{2,1,0:T(8,128)S(1)} %select_maximum_fusion.refs_6_), channel_id=1, source_target_pairs={{1,2},{3,4},{5,6},{7,8},{9,10},{11,12},{13,14},{2,1},{4,3},{6,5},{... | collective-permute-start | bytes 417800 | tf_op jit(solution)/shard_map/ppermute | solution.py:468
  12.1 4.2 %collective-permute-start.2 = (f32[2,136,128]{2,1,0:T(8,128)S(1)}, f32[2,136,128]{2,1,0:T(8,128)S(1)}, u32[]{:S(2)}, u32[]{:S(2)}) collective-permute-start(f32[2,136,128]{2,1,0:T(8,128)S(1)} %select_maximum_fusion.refs_6_), channel_id=1, source_target_pairs={{16,32},{48,64},{80,96},{112,128},{144,160},{176,192},{208,224},{3... | collective-permute-start | bytes 417800 | tf_op jit(solution)/shard_map/ppermute | solution.py:469
  18.6 3.1 %collective-permute-start.1 = (f32[2,136,128]{2,1,0:T(8,128)S(1)}, f32[2,136,128]{2,1,0:T(8,128)S(1)}, u32[]{:S(2)}, u32[]{:S(2)}) collective-permute-start(f32[2,136,128]{2,1,0:T(8,128)S(1)} %collective-permute-done.refs_5_), channel_id=1, source_target_pairs={{16,32},{48,64},{80,96},{112,128},{144,160},{176,192},{208,224},{3... | collective-permute-start | bytes 417800 | tf_op jit(solution)/shard_map/ppermute | solution.py:471
  24.0 3.1 %collective-permute-done.1.refs_2_ = f32[2,136,128]{2,1,0:T(8,128)S(1)} collective-permute-done((f32[2,136,128]{2,1,0:T(8,128)S(1)}, f32[2,136,128]{2,1,0:T(8,128)S(1)}, u32[]{:S(2)}, u32[]{:S(2)}) %collective-permute-start.1) | collective-permute-done | bytes 139296 | tf_op jit(solution)/shard_map/ppermute | solution.py:471
  27.1 9.8 %step.2 = (f32[16,5,8,256]{3,2,1,0:T(8,128)S(1)}, f32[16,5,8,256]{3,2,1,0:T(8,128)S(1)}, f32[3,2,128,128]{3,2,1,0:T(8,128)S(1)}, f32[3,2,128,128]{3,2,1,0:T(8,12...) custom-call(s32[1,1,2,2]{3,2,1,0:T(2,128)S(1)} %copy-done.1, s32[2]{0:T(128)S(1)} %pad_add_fusion.parity_ref, ...), custom_call_target="tpu_custom_call" | custom-call | tf_op jit(solution)/shard_map/step/pallas_call | solution.py:437
  41.2 4.5 %all-to-all-start = ((f32[16,5,8,256]{3,2,1,0:T(8,128)}), f32[16,5,8,256]{3,2,1,0:T(8,128)S(1)}, u32[]{:S(2)}, u32[]{:S(2)}) async-start(f32[16,5,8,256]{3,2,1,0:T(8,128)} %add.106), calls=%async_computation | async-start | bytes 1310720 | tf_op jit(solution)/shard_map/all_to_all | solution.py:513
  47.0 4.1 %collective-permute-start.10 = (f32[3,2,128,128]{3,2,1,0:T(8,128)S(1)}, f32[3,2,128,128]{3,2,1,0:T(8,128)}, u32[]{:S(2)}, u32[]{:S(2)}) collective-permute-start(f32[3,2,128,128]{3,2,1,0:T(8,128)S(1)} %get-tuple-element.41), channel_id=1, source_target_pairs={{16,32},{48,64},{80,96},{112,128},{144,160},{176,192},{208,224},{3... | collective-permute-start | bytes 1179656 | tf_op jit(solution)/shard_map/ppermute | solution.py:573
  56.3 8.1 %all-to-all-start.1 = ((f32[8,5,8,256]{3,2,1,0:T(8,128)}), f32[8,5,8,256]{3,2,1,0:T(8,128)S(1)}, u32[]{:S(2)}, u32[]{:S(2)}) async-start(f32[8,5,8,256]{3,2,1,0:T(8,128)} %spread.2), calls=%async_computation.1 | async-start | bytes 655360 | tf_op jit(solution)/shard_map/all_to_all | solution.py:513
  66.4 7.5 %collective-permute-start.11 = (f32[2,128,128]{2,1,0:T(8,128)S(1)}, f32[2,128,128]{2,1,0:T(8,128)S(1)}, u32[]{:S(2)}, u32[]{:S(2)}) collective-permute-start(f32[2,128,128]{2,1,0:T(8,128)S(1)} %get-tuple-element.63), channel_id=1, source_target_pairs={{0,1},{2,3},{4,5},{6,7},{8,9},{10,11},{12,13},{14,15},{1,0},{3,2},... | collective-permute-start | bytes 393224 | tf_op jit(solution)/shard_map/ppermute | solution.py:579
  76.9 5.1 %all-to-all-start.2 = ((f32[16,4,8,256]{3,2,1,0:T(8,128)}), f32[16,4,8,256]{3,2,1,0:T(8,128)S(1)}, u32[]{:S(2)}, u32[]{:S(2)}) async-start(f32[16,4,8,256]{3,2,1,0:T(8,128)} %get-tuple-element.45), calls=%async_computation.2 | async-start | bytes 1048576 | tf_op jit(solution)/shard_map/all_to_all | solution.py:513
  82.1 4.9 %collective-permute-done.12 = f32[2,128,128]{2,1,0:T(8,128)S(1)} collective-permute-done((f32[2,128,128]{2,1,0:T(8,128)S(1)}, f32[2,128,128]{2,1,0:T(8,128)S(1)}, u32[]{:S(2)}, u32[]{:S(2)}) %collective-permute-start.12) | collective-permute-done | bytes 131104 | tf_op jit(solution)/shard_map/ppermute | solution.py:580
  87.6 3.7 %collective-permute-start.14 = (f32[2,128,128]{2,1,0:T(8,128)S(1)}, f32[2,128,128]{2,1,0:T(8,128)S(1)}, u32[]{:S(2)}, u32[]{:S(2)}) collective-permute-start(f32[2,128,128]{2,1,0:T(8,128)S(1)} %divide_add_fusion.1.refs_4_), channel_id=1, source_target_pairs={{1,2},{3,4},{5,6},{7,8},{9,10},{11,12},{13,14},{2,1},{4,3},{6,5},{... | collective-permute-start | bytes 393224 | tf_op jit(solution)/shard_map/ppermute | solution.py:484
  94.0 7.3 %collective-permute-done.14.refs_3_ = f32[2,128,128]{2,1,0:T(8,128)S(1)} collective-permute-done((f32[2,128,128]{2,1,0:T(8,128)S(1)}, f32[2,128,128]{2,1,0:T(8,128)S(1)}, u32[]{:S(2)}, u32[]{:S(2)}) %collective-permute-start.14) | collective-permute-done | bytes 131104 | tf_op jit(solution)/shard_map/ppermute | solution.py:484
  104.0 4.1 %collective-permute-done.17.refs_7_ = f32[3,2,128,128]{3,2,1,0:T(8,128)S(1)} collective-permute-done((f32[3,2,128,128]{3,2,1,0:T(8,128)S(1)}, f32[3,2,128,128]{3,2,1,0:T(8,128)S(1)}, u32[]{:S(2)}, u32[]{:S(2)}) %collective-permute-start.17) | collective-permute-done | bytes 393248 | tf_op jit(solution)/shard_map/ppermute | solution.py:486
  108.1 4.6 %collective-permute-done.16.refs_6_ = f32[3,2,128,128]{3,2,1,0:T(8,128)S(1)} collective-permute-done((f32[3,2,128,128]{3,2,1,0:T(8,128)S(1)}, f32[3,2,128,128]{3,2,1,0:T(8,128)S(1)}, u32[]{:S(2)}, u32[]{:S(2)}) %collective-permute-start.16) | collective-permute-done | bytes 393248 | tf_op jit(solution)/shard_map/ppermute | solution.py:486
  112.7 9.6 %step.3 = (f32[16,5,8,256]{3,2,1,0:T(8,128)S(1)}, f32[16,5,8,256]{3,2,1,0:T(8,128)S(1)}, f32[3,2,128,128]{3,2,1,0:T(8,128)S(1)}, f32[3,2,128,128]{3,2,1,0:T(8,12...) custom-call(s32[1,1,2,2]{3,2,1,0:T(2,128)S(1)} %copy-done.1, s32[2]{0:T(128)S(1)} %pad_add_fusion.parity_ref, ...), custom_call_target="tpu_custom_call" | custom-call | tf_op jit(solution)/shard_map/step/pallas_call | solution.py:437
  125.5 5.5 %all-to-all-start.3 = ((f32[16,5,8,256]{3,2,1,0:T(8,128)}), f32[16,5,8,256]{3,2,1,0:T(8,128)S(1)}, u32[]{:S(2)}, u32[]{:S(2)}) async-start(f32[16,5,8,256]{3,2,1,0:T(8,128)} %add.123), calls=%async_computation.3 | async-start | bytes 1310720 | tf_op jit(solution)/shard_map/all_to_all | solution.py:513
  134.1 3.0 %weigh.3 = f32[128,128]{1,0:T(8,128)S(1)} custom-call(s32[2]{0:T(128)S(1)} %pad_add_fusion.parity_ref, s32[9,4]{1,0:T(8,128)S(1)} %convert_element_type.9.near_ref, f32[256,256]{1,0:T(8,128)S(1)} %get-tuple-element.50.power_ref), custom_call_target="tpu_custom_call" | custom-call | tf_op jit(solution)/shard_map/weigh/pallas_call | solution.py:517
  137.1 6.3 %all-to-all-done.3.pieces_ref = f32[16,5,8,256]{3,2,1,0:T(8,128)S(1)} async-done(((f32[16,5,8,256]{3,2,1,0:T(8,128)}), f32[16,5,8,256]{3,2,1,0:T(8,128)S(1)}, u32[]{:S(2)}, u32[]{:S(2)}) %all-to-all-start.3) | async-done | bytes 655392 | tf_op jit(solution)/shard_map/all_to_all | solution.py:513
  144.1 3.4 %all-to-all-start.4 = ((f32[8,5,8,256]{3,2,1,0:T(8,128)}), f32[8,5,8,256]{3,2,1,0:T(8,128)S(1)}, u32[]{:S(2)}, u32[]{:S(2)}) async-start(f32[8,5,8,256]{3,2,1,0:T(8,128)} %spread.3), calls=%async_computation.4 | async-start | bytes 655360 | tf_op jit(solution)/shard_map/all_to_all | solution.py:513
  150.1 8.8 %all-to-all-done.4.pieces_ref = f32[8,5,8,256]{3,2,1,0:T(8,128)S(1)} async-done(((f32[8,5,8,256]{3,2,1,0:T(8,128)}), f32[8,5,8,256]{3,2,1,0:T(8,128)S(1)}, u32[]{:S(2)}, u32[]{:S(2)}) %all-to-all-start.4) | async-done | bytes 327712 | tf_op jit(solution)/shard_map/all_to_all | solution.py:513
  159.7 5.1 %all-to-all-start.5 = ((f32[16,4,8,256]{3,2,1,0:T(8,128)}), f32[16,4,8,256]{3,2,1,0:T(8,128)S(1)}, u32[]{:S(2)}, u32[]{:S(2)}) async-start(f32[16,4,8,256]{3,2,1,0:T(8,128)} %get-tuple-element.58), calls=%async_computation.5 | async-start | bytes 1048576 | tf_op jit(solution)/shard_map/all_to_all | solution.py:513
  165.9 3.4 %collective-permute-start.22 = (f32[2,128,128]{2,1,0:T(8,128)S(1)}, f32[2,128,128]{2,1,0:T(8,128)S(1)}, u32[]{:S(2)}, u32[]{:S(2)}) collective-permute-start(f32[2,128,128]{2,1,0:T(8,128)S(1)} %get-tuple-element.61), channel_id=1, source_target_pairs={{1,2},{3,4},{5,6},{7,8},{9,10},{11,12},{13,14},{2,1},{4,3},{6,5},{... | collective-permute-start | bytes 393224 | tf_op jit(solution)/shard_map/ppermute | solution.py:580
  169.3 9.8 %collective-permute-done.22 = f32[2,128,128]{2,1,0:T(8,128)S(1)} collective-permute-done((f32[2,128,128]{2,1,0:T(8,128)S(1)}, f32[2,128,128]{2,1,0:T(8,128)S(1)}, u32[]{:S(2)}, u32[]{:S(2)}) %collective-permute-start.22) | collective-permute-done | bytes 131104 | tf_op jit(solution)/shard_map/ppermute | solution.py:580
  (77 shorter events, 44.4 us)
Async XLA Ops:
  2.3 16.2 %collective-permute-start = (f32[2,136,128]{2,1,0:T(8,128)S(1)}, f32[2,136,128]{2,1,0:T(8,128)S(1)}, u32[]{:S(2)}, u32[]{:S(2)}) collective-permute-start(f32[2,136,128]{2,1,0:T(8,128)S(1)} %select_maximum_fusion.refs_6_), channel_id=1, source_target_pairs={{1,2},{3,4},{5,6},{7,8},{9,10},{11,12},{13,14},{2,1},{4,3},{6,5},{... | collective-permute-start | bytes 417800 | tf_op jit(solution)/shard_map/ppermute | solution.py:468
  10.7 11.0 %collective-permute-start.6 = (f32[2,136,128]{2,1,0:T(8,128)S(1)}, f32[2,136,128]{2,1,0:T(8,128)S(1)}, u32[]{:S(2)}, u32[]{:S(2)}) collective-permute-start(f32[2,136,128]{2,1,0:T(8,128)S(1)} %select_maximum_fusion.refs_6_), channel_id=1, source_target_pairs={{0,16},{32,48},{64,80},{96,112},{128,144},{160,176},{192,208},{224... | collective-permute-start | bytes 417800 | tf_op jit(solution)/shard_map/ppermute | solution.py:469
  12.1 10.6 %collective-permute-start.2 = (f32[2,136,128]{2,1,0:T(8,128)S(1)}, f32[2,136,128]{2,1,0:T(8,128)S(1)}, u32[]{:S(2)}, u32[]{:S(2)}) collective-permute-start(f32[2,136,128]{2,1,0:T(8,128)S(1)} %select_maximum_fusion.refs_6_), channel_id=1, source_target_pairs={{16,32},{48,64},{80,96},{112,128},{144,160},{176,192},{208,224},{3... | collective-permute-start | bytes 417800 | tf_op jit(solution)/shard_map/ppermute | solution.py:469
  16.3 6.4 %collective-permute-start.4 = (f32[2,136,128]{2,1,0:T(8,128)S(1)}, f32[2,136,128]{2,1,0:T(8,128)S(1)}, u32[]{:S(2)}, u32[]{:S(2)}) collective-permute-start(f32[2,136,128]{2,1,0:T(8,128)S(1)} %select_maximum_fusion.refs_6_), channel_id=1, source_target_pairs={{0,1},{2,3},{4,5},{6,7},{8,9},{10,11},{12,13},{14,15},{1,0},{3,2},... | collective-permute-start | bytes 417800 | tf_op jit(solution)/shard_map/ppermute | solution.py:468
  18.5 5.5 %collective-permute-start.5 = (f32[2,136,128]{2,1,0:T(8,128)S(1)}, f32[2,136,128]{2,1,0:T(8,128)S(1)}, u32[]{:S(2)}, u32[]{:S(2)}) collective-permute-start(f32[2,136,128]{2,1,0:T(8,128)S(1)} %collective-permute-done.refs_5_), channel_id=1, source_target_pairs={{0,16},{32,48},{64,80},{96,112},{128,144},{160,176},{192,208},{224... | collective-permute-start | bytes 417800 | tf_op jit(solution)/shard_map/ppermute | solution.py:477
  18.6 8.5 %collective-permute-start.1 = (f32[2,136,128]{2,1,0:T(8,128)S(1)}, f32[2,136,128]{2,1,0:T(8,128)S(1)}, u32[]{:S(2)}, u32[]{:S(2)}) collective-permute-start(f32[2,136,128]{2,1,0:T(8,128)S(1)} %collective-permute-done.refs_5_), channel_id=1, source_target_pairs={{16,32},{48,64},{80,96},{112,128},{144,160},{176,192},{208,224},{3... | collective-permute-start | bytes 417800 | tf_op jit(solution)/shard_map/ppermute | solution.py:471
  41.2 14.3 %all-to-all-start = ((f32[16,5,8,256]{3,2,1,0:T(8,128)}), f32[16,5,8,256]{3,2,1,0:T(8,128)S(1)}, u32[]{:S(2)}, u32[]{:S(2)}) async-start(f32[16,5,8,256]{3,2,1,0:T(8,128)} %add.106), calls=%async_computation | async-start | bytes 1310720 | tf_op jit(solution)/shard_map/all_to_all | solution.py:513
  45.7 19.5 %collective-permute-start.9 = (f32[3,2,128,128]{3,2,1,0:T(8,128)S(1)}, f32[3,2,128,128]{3,2,1,0:T(8,128)}, u32[]{:S(2)}, u32[]{:S(2)}) collective-permute-start(f32[3,2,128,128]{3,2,1,0:T(8,128)S(1)} %get-tuple-element.39), channel_id=1, source_target_pairs={{0,16},{32,48},{64,80},{96,112},{128,144},{160,176},{192,208},{224... | collective-permute-start | bytes 1179656 | tf_op jit(solution)/shard_map/ppermute | solution.py:572
  47.0 18.2 %collective-permute-start.10 = (f32[3,2,128,128]{3,2,1,0:T(8,128)S(1)}, f32[3,2,128,128]{3,2,1,0:T(8,128)}, u32[]{:S(2)}, u32[]{:S(2)}) collective-permute-start(f32[3,2,128,128]{3,2,1,0:T(8,128)S(1)} %get-tuple-element.41), channel_id=1, source_target_pairs={{16,32},{48,64},{80,96},{112,128},{144,160},{176,192},{208,224},{3... | collective-permute-start | bytes 1179656 | tf_op jit(solution)/shard_map/ppermute | solution.py:573
  56.3 19.8 %all-to-all-start.1 = ((f32[8,5,8,256]{3,2,1,0:T(8,128)}), f32[8,5,8,256]{3,2,1,0:T(8,128)S(1)}, u32[]{:S(2)}, u32[]{:S(2)}) async-start(f32[8,5,8,256]{3,2,1,0:T(8,128)} %spread.2), calls=%async_computation.1 | async-start | bytes 655360 | tf_op jit(solution)/shard_map/all_to_all | solution.py:513
  66.4 15.6 %collective-permute-start.11 = (f32[2,128,128]{2,1,0:T(8,128)S(1)}, f32[2,128,128]{2,1,0:T(8,128)S(1)}, u32[]{:S(2)}, u32[]{:S(2)}) collective-permute-start(f32[2,128,128]{2,1,0:T(8,128)S(1)} %get-tuple-element.63), channel_id=1, source_target_pairs={{0,1},{2,3},{4,5},{6,7},{8,9},{10,11},{12,13},{14,15},{1,0},{3,2},... | collective-permute-start | bytes 393224 | tf_op jit(solution)/shard_map/ppermute | solution.py:579
  74.0 13.0 %collective-permute-start.12 = (f32[2,128,128]{2,1,0:T(8,128)S(1)}, f32[2,128,128]{2,1,0:T(8,128)S(1)}, u32[]{:S(2)}, u32[]{:S(2)}) collective-permute-start(f32[2,128,128]{2,1,0:T(8,128)S(1)} %get-tuple-element.64), channel_id=1, source_target_pairs={{1,2},{3,4},{5,6},{7,8},{9,10},{11,12},{13,14},{2,1},{4,3},{6,5},{... | collective-permute-start | bytes 393224 | tf_op jit(solution)/shard_map/ppermute | solution.py:580
  76.9 14.3 %all-to-all-start.2 = ((f32[16,4,8,256]{3,2,1,0:T(8,128)}), f32[16,4,8,256]{3,2,1,0:T(8,128)S(1)}, u32[]{:S(2)}, u32[]{:S(2)}) async-start(f32[16,4,8,256]{3,2,1,0:T(8,128)} %get-tuple-element.45), calls=%async_computation.2 | async-start | bytes 1048576 | tf_op jit(solution)/shard_map/all_to_all | solution.py:513
  87.0 7.0 %collective-permute-start.15 = (f32[2,128,128]{2,1,0:T(8,128)S(1)}, f32[2,128,128]{2,1,0:T(8,128)S(1)}, u32[]{:S(2)}, u32[]{:S(2)}) collective-permute-start(f32[2,128,128]{2,1,0:T(8,128)S(1)} %divide_add_fusion.1.refs_4_), channel_id=1, source_target_pairs={{0,1},{2,3},{4,5},{6,7},{8,9},{10,11},{12,13},{14,15},{1,0},{3,2},... | collective-permute-start | bytes 393224 | tf_op jit(solution)/shard_map/ppermute | solution.py:484
  87.6 13.8 %collective-permute-start.14 = (f32[2,128,128]{2,1,0:T(8,128)S(1)}, f32[2,128,128]{2,1,0:T(8,128)S(1)}, u32[]{:S(2)}, u32[]{:S(2)}) collective-permute-start(f32[2,128,128]{2,1,0:T(8,128)S(1)} %divide_add_fusion.1.refs_4_), channel_id=1, source_target_pairs={{1,2},{3,4},{5,6},{7,8},{9,10},{11,12},{13,14},{2,1},{4,3},{6,5},{... | collective-permute-start | bytes 393224 | tf_op jit(solution)/shard_map/ppermute | solution.py:484
  91.3 21.5 %collective-permute-start.13 = (f32[16,4,8,256]{3,2,1,0:T(8,128)S(1)}, f32[16,4,8,256]{3,2,1,0:T(8,128)S(1)}, u32[]{:S(2)}, u32[]{:S(2)}) collective-permute-start(f32[16,4,8,256]{3,2,1,0:T(8,128)S(1)} %all-to-all-done.2.refs_0_), channel_id=1, source_target_pairs={{0,1},{1,0},{2,3},{3,2},{4,5},{5,4},{6,7},{7,6},{8,9},{9,8},{10,11... | collective-permute-start | bytes 1572872 | tf_op jit(solution)/shard_map/ppermute | solution.py:590
  101.4 6.7 %collective-permute-start.17 = (f32[3,2,128,128]{3,2,1,0:T(8,128)S(1)}, f32[3,2,128,128]{3,2,1,0:T(8,128)S(1)}, u32[]{:S(2)}, u32[]{:S(2)}) collective-permute-start(f32[3,2,128,128]{3,2,1,0:T(8,128)S(1)} %pad_maximum_fusion), channel_id=1, source_target_pairs={{0,16},{32,48},{64,80},{96,112},{128,144},{160,176},{192,208},{224... | collective-permute-start | bytes 1179656 | tf_op jit(solution)/shard_map/ppermute | solution.py:486
  102.1 10.6 %collective-permute-start.16 = (f32[3,2,128,128]{3,2,1,0:T(8,128)S(1)}, f32[3,2,128,128]{3,2,1,0:T(8,128)S(1)}, u32[]{:S(2)}, u32[]{:S(2)}) collective-permute-start(f32[3,2,128,128]{3,2,1,0:T(8,128)S(1)} %pad_maximum_fusion), channel_id=1, source_target_pairs={{16,32},{48,64},{80,96},{112,128},{144,160},{176,192},{208,224},{3... | collective-permute-start | bytes 1179656 | tf_op jit(solution)/shard_map/ppermute | solution.py:486
  125.5 17.9 %all-to-all-start.3 = ((f32[16,5,8,256]{3,2,1,0:T(8,128)}), f32[16,5,8,256]{3,2,1,0:T(8,128)S(1)}, u32[]{:S(2)}, u32[]{:S(2)}) async-start(f32[16,5,8,256]{3,2,1,0:T(8,128)} %add.123), calls=%async_computation.3 | async-start | bytes 1310720 | tf_op jit(solution)/shard_map/all_to_all | solution.py:513
  131.0 17.3 %collective-permute-start.19 = (f32[3,2,128,128]{3,2,1,0:T(8,128)S(1)}, f32[3,2,128,128]{3,2,1,0:T(8,128)S(1)}, u32[]{:S(2)}, u32[]{:S(2)}) collective-permute-start(f32[3,2,128,128]{3,2,1,0:T(8,128)S(1)} %get-tuple-element.54), channel_id=1, source_target_pairs={{0,16},{32,48},{64,80},{96,112},{128,144},{160,176},{192,208},{224... | collective-permute-start | bytes 1179656 | tf_op jit(solution)/shard_map/ppermute | solution.py:572
  132.1 16.9 %collective-permute-start.20 = (f32[3,2,128,128]{3,2,1,0:T(8,128)S(1)}, f32[3,2,128,128]{3,2,1,0:T(8,128)}, u32[]{:S(2)}, u32[]{:S(2)}) collective-permute-start(f32[3,2,128,128]{3,2,1,0:T(8,128)S(1)} %get-tuple-element.56), channel_id=1, source_target_pairs={{16,32},{48,64},{80,96},{112,128},{144,160},{176,192},{208,224},{3... | collective-permute-start | bytes 1179656 | tf_op jit(solution)/shard_map/ppermute | solution.py:573
  144.1 14.8 %all-to-all-start.4 = ((f32[8,5,8,256]{3,2,1,0:T(8,128)}), f32[8,5,8,256]{3,2,1,0:T(8,128)S(1)}, u32[]{:S(2)}, u32[]{:S(2)}) async-start(f32[8,5,8,256]{3,2,1,0:T(8,128)} %spread.3), calls=%async_computation.4 | async-start | bytes 655360 | tf_op jit(solution)/shard_map/all_to_all | solution.py:513
  159.7 19.4 %all-to-all-start.5 = ((f32[16,4,8,256]{3,2,1,0:T(8,128)}), f32[16,4,8,256]{3,2,1,0:T(8,128)S(1)}, u32[]{:S(2)}, u32[]{:S(2)}) async-start(f32[16,4,8,256]{3,2,1,0:T(8,128)} %get-tuple-element.58), calls=%async_computation.5 | async-start | bytes 1048576 | tf_op jit(solution)/shard_map/all_to_all | solution.py:513
  165.9 13.3 %collective-permute-start.22 = (f32[2,128,128]{2,1,0:T(8,128)S(1)}, f32[2,128,128]{2,1,0:T(8,128)S(1)}, u32[]{:S(2)}, u32[]{:S(2)}) collective-permute-start(f32[2,128,128]{2,1,0:T(8,128)S(1)} %get-tuple-element.61), channel_id=1, source_target_pairs={{1,2},{3,4},{5,6},{7,8},{9,10},{11,12},{13,14},{2,1},{4,3},{6,5},{... | collective-permute-start | bytes 393224 | tf_op jit(solution)/shard_map/ppermute | solution.py:580
  (9 other events, 25.5 us)

commit v12 on v11

--- a/solution.py
+++ b/solution.py
@@ -175,7 +175,7 @@
                     )
         return carry
 
-    lax.fori_loop(0, 2, cut, 0)
+    lax.fori_loop(0, 2, cut, 0, unroll=2)
     for copy in copies[near:operands]:
         copy.wait()
 
@@ -237,7 +237,7 @@
         return carry
 
     copies[operands].wait()
-    lax.fori_loop(0, 4, scale, 0)
+    lax.fori_loop(0, 4, scale, 0, unroll=4)
 
     def backward(image, carry):
         scan, mode = image // 2, image % 2

time: 184 us -> 184 us (level)
  no operation moved by 1% of the time
where the time goes in v12:
time: 184 us; the launch traced here: 182 us
  starting transfers between devices  83.9 us (46%)
  waiting for transfers between devices  58 us (32%)
  Pallas kernels  30.8 us (17%)
  other arithmetic  6.66 us (4%)
  local copies, waits for them, and re-layouts  2.03 us (1%)
    all_to_all x6, starting transfers between devices, exchange(): lax.all_to_all(value, BOTH, 0, 0, axis_index_groups=groups, tiled=True)  31.6 us
    pallas_call x2, Pallas kernels, step(): pl.pallas_call(functools.partial(step_kernel, halves), out_shape=[half, h...  19.1 us
    all_to_all x6, waiting for transfers between devices, exchange(): lax.all_to_all(value, BOTH, 0, 0, axis_index_groups=groups, tiled=True)  16.5 us
    ppermute x2, waiting for transfers between devices, local(): outer = lax.ppermute(outer, 'col', pairs(1))  14.7 us
    ppermute x2, starting transfers between devices, local(): inner = lax.ppermute(inner, 'col', pairs(0))  8.77 us
    ppermute x1, starting transfers between devices, neighbourhood(): lax.ppermute(tile, 'col', pairs(1))  8.39 us
    ppermute x1, waiting for transfers between devices, band_neighbourhood(): lax.ppermute(tile, 'col', pairs(1))  7.32 us
    ppermute x2, starting transfers between devices, local(): second = lax.ppermute(after(second, mine), 'row', pairs(1))  6.04 us
  transfers between devices with their start and end apart: 30, of which 16 were waited for; matrix products, arithmetic and copies ran while one was open for 2% of the time, Pallas kernels for 5%

profile of v12, /device:TPU:39, one launch (start us, length us, event | category | flops | bytes accessed | tf_op | source)
XLA Modules:
  0.0 182.3 jit_solution(3466505649285181496)
XLA Ops:
  2.3 8.4 %collective-permute-start = (f32[2,136,128]{2,1,0:T(8,128)S(1)}, f32[2,136,128]{2,1,0:T(8,128)S(1)}, u32[]{:S(2)}, u32[]{:S(2)}) collective-permute-start(f32[2,136,128]{2,1,0:T(8,128)S(1)} %select_maximum_fusion.refs_6_), channel_id=1, source_target_pairs={{1,2},{3,4},{5,6},{7,8},{9,10},{11,12},{13,14},{2,1},{4,3},{6,5},{... | collective-permute-start | bytes 417800 | tf_op jit(solution)/shard_map/ppermute | solution.py:468
  12.1 4.2 %collective-permute-start.2 = (f32[2,136,128]{2,1,0:T(8,128)S(1)}, f32[2,136,128]{2,1,0:T(8,128)S(1)}, u32[]{:S(2)}, u32[]{:S(2)}) collective-permute-start(f32[2,136,128]{2,1,0:T(8,128)S(1)} %select_maximum_fusion.refs_6_), channel_id=1, source_target_pairs={{16,32},{48,64},{80,96},{112,128},{144,160},{176,192},{208,224},{3... | collective-permute-start | bytes 417800 | tf_op jit(solution)/shard_map/ppermute | solution.py:469
  18.6 3.1 %collective-permute-start.1 = (f32[2,136,128]{2,1,0:T(8,128)S(1)}, f32[2,136,128]{2,1,0:T(8,128)S(1)}, u32[]{:S(2)}, u32[]{:S(2)}) collective-permute-start(f32[2,136,128]{2,1,0:T(8,128)S(1)} %collective-permute-done.refs_5_), channel_id=1, source_target_pairs={{16,32},{48,64},{80,96},{112,128},{144,160},{176,192},{208,224},{3... | collective-permute-start | bytes 417800 | tf_op jit(solution)/shard_map/ppermute | solution.py:471
  24.0 3.1 %collective-permute-done.1.refs_2_ = f32[2,136,128]{2,1,0:T(8,128)S(1)} collective-permute-done((f32[2,136,128]{2,1,0:T(8,128)S(1)}, f32[2,136,128]{2,1,0:T(8,128)S(1)}, u32[]{:S(2)}, u32[]{:S(2)}) %collective-permute-start.1) | collective-permute-done | bytes 139296 | tf_op jit(solution)/shard_map/ppermute | solution.py:471
  27.1 9.6 %step.2 = (f32[16,5,8,256]{3,2,1,0:T(8,128)S(1)}, f32[16,5,8,256]{3,2,1,0:T(8,128)S(1)}, f32[3,2,128,128]{3,2,1,0:T(8,128)S(1)}, f32[3,2,128,128]{3,2,1,0:T(8,12...) custom-call(s32[1,1,2,2]{3,2,1,0:T(2,128)S(1)} %copy-done.1, s32[2]{0:T(128)S(1)} %pad_add_fusion.parity_ref, ...), custom_call_target="tpu_custom_call" | custom-call | tf_op jit(solution)/shard_map/step/pallas_call | solution.py:437
  41.1 4.5 %all-to-all-start = ((f32[16,5,8,256]{3,2,1,0:T(8,128)}), f32[16,5,8,256]{3,2,1,0:T(8,128)S(1)}, u32[]{:S(2)}, u32[]{:S(2)}) async-start(f32[16,5,8,256]{3,2,1,0:T(8,128)} %add.106), calls=%async_computation | async-start | bytes 1310720 | tf_op jit(solution)/shard_map/all_to_all | solution.py:513
  46.8 4.1 %collective-permute-start.10 = (f32[3,2,128,128]{3,2,1,0:T(8,128)S(1)}, f32[3,2,128,128]{3,2,1,0:T(8,128)}, u32[]{:S(2)}, u32[]{:S(2)}) collective-permute-start(f32[3,2,128,128]{3,2,1,0:T(8,128)S(1)} %get-tuple-element.41), channel_id=1, source_target_pairs={{16,32},{48,64},{80,96},{112,128},{144,160},{176,192},{208,224},{3... | collective-permute-start | bytes 1179656 | tf_op jit(solution)/shard_map/ppermute | solution.py:573
  56.1 8.1 %all-to-all-start.1 = ((f32[8,5,8,256]{3,2,1,0:T(8,128)}), f32[8,5,8,256]{3,2,1,0:T(8,128)S(1)}, u32[]{:S(2)}, u32[]{:S(2)}) async-start(f32[8,5,8,256]{3,2,1,0:T(8,128)} %spread.2), calls=%async_computation.1 | async-start | bytes 655360 | tf_op jit(solution)/shard_map/all_to_all | solution.py:513
  66.3 7.7 %collective-permute-start.11 = (f32[2,128,128]{2,1,0:T(8,128)S(1)}, f32[2,128,128]{2,1,0:T(8,128)S(1)}, u32[]{:S(2)}, u32[]{:S(2)}) collective-permute-start(f32[2,128,128]{2,1,0:T(8,128)S(1)} %get-tuple-element.63), channel_id=1, source_target_pairs={{0,1},{2,3},{4,5},{6,7},{8,9},{10,11},{12,13},{14,15},{1,0},{3,2},... | collective-permute-start | bytes 393224 | tf_op jit(solution)/shard_map/ppermute | solution.py:579
  76.8 5.1 %all-to-all-start.2 = ((f32[16,4,8,256]{3,2,1,0:T(8,128)}), f32[16,4,8,256]{3,2,1,0:T(8,128)S(1)}, u32[]{:S(2)}, u32[]{:S(2)}) async-start(f32[16,4,8,256]{3,2,1,0:T(8,128)} %get-tuple-element.45), calls=%async_computation.2 | async-start | bytes 1048576 | tf_op jit(solution)/shard_map/all_to_all | solution.py:513
  81.9 4.9 %collective-permute-done.12 = f32[2,128,128]{2,1,0:T(8,128)S(1)} collective-permute-done((f32[2,128,128]{2,1,0:T(8,128)S(1)}, f32[2,128,128]{2,1,0:T(8,128)S(1)}, u32[]{:S(2)}, u32[]{:S(2)}) %collective-permute-start.12) | collective-permute-done | bytes 131104 | tf_op jit(solution)/shard_map/ppermute | solution.py:580
  87.4 3.7 %collective-permute-start.14 = (f32[2,128,128]{2,1,0:T(8,128)S(1)}, f32[2,128,128]{2,1,0:T(8,128)S(1)}, u32[]{:S(2)}, u32[]{:S(2)}) collective-permute-start(f32[2,128,128]{2,1,0:T(8,128)S(1)} %divide_add_fusion.1.refs_4_), channel_id=1, source_target_pairs={{1,2},{3,4},{5,6},{7,8},{9,10},{11,12},{13,14},{2,1},{4,3},{6,5},{... | collective-permute-start | bytes 393224 | tf_op jit(solution)/shard_map/ppermute | solution.py:484
  93.9 7.3 %collective-permute-done.14.refs_3_ = f32[2,128,128]{2,1,0:T(8,128)S(1)} collective-permute-done((f32[2,128,128]{2,1,0:T(8,128)S(1)}, f32[2,128,128]{2,1,0:T(8,128)S(1)}, u32[]{:S(2)}, u32[]{:S(2)}) %collective-permute-start.14) | collective-permute-done | bytes 131104 | tf_op jit(solution)/shard_map/ppermute | solution.py:484
  103.9 4.1 %collective-permute-done.17.refs_7_ = f32[3,2,128,128]{3,2,1,0:T(8,128)S(1)} collective-permute-done((f32[3,2,128,128]{3,2,1,0:T(8,128)S(1)}, f32[3,2,128,128]{3,2,1,0:T(8,128)S(1)}, u32[]{:S(2)}, u32[]{:S(2)}) %collective-permute-start.17) | collective-permute-done | bytes 393248 | tf_op jit(solution)/shard_map/ppermute | solution.py:486
  107.9 4.6 %collective-permute-done.16.refs_6_ = f32[3,2,128,128]{3,2,1,0:T(8,128)S(1)} collective-permute-done((f32[3,2,128,128]{3,2,1,0:T(8,128)S(1)}, f32[3,2,128,128]{3,2,1,0:T(8,128)S(1)}, u32[]{:S(2)}, u32[]{:S(2)}) %collective-permute-start.16) | collective-permute-done | bytes 393248 | tf_op jit(solution)/shard_map/ppermute | solution.py:486
  112.6 9.5 %step.3 = (f32[16,5,8,256]{3,2,1,0:T(8,128)S(1)}, f32[16,5,8,256]{3,2,1,0:T(8,128)S(1)}, f32[3,2,128,128]{3,2,1,0:T(8,128)S(1)}, f32[3,2,128,128]{3,2,1,0:T(8,12...) custom-call(s32[1,1,2,2]{3,2,1,0:T(2,128)S(1)} %copy-done.1, s32[2]{0:T(128)S(1)} %pad_add_fusion.parity_ref, ...), custom_call_target="tpu_custom_call" | custom-call | tf_op jit(solution)/shard_map/step/pallas_call | solution.py:437
  125.2 5.5 %all-to-all-start.3 = ((f32[16,5,8,256]{3,2,1,0:T(8,128)}), f32[16,5,8,256]{3,2,1,0:T(8,128)S(1)}, u32[]{:S(2)}, u32[]{:S(2)}) async-start(f32[16,5,8,256]{3,2,1,0:T(8,128)} %add.123), calls=%async_computation.3 | async-start | bytes 1310720 | tf_op jit(solution)/shard_map/all_to_all | solution.py:513
  133.7 3.0 %weigh.3 = f32[128,128]{1,0:T(8,128)S(1)} custom-call(s32[2]{0:T(128)S(1)} %pad_add_fusion.parity_ref, s32[9,4]{1,0:T(8,128)S(1)} %convert_element_type.9.near_ref, f32[256,256]{1,0:T(8,128)S(1)} %get-tuple-element.50.power_ref), custom_call_target="tpu_custom_call" | custom-call | tf_op jit(solution)/shard_map/weigh/pallas_call | solution.py:517
  136.7 6.3 %all-to-all-done.3.pieces_ref = f32[16,5,8,256]{3,2,1,0:T(8,128)S(1)} async-done(((f32[16,5,8,256]{3,2,1,0:T(8,128)}), f32[16,5,8,256]{3,2,1,0:T(8,128)S(1)}, u32[]{:S(2)}, u32[]{:S(2)}) %all-to-all-start.3) | async-done | bytes 655392 | tf_op jit(solution)/shard_map/all_to_all | solution.py:513
  143.8 3.4 %all-to-all-start.4 = ((f32[8,5,8,256]{3,2,1,0:T(8,128)}), f32[8,5,8,256]{3,2,1,0:T(8,128)S(1)}, u32[]{:S(2)}, u32[]{:S(2)}) async-start(f32[8,5,8,256]{3,2,1,0:T(8,128)} %spread.3), calls=%async_computation.4 | async-start | bytes 655360 | tf_op jit(solution)/shard_map/all_to_all | solution.py:513
  149.8 8.8 %all-to-all-done.4.pieces_ref = f32[8,5,8,256]{3,2,1,0:T(8,128)S(1)} async-done(((f32[8,5,8,256]{3,2,1,0:T(8,128)}), f32[8,5,8,256]{3,2,1,0:T(8,128)S(1)}, u32[]{:S(2)}, u32[]{:S(2)}) %all-to-all-start.4) | async-done | bytes 327712 | tf_op jit(solution)/shard_map/all_to_all | solution.py:513
  159.4 5.1 %all-to-all-start.5 = ((f32[16,4,8,256]{3,2,1,0:T(8,128)}), f32[16,4,8,256]{3,2,1,0:T(8,128)S(1)}, u32[]{:S(2)}, u32[]{:S(2)}) async-start(f32[16,4,8,256]{3,2,1,0:T(8,128)} %get-tuple-element.58), calls=%async_computation.5 | async-start | bytes 1048576 | tf_op jit(solution)/shard_map/all_to_all | solution.py:513
  165.5 3.4 %collective-permute-start.22 = (f32[2,128,128]{2,1,0:T(8,128)S(1)}, f32[2,128,128]{2,1,0:T(8,128)S(1)}, u32[]{:S(2)}, u32[]{:S(2)}) collective-permute-start(f32[2,128,128]{2,1,0:T(8,128)S(1)} %get-tuple-element.61), channel_id=1, source_target_pairs={{1,2},{3,4},{5,6},{7,8},{9,10},{11,12},{13,14},{2,1},{4,3},{6,5},{... | collective-permute-start | bytes 393224 | tf_op jit(solution)/shard_map/ppermute | solution.py:580
  169.0 9.8 %collective-permute-done.22 = f32[2,128,128]{2,1,0:T(8,128)S(1)} collective-permute-done((f32[2,128,128]{2,1,0:T(8,128)S(1)}, f32[2,128,128]{2,1,0:T(8,128)S(1)}, u32[]{:S(2)}, u32[]{:S(2)}) %collective-permute-start.22) | collective-permute-done | bytes 131104 | tf_op jit(solution)/shard_map/ppermute | solution.py:580
  (77 shorter events, 44.2 us)
Async XLA Ops:
  2.3 16.2 %collective-permute-start = (f32[2,136,128]{2,1,0:T(8,128)S(1)}, f32[2,136,128]{2,1,0:T(8,128)S(1)}, u32[]{:S(2)}, u32[]{:S(2)}) collective-permute-start(f32[2,136,128]{2,1,0:T(8,128)S(1)} %select_maximum_fusion.refs_6_), channel_id=1, source_target_pairs={{1,2},{3,4},{5,6},{7,8},{9,10},{11,12},{13,14},{2,1},{4,3},{6,5},{... | collective-permute-start | bytes 417800 | tf_op jit(solution)/shard_map/ppermute | solution.py:468
  10.7 11.0 %collective-permute-start.6 = (f32[2,136,128]{2,1,0:T(8,128)S(1)}, f32[2,136,128]{2,1,0:T(8,128)S(1)}, u32[]{:S(2)}, u32[]{:S(2)}) collective-permute-start(f32[2,136,128]{2,1,0:T(8,128)S(1)} %select_maximum_fusion.refs_6_), channel_id=1, source_target_pairs={{0,16},{32,48},{64,80},{96,112},{128,144},{160,176},{192,208},{224... | collective-permute-start | bytes 417800 | tf_op jit(solution)/shard_map/ppermute | solution.py:469
  12.1 10.6 %collective-permute-start.2 = (f32[2,136,128]{2,1,0:T(8,128)S(1)}, f32[2,136,128]{2,1,0:T(8,128)S(1)}, u32[]{:S(2)}, u32[]{:S(2)}) collective-permute-start(f32[2,136,128]{2,1,0:T(8,128)S(1)} %select_maximum_fusion.refs_6_), channel_id=1, source_target_pairs={{16,32},{48,64},{80,96},{112,128},{144,160},{176,192},{208,224},{3... | collective-permute-start | bytes 417800 | tf_op jit(solution)/shard_map/ppermute | solution.py:469
  16.3 6.4 %collective-permute-start.4 = (f32[2,136,128]{2,1,0:T(8,128)S(1)}, f32[2,136,128]{2,1,0:T(8,128)S(1)}, u32[]{:S(2)}, u32[]{:S(2)}) collective-permute-start(f32[2,136,128]{2,1,0:T(8,128)S(1)} %select_maximum_fusion.refs_6_), channel_id=1, source_target_pairs={{0,1},{2,3},{4,5},{6,7},{8,9},{10,11},{12,13},{14,15},{1,0},{3,2},... | collective-permute-start | bytes 417800 | tf_op jit(solution)/shard_map/ppermute | solution.py:468
  18.5 5.5 %collective-permute-start.5 = (f32[2,136,128]{2,1,0:T(8,128)S(1)}, f32[2,136,128]{2,1,0:T(8,128)S(1)}, u32[]{:S(2)}, u32[]{:S(2)}) collective-permute-start(f32[2,136,128]{2,1,0:T(8,128)S(1)} %collective-permute-done.refs_5_), channel_id=1, source_target_pairs={{0,16},{32,48},{64,80},{96,112},{128,144},{160,176},{192,208},{224... | collective-permute-start | bytes 417800 | tf_op jit(solution)/shard_map/ppermute | solution.py:477
  18.6 8.5 %collective-permute-start.1 = (f32[2,136,128]{2,1,0:T(8,128)S(1)}, f32[2,136,128]{2,1,0:T(8,128)S(1)}, u32[]{:S(2)}, u32[]{:S(2)}) collective-permute-start(f32[2,136,128]{2,1,0:T(8,128)S(1)} %collective-permute-done.refs_5_), channel_id=1, source_target_pairs={{16,32},{48,64},{80,96},{112,128},{144,160},{176,192},{208,224},{3... | collective-permute-start | bytes 417800 | tf_op jit(solution)/shard_map/ppermute | solution.py:471
  41.1 14.3 %all-to-all-start = ((f32[16,5,8,256]{3,2,1,0:T(8,128)}), f32[16,5,8,256]{3,2,1,0:T(8,128)S(1)}, u32[]{:S(2)}, u32[]{:S(2)}) async-start(f32[16,5,8,256]{3,2,1,0:T(8,128)} %add.106), calls=%async_computation | async-start | bytes 1310720 | tf_op jit(solution)/shard_map/all_to_all | solution.py:513
  45.5 19.5 %collective-permute-start.9 = (f32[3,2,128,128]{3,2,1,0:T(8,128)S(1)}, f32[3,2,128,128]{3,2,1,0:T(8,128)}, u32[]{:S(2)}, u32[]{:S(2)}) collective-permute-start(f32[3,2,128,128]{3,2,1,0:T(8,128)S(1)} %get-tuple-element.39), channel_id=1, source_target_pairs={{0,16},{32,48},{64,80},{96,112},{128,144},{160,176},{192,208},{224... | collective-permute-start | bytes 1179656 | tf_op jit(solution)/shard_map/ppermute | solution.py:572
  46.8 18.2 %collective-permute-start.10 = (f32[3,2,128,128]{3,2,1,0:T(8,128)S(1)}, f32[3,2,128,128]{3,2,1,0:T(8,128)}, u32[]{:S(2)}, u32[]{:S(2)}) collective-permute-start(f32[3,2,128,128]{3,2,1,0:T(8,128)S(1)} %get-tuple-element.41), channel_id=1, source_target_pairs={{16,32},{48,64},{80,96},{112,128},{144,160},{176,192},{208,224},{3... | collective-permute-start | bytes 1179656 | tf_op jit(solution)/shard_map/ppermute | solution.py:573
  56.1 19.8 %all-to-all-start.1 = ((f32[8,5,8,256]{3,2,1,0:T(8,128)}), f32[8,5,8,256]{3,2,1,0:T(8,128)S(1)}, u32[]{:S(2)}, u32[]{:S(2)}) async-start(f32[8,5,8,256]{3,2,1,0:T(8,128)} %spread.2), calls=%async_computation.1 | async-start | bytes 655360 | tf_op jit(solution)/shard_map/all_to_all | solution.py:513
  66.3 15.6 %collective-permute-start.11 = (f32[2,128,128]{2,1,0:T(8,128)S(1)}, f32[2,128,128]{2,1,0:T(8,128)S(1)}, u32[]{:S(2)}, u32[]{:S(2)}) collective-permute-start(f32[2,128,128]{2,1,0:T(8,128)S(1)} %get-tuple-element.63), channel_id=1, source_target_pairs={{0,1},{2,3},{4,5},{6,7},{8,9},{10,11},{12,13},{14,15},{1,0},{3,2},... | collective-permute-start | bytes 393224 | tf_op jit(solution)/shard_map/ppermute | solution.py:579
  74.0 12.8 %collective-permute-start.12 = (f32[2,128,128]{2,1,0:T(8,128)S(1)}, f32[2,128,128]{2,1,0:T(8,128)S(1)}, u32[]{:S(2)}, u32[]{:S(2)}) collective-permute-start(f32[2,128,128]{2,1,0:T(8,128)S(1)} %get-tuple-element.64), channel_id=1, source_target_pairs={{1,2},{3,4},{5,6},{7,8},{9,10},{11,12},{13,14},{2,1},{4,3},{6,5},{... | collective-permute-start | bytes 393224 | tf_op jit(solution)/shard_map/ppermute | solution.py:580
  76.8 14.3 %all-to-all-start.2 = ((f32[16,4,8,256]{3,2,1,0:T(8,128)}), f32[16,4,8,256]{3,2,1,0:T(8,128)S(1)}, u32[]{:S(2)}, u32[]{:S(2)}) async-start(f32[16,4,8,256]{3,2,1,0:T(8,128)} %get-tuple-element.45), calls=%async_computation.2 | async-start | bytes 1048576 | tf_op jit(solution)/shard_map/all_to_all | solution.py:513
  86.8 7.0 %collective-permute-start.15 = (f32[2,128,128]{2,1,0:T(8,128)S(1)}, f32[2,128,128]{2,1,0:T(8,128)S(1)}, u32[]{:S(2)}, u32[]{:S(2)}) collective-permute-start(f32[2,128,128]{2,1,0:T(8,128)S(1)} %divide_add_fusion.1.refs_4_), channel_id=1, source_target_pairs={{0,1},{2,3},{4,5},{6,7},{8,9},{10,11},{12,13},{14,15},{1,0},{3,2},... | collective-permute-start | bytes 393224 | tf_op jit(solution)/shard_map/ppermute | solution.py:484
  87.4 13.8 %collective-permute-start.14 = (f32[2,128,128]{2,1,0:T(8,128)S(1)}, f32[2,128,128]{2,1,0:T(8,128)S(1)}, u32[]{:S(2)}, u32[]{:S(2)}) collective-permute-start(f32[2,128,128]{2,1,0:T(8,128)S(1)} %divide_add_fusion.1.refs_4_), channel_id=1, source_target_pairs={{1,2},{3,4},{5,6},{7,8},{9,10},{11,12},{13,14},{2,1},{4,3},{6,5},{... | collective-permute-start | bytes 393224 | tf_op jit(solution)/shard_map/ppermute | solution.py:484
  91.1 21.5 %collective-permute-start.13 = (f32[16,4,8,256]{3,2,1,0:T(8,128)S(1)}, f32[16,4,8,256]{3,2,1,0:T(8,128)S(1)}, u32[]{:S(2)}, u32[]{:S(2)}) collective-permute-start(f32[16,4,8,256]{3,2,1,0:T(8,128)S(1)} %all-to-all-done.2.refs_0_), channel_id=1, source_target_pairs={{0,1},{1,0},{2,3},{3,2},{4,5},{5,4},{6,7},{7,6},{8,9},{9,8},{10,11... | collective-permute-start | bytes 1572872 | tf_op jit(solution)/shard_map/ppermute | solution.py:590
  101.2 6.7 %collective-permute-start.17 = (f32[3,2,128,128]{3,2,1,0:T(8,128)S(1)}, f32[3,2,128,128]{3,2,1,0:T(8,128)S(1)}, u32[]{:S(2)}, u32[]{:S(2)}) collective-permute-start(f32[3,2,128,128]{3,2,1,0:T(8,128)S(1)} %pad_maximum_fusion), channel_id=1, source_target_pairs={{0,16},{32,48},{64,80},{96,112},{128,144},{160,176},{192,208},{224... | collective-permute-start | bytes 1179656 | tf_op jit(solution)/shard_map/ppermute | solution.py:486
  101.9 10.6 %collective-permute-start.16 = (f32[3,2,128,128]{3,2,1,0:T(8,128)S(1)}, f32[3,2,128,128]{3,2,1,0:T(8,128)S(1)}, u32[]{:S(2)}, u32[]{:S(2)}) collective-permute-start(f32[3,2,128,128]{3,2,1,0:T(8,128)S(1)} %pad_maximum_fusion), channel_id=1, source_target_pairs={{16,32},{48,64},{80,96},{112,128},{144,160},{176,192},{208,224},{3... | collective-permute-start | bytes 1179656 | tf_op jit(solution)/shard_map/ppermute | solution.py:486
  125.2 17.9 %all-to-all-start.3 = ((f32[16,5,8,256]{3,2,1,0:T(8,128)}), f32[16,5,8,256]{3,2,1,0:T(8,128)S(1)}, u32[]{:S(2)}, u32[]{:S(2)}) async-start(f32[16,5,8,256]{3,2,1,0:T(8,128)} %add.123), calls=%async_computation.3 | async-start | bytes 1310720 | tf_op jit(solution)/shard_map/all_to_all | solution.py:513
  130.6 17.3 %collective-permute-start.19 = (f32[3,2,128,128]{3,2,1,0:T(8,128)S(1)}, f32[3,2,128,128]{3,2,1,0:T(8,128)S(1)}, u32[]{:S(2)}, u32[]{:S(2)}) collective-permute-start(f32[3,2,128,128]{3,2,1,0:T(8,128)S(1)} %get-tuple-element.54), channel_id=1, source_target_pairs={{0,16},{32,48},{64,80},{96,112},{128,144},{160,176},{192,208},{224... | collective-permute-start | bytes 1179656 | tf_op jit(solution)/shard_map/ppermute | solution.py:572
  131.8 16.9 %collective-permute-start.20 = (f32[3,2,128,128]{3,2,1,0:T(8,128)S(1)}, f32[3,2,128,128]{3,2,1,0:T(8,128)}, u32[]{:S(2)}, u32[]{:S(2)}) collective-permute-start(f32[3,2,128,128]{3,2,1,0:T(8,128)S(1)} %get-tuple-element.56), channel_id=1, source_target_pairs={{16,32},{48,64},{80,96},{112,128},{144,160},{176,192},{208,224},{3... | collective-permute-start | bytes 1179656 | tf_op jit(solution)/shard_map/ppermute | solution.py:573
  143.8 14.8 %all-to-all-start.4 = ((f32[8,5,8,256]{3,2,1,0:T(8,128)}), f32[8,5,8,256]{3,2,1,0:T(8,128)S(1)}, u32[]{:S(2)}, u32[]{:S(2)}) async-start(f32[8,5,8,256]{3,2,1,0:T(8,128)} %spread.3), calls=%async_computation.4 | async-start | bytes 655360 | tf_op jit(solution)/shard_map/all_to_all | solution.py:513
  159.4 19.4 %all-to-all-start.5 = ((f32[16,4,8,256]{3,2,1,0:T(8,128)}), f32[16,4,8,256]{3,2,1,0:T(8,128)S(1)}, u32[]{:S(2)}, u32[]{:S(2)}) async-start(f32[16,4,8,256]{3,2,1,0:T(8,128)} %get-tuple-element.58), calls=%async_computation.5 | async-start | bytes 1048576 | tf_op jit(solution)/shard_map/all_to_all | solution.py:513
  165.5 13.3 %collective-permute-start.22 = (f32[2,128,128]{2,1,0:T(8,128)S(1)}, f32[2,128,128]{2,1,0:T(8,128)S(1)}, u32[]{:S(2)}, u32[]{:S(2)}) collective-permute-start(f32[2,128,128]{2,1,0:T(8,128)S(1)} %get-tuple-element.61), channel_id=1, source_target_pairs={{1,2},{3,4},{5,6},{7,8},{9,10},{11,12},{13,14},{2,1},{4,3},{6,5},{... | collective-permute-start | bytes 393224 | tf_op jit(solution)/shard_map/ppermute | solution.py:580
  (9 other events, 25.5 us)
